TPU v7x, 32 devices: a whole 2x2x4 slice. The times are simulated.
32 devices in a mesh: seq: 4 (over y, core), rows: 8 (over z, x).
Axes of the slice: x: 2, y: 2, z: 4, core: 2. Of those that a mesh axis runs over, the one named last changes fastest.
Arguments:
- tokens: bfloat16 [8, 1024, 2048], P('rows', 'seq'), may hold values from -6 to 6
- doc_starts: int32 [8, 1024], P('rows', 'seq'), may hold values 0 or 1
- cotangent: bfloat16 [8, 1024, 2048], P('rows', 'seq'), may hold values from -6 to 6
- norm_first: bfloat16 [2048], replicated, may hold values from 0.5 to 1.5
- norm_second: bfloat16 [2048], replicated, may hold values from 0.5 to 1.5
- w_query: bfloat16 [2048, 2048], P('rows'), may hold values from -0.125 to 0.125
- w_key: bfloat16 [2048, 512], P('rows'), may hold values from -0.125 to 0.125
- w_value: bfloat16 [2048, 512], P('rows'), may hold values from -0.125 to 0.125
- w_out: bfloat16 [2048, 2048], P('rows'), may hold values from -0.75 to 0.75
- w_gate_up: bfloat16 [2, 2048, 8192], P(None, None, 'rows'), may hold values from -0.125 to 0.125
- w_down: bfloat16 [8192, 2048], P('rows'), may hold values from -0.0625 to 0.0625
- query_in: bfloat16 [2048, 8], replicated, may hold values from -0.125 to 0.125
- query_out: bfloat16 [8, 2048], replicated, may hold values from -1 to 1
- key_in: bfloat16 [2048, 8], replicated, may hold values from -0.125 to 0.125
- key_out: bfloat16 [8, 512], replicated, may hold values from -1 to 1
- value_in: bfloat16 [2048, 8], replicated, may hold values from -0.125 to 0.125
- value_out: bfloat16 [8, 512], replicated, may hold values from -1 to 1
- proj_in: bfloat16 [2048, 8], replicated, may hold values from -0.75 to 0.75
- proj_out: bfloat16 [8, 2048], replicated, may hold values from -1 to 1
- map_query: bfloat16 [32, 64, 64], replicated, may hold values from -0.75 to 0.75
- map_key: bfloat16 [8, 64, 64], replicated, may hold values from -0.75 to 0.75
- window_logit: float32 [32], replicated, may hold values from -1 to 3
Outputs:
- block_out: bfloat16 [8, 1024, 2048], P('rows', 'seq')
- grad_tokens: float32 [8, 1024, 2048], P('rows', 'seq')
- grad_norm_first: float32 [2048], P('seq')
- grad_norm_second: float32 [2048], P('seq')
- grad_query_in: float32 [2048, 8], P('seq')
- grad_query_out: float32 [8, 2048], P(None, 'seq')
- grad_key_in: float32 [2048, 8], P('seq')
- grad_key_out: float32 [8, 512], P(None, 'seq')
- grad_value_in: float32 [2048, 8], P('seq')
- grad_value_out: float32 [8, 512], P(None, 'seq')
- grad_proj_in: float32 [2048, 8], P('seq')
- grad_proj_out: float32 [8, 2048], P(None, 'seq')
- grad_map_query: float32 [32, 64, 64], P('seq')
- grad_map_key: float32 [8, 64, 64], P(None, 'seq')
- grad_window_logit: float32 [32], P('seq')
All inputs are finite; a program needn't handle non-finite values. No bound on the sum of `doc_starts` on one device may be relied on, other than what follows from the above.
Results may differ from a plain program's by a relative error of at most 0.025.
Values may be sent and summed in bfloat16 or wider, within the bound.
No kernel may reach another device: no remote copies, remote signals or barrier semaphores. Data moves between devices by JAX's collectives and lax.ppermute only.
A program may use at most 448 MiB of HBM per device.

v0:
```python
import jax
import jax.numpy as jnp
from jax import lax
from jax.sharding import PartitionSpec as P

D = 2048
HEADS = 32
KV_HEADS = 8
HEAD = 64
WINDOW = 64


EPSILON = 1e-05
THETA = 500000.0


def shifted(block, axis, distance):
    devices = range(lax.axis_size(axis))
    route = [(i - distance, i) for i in devices if i - distance in devices]
    return lax.ppermute(block, axis, route)


def prefix(x, axis, join, neutral, backward):
    count = lax.axis_size(axis)
    place = lax.axis_index(axis)
    ahead = count - 1 - place if backward else place
    gathered = jax.tree.map(
        lambda a, kind: lax.all_gather(a.astype(kind), axis),
        x,
        (jnp.bfloat16, jnp.bfloat16, jnp.bfloat16),
    )
    state = jax.tree.map(lambda a, e: jnp.zeros_like(a) + jnp.asarray(e, a.dtype), x, neutral)

    def one(step, state):
        source = count - 1 - step if backward else step
        return join(
            state,
            jax.tree.map(
                lambda a, own: lax.dynamic_index_in_dim(a, source, 0, False).astype(own.dtype),
                gathered,
                x,
            ),
        )

    return lax.fori_loop(0, ahead, one, state)


def rotate(values, places, inverse):
    half_width = HEAD // 2
    inverse_freq = jnp.power(THETA, -(jnp.arange(half_width, dtype=jnp.float32) * 2.0 / HEAD))
    angles = places[:, None] * inverse_freq[None, :]
    cosine = jnp.cos(angles)[:, None, :]
    sine = jnp.sin(angles)[:, None, :]
    if inverse:
        sine = -sine
    first = values[..., :half_width]
    second = values[..., half_width:]
    return jnp.concatenate(
        [first * cosine - second * sine, second * cosine + first * sine], axis=-1
    )


def feature_map(rolled, maps):
    projected = jnp.einsum("thd,hde->the", rolled, maps, preferred_element_type=jnp.float32)
    upper = jax.nn.softmax(projected, axis=-1)
    lower = jax.nn.softmax(-projected, axis=-1)
    return (jnp.concatenate([upper, lower], axis=-1).astype(jnp.bfloat16), upper, lower)


def feature_back(grads, upper, lower, rolled, maps):
    width = upper.shape[-1]
    grad_upper = grads[..., :width]
    grad_lower = grads[..., width:]
    proj_grad = upper * (grad_upper - jnp.sum(grad_upper * upper, axis=-1, keepdims=True))
    proj_grad = proj_grad - lower * (
        grad_lower - jnp.sum(grad_lower * lower, axis=-1, keepdims=True)
    )
    proj_grad = proj_grad.astype(jnp.bfloat16)
    rolled_grad = jnp.einsum("the,hde->thd", proj_grad, maps, preferred_element_type=jnp.float32)
    maps_grad = jnp.einsum("thd,the->hde", rolled, proj_grad, preferred_element_type=jnp.float32)
    return (rolled_grad, maps_grad)


def lowrank(source, full, inner, outer):
    reduced = jnp.dot(source, inner, preferred_element_type=jnp.float32).astype(jnp.bfloat16)
    result = jnp.dot(source, full, preferred_element_type=jnp.float32) + jnp.dot(
        reduced, outer, preferred_element_type=jnp.float32
    )
    return (result, reduced)


def lowrank_back(source, grad_raw, full, inner, outer, reduced):
    grad_low = jnp.einsum("to,ro->tr", grad_raw, outer, preferred_element_type=jnp.float32).astype(
        jnp.bfloat16
    )
    grad_outer = jnp.einsum("tr,to->ro", reduced, grad_raw, preferred_element_type=jnp.float32)
    grad_inner = jnp.einsum("ti,tr->ir", source, grad_low, preferred_element_type=jnp.float32)
    grad_source = jnp.einsum("to,io->ti", grad_raw, full, preferred_element_type=jnp.float32)
    grad_source = grad_source + jnp.einsum(
        "tr,ir->ti", grad_low, inner, preferred_element_type=jnp.float32
    )
    return (grad_source, grad_inner, grad_outer)


def norm_back(grad_normed, normed, inverse_rms, gain):
    scaled = grad_normed * gain
    grad_input = inverse_rms * (scaled - normed * jnp.mean(scaled * normed, axis=-1, keepdims=True))
    return (grad_input, jnp.sum(grad_normed * normed, axis=0))


def combine_states(former, latter):
    keep_rate = 1.0 - latter[2]
    return (
        latter[0] + keep_rate * former[0],
        latter[1] + keep_rate * former[1],
        jnp.maximum(former[2], latter[2]),
    )


def gate_grads(grad_act, gate_vals, up_vals):
    sigmoid_gate = jax.nn.sigmoid(gate_vals)
    grad_gate = grad_act * up_vals * sigmoid_gate * (1.0 + gate_vals * (1.0 - sigmoid_gate))
    grad_up = grad_act * gate_vals * sigmoid_gate
    return jnp.stack([grad_gate, grad_up], axis=1).astype(jnp.bfloat16)


def local(
    tokens,
    doc_starts,
    cotangent,
    norm_first,
    norm_second,
    w_query,
    w_key,
    w_value,
    w_out,
    w_gate_up,
    w_down,
    query_in,
    query_out,
    key_in,
    key_out,
    value_in,
    value_out,
    proj_in,
    proj_out,
    map_query,
    map_key,
    window_logit,
):
    groups = HEADS // KV_HEADS
    feat_width = 2 * HEAD
    kv_width = KV_HEADS * HEAD
    length = tokens.shape[1]
    extended = length + WINDOW
    highest = lax.Precision.HIGHEST
    hidden = tokens[0].astype(jnp.float32)
    grad_out = cotangent[0]
    places_int = lax.axis_index("seq") * length + jnp.arange(length, dtype=jnp.int32)
    resets = jnp.where(places_int == 0, 1, doc_starts[0])
    places = places_int.astype(jnp.float32)
    gain_first = norm_first.astype(jnp.float32)
    gain_second = norm_second.astype(jnp.float32)
    inverse_first = lax.rsqrt(jnp.mean(hidden * hidden, axis=-1, keepdims=True) + EPSILON)
    normed_first = hidden * inverse_first
    inputs = (normed_first * gain_first).astype(jnp.bfloat16)
    query_full, key_full, value_full, output_full = (
        lax.all_gather(w_query, "rows", axis=0, tiled=True),
        lax.all_gather(w_key, "rows", axis=0, tiled=True),
        lax.all_gather(w_value, "rows", axis=0, tiled=True),
        lax.all_gather(w_out, "rows", axis=0, tiled=True),
    )
    query_raw, query_low = lowrank(inputs, query_full, query_in, query_out)
    key_raw, key_low = lowrank(inputs, key_full, key_in, key_out)
    value_raw, value_low = lowrank(inputs, value_full, value_in, value_out)
    queries = rotate(query_raw.reshape(length, HEADS, HEAD), places, False).astype(jnp.bfloat16)
    keys = rotate(key_raw.reshape(length, KV_HEADS, HEAD), places, False).astype(jnp.bfloat16)
    values = value_raw.astype(jnp.bfloat16)
    query_feats, query_upper, query_lower = feature_map(queries, map_query)
    key_feats, key_upper, key_lower = feature_map(keys, map_key)
    keys_flat = keys.reshape(length, kv_width)
    kfeat_flat = key_feats.reshape(length, KV_HEADS * feat_width)
    cut = length - WINDOW
    rim_keys, rim_values, rim_feats, rim_resets = shifted(
        (keys_flat[cut:], values[cut:], kfeat_flat[cut:], resets[cut:].astype(jnp.bfloat16)),
        "seq",
        1,
    )
    ext_keys = jnp.concatenate([rim_keys, keys_flat], axis=0).reshape(extended, KV_HEADS, HEAD)
    ext_values = jnp.concatenate([rim_values, values], axis=0).reshape(extended, KV_HEADS, HEAD)
    ext_feats = jnp.concatenate([rim_feats, kfeat_flat], axis=0).reshape(
        extended, KV_HEADS, feat_width
    )
    ext_resets = jnp.concatenate([rim_resets.astype(jnp.int32), resets], axis=0)
    doc_ids = jnp.cumsum(ext_resets)
    survive = doc_ids[:length] == doc_ids[length - 1]
    keep_feats = ext_feats[:length] * survive.astype(jnp.bfloat16)[:, None, None]
    state_kv = jnp.einsum(
        "jgf,jgd->gfd", keep_feats, ext_values[:length], preferred_element_type=jnp.float32
    )
    state_sum = jnp.sum(keep_feats.astype(jnp.float32), axis=0)
    state_flag = jnp.max(ext_resets[:length]).astype(jnp.float32)
    identity = (jnp.zeros_like(state_kv), jnp.zeros_like(state_sum), jnp.zeros((), jnp.float32))
    carry_kv, carry_sum, carry_flag = prefix(
        (state_kv, state_sum, state_flag), "seq", combine_states, identity, False
    )
    query_rows = queries.reshape(length, KV_HEADS, groups, HEAD)
    qfeat_rows = query_feats.reshape(length, KV_HEADS, groups, feat_width)
    scaling = HEAD ** (-0.5)
    query_ids = doc_ids[WINDOW:]
    distance = (
        jnp.arange(length, dtype=jnp.int32)[:, None]
        + WINDOW
        - jnp.arange(extended, dtype=jnp.int32)[None, :]
    )
    same_doc = query_ids[:, None] == doc_ids[None, :]
    inside = (same_doc & (distance >= 0) & (distance < WINDOW))[:, None, None, :]
    beyond = (same_doc & (distance >= WINDOW))[:, None, None, :]
    fresh = (query_ids == 0).astype(jnp.float32)[:, None, None]
    scores = (
        jnp.einsum("tgrd,jgd->tgrj", query_rows, ext_keys, preferred_element_type=jnp.float32)
        * scaling
    )
    exp_scores = jnp.where(inside, jnp.exp(scores), 0.0)
    soft_probs = exp_scores.astype(jnp.bfloat16)
    soft_part = jnp.einsum(
        "tgrj,jgd->tgrd", soft_probs, ext_values, preferred_element_type=jnp.float32
    )
    linear_w = jnp.where(
        beyond,
        jnp.einsum("tgrf,jgf->tgrj", qfeat_rows, ext_feats, preferred_element_type=jnp.float32),
        0.0,
    )
    values_f = ext_values.astype(jnp.float32)
    ext_feats_f = ext_feats.astype(jnp.float32)
    qfeat_f = qfeat_rows.astype(jnp.float32)
    linear = jnp.einsum("tgrj,jgd->tgrd", linear_w, values_f, precision=highest)
    carried_num = (
        jnp.einsum("tgrf,gfd->tgrd", qfeat_f, carry_kv, precision=highest) * fresh[..., None]
    )
    carried_den = jnp.einsum("tgrf,gf->tgr", qfeat_f, carry_sum, precision=highest) * fresh
    mixing = jax.nn.sigmoid(window_logit).reshape(KV_HEADS, groups)
    linear_sum = jnp.sum(linear_w, axis=-1) + carried_den
    linear_all = linear + carried_num
    totals = jnp.sum(exp_scores, axis=-1) + mixing * linear_sum
    attended = (soft_part + mixing[..., None] * linear_all) / totals[..., None]
    merged = attended.reshape(length, D).astype(jnp.bfloat16)
    attn_out, out_low = lowrank(merged, output_full, proj_in, proj_out)
    residual = hidden + attn_out
    inverse_second = lax.rsqrt(jnp.mean(residual * residual, axis=-1, keepdims=True) + EPSILON)
    normed_second = residual * inverse_second
    second_in = (normed_second * gain_second).astype(jnp.bfloat16)
    gate_up = jnp.einsum(
        "tm,smf->tsf",
        second_in,
        lax.all_gather(w_gate_up, "rows", axis=2, tiled=True),
        preferred_element_type=jnp.float32,
    )
    activation = (jax.nn.silu(gate_up[:, 0]) * gate_up[:, 1]).astype(jnp.bfloat16)
    part = activation
    mlp_out = jnp.dot(
        part, lax.all_gather(w_down, "rows", axis=0, tiled=True), preferred_element_type=jnp.float32
    )
    block_out = (residual + mlp_out).astype(jnp.bfloat16)
    grad_act = jnp.einsum(
        "tm,fm->tf",
        grad_out,
        lax.all_gather(w_down, "rows", axis=0, tiled=True),
        preferred_element_type=jnp.float32,
    )
    grad_gate_up = gate_grads(grad_act, gate_up[:, 0], gate_up[:, 1])
    part = grad_gate_up
    grad_second = jnp.einsum(
        "tsf,smf->tm",
        part,
        lax.all_gather(w_gate_up, "rows", axis=2, tiled=True),
        preferred_element_type=jnp.float32,
    )
    grad_norm_part, grad_gain_two = norm_back(
        grad_second, normed_second, inverse_second, gain_second
    )
    grad_residual = grad_out.astype(jnp.float32) + grad_norm_part
    grad_branch = grad_residual.astype(jnp.bfloat16)
    grad_merged_f, grad_proj_in, grad_proj_out = lowrank_back(
        merged, grad_branch, output_full, proj_in, proj_out, out_low
    )
    grad_merged = grad_merged_f.astype(jnp.bfloat16)
    grad_att = grad_merged.reshape(length, KV_HEADS, groups, HEAD).astype(jnp.float32)
    grad_numer = grad_att / totals[..., None]
    grad_total = -jnp.sum(grad_att * attended, axis=-1) / totals
    grad_soft = grad_numer.astype(jnp.bfloat16)
    grad_probs = jnp.einsum(
        "tgrd,jgd->tgrj", grad_soft, ext_values, preferred_element_type=jnp.float32
    )
    grad_scores = ((grad_probs + grad_total[..., None]) * exp_scores).astype(jnp.bfloat16)
    grad_queries = (
        jnp.einsum("tgrj,jgd->tgrd", grad_scores, ext_keys, preferred_element_type=jnp.float32)
        * scaling
    )
    grad_keys = (
        jnp.einsum("tgrj,tgrd->jgd", grad_scores, query_rows, preferred_element_type=jnp.float32)
        * scaling
    )
    grad_values = jnp.einsum(
        "tgrj,tgrd->jgd", soft_probs, grad_soft, preferred_element_type=jnp.float32
    )
    grad_linear = mixing[..., None] * grad_numer
    mixed_total = mixing * grad_total
    grad_lin_w = jnp.where(
        beyond,
        jnp.einsum("tgrd,jgd->tgrj", grad_linear, values_f, precision=highest)
        + mixed_total[..., None],
        0.0,
    )
    grad_values = grad_values + jnp.einsum(
        "tgrj,tgrd->jgd", linear_w, grad_linear, precision=highest
    )
    grad_qfeat = jnp.einsum("tgrj,jgf->tgrf", grad_lin_w, ext_feats_f, precision=highest)
    grad_kfeat = jnp.einsum("tgrj,tgrf->jgf", grad_lin_w, qfeat_f, precision=highest)
    carry_grad = (
        jnp.einsum("tgrd,gfd->tgrf", grad_linear, carry_kv, precision=highest)
        + mixed_total[..., None] * carry_sum[None, :, None, :]
    )
    grad_qfeat = grad_qfeat + fresh[..., None] * carry_grad
    fresh_feats = qfeat_f * fresh[..., None]
    local_kv = jnp.einsum("tgrf,tgrd->gfd", fresh_feats, grad_linear, precision=highest)
    local_sum = jnp.einsum("tgrf,tgr->gf", fresh_feats, mixed_total, precision=highest)
    mixing_grad = jnp.sum(grad_numer * linear_all, axis=(0, 3)) + jnp.sum(
        grad_total * linear_sum, axis=0
    )
    grad_logit = (mixing_grad * mixing * (1.0 - mixing)).reshape(HEADS)
    back_kv, back_sum, back_flag = prefix(
        (local_kv, local_sum, state_flag), "seq", combine_states, identity, True
    )
    survive_f = survive.astype(jnp.float32)[:, None, None]
    grad_kfeat = grad_kfeat.at[:length].add(
        survive_f
        * (
            jnp.einsum("jgd,gfd->jgf", values_f[:length], back_kv, precision=highest)
            + back_sum[None]
        )
    )
    grad_values = grad_values.at[:length].add(
        survive_f * jnp.einsum("jgf,gfd->jgd", ext_feats_f[:length], back_kv, precision=highest)
    )
    from_next = (
        shifted(
            grad_keys[:WINDOW].reshape(WINDOW, kv_width).astype(jnp.bfloat16), "seq", -1
        ).astype(jnp.float32),
        shifted(
            grad_values[:WINDOW].reshape(WINDOW, kv_width).astype(jnp.bfloat16), "seq", -1
        ).astype(jnp.float32),
        shifted(
            grad_kfeat[:WINDOW].reshape(WINDOW, KV_HEADS * feat_width).astype(jnp.bfloat16),
            "seq",
            -1,
        ).astype(jnp.float32),
    )
    tail_pad = ((cut, 0), (0, 0))
    own_key_grad = grad_keys[WINDOW:].reshape(length, kv_width) + jnp.pad(from_next[0], tail_pad)
    own_value_grad = grad_values[WINDOW:].reshape(length, kv_width) + jnp.pad(
        from_next[1], tail_pad
    )
    own_kfeat_grad = grad_kfeat[WINDOW:].reshape(length, KV_HEADS * feat_width) + jnp.pad(
        from_next[2], tail_pad
    )
    key_rolled_grad, grad_map_key = feature_back(
        own_kfeat_grad.reshape(length, KV_HEADS, feat_width), key_upper, key_lower, keys, map_key
    )
    query_rolled_grad, grad_map_query = feature_back(
        grad_qfeat.reshape(length, HEADS, feat_width), query_upper, query_lower, queries, map_query
    )
    key_total = own_key_grad.reshape(length, KV_HEADS, HEAD) + key_rolled_grad
    query_total = grad_queries.reshape(length, HEADS, HEAD) + query_rolled_grad
    grad_raw_query = rotate(query_total, places, True).reshape(length, D).astype(jnp.bfloat16)
    grad_raw_key = rotate(key_total, places, True).reshape(length, kv_width).astype(jnp.bfloat16)
    grad_raw_value = own_value_grad.astype(jnp.bfloat16)
    query_source, grad_query_in, grad_query_out = lowrank_back(
        inputs, grad_raw_query, query_full, query_in, query_out, query_low
    )
    key_source, grad_key_in, grad_key_out = lowrank_back(
        inputs, grad_raw_key, key_full, key_in, key_out, key_low
    )
    value_source, grad_value_in, grad_value_out = lowrank_back(
        inputs, grad_raw_value, value_full, value_in, value_out, value_low
    )
    grad_inputs = query_source + key_source + value_source
    grad_first_part, grad_gain_one = norm_back(grad_inputs, normed_first, inverse_first, gain_first)
    grad_tokens = grad_residual + grad_first_part
    trained = (
        grad_gain_one,
        grad_gain_two,
        grad_query_in,
        grad_query_out,
        grad_key_in,
        grad_key_out,
        grad_value_in,
        grad_value_out,
        grad_proj_in,
        grad_proj_out,
        grad_map_query,
        grad_map_key,
        grad_logit,
    )
    shares = (
        lax.psum_scatter(
            trained[0].astype(jnp.bfloat16), "seq", scatter_dimension=0, tiled=True
        ).astype(jnp.float32),
        lax.psum_scatter(
            trained[1].astype(jnp.bfloat16), "seq", scatter_dimension=0, tiled=True
        ).astype(jnp.float32),
        lax.psum_scatter(
            trained[2].astype(jnp.bfloat16), "seq", scatter_dimension=0, tiled=True
        ).astype(jnp.float32),
        lax.psum_scatter(
            trained[3].astype(jnp.bfloat16), "seq", scatter_dimension=1, tiled=True
        ).astype(jnp.float32),
        lax.psum_scatter(
            trained[4].astype(jnp.bfloat16), "seq", scatter_dimension=0, tiled=True
        ).astype(jnp.float32),
        lax.psum_scatter(
            trained[5].astype(jnp.bfloat16), "seq", scatter_dimension=1, tiled=True
        ).astype(jnp.float32),
        lax.psum_scatter(
            trained[6].astype(jnp.bfloat16), "seq", scatter_dimension=0, tiled=True
        ).astype(jnp.float32),
        lax.psum_scatter(
            trained[7].astype(jnp.bfloat16), "seq", scatter_dimension=1, tiled=True
        ).astype(jnp.float32),
        lax.psum_scatter(
            trained[8].astype(jnp.bfloat16), "seq", scatter_dimension=0, tiled=True
        ).astype(jnp.float32),
        lax.psum_scatter(
            trained[9].astype(jnp.bfloat16), "seq", scatter_dimension=1, tiled=True
        ).astype(jnp.float32),
        lax.psum_scatter(
            trained[10].astype(jnp.bfloat16), "seq", scatter_dimension=0, tiled=True
        ).astype(jnp.float32),
        lax.psum_scatter(
            trained[11].astype(jnp.bfloat16), "seq", scatter_dimension=1, tiled=True
        ).astype(jnp.float32),
        lax.psum_scatter(
            trained[12].astype(jnp.bfloat16), "seq", scatter_dimension=0, tiled=True
        ).astype(jnp.float32),
    )
    summed = (
        lax.psum(shares[0].astype(jnp.bfloat16), "rows").astype(jnp.float32),
        lax.psum(shares[1].astype(jnp.bfloat16), "rows").astype(jnp.float32),
        lax.psum(shares[2].astype(jnp.bfloat16), "rows").astype(jnp.float32),
        lax.psum(shares[3].astype(jnp.bfloat16), "rows").astype(jnp.float32),
        lax.psum(shares[4].astype(jnp.bfloat16), "rows").astype(jnp.float32),
        lax.psum(shares[5].astype(jnp.bfloat16), "rows").astype(jnp.float32),
        lax.psum(shares[6].astype(jnp.bfloat16), "rows").astype(jnp.float32),
        lax.psum(shares[7].astype(jnp.bfloat16), "rows").astype(jnp.float32),
        lax.psum(shares[8].astype(jnp.bfloat16), "rows").astype(jnp.float32),
        lax.psum(shares[9].astype(jnp.bfloat16), "rows").astype(jnp.float32),
        lax.psum(shares[10].astype(jnp.bfloat16), "rows").astype(jnp.float32),
        lax.psum(shares[11].astype(jnp.bfloat16), "rows").astype(jnp.float32),
        lax.psum(shares[12].astype(jnp.bfloat16), "rows").astype(jnp.float32),
    )
    return (
        block_out[None],
        grad_tokens[None],
        summed[0],
        summed[1],
        summed[2],
        summed[3],
        summed[4],
        summed[5],
        summed[6],
        summed[7],
        summed[8],
        summed[9],
        summed[10],
        summed[11],
        summed[12],
    )


def solution(mesh):
    placed = (
        P("rows", "seq", None),
        P("rows", "seq"),
        P("rows", "seq", None),
        P(),
        P(),
        P("rows", None),
        P("rows", None),
        P("rows", None),
        P("rows", None),
        P(None, None, "rows"),
        P("rows", None),
        P(),
        P(),
        P(),
        P(),
        P(),
        P(),
        P(),
        P(),
        P(),
        P(),
        P(),
    )
    return jax.shard_map(
        local,
        mesh=mesh,
        in_specs=placed,
        out_specs=(
            P("rows", "seq", None),
            P("rows", "seq", None),
            P("seq"),
            P("seq"),
            P("seq", None),
            P(None, "seq"),
            P("seq", None),
            P(None, "seq"),
            P("seq", None),
            P(None, "seq"),
            P("seq", None),
            P(None, "seq"),
            P("seq", None, None),
            P(None, "seq", None),
            P("seq"),
        ),
        check_vma=False,
    )
```

profile of v0, /device:TPU:0, one launch (start us, length us, event | category | flops | bytes accessed | tf_op | source)
XLA Modules:
  0.0 2863.9 jit_solution(1911513040486509724)
XLA Ops:
  21.8 8.8 all-reduce.4
  34.7 27.6 all-gather.12.cloned.1.call-done
  67.8 44.5 %all-gather.10.cloned.1.call-done = bf16[2048,512]{1,0:T(8,128)(2,1)} async-done(((bf16[256,512]{1,0:T(8,128)(2,1)}), bf16[2048,512]{1,0:T(8,128)(2,1)}) %all-gather.10.cloned.1.call-update) | async-done | bytes 2097168 | tf_op jit(solution)/shard_map/all_gather | solution.py:170
  125.1 8.1 all_gather.60
  134.4 7.7 all-gather
  142.5 95.4 %all-gather.14.cloned.1.call-done = bf16[2048,2048]{1,0:T(8,128)(2,1)} async-done(((bf16[256,2048]{1,0:T(8,128)(2,1)}), bf16[2048,2048]{1,0:T(8,128)(2,1)}) %all-gather.14.cloned.1.call-update) | async-done | bytes 8388624 | tf_op jit(solution)/shard_map/all_gather | solution.py:168
  289.2 73.8 %all-gather.16.cloned.1.call-done = bf16[2048,2048]{1,0:T(8,128)(2,1)} async-done(((bf16[256,2048]{1,0:T(8,128)(2,1)}), bf16[2048,2048]{1,0:T(8,128)(2,1)}) %all-gather.16.cloned.1.call-update) | async-done | bytes 8388624 | tf_op jit(solution)/shard_map/all_gather | solution.py:171
  363.0 6.1 fusion.226
  371.0 1258.5 %all-gather.18.cloned.1.call-done = bf16[2,2048,8192]{2,1,0:T(8,128)(2,1)} async-done(((bf16[2,2048,1024]{2,1,0:T(8,128)(2,1)}), bf16[2,2048,8192]{2,1,0:T(8,128)(2,1)}) %all-gather.18.cloned.1.call-update) | async-done | bytes 67108880 | tf_op jit(solution)/shard_map/all_gather | solution.py:256
  1629.5 33.2 %fusion.134 = f32[256,2,8192]{2,0,1:T(8,128)} fusion(bf16[2,2048,8192]{2,1,0:T(8,128)(2,1)} %all-gather.18.cloned.1.call-done, f32[256,2048]{1,0:T(8,128)} %get-tuple-element.344, f32[2048]{0:T(1024)S(1)} %convert_element_type.354, f32[256]{0:T(256)S(1)} %add_rsqrt_fusion), kind=kOutput, calls=%fused_computation.180 | convolution fusion | flops 17181442048 | bytes 85992448 | tf_op jit(solution)/shard_map/tm,smf->tsf/dot_general | solution.py:253
  1662.7 605.9 %all-gather.20.cloned.1.call-done = bf16[8192,2048]{1,0:T(8,128)(2,1)} async-done(((bf16[1024,2048]{1,0:T(8,128)(2,1)}), bf16[8192,2048]{1,0:T(8,128)(2,1)}) %all-gather.20.cloned.1.call-update) | async-done | bytes 33554448 | tf_op jit(solution)/shard_map/all_gather | solution.py:262
  2268.6 22.5 fusion.43
  2291.1 30.5 %multiply_reduce_fusion = (bf16[2048]{0:T(1024)(128)(2,1)}, f32[256]{0:T(256)}, f32[256,2048]{1,0:T(8,128)}) fusion(f32[256,2048]{1,0:T(8,128)} %get-tuple-element.344, f32[256]{0:T(256)S(1)} %add_rsqrt_fusion, f32[2048]{0:T(1024)S(1)} %convert_element_type.354, bf16[2,2048,8192]{2,1,0:T(8,128)(2,1)} %all-gather.18.cloned.1.call-done, ...), kind=kOutput, calls=%fused_computation.107 | convolution fusion | flops 17187207168 | bytes 79706112 | tf_op jit(solution)/shard_map/tsf,smf->tm/dot_general | solution.py:273
  2336.7 9.7 fusion.88
  2346.4 7.0 fusion.90
  2377.3 10.8 fusion.16
  2388.1 15.3 fusion.38
  2412.5 8.4 bitcast_add_fusion.3
  2425.8 8.8 all-gather.1
  2458.7 11.9 fusion.113
  2496.2 7.1 fusion.100
  2509.4 21.7 fusion.57
  2541.1 7.6 all-reduce.9
  2552.0 18.2 reduce-scatter.17.cloned.1.call-done
  2570.3 21.8 reduce-scatter.23.cloned.1.call-done
  2592.1 21.8 reduce-scatter.25.cloned.1.call-done
  2613.8 21.8 reduce-scatter.21.cloned.1.call-done
  2635.6 21.8 reduce-scatter.19.cloned.1.call-done
  2657.4 21.9 reduce-scatter.29.cloned.1.call-done
  2679.4 24.1 reduce-scatter.27.cloned.1.call-done
  2707.3 75.2 %all-reduce.15.cloned.1.call-done = (bf16[512]{0:T(512)(128)(2,1)}, bf16[512]{0:T(512)(128)(2,1)}, bf16[512,8]{0,1:T(8,128)(2,1)}, bf16[8,512]{1,0:T(8,128)(2,1)...) async-done(((bf16[512]{0:T(512)(128)(2,1)}, ...) | async-done | bytes 71712 | tf_op jit(solution)/shard_map/psum | solution.py:447
  2797.6 57.4 %all-reduce.13.cloned.1.call-done = bf16[8,64,64]{2,1,0:T(8,128)(2,1)} async-done(((bf16[8,64,64]{2,1,0:T(8,128)(2,1)}), bf16[8,64,64]{2,1,0:T(8,128)(2,1)}) %all-reduce.13.cloned.1.call-update) | async-done | bytes 65552 | tf_op jit(solution)/shard_map/psum | solution.py:457
  (475 shorter events, 233.6 us)
Async XLA Ops:
  7.2 240.8 %copy-start = (bf16[32,64,64]{2,1,0:T(8,128)(2,1)S(1)}, bf16[32,64,64]{2,1,0:T(8,128)(2,1)}, u32[]{:S(2)}) copy-start(bf16[32,64,64]{2,1,0:T(8,128)(2,1)} %param.49) | copy-start | bytes 786436
  7.2 55.1 %all-gather.12.cloned.1.call-start = ((), (), s32[]{:S(2)}) async-start(), calls=%async_computation.11 | async-start | bytes 2359296 | tf_op jit(solution)/shard_map/all_gather | solution.py:169
  7.9 104.3 %all-gather.10.cloned.1.call-start = ((), (), s32[]{:S(2)}) async-start(), calls=%async_computation.10 | async-start | bytes 2359296 | tf_op jit(solution)/shard_map/all_gather | solution.py:170
  8.7 229.2 %all-gather.14.cloned.1.call-start = ((), (), s32[]{:S(2)}) async-start(), calls=%async_computation.12 | async-start | bytes 9437184 | tf_op jit(solution)/shard_map/all_gather | solution.py:168
  9.4 353.6 %all-gather.16.cloned.1.call-start = ((), (), s32[]{:S(2)}) async-start(), calls=%async_computation.13 | async-start | bytes 9437184 | tf_op jit(solution)/shard_map/all_gather | solution.py:171
  10.0 1619.5 %all-gather.18.cloned.1.call-start = ((), (), s32[]{:S(2)}) async-start(), calls=%async_computation.14 | async-start | bytes 75497472 | tf_op jit(solution)/shard_map/all_gather | solution.py:256
  10.6 2258.0 %all-gather.20.cloned.1.call-start = ((), (), s32[]{:S(2)}) async-start(), calls=%async_computation.15 | async-start | bytes 37748736 | tf_op jit(solution)/shard_map/all_gather | solution.py:262
  11.2 2521.7 %reduce-scatter.33.cloned.1.call-start = ((), (), s32[]{:S(2)}) async-start(), calls=%async_computation.26 | async-start | bytes 163840
  11.4 7.6 collective-permute-start.1
  16.0 221.8 %copy-start.1 = (bf16[256,2048]{1,0:T(8,128)(2,1)}, bf16[256,2048]{1,0:T(8,128)(2,1)S(1)}, u32[]{:S(2)}) copy-start(bf16[256,2048]{1,0:T(8,128)(2,1)S(1)} %fusion.60) | copy-start | bytes 3145732
  65.0 51.3 %copy-start.52 = (bf16[256,8,32]{0,2,1:T(8,128)(2,1)}, bf16[256,8,32]{0,2,1:T(8,128)(2,1)S(1)}, u32[]{:S(2)}) copy-start(bf16[256,8,32]{0,2,1:T(8,128)(2,1)S(1)} %get-tuple-element.318) | copy-start | bytes 393220
  65.0 51.3 %copy-start.55 = (bf16[256,8,32]{0,2,1:T(8,128)(2,1)}, bf16[256,8,32]{0,2,1:T(8,128)(2,1)S(1)}, u32[]{:S(2)}) copy-start(bf16[256,8,32]{0,2,1:T(8,128)(2,1)S(1)} %get-tuple-element.319) | copy-start | bytes 393220
  65.7 204.8 %collective-permute-start.2 = (bf16[64,512]{0,1:T(8,128)(2,1)}, bf16[64,512]{0,1:T(8,128)(2,1)}, u32[]{:S(2)}, u32[]{:S(2)}) collective-permute-start(bf16[64,512]{0,1:T(8,128)(2,1)} %bitcast.15), channel_id=1, source_target_pairs={{0,8},{8,16},{16,24},{1,9},{9,17},{17,25},{2,10},{10,18},{18,26},{... | collective-permute-start | bytes 196616 | tf_op jit(solution)/shard_map/ppermute | solution.py:20
  114.6 8.7 collective-permute-start
  119.2 5.5 collective-permute-start.3
  142.5 120.9 %copy-start.69 = (f32[8,128]{1,0:T(8,128)}, f32[8,128]{1,0:T(8,128)S(1)}, u32[]{:S(2)}) copy-start(f32[8,128]{1,0:T(8,128)S(1)} %get-tuple-element.212) | copy-start | bytes 12292
  289.2 79.9 %copy-start.95 = (bf16[256,8]{0,1:T(8,128)(2,1)}, bf16[256,8]{0,1:T(8,128)(2,1)S(1)}, u32[]{:S(2)}) copy-start(bf16[256,8]{0,1:T(8,128)(2,1)S(1)} %convolution_convert_fusion.14) | copy-start | bytes 12292
  2423.2 59.0 %collective-permute-start.4 = (bf16[64,512]{0,1:T(8,128)(2,1)}, bf16[64,512]{0,1:T(8,128)(2,1)}, u32[]{:S(2)}, u32[]{:S(2)}) collective-permute-start(bf16[64,512]{0,1:T(8,128)(2,1)} %bitcast.75), channel_id=1, source_target_pairs={{8,0},{16,8},{24,16},{9,1},{17,9},{25,17},{10,2},{18,10},{26,18},{... | collective-permute-start | bytes 196616 | tf_op jit(solution)/shard_map/ppermute | solution.py:20
  2457.3 26.9 collective-permute-start.5
  2471.3 9.5 collective-permute-start.6
  2482.2 68.4 %reduce-scatter.31.cloned.1.call-start = ((), (), s32[]{:S(2)}) async-start(), calls=%async_computation.25 | async-start | bytes 163840
  2491.8 60.3 %reduce-scatter.15.cloned.1.call-start = ((), (), s32[]{:S(2)}) async-start(), calls=%async_computation.16 | async-start | bytes 40960 | tf_op jit(solution)/shard_map/reduce_scatter | solution.py:412
  2492.7 77.6 %reduce-scatter.17.cloned.1.call-start = ((), (), s32[]{:S(2)}) async-start(), calls=%async_computation.17 | async-start | bytes 40960 | tf_op jit(solution)/shard_map/reduce_scatter | solution.py:415
  2495.0 97.0 %reduce-scatter.23.cloned.1.call-start = ((), (), s32[]{:S(2)}) async-start(), calls=%async_computation.20 | async-start | bytes 40960 | tf_op jit(solution)/shard_map/reduce_scatter | solution.py:430
  2496.2 117.7 %reduce-scatter.25.cloned.1.call-start = ((), (), s32[]{:S(2)}) async-start(), calls=%async_computation.21 | async-start | bytes 40960 | tf_op jit(solution)/shard_map/reduce_scatter | solution.py:433
  2503.5 132.1 %reduce-scatter.21.cloned.1.call-start = ((), (), s32[]{:S(2)}) async-start(), calls=%async_computation.19 | async-start | bytes 40960 | tf_op jit(solution)/shard_map/reduce_scatter | solution.py:424
  2504.6 152.8 %reduce-scatter.19.cloned.1.call-start = ((), (), s32[]{:S(2)}) async-start(), calls=%async_computation.18 | async-start | bytes 40960 | tf_op jit(solution)/shard_map/reduce_scatter | solution.py:418
  2505.7 173.6 %reduce-scatter.29.cloned.1.call-start = ((), (), s32[]{:S(2)}) async-start(), calls=%async_computation.24 | async-start | bytes 163840 | tf_op jit(solution)/shard_map/reduce_scatter | solution.py:439
  2508.5 195.0 %reduce-scatter.27.cloned.1.call-start = ((), (), s32[]{:S(2)}) async-start(), calls=%async_computation.22 | async-start | bytes 655360 | tf_op jit(solution)/shard_map/reduce_scatter | solution.py:436
  2509.1 273.3 %all-reduce.15.cloned.1.call-start = ((), (), s32[]{:S(2)}) async-start(), calls=%async_computation.27 | async-start | bytes 177152 | tf_op jit(solution)/shard_map/psum | solution.py:447
  2538.5 165.0 %copy-start.6 = (f32[256,2048]{1,0:T(8,128)S(1)}, f32[256,2048]{1,0:T(8,128)}, u32[]{:S(2)}) copy-start(f32[256,2048]{1,0:T(8,128)} %copy-done.4) | copy-start | bytes 6291460
  2679.3 175.6 %all-reduce.13.cloned.1.call-start = ((), (), s32[]{:S(2)}) async-start(), calls=%async_computation.23 | async-start | bytes 262144 | tf_op jit(solution)/shard_map/psum | solution.py:457
  (113 other events, 779.1 us)
Sparse Core Ops, SparseCore 0:
  10.2 52.1 all-gather.11
  64.5 47.7 all-gather.9
  114.4 123.4 all-gather.13
  239.8 123.1 all-gather.15
  364.4 1265.0 all-gather.17
  1630.9 637.6 all-gather.19
  2482.4 21.4 reduce-scatter.32
  2506.4 19.6 reduce-scatter.30
  2529.1 19.3 reduce-scatter.14
  2550.9 19.3 reduce-scatter.16
  2572.7 19.3 reduce-scatter.22
  2594.4 19.3 reduce-scatter.24
  2616.2 19.3 reduce-scatter.20
  2638.0 19.3 reduce-scatter.18
  2659.7 19.5 reduce-scatter.28
  2681.8 21.6 reduce-scatter.26
  2709.5 72.9 all-reduce.14
  2785.6 69.2 all-reduce.12
where the time goes:
time: 2870 us; the launch traced here: 2860 us
  waiting for transfers between devices  2390 us (83%)
  matrix products  285 us (10%)
  other arithmetic  54.2 us (2%)
  local copies, waits for them, and re-layouts  48.8 us (2%)
  blocking collectives  46.2 us (2%)
    all_gather x1, waiting for transfers between devices, local(): lax.all_gather(w_gate_up, 'rows', axis=2, tiled=True)  1260 us
    all_gather x1, waiting for transfers between devices, local(): lax.all_gather(w_down, 'rows', axis=0, tiled=True)  606 us
    all_gather x1, waiting for transfers between devices, local(): lax.all_gather(w_query, 'rows', axis=0, tiled=True)  95.4 us
    psum x1, waiting for transfers between devices, local(): lax.psum(shares[0].astype(jnp.bfloat16), 'rows').astype(jnp.float32)  75.2 us
    all_gather x1, waiting for transfers between devices, local(): lax.all_gather(w_out, 'rows', axis=0, tiled=True)  73.8 us
  transfers between devices with their start and end apart: 25, of which 16 were waited for; matrix products, arithmetic and copies ran while one was open for 8% of the time, Pallas kernels for 0%

commit v1 on v0

v1 whole, which is shorter than its diff:
```python
import functools

import jax
import jax.numpy as jnp
from jax import lax
from jax.experimental import pallas as pl
from jax.experimental.pallas import tpu as pltpu
from jax.sharding import PartitionSpec as P

D = 2048
HEADS = 32
KV_HEADS = 8
HEAD = 64
WINDOW = 64
KVD = KV_HEADS * HEAD
GROUPS = HEADS // KV_HEADS
QKV = D + 2 * KVD
WIDE = GROUPS * HEAD
FEAT = 2 * HEAD
LOW = 128
STATE = 80
SCALE = HEAD ** (-0.5)

EPSILON = 1e-05
THETA = 500000.0

Z_SIZE = 4
CORES = 2
F32 = jnp.float32
BF16 = jnp.bfloat16


def dot_nn(a, b):
    return jnp.dot(a, b, preferred_element_type=F32)


def dot_nt(a, b):
    return lax.dot_general(a, b, (((1,), (1,)), ((), ())), preferred_element_type=F32)


def dot_tn(a, b):
    return lax.dot_general(a, b, (((0,), (0,)), ((), ())), preferred_element_type=F32)


def lane(shape):
    return lax.broadcasted_iota(jnp.int32, shape, 1)


def row(shape):
    return lax.broadcasted_iota(jnp.int32, shape, 0)


def low_half(shape):
    return lane(shape) % FEAT < HEAD


def turn(x, cosine, sine):
    width = x.shape[1]
    first = lane(x.shape) % HEAD < HEAD // 2
    swapped = jnp.where(
        first, pltpu.roll(x, width - HEAD // 2, 1), pltpu.roll(x, HEAD // 2, 1)
    )
    return x * cosine + swapped * sine


def halves_softmax(u):
    lo = low_half(u.shape)
    top = jnp.where(
        lo,
        jnp.max(jnp.where(lo, u, -jnp.inf), axis=1, keepdims=True),
        jnp.max(jnp.where(lo, -jnp.inf, u), axis=1, keepdims=True),
    )
    e = jnp.exp(u - top)
    total = jnp.where(
        lo,
        jnp.sum(jnp.where(lo, e, 0.0), axis=1, keepdims=True),
        jnp.sum(jnp.where(lo, 0.0, e), axis=1, keepdims=True),
    )
    return e / total


def halves_softmax_back(f, g):
    lo = low_half(f.shape)
    t = f * g
    total = jnp.where(
        lo,
        jnp.sum(jnp.where(lo, t, 0.0), axis=1, keepdims=True),
        jnp.sum(jnp.where(lo, 0.0, t), axis=1, keepdims=True),
    )
    v = f * (g - total)
    return v - pltpu.roll(v, HEAD, 1), t


def pair_features(x, maps):
    u = dot_nn(x, maps)
    return jnp.concatenate(
        [halves_softmax(u[:, :FEAT]), halves_softmax(u[:, FEAT:])], axis=1
    )


def same_head(size):
    shape = (GROUPS * size, WIDE)
    return (row(shape) // size == lane(shape) // HEAD).astype(F32)


def diagonal(tile, mask):
    wide = jnp.concatenate([tile, tile], axis=1)
    return (jnp.concatenate([wide] * GROUPS, axis=0) * mask).astype(BF16)


def diagonal_pair(tile):
    none = jnp.zeros_like(tile)
    return jnp.concatenate(
        [jnp.concatenate([tile, none], axis=1), jnp.concatenate([none, tile], axis=1)], axis=0
    )


def both_halves(kv):
    kv = kv.astype(F32)
    lo = low_half(kv.shape)
    other = pltpu.roll(kv, HEAD, 1)
    return jnp.where(lo, kv, other), jnp.where(lo, other, kv)


def fold_heads(r, mask):
    r = r * mask
    r = r[:64] + r[64:128] + r[128:192] + r[192:]
    r = r[:, :FEAT] + r[:, FEAT:]
    return r + pltpu.roll(r, HEAD, 1)


def fold_pair(r, size):
    return r[:size, :FEAT] + r[size:, FEAT:]


def project_kernel(
    x_ref, low_ref, w_ref, p_ref, cos_ref, sin_ref, maps_ref, survive_ref,
    q_ref, kv_ref, kf_ref, rim_ref, near_ref, full_ref, keys_ref,
):
    n = pl.program_id(0)
    length = x_ref.shape[0]
    q_steps = D // WIDE
    k_steps = KVD // WIDE
    raw = dot_nn(x_ref[...], w_ref[...]) + dot_nn(low_ref[...], p_ref[...])

    @pl.when(n < q_steps)
    def _():
        q_ref[...] = turn(raw, cos_ref[...], sin_ref[...]).astype(BF16)

    for i in range(k_steps):

        @pl.when(n == q_steps + i)
        def _():
            keys = turn(raw, cos_ref[...], sin_ref[...]).astype(BF16)
            keys_ref[i] = keys
            for p in range(WIDE // FEAT):
                at = (i * GROUPS + 2 * p) * FEAT
                feats = pair_features(keys[:, p * FEAT : (p + 1) * FEAT], maps_ref[2 * i + p])
                kf_ref[:, at : at + 2 * FEAT] = feats.astype(BF16)

        @pl.when(n == q_steps + k_steps + i)
        def _():
            survive = survive_ref[...]
            lo = low_half((length, FEAT))
            for h in range(GROUPS):
                p = h // 2
                k2 = keys_ref[i][:, p * FEAT : (p + 1) * FEAT].astype(F32)
                v2 = raw[:, p * FEAT : (p + 1) * FEAT].astype(BF16).astype(F32)
                if h % 2:
                    k2 = pltpu.roll(k2, HEAD, 1)
                    v_low = pltpu.roll(v2, HEAD, 1)
                else:
                    v_low = v2
                    v2 = pltpu.roll(v2, HEAD, 1)
                g = i * GROUPS + h
                at = g * FEAT
                kv_ref[:, at : at + FEAT] = jnp.where(lo, k2, v2).astype(BF16)
                ones = jnp.where(lane((length, FEAT)) < HEAD + 8, 1.0, 0.0)
                v_one = jnp.where(lo, v_low, ones).astype(BF16)
                feats = (kf_ref[:, at : at + FEAT].astype(F32) * survive).astype(BF16)
                cut = length - WINDOW
                head = dot_tn(v_one[:cut], feats[:cut])
                tail = dot_tn(v_one[cut:], feats[cut:])
                near_ref[g] = head[:STATE].astype(BF16)
                full_ref[g] = (head + tail)[:STATE].astype(BF16)

    @pl.when(n == pl.num_programs(0) - 1)
    def _():
        cut = length - WINDOW
        rim_ref[:, : KV_HEADS * FEAT] = kv_ref[cut:, :]
        rim_ref[:, KV_HEADS * FEAT :] = kf_ref[cut:, :]


def project(x, low, w, p, cosine, sine, maps, survive):
    length = x.shape[0]
    steps = QKV // WIDE
    whole = lambda a: pl.BlockSpec(a.shape, lambda n: (0,) * a.ndim)
    q_last = D // WIDE - 1
    shapes = (
        jax.ShapeDtypeStruct((length, D), BF16),
        jax.ShapeDtypeStruct((length, KV_HEADS * FEAT), BF16),
        jax.ShapeDtypeStruct((length, KV_HEADS * FEAT), BF16),
        jax.ShapeDtypeStruct((WINDOW, 2 * KV_HEADS * FEAT), BF16),
        jax.ShapeDtypeStruct((KV_HEADS, STATE, FEAT), BF16),
        jax.ShapeDtypeStruct((KV_HEADS, STATE, FEAT), BF16),
    )
    return pl.pallas_call(
        project_kernel,
        grid=(steps,),
        in_specs=[
            whole(x), whole(low),
            pl.BlockSpec((D, WIDE), lambda n: (0, n)),
            pl.BlockSpec((LOW, WIDE), lambda n: (0, n)),
            whole(cosine), whole(sine), whole(maps), whole(survive),
        ],
        out_specs=[pl.BlockSpec((length, WIDE), lambda n: (0, jnp.minimum(n, q_last)))]
        + [whole(s) for s in shapes[1:]],
        out_shape=shapes,
        scratch_shapes=[pltpu.VMEM((KVD // WIDE, length, WIDE), BF16)],
        compiler_params=pltpu.CompilerParams(vmem_limit_bytes=40 << 20),
        cost_estimate=pl.CostEstimate(
            flops=2 * length * D * QKV, bytes_accessed=2 * D * QKV, transcendentals=0
        ),
        name="project",
    )(x, low, w, p, cosine, sine, maps, survive)


def features_kernel(q_ref, maps_ref, out_ref):
    for p in range(WIDE // FEAT):
        feats = pair_features(q_ref[:, p * FEAT : (p + 1) * FEAT], maps_ref[p])
        out_ref[:, 2 * p * FEAT : 2 * (p + 1) * FEAT] = feats.astype(BF16)


def features(q, maps):
    length = q.shape[0]
    pairs = WIDE // FEAT
    return pl.pallas_call(
        features_kernel,
        grid=(D // WIDE,),
        in_specs=[
            pl.BlockSpec((length, WIDE), lambda g: (0, g)),
            pl.BlockSpec((pairs, FEAT, 2 * FEAT), lambda g: (g, 0, 0)),
        ],
        out_specs=pl.BlockSpec((length, 2 * WIDE), lambda g: (0, g)),
        out_shape=jax.ShapeDtypeStruct((length, 2 * D), BF16),
        cost_estimate=pl.CostEstimate(
            flops=8_000_000_000, bytes_accessed=6 * length * D, transcendentals=2 * length * D
        ),
        name="features",
    )(q, maps)


def key_tiles(kv_ref, kf_ref, rim_kv_ref, rim_kf_ref, mask):
    tiles = []
    for t in range(1 + kv_ref.shape[0] // WINDOW):
        if t == 0:
            kv, kf = rim_kv_ref[...], rim_kf_ref[...]
        else:
            at = (t - 1) * WINDOW
            kv, kf = kv_ref[at : at + WINDOW, :], kf_ref[at : at + WINDOW, :]
        kk, vv = both_halves(kv)
        tiles.append((diagonal(kk, mask * SCALE), diagonal(vv, mask), diagonal_pair(kf)))
    return tiles


def spans(t, length):
    edge = lambda v: min(max(v, 0), length)
    a, b, c = edge((t - 1) * WINDOW), edge(t * WINDOW), edge((t + 1) * WINDOW)
    return (a, b), (b, c), (c, length)


def weights_of(t, tile, q_ref, qf_ref, same, upper, gamma):
    length = q_ref.shape[0]
    (a, b), (_, c), _ = spans(t, length)
    e = jnp.exp(dot_nt(q_ref[a:c, :], tile[0]))
    linear = None
    if b < length:
        linear = gamma * jnp.concatenate(
            [
                dot_nt(qf_ref[b:, 2 * p * FEAT : 2 * (p + 1) * FEAT], tile[2])
                for p in range(GROUPS // 2)
            ],
            axis=1,
        )
    parts = []
    if b > a:
        parts.append(jnp.where(same(a, b) & upper, e[: b - a], 0.0))
    if c > b:
        mixed = jnp.where(upper, linear[: c - b], e[b - a :])
        parts.append(jnp.where(same(b, c), mixed, 0.0))
    if length > c:
        parts.append(jnp.where(same(c, length), linear[c - b :], 0.0))
    return e, jnp.concatenate(parts, axis=0).astype(BF16)


def carried(carry_ref):
    state = carry_ref[0]
    ones = jnp.zeros((HEAD, FEAT), BF16) + state[HEAD : HEAD + 1, :]
    return diagonal_pair(state[:HEAD, :]), diagonal_pair(ones)


def attend_kernel(
    q_ref, qf_ref, kv_ref, kf_ref, rim_kv_ref, rim_kf_ref, carry_ref,
    qdoc_ref, kdoc_ref, fresh_ref, gamma_ref,
    out_ref, att_ref, inv_ref, num_ref, den_ref,
):
    length = q_ref.shape[0]
    mask = same_head(WINDOW)
    ones = mask.astype(BF16)
    gamma = gamma_ref[...]
    shape = (WINDOW, WIDE)
    upper = row(shape) >= lane(shape) % HEAD
    state, state_sum = carried(carry_ref)
    fresh = fresh_ref[...] * gamma
    for p in range(GROUPS // 2):
        feats = qf_ref[:, 2 * p * FEAT : 2 * (p + 1) * FEAT]
        at = slice(p * FEAT, (p + 1) * FEAT)
        num_ref[:, at] = dot_nt(feats, state) * fresh[:, at]
        den_ref[:, at] = dot_nt(feats, state_sum) * fresh[:, at]
    for t, tile in enumerate(key_tiles(kv_ref, kf_ref, rim_kv_ref, rim_kf_ref, mask)):
        a = spans(t, length)[0][0]
        same = lambda i, j, t=t: qdoc_ref[i:j, :] == kdoc_ref[t : t + 1, :]
        _, w = weights_of(t, tile, q_ref, qf_ref, same, upper, gamma)
        num_ref[a:, :] += dot_nn(w, tile[1])
        den_ref[a:, :] += dot_nn(w, ones)
    inv = 1.0 / den_ref[...]
    att = num_ref[...] * inv
    inv_ref[...] = inv
    att_ref[...] = att
    out_ref[...] = att.astype(BF16)


def group_specs(length):
    column = lambda rows, width: pl.BlockSpec((rows, width), lambda g: (0, g))
    whole = lambda rows, width: pl.BlockSpec((rows, width), lambda g: (0, 0))
    return dict(
        q=column(length, WIDE),
        qf=column(length, 2 * WIDE),
        k=column(length, FEAT),
        rim_kv=pl.BlockSpec((WINDOW, FEAT), lambda g: (0, g)),
        rim_kf=pl.BlockSpec((WINDOW, FEAT), lambda g: (0, KV_HEADS + g)),
        state=pl.BlockSpec((1, STATE, FEAT), lambda g: (g, 0, 0)),
        qdoc=whole(length, 1),
        kdoc=whole(8, WIDE),
        gamma=column(1, WIDE),
        wide=whole(length, WIDE),
        maps=pl.BlockSpec((GROUPS // 2, FEAT, 2 * FEAT), lambda g: (g, 0, 0)),
    )


def attend(q, qf, kv, kf, rim, carry, masks):
    length = q.shape[0]
    s = group_specs(length)
    return pl.pallas_call(
        attend_kernel,
        grid=(KV_HEADS,),
        in_specs=[
            s["q"], s["qf"], s["k"], s["k"], s["rim_kv"], s["rim_kf"], s["state"],
            s["qdoc"], s["kdoc"], s["qdoc"], s["gamma"],
        ],
        out_specs=[s["q"]] * 3,
        out_shape=[
            jax.ShapeDtypeStruct((length, D), BF16),
            jax.ShapeDtypeStruct((length, D), F32),
            jax.ShapeDtypeStruct((length, D), F32),
        ],
        scratch_shapes=[pltpu.VMEM((length, WIDE), F32)] * 2,
        compiler_params=pltpu.CompilerParams(vmem_limit_bytes=32 << 20),
        cost_estimate=pl.CostEstimate(
            flops=10_000_000_000, bytes_accessed=16 * length * D, transcendentals=0
        ),
        name="attend",
    )(q, qf, kv, kf, rim, rim, carry, masks["qdoc"], masks["kdoc"], masks["fresh"], masks["gamma"])


def scaled_grads_kernel(
    ga_ref, att_ref, inv_ref, qf_ref, fresh_ref, gamma_ref, g_ref, gd_ref, back_ref
):
    mask = same_head(HEAD)
    ga = ga_ref[...].astype(F32)
    inv = inv_ref[...]
    product = ga * att_ref[...]
    high = product.astype(BF16)
    rest = (product - high.astype(F32)).astype(BF16)
    ones = mask.astype(BF16)
    gd = -(dot_nn(high, ones) + dot_nn(rest, ones)) * inv
    g = ga * inv
    g_ref[...] = g.astype(BF16)
    gd_ref[...] = gd
    fresh = fresh_ref[...] * gamma_ref[...]
    fresh_g = (g * fresh).astype(BF16)
    fresh_gd = (gd * fresh).astype(BF16)
    kv = sums = 0.0
    for p in range(GROUPS // 2):
        feats = qf_ref[:, 2 * p * FEAT : 2 * (p + 1) * FEAT]
        at = slice(p * FEAT, (p + 1) * FEAT)
        kv += fold_pair(dot_tn(fresh_g[:, at], feats), HEAD)
        sums += fold_pair(dot_tn(fresh_gd[:, at], feats), HEAD)
    back_ref[0, :HEAD, :] = kv.astype(BF16)
    back_ref[0, HEAD:, :] = sums[: STATE - HEAD].astype(BF16)


def scaled_grads(ga, att, inv, qf, masks):
    length = ga.shape[0]
    s = group_specs(length)
    return pl.pallas_call(
        scaled_grads_kernel,
        grid=(KV_HEADS,),
        in_specs=[s["q"], s["q"], s["q"], s["qf"], s["qdoc"], s["gamma"]],
        out_specs=[s["q"], s["q"], s["state"]],
        out_shape=[
            jax.ShapeDtypeStruct((length, D), BF16),
            jax.ShapeDtypeStruct((length, D), F32),
            jax.ShapeDtypeStruct((KV_HEADS, STATE, FEAT), BF16),
        ],
        name="scaled_grads",
    )(ga, att, inv, qf, masks["fresh"], masks["gamma"])


def attend_back_kernel(
    q_ref, qf_ref, kv_ref, kf_ref, rim_kv_ref, rim_kf_ref, carry_ref, g_ref, gd_ref,
    qdoc_ref, kdoc_ref, fresh_ref, gamma_ref, maps_ref, cos_ref, sin_ref,
    raw_ref, dkv_ref, dkf_ref, dmap_ref, logit_ref, dq_ref, dqf_ref,
):
    length = q_ref.shape[0]
    mask = same_head(WINDOW)
    gamma = gamma_ref[...]
    shape = (WINDOW, WIDE)
    upper = row(shape) >= lane(shape) % HEAD
    state, state_sum = carried(carry_ref)
    fresh = fresh_ref[...] * gamma
    pairs = range(GROUPS // 2)
    half = lambda p: slice(p * FEAT, (p + 1) * FEAT)
    full = lambda p: slice(2 * p * FEAT, 2 * (p + 1) * FEAT)
    fresh_g = (g_ref[...].astype(F32) * fresh).astype(BF16)
    fresh_gd = (gd_ref[...] * fresh * (1.0 / HEAD)).astype(BF16)
    for p in pairs:
        dqf_ref[:, full(p)] = dot_nn(fresh_g[:, half(p)], state) + dot_nn(
            fresh_gd[:, half(p)], state_sum
        )
    dq_ref[...] = jnp.zeros_like(dq_ref)
    lo = low_half((WINDOW, FEAT))
    for t, tile in enumerate(key_tiles(kv_ref, kf_ref, rim_kv_ref, rim_kf_ref, mask)):
        (a, b), (_, c), _ = spans(t, length)
        same = lambda i, j, t=t: qdoc_ref[i:j, :] == kdoc_ref[t : t + 1, :]
        e, w = weights_of(t, tile, q_ref, qf_ref, same, upper, gamma)
        g = g_ref[a:, :]
        x = dot_nt(g, tile[1]) + gd_ref[a:, :]
        near = x[: c - a] * e
        parts = []
        if b > a:
            parts.append(jnp.where(same(a, b) & upper, near[: b - a], 0.0))
        if c > b:
            parts.append(jnp.where(same(b, c), jnp.where(upper, 0.0, near[b - a :]), 0.0))
        ds = jnp.concatenate(parts, axis=0).astype(BF16)
        dq_ref[a:c, :] += dot_nn(ds, tile[0])
        dk = fold_heads(dot_tn(ds, q_ref[a:c, :]), mask) * SCALE
        dv = fold_heads(dot_tn(w, g), mask)
        at = slice(t * WINDOW, (t + 1) * WINDOW)
        dkv_ref[at, :] = jnp.where(lo, dk, dv)
        if b < length:
            far = x[b - a :] * gamma
            parts = [jnp.where(same(b, c) & upper, far[: c - b], 0.0)]
            if c < length:
                parts.append(jnp.where(same(c, length), far[c - b :], 0.0))
            dl = jnp.concatenate(parts, axis=0).astype(BF16)
            dkf = 0.0
            for p in pairs:
                dqf_ref[b:, full(p)] += dot_nn(dl[:, half(p)], tile[2])
                dkf += fold_pair(dot_tn(dl[:, half(p)], qf_ref[b:, full(p)]), HEAD)
            dkf_ref[at, :] = dkf
        else:
            dkf_ref[at, :] = jnp.zeros((WINDOW, FEAT), F32)
    for p in pairs:
        grads = []
        for h in (2 * p, 2 * p + 1):
            f = qf_ref[:, h * FEAT : (h + 1) * FEAT].astype(F32)
            gu, t = halves_softmax_back(f, dqf_ref[:, h * FEAT : (h + 1) * FEAT])
            grads.append(gu.astype(BF16))
            total = jnp.sum(jnp.sum(t, axis=0, keepdims=True), axis=1, keepdims=True)
            logit_ref[0, h : h + 1, :] = jnp.zeros((1, FEAT), F32) + total
        gu = jnp.concatenate(grads, axis=1)
        dq_ref[:, half(p)] += 0.5 * dot_nt(gu, maps_ref[p])
        dmap = dot_tn(q_ref[:, half(p)], gu)
        dmap_ref[2 * p] = dmap[:HEAD, :FEAT]
        dmap_ref[2 * p + 1] = dmap[HEAD:, FEAT:]
    raw_ref[...] = turn(dq_ref[...], cos_ref[...], -sin_ref[...]).astype(BF16)


def attend_back(q, qf, kv, kf, rim, carry, g, gd, masks, maps):
    length = q.shape[0]
    extended = length + WINDOW
    s = group_specs(length)
    column = pl.BlockSpec((extended, FEAT), lambda g: (0, g))
    return pl.pallas_call(
        attend_back_kernel,
        grid=(KV_HEADS,),
        in_specs=[
            s["q"], s["qf"], s["k"], s["k"], s["rim_kv"], s["rim_kf"], s["state"], s["q"], s["q"],
            s["qdoc"], s["kdoc"], s["qdoc"], s["gamma"], s["maps"], s["wide"], s["wide"],
        ],
        out_specs=[
            s["q"], column, column,
            pl.BlockSpec((GROUPS, HEAD, FEAT), lambda g: (g, 0, 0)),
            pl.BlockSpec((1, 8, FEAT), lambda g: (g, 0, 0)),
        ],
        out_shape=[
            jax.ShapeDtypeStruct((length, D), BF16),
            jax.ShapeDtypeStruct((extended, KV_HEADS * FEAT), F32),
            jax.ShapeDtypeStruct((extended, KV_HEADS * FEAT), F32),
            jax.ShapeDtypeStruct((HEADS, HEAD, FEAT), F32),
            jax.ShapeDtypeStruct((KV_HEADS, 8, FEAT), F32),
        ],
        scratch_shapes=[pltpu.VMEM((length, WIDE), F32), pltpu.VMEM((length, 2 * WIDE), F32)],
        compiler_params=pltpu.CompilerParams(vmem_limit_bytes=32 << 20),
        cost_estimate=pl.CostEstimate(
            flops=30_000_000_000, bytes_accessed=16 * length * D, transcendentals=0
        ),
        name="attend_back",
    )(
        q, qf, kv, kf, rim, rim, carry, g, gd,
        masks["qdoc"], masks["kdoc"], masks["fresh"], masks["gamma"],
        maps, masks["cos"], masks["sin"],
    )


def keys_back_kernel(
    kv_ref, kf_ref, dkv_ref, dkf_ref, rim_kv_ref, rim_kf_ref, near_ref, far_ref, survive_ref,
    maps_ref, cos_ref, sin_ref, rk_ref, rv_ref, dmap_ref,
):
    length = kv_ref.shape[0]
    cut = length - WINDOW
    lo = low_half((length, FEAT))
    survive = survive_ref[...]
    dkv, grads = [], []
    for h in range(2):
        at = slice(h * FEAT, (h + 1) * FEAT)
        kv = kv_ref[:, at].astype(F32)
        kf = kf_ref[:, at]
        v_low = pltpu.roll(kv, HEAD, 1)
        ones = jnp.where(lane((length, FEAT)) == HEAD, 1.0, 0.0)
        v_one = jnp.where(lo, v_low, ones).astype(BF16)[:, :STATE]
        dkf, dv = [], []
        for back, part in ((near_ref, slice(0, cut)), (far_ref, slice(cut, length))):
            state = back[h]
            twice = jnp.concatenate([state[:HEAD], state[:HEAD]], axis=0)
            dkf.append(dot_nn(v_one[part], state))
            dv.append(dot_nt(kf[part], twice))
        rim = jnp.zeros((cut, FEAT), F32)
        dkf = (
            jnp.concatenate(dkf, axis=0) * survive
            + dkf_ref[WINDOW:, at]
            + jnp.concatenate([rim, rim_kf_ref[:, at].astype(F32)], axis=0)
        )
        dv = jnp.concatenate(dv, axis=0) * survive
        total = (
            dkv_ref[WINDOW:, at]
            + jnp.concatenate([rim, rim_kv_ref[:, at].astype(F32)], axis=0)
            + jnp.where(lo, 0.0, dv)
        )
        gu, _ = halves_softmax_back(kf.astype(F32), dkf)
        grads.append(gu.astype(BF16))
        dkv.append(total)
    gu = jnp.concatenate(grads, axis=1)
    keys = jnp.where(lo, kv_ref[:, :FEAT].astype(F32), pltpu.roll(kv_ref[:, FEAT:].astype(F32), HEAD, 1))
    dmap = dot_tn(keys.astype(BF16), gu)
    dmap_ref[0] = dmap[:HEAD, :FEAT]
    dmap_ref[1] = dmap[HEAD:, FEAT:]
    dk = jnp.where(lo, dkv[0], pltpu.roll(dkv[1], HEAD, 1)) + 0.5 * dot_nt(gu, maps_ref[0])
    rk_ref[...] = turn(dk, cos_ref[...], -sin_ref[...]).astype(BF16)
    rv_ref[...] = jnp.where(lo, pltpu.roll(dkv[0], HEAD, 1), dkv[1]).astype(BF16)


def keys_back(kv, kf, dkv, dkf, rim, near, far, masks, maps):
    length = kv.shape[0]
    extended = length + WINDOW
    pairs = KV_HEADS // 2
    column = lambda rows: pl.BlockSpec((rows, 2 * FEAT), lambda g: (0, g))
    state = pl.BlockSpec((2, STATE, FEAT), lambda g: (g, 0, 0))
    narrow = pl.BlockSpec((length, FEAT), lambda g: (0, 0))
    out = pl.BlockSpec((length, FEAT), lambda g: (0, g))
    return pl.pallas_call(
        keys_back_kernel,
        grid=(pairs,),
        in_specs=[
            column(length), column(length), column(extended), column(extended),
            column(WINDOW), pl.BlockSpec((WINDOW, 2 * FEAT), lambda g: (0, pairs + g)),
            state, state, pl.BlockSpec((length, 1), lambda g: (0, 0)),
            pl.BlockSpec((1, FEAT, 2 * FEAT), lambda g: (g, 0, 0)), narrow, narrow,
        ],
        out_specs=[out, out, pl.BlockSpec((2, HEAD, FEAT), lambda g: (g, 0, 0))],
        out_shape=[
            jax.ShapeDtypeStruct((length, KVD), BF16),
            jax.ShapeDtypeStruct((length, KVD), BF16),
            jax.ShapeDtypeStruct((KV_HEADS, HEAD, FEAT), F32),
        ],
        name="keys_back",
    )(
        kv, kf, dkv, dkf, rim, rim, near, far, masks["survive"], maps, masks["cos"], masks["sin"]
    )


class Grid:
    def __init__(self):
        self.seq = lax.axis_size("seq")
        self.rows = lax.axis_size("rows")
        self.zs = Z_SIZE
        self.xs = self.rows // Z_SIZE
        self.ys = self.seq // CORES
        s = lax.axis_index("seq")
        r = lax.axis_index("rows")
        self.y, self.c = s // CORES, s % CORES
        self.z, self.x = r // self.xs, r % self.xs
        self.s, self.r = s, r

    def send(self, value, move):
        route = []
        for s in range(self.seq):
            for r in range(self.rows):
                there = move(s // CORES, s % CORES, r // self.xs, r % self.xs)
                if there is not None:
                    y, c, z, x = there
                    target = (y * CORES + c) * self.rows + z * self.xs + x
                    route.append((s * self.rows + r, target))
        return jax.tree.map(lambda v: lax.ppermute(v, ("seq", "rows"), route), value)

    def along_z(self, value, k):
        return self.send(value, lambda y, c, z, x: (y, c, (z + k) % self.zs, x))

    def along_x(self, value, k):
        return self.send(value, lambda y, c, z, x: (y, c, z, (x + k) % self.xs))

    def along_y(self, value, k):
        return self.send(value, lambda y, c, z, x: ((y + k) % self.ys, c, z, x))

    def flip_z(self, value, bit):
        return self.send(value, lambda y, c, z, x: (y, c, z ^ bit, x))

    def flip_core(self, value):
        return self.send(value, lambda y, c, z, x: (y, 1 - c, z, x))

    def flip_row(self, value, bit):
        def move(y, c, z, x):
            r = (z * self.xs + x) ^ bit
            return (y, c, r // self.xs, r % self.xs)

        return self.send(value, move)

    def along_seq(self, value, k):
        def move(y, c, z, x):
            s = y * CORES + c + k
            return (s // CORES, s % CORES, z, x) if 0 <= s < self.seq else None

        return self.send(value, move)


def after(values, *events):
    return lax.optimization_barrier((values, *events))[0]


def gather_rows(grid, shard):
    half = shard.shape[0] // CORES
    own = lax.dynamic_slice_in_dim(shard, grid.c * half, half, 0)
    pieces = []
    for kz in range(grid.zs):
        from_z = own if kz == 0 else grid.along_z(own, kz)
        for kx in range(grid.xs):
            piece = from_z if kx == 0 else grid.along_x(from_z, kx)
            row = ((grid.z - kz) % grid.zs) * grid.xs + (grid.x - kx) % grid.xs
            pieces.append((piece, (row * CORES + grid.c) * half))
            if kz + kx:
                other = grid.flip_core(piece)
            else:
                other = lax.dynamic_slice_in_dim(shard, (1 - grid.c) * half, half, 0)
            pieces.append((other, (row * CORES + 1 - grid.c) * half))
    return pieces


def assemble(grid, pieces):
    piece = pieces[0][0]
    full = jnp.zeros((piece.shape[0] * len(pieces), piece.shape[1]), piece.dtype)
    for piece, row in pieces:
        full = lax.dynamic_update_slice(full, piece, (row, 0))
    return full


def gather_pair(grid, gate_up, down):
    part = gate_up.shape[2] // grid.seq
    gu = lax.dynamic_slice_in_dim(gate_up, grid.s * part, part, 2)
    dn = lax.dynamic_slice_in_dim(down, grid.s * part, part, 0)
    got = [grid.flip_z((gu, dn), 1)]
    for ky in range(1, grid.ys):
        got.append(grid.along_y(got[0], ky))
    got = got + [grid.flip_core(v) for v in got]
    return (
        jnp.concatenate([v[0] for v in got], axis=2),
        jnp.concatenate([v[1] for v in got], axis=0),
    )


def spread(grid, block):
    near = [block] + [grid.along_x(block, k) for k in range(1, grid.xs)]
    parts = 4
    size = block.shape[0] // parts
    far = [[] for _ in range(grid.xs)]
    for p in range(parts):
        piece = grid.flip_z(block[p * size : (p + 1) * size], 2)
        far[0].append(piece)
        for k in range(1, grid.xs):
            far[k].append(grid.along_x(piece, k))
    return jnp.concatenate(near, axis=0), jnp.concatenate([v for f in far for v in f], axis=0)


def collect(grid, near, far, length):
    parts = 4
    size = length // parts
    total = near[:length]
    for k in range(1, grid.xs):
        total = total + grid.along_x(
            near[k * length : (k + 1) * length].astype(BF16), -k
        ).astype(F32)
    back = []
    for p in range(parts):
        lo = p * size
        piece = far[lo : lo + size]
        for k in range(1, grid.xs):
            piece = piece + grid.along_x(
                far[k * length + lo : k * length + lo + size].astype(BF16), -k
            ).astype(F32)
        back.append(grid.flip_z(piece.astype(BF16), 2).astype(F32))
    return total + jnp.concatenate(back, axis=0)


def total_over_all(grid, values):
    widths = [v.shape[2] for v in values]
    packed = jnp.concatenate([v.astype(BF16) for v in values], axis=2)
    packed = jnp.pad(packed, ((0, 0), (0, 0), (0, -packed.shape[2] % FEAT)))
    packed = packed.reshape(grid.ys, CORES, 8, -1)
    own = lax.dynamic_index_in_dim(packed, grid.c, 1, False)
    other = lax.dynamic_index_in_dim(packed, 1 - grid.c, 1, False)
    both = (own.astype(F32) + grid.flip_core(other).astype(F32)).astype(BF16)
    total = lax.dynamic_index_in_dim(both, grid.y, 0, False).astype(F32)
    for k in range(1, grid.ys):
        part = lax.dynamic_index_in_dim(both, (grid.y + k) % grid.ys, 0, False)
        total = total + grid.along_y(part, k).astype(F32)
    bit = 1
    while bit < grid.rows:
        mine = total.astype(BF16)
        total = mine.astype(F32) + grid.flip_row(mine, bit).astype(F32)
        bit *= 2
    out, at = [], 0
    for w in widths:
        out.append(total[:, at : at + w])
        at += w
    return out


def pair_maps(maps):
    both = jnp.concatenate([maps, -maps], axis=-1)
    both = both.reshape(-1, 2, HEAD, FEAT)
    none = jnp.zeros_like(both[:, 0])
    return jnp.concatenate(
        [
            jnp.concatenate([both[:, 0], none], axis=-1),
            jnp.concatenate([none, both[:, 1]], axis=-1),
        ],
        axis=1,
    )


def adapters(query, key, value, axis):
    if axis == 1:
        joined = jnp.concatenate([query, key, value], axis=1)
        return jnp.pad(joined, ((0, 0), (0, LOW - joined.shape[1])))
    rank = query.shape[0]
    joined = jnp.zeros((LOW, QKV), query.dtype)
    joined = joined.at[:rank, :D].set(query)
    joined = joined.at[rank : 2 * rank, D : D + KVD].set(key)
    return joined.at[2 * rank : 3 * rank, D + KVD :].set(value)


def documents(grid, starts, length):
    resets = lax.all_gather(starts.astype(BF16), "seq", tiled=True).astype(jnp.int32)
    places = jnp.arange(resets.shape[0], dtype=jnp.int32)
    docs = jnp.cumsum(jnp.where(places == 0, 1, resets))
    padded = jnp.concatenate([jnp.full((WINDOW,), -1, jnp.int32), docs])
    extended = lax.dynamic_slice_in_dim(padded, grid.s * length, length + WINDOW, 0)
    own = extended[WINDOW:]
    before = extended[WINDOW - 1]
    last = own[-1]
    ends = docs[length - 1 :: length]
    places = jnp.arange(grid.seq, dtype=jnp.int32)
    tiles = jnp.tile(extended.reshape(-1, 1, WINDOW), (1, GROUPS, 1)).reshape(-1, WIDE)
    masks = dict(
        qdoc=own[:, None],
        kdoc=jnp.pad(tiles, ((0, 8 - tiles.shape[0]), (0, 0))),
        fresh=(own == before).astype(F32)[:, None],
        survive=(own == last).astype(F32)[:, None],
    )
    earlier = ((ends == before) & (places < grid.s)).astype(F32)
    entered = jnp.concatenate([jnp.full((1,), -1, jnp.int32), ends[:-1]])
    later = ((entered == last) & (places > grid.s)).astype(F32)
    pick = lambda v, k: lax.dynamic_index_in_dim(v, jnp.clip(grid.s + k, 0, grid.seq - 1), 0, False)
    former = [pick(earlier, -k) * (grid.s - k >= 0) for k in range(1, grid.seq)]
    latter = [pick(later, k) * (grid.s + k < grid.seq) for k in range(1, grid.seq)]
    return masks, former, latter


def local(
    tokens, doc_starts, cotangent, norm_first, norm_second,
    w_query, w_key, w_value, w_out, w_gate_up, w_down,
    query_in, query_out, key_in, key_out, value_in, value_out, proj_in, proj_out,
    map_query, map_key, window_logit,
):
    grid = Grid()
    length = tokens.shape[1]
    rank = query_in.shape[1]
    hidden = tokens[0].astype(F32)
    grad_out = cotangent[0]
    gain_first = norm_first.astype(F32)
    gain_second = norm_second.astype(F32)

    qkv_shard = jnp.concatenate([w_query, w_key, w_value], axis=1)
    qkv_full = assemble(grid, gather_rows(grid, qkv_shard))
    grad_out, w_out, w_gate_up, w_down = after((grad_out, w_out, w_gate_up, w_down), qkv_full)
    output_full = assemble(grid, gather_rows(grid, w_out))
    pair_gate_up, pair_down = gather_pair(grid, w_gate_up, w_down)
    cot_near, cot_far = spread(grid, grad_out)

    inverse_first = lax.rsqrt(jnp.mean(hidden * hidden, axis=-1, keepdims=True) + EPSILON)
    normed_first = hidden * inverse_first
    inputs = (normed_first * gain_first).astype(BF16)
    masks, former, latter = documents(grid, doc_starts[0], length)
    gamma = jax.nn.sigmoid(window_logit)
    masks["gamma"] = jnp.repeat(gamma, HEAD)[None, :]
    half = HEAD // 2
    inverse_freq = jnp.power(THETA, -(jnp.arange(half, dtype=F32) * 2.0 / HEAD))
    places = (grid.s * length + jnp.arange(length, dtype=jnp.int32)).astype(F32)
    angles = places[:, None] * inverse_freq[None, :]
    sine = jnp.sin(angles)
    masks["cos"] = jnp.tile(jnp.cos(angles), (1, WIDE // half))
    masks["sin"] = jnp.tile(jnp.concatenate([-sine, sine], axis=1), (1, WIDE // HEAD))
    maps_q, maps_k = pair_maps(map_query), pair_maps(map_key)
    qkv_in = adapters(query_in, key_in, value_in, 1)
    qkv_out = adapters(query_out, key_out, value_out, 0)

    low = dot_nn(inputs, qkv_in).astype(BF16)
    queries, kv, kf, rim, near, full = project(
        inputs, low, qkv_full, qkv_out, masks["cos"], masks["sin"], maps_k, masks["survive"]
    )
    rim = grid.along_seq(rim, 1)
    carry = former[0] * grid.along_seq(near, 1).astype(F32)
    for k in range(2, grid.seq):
        carry = carry + former[k - 1] * grid.along_seq(full, k).astype(F32)
    carry = carry.astype(BF16)
    qf = features(queries, maps_q)
    merged, attended, inverse = attend(queries, qf, kv, kf, rim, carry, masks)

    out_low = dot_nn(merged, proj_in).astype(BF16)
    residual = hidden + dot_nn(merged, output_full) + dot_nn(out_low, proj_out)
    inverse_second = lax.rsqrt(jnp.mean(residual * residual, axis=-1, keepdims=True) + EPSILON)
    normed_second = residual * inverse_second
    second_in = (normed_second * gain_second).astype(BF16)
    sides = spread(grid, second_in)
    grad_act = [
        [
            dot_nt(cot, down)
            for down in (w_down, pair_down)
        ]
        for cot in (cot_near, cot_far)
    ]
    mlp_parts, back_parts = [], []
    for side, rows in enumerate(sides):
        mlp_part = back_part = 0.0
        for which, (both, down) in enumerate(((w_gate_up, w_down), (pair_gate_up, pair_down))):
            gate = dot_nn(rows, both[0])
            up = dot_nn(rows, both[1])
            sigmoid_gate = jax.nn.sigmoid(gate)
            silu = gate * sigmoid_gate
            activation = (silu * up).astype(BF16)
            mlp_part = mlp_part + dot_nn(activation, down)
            grads = grad_act[side][which]
            grad_gate = grads * up * sigmoid_gate * (1.0 + gate * (1.0 - sigmoid_gate))
            grad_up = (grads * silu).astype(BF16)
            for grad, full in ((grad_gate.astype(BF16), both[0]), (grad_up, both[1])):
                back_part = back_part + dot_nt(grad, full)
        mlp_parts.append(mlp_part)
        back_parts.append(back_part)
    grad_second = collect(grid, back_parts[0], back_parts[1], length)
    mlp_parts = after(mlp_parts, grad_second)
    mlp_out = collect(grid, mlp_parts[0], mlp_parts[1], length)
    block_out = (residual + mlp_out).astype(BF16)

    def norm_back(grad_normed, normed, inverse_rms, gain):
        scaled = grad_normed * gain
        back = inverse_rms * (scaled - normed * jnp.mean(scaled * normed, axis=-1, keepdims=True))
        return back, jnp.sum(grad_normed * normed, axis=0)

    grad_norm_part, grad_gain_two = norm_back(
        grad_second, normed_second, inverse_second, gain_second
    )
    grad_residual = grad_out.astype(F32) + grad_norm_part
    grad_branch = grad_residual.astype(BF16)
    grad_out_low = dot_nt(grad_branch, proj_out).astype(BF16)
    grad_merged = (dot_nt(grad_branch, output_full) + dot_nt(grad_out_low, proj_in)).astype(BF16)
    grad_proj_out = dot_tn(out_low, grad_branch)
    grad_proj_in = dot_tn(grad_out_low, merged)

    grads, grad_den, back = scaled_grads(grad_merged, attended, inverse, qf, masks)
    far_back = jnp.zeros(back.shape, F32)
    for k in range(2, grid.seq):
        far_back = far_back + latter[k - 1] * grid.along_seq(back, -k).astype(F32)
    near_back = far_back + latter[0] * grid.along_seq(back, -1).astype(F32)
    raw_query, dkv, dkf, dmap_query, dlogit = attend_back(
        queries, qf, kv, kf, rim, carry, grads, grad_den, masks, maps_q
    )
    rim_back = jnp.concatenate([dkv[:WINDOW], dkf[:WINDOW]], axis=1).astype(BF16)
    rim_back = grid.along_seq(rim_back, -1)
    raw_key, raw_value, dmap_key = keys_back(
        kv, kf, dkv, dkf, rim_back, near_back.astype(BF16), far_back.astype(BF16), masks, maps_k
    )
    raw = jnp.concatenate([raw_query, raw_key, raw_value], axis=1)
    grad_low = dot_nt(raw, qkv_out).astype(BF16)
    grad_inputs = dot_nt(raw, qkv_full) + dot_nt(grad_low, qkv_in)
    grad_qkv_out = dot_tn(low, raw)
    grad_qkv_in = dot_tn(grad_low, inputs)
    grad_first_part, grad_gain_one = norm_back(grad_inputs, normed_first, inverse_first, gain_first)
    grad_tokens = grad_residual + grad_first_part
    grad_logit = dlogit[:, :GROUPS, 0].reshape(HEADS) * (1.0 - gamma)

    blocks = lambda v: v.reshape(8, grid.seq, -1).swapaxes(0, 1)
    plain = lambda v: v.reshape(grid.seq, 8, -1)
    outs = (
        blocks(grad_qkv_out[:rank, :D]),
        blocks(grad_qkv_out[rank : 2 * rank, D : D + KVD]),
        blocks(grad_qkv_out[2 * rank : 3 * rank, D + KVD :]),
        blocks(grad_proj_out),
    )
    ins = [blocks(grad_qkv_in[i * rank : (i + 1) * rank]) for i in range(3)]
    ins.append(blocks(grad_proj_in))
    map_q = plain(dmap_query[:, :, :HEAD].reshape(HEADS, -1))
    map_k = dmap_key[:, :, :HEAD].reshape(KV_HEADS, grid.seq, -1).swapaxes(0, 1)
    logit = jnp.pad(grad_logit.reshape(grid.seq, -1, 1), ((0, 0), (0, 8 - HEADS // grid.seq), (0, 0)))
    sums = total_over_all(
        grid, [*outs, *ins, map_q, map_k, plain(grad_gain_one), plain(grad_gain_two), logit]
    )
    outs, ins, (map_q, map_k, gain_one, gain_two, logit) = sums[:4], sums[4:8], sums[8:]
    width = D // grid.seq
    return (
        block_out[None],
        grad_tokens[None],
        gain_one.reshape(width),
        gain_two.reshape(width),
        ins[0].T,
        outs[0],
        ins[1].T,
        outs[1],
        ins[2].T,
        outs[2],
        ins[3].T,
        outs[3],
        map_q.reshape(-1, HEAD, HEAD),
        map_k.reshape(KV_HEADS, -1, HEAD),
        logit[: HEADS // grid.seq, 0],
    )


def solution(mesh):
    placed = (
        P("rows", "seq", None),
        P("rows", "seq"),
        P("rows", "seq", None),
        P(),
        P(),
        P("rows", None),
        P("rows", None),
        P("rows", None),
        P("rows", None),
        P(None, None, "rows"),
        P("rows", None),
        P(),
        P(),
        P(),
        P(),
        P(),
        P(),
        P(),
        P(),
        P(),
        P(),
        P(),
    )
    return jax.shard_map(
        local,
        mesh=mesh,
        in_specs=placed,
        out_specs=(
            P("rows", "seq", None),
            P("rows", "seq", None),
            P("seq"),
            P("seq"),
            P("seq", None),
            P(None, "seq"),
            P("seq", None),
            P(None, "seq"),
            P("seq", None),
            P(None, "seq"),
            P("seq", None),
            P(None, "seq"),
            P("seq", None, None),
            P(None, "seq", None),
            P("seq"),
        ),
        check_vma=False,
    )
```

time: 2870 us -> 860 us (0.30)
  waiting for transfers between devices: 2390 us -> 365 us
  matrix products: 285 us -> 156 us
  starting transfers between devices: 15.2 us -> 105 us
  Pallas kernels: 0 us -> 79.8 us
  local copies, waits for them, and re-layouts: 48.8 us -> 105 us
  blocking collectives: 46.2 us -> 5.07 us
    all_gather x6 -> x0, waiting for transfers between devices: 2110 us -> none  [the longest x1 1260 us: local(): lax.all_gather(w_gate_up, 'rows', axis=2, tiled=True)]
    ppermute x7 -> x85, waiting for transfers between devices: 0.24 us -> 365 us  [send(): lax.ppermute(v, ('seq', 'rows'), route)]
    reduce_scatter x8 -> x0, waiting for transfers between devices: 151 us -> none  [the longest x1 24.1 us: local(): lax.psum_scatter(trained[10].astype(jnp.bfloat16), 'seq', scatter_dimensi...]
    psum x2 -> x0, waiting for transfers between devices: 133 us -> none  [the longest x1 75.2 us: local(): lax.psum(shares[0].astype(jnp.bfloat16), 'rows').astype(jnp.float32)]
    dot_general x61 -> x38, matrix products: 282 us -> 156 us  [the longest x18 91.4 us: dot_nt(): lax.dot_general(a, b, (((1,), (1,)), ((), ())), preferred_element_type=F32)]
    ppermute x7 -> x85, starting transfers between devices: 14.2 us -> 105 us  [send(): lax.ppermute(v, ('seq', 'rows'), route)]
    pallas_call x0 -> x6, Pallas kernels: none -> 79.8 us  [the longest x1 27.5 us: attend_back(): pl.pallas_call(attend_back_kernel, grid=(KV_HEADS,), in_specs=[s['q'], s[...]
    dynamic_update_slice x0 -> x32, local copies, waits for them, and re-layouts: none -> 37.4 us  [assemble(): full = lax.dynamic_update_slice(full, piece, (row, 0))]
  transfers between devices with their start and end apart: 25 -> 85, of which waited for: 16 -> 38; matrix products, arithmetic and copies ran while one was open for 8% -> 23% of each run, Pallas kernels for 0% -> 6%
where the time goes in v1:
time: 860 us; the launch traced here: 850 us
  waiting for transfers between devices  365 us (42%)
  matrix products  156 us (18%)
  local copies, waits for them, and re-layouts  105 us (12%)
  starting transfers between devices  105 us (12%)
  Pallas kernels  79.8 us (9%)
  other arithmetic  27.7 us (3%)
    ppermute x85, waiting for transfers between devices, send(): lax.ppermute(v, ('seq', 'rows'), route)  365 us
    ppermute x85, starting transfers between devices, send(): lax.ppermute(v, ('seq', 'rows'), route)  105 us
    dot_general x18, matrix products, dot_nt(): lax.dot_general(a, b, (((1,), (1,)), ((), ())), preferred_element_type=F32)  91.4 us
    dot_general x16, matrix products, dot_nn(): return jnp.dot(a, b, preferred_element_type=F32)  61.5 us
    dynamic_update_slice x32, local copies, waits for them, and re-layouts, assemble(): full = lax.dynamic_update_slice(full, piece, (row, 0))  37.4 us
    unnamed x255, local copies, waits for them, and re-layouts  30.3 us
    pallas_call x1, Pallas kernels, attend_back(): pl.pallas_call(attend_back_kernel, grid=(KV_HEADS,), in_specs=[s['q'], s[...  27.5 us
  transfers between devices with their start and end apart: 85, of which 38 were waited for; matrix products, arithmetic and copies ran while one was open for 23% of the time, Pallas kernels for 6%

profile of v1, /device:TPU:0, one launch (start us, length us, event | category | flops | bytes accessed | tf_op | source)
XLA Modules:
  0.0 850.3 jit_solution(4147101218599823024)
XLA Ops:
  3.4 6.2 broadcast_in_dim.46
  44.2 25.9 %collective-permute-done.6 = bf16[128,3072]{1,0:T(8,128)(2,1)} collective-permute-done((bf16[128,3072]{1,0:T(8,128)(2,1)}, bf16[128,3072]{1,0:T(8,128)(2,1)}, u32[]{:S(2)}, u32[]{:S(2)}) %collective-permute-start.6) | collective-permute-done | bytes 786464 | tf_op jit(solution)/shard_map/ppermute | solution.py:625
  77.9 12.9 %collective-permute-done.8 = bf16[128,3072]{1,0:T(8,128)(2,1)S(1)} collective-permute-done((bf16[128,3072]{1,0:T(8,128)(2,1)}, bf16[128,3072]{1,0:T(8,128)(2,1)S(1)}, u32[]{:S(2)}, u32[]{:S(2)}) %collective-permute-start.8) | collective-permute-done | bytes 786464 | tf_op jit(solution)/shard_map/ppermute | solution.py:625
  90.7 15.8 %collective-permute-done.12 = bf16[128,3072]{1,0:T(8,128)(2,1)S(1)} collective-permute-done((bf16[128,3072]{1,0:T(8,128)(2,1)}, bf16[128,3072]{1,0:T(8,128)(2,1)S(1)}, u32[]{:S(2)}, u32[]{:S(2)}) %collective-permute-start.12) | collective-permute-done | bytes 786464 | tf_op jit(solution)/shard_map/ppermute | solution.py:625
  119.4 15.5 %project.1 = (bf16[256,2048]{1,0:T(8,128)(2,1)S(1)}, bf16[256,1024]{1,0:T(8,128)(2,1)S(1)}, bf16[256,1024]{1,0:T(8,128)(2,1)S(1)}, bf16[64,2048]{1,0:T(8,128)(2,...) custom-call(bf16[256,2048]{1,0:T(8,128)(2,1)S(1)} %fusion.38.x_ref, ...), custom_call_target="tpu_custom_call" | custom-call | flops 3221225472 | bytes 12582912 | tf_op jit(solution)/shard_map/project/pallas_call | solution.py:207
  158.6 9.3 %features.1.qf_ref = bf16[256,4096]{1,0:T(8,128)(2,1)} custom-call(bf16[256,2048]{1,0:T(8,128)(2,1)} %copy-done.34, bf16[16,128,256]{2,1,0:T(8,128)(2,1)} %fusion.53.maps_ref), custom_call_target="tpu_custom_call" | custom-call | flops 8000000000 | bytes 3145728 | tf_op jit(solution)/shard_map/features/pallas_call | solution.py:237
  169.9 14.1 %collective-permute-start.20 = (bf16[128,2048]{1,0:T(8,128)(2,1)}, bf16[128,2048]{1,0:T(8,128)(2,1)S(1)}, u32[]{:S(2)}, u32[]{:S(2)}) collective-permute-start(bf16[128,2048]{1,0:T(8,128)(2,1)} %get-tuple-element.109), channel_id=1, source_target_pairs={{0,2},{1,3},{2,4},{3,5},{4,6},{5,7},{6,0},{7,1},{8,10},{9,11},{10,... | collective-permute-start | bytes 1572872 | tf_op jit(solution)/shard_map/ppermute | solution.py:625
  194.5 12.4 %attend.1 = (bf16[256,2048]{1,0:T(8,128)(2,1)S(1)}, f32[256,2048]{1,0:T(8,128)S(1)}, f32[256,2048]{1,0:T(8,128)S(1)}) custom-call(bf16[256,2048]{1,0:T(8,128)(2,1)S(1)} %copy-done.35, bf16[256,4096]{1,0:T(8,128)(2,1)S(1)} %copy-done.8, bf16[256,1024]{1,0:T(8,128)(2,1)S(1)} %get-tuple-element.78.kv_ref, bf16[256,1024]{1,0:T(8,128)(2,1)S(1)} %get-tuple-element.79.kf_ref, ...), custom_call_target="tpu_custom_call" | custom-call | flops 10000000000 | bytes 8388608 | tf_op jit(solution)/shard_map/attend/pallas_call | solution.py:354
  209.1 39.8 %collective-permute-done.51 = bf16[64,2048]{1,0:T(8,128)(2,1)S(1)} collective-permute-done((bf16[64,2048]{1,0:T(8,128)(2,1)}, bf16[64,2048]{1,0:T(8,128)(2,1)S(1)}, u32[]{:S(2)}, u32[]{:S(2)}) %collective-permute-start.51) | collective-permute-done | bytes 262176 | tf_op jit(solution)/shard_map/ppermute | solution.py:625
  298.5 21.3 %collective-permute-done.22 = bf16[128,2048]{1,0:T(8,128)(2,1)S(1)} collective-permute-done((bf16[128,2048]{1,0:T(8,128)(2,1)S(1)}, bf16[128,2048]{1,0:T(8,128)(2,1)S(1)}, u32[]{:S(2)}, u32[]{:S(2)}) %collective-permute-start.22) | collective-permute-done | bytes 524320 | tf_op jit(solution)/shard_map/ppermute | solution.py:625
  323.7 7.3 collective-permute-done.26
  333.4 8.0 collective-permute-done.30
  347.3 6.0 multiply_reduce_fusion.2
  360.4 26.2 %collective-permute-done.37 = bf16[256,2048]{1,0:T(8,128)(2,1)S(1)} collective-permute-done((bf16[256,2048]{1,0:T(8,128)(2,1)S(1)}, bf16[256,2048]{1,0:T(8,128)(2,1)S(1)}, u32[]{:S(2)}, u32[]{:S(2)}) %collective-permute-start.37) | collective-permute-done | bytes 1048608 | tf_op jit(solution)/shard_map/ppermute | solution.py:625
  390.8 17.2 %collective-permute-done.43 = bf16[64,2048]{1,0:T(8,128)(2,1)S(1)} collective-permute-done((bf16[64,2048]{1,0:T(8,128)(2,1)S(1)}, bf16[64,2048]{1,0:T(8,128)(2,1)S(1)}, u32[]{:S(2)}, u32[]{:S(2)}) %collective-permute-start.43) | collective-permute-done | bytes 262176 | tf_op jit(solution)/shard_map/ppermute | solution.py:625
  453.7 7.1 fusion.8
  471.3 7.9 fusion.10
  479.2 6.6 fusion.2
  492.4 6.7 fusion.124
  512.3 9.6 %fusion.121 = (bf16[512,2048]{1,0:T(8,128)(2,1)S(1)}, f32[512,2048]{1,0:T(8,128)}) fusion(bf16[2,2048,1024]{2,1,0:T(8,128)(2,1)S(1)} %constant_dynamic-update-slice_fusion.3, f32[512,1024]{1,0:T(8,128)} %copy-done.58, f32[512,1024]{1,0:T(8,128)} %copy-done.56, f32[512,2048]{1,0:T(8,128)} %fusion.20, f32[512,2048]{1,0:T(8,128)} %fusion.8, ...), kind=kOutput, calls=%fused_computation.288 | convolution fusion | flops 2154823680 | bytes 27262976 | tf_op jit(solution)/shard_map/dot_general | solution.py:38
  534.5 6.7 fusion.54
  546.1 7.3 add_add_fusion.1
  555.0 6.7 convolution_add_fusion.1
  561.8 6.1 fusion.55
  576.9 22.0 %collective-permute-done.66 = bf16[64,2048]{1,0:T(8,128)(2,1)S(1)} collective-permute-done((bf16[64,2048]{1,0:T(8,128)(2,1)S(1)}, bf16[64,2048]{1,0:T(8,128)(2,1)S(1)}, u32[]{:S(2)}, u32[]{:S(2)}) %collective-permute-start.66) | collective-permute-done | bytes 262176 | tf_op jit(solution)/shard_map/ppermute | solution.py:625
  624.3 26.8 %collective-permute-done.68 = bf16[64,2048]{1,0:T(8,128)(2,1)S(1)} collective-permute-done((bf16[64,2048]{1,0:T(8,128)(2,1)S(1)}, bf16[64,2048]{1,0:T(8,128)(2,1)S(1)}, u32[]{:S(2)}, u32[]{:S(2)}) %collective-permute-start.68) | collective-permute-done | bytes 262176 | tf_op jit(solution)/shard_map/ppermute | solution.py:625
  676.7 22.1 %collective-permute-done.75 = bf16[64,2048]{1,0:T(8,128)(2,1)} collective-permute-done((bf16[64,2048]{1,0:T(8,128)(2,1)}, bf16[64,2048]{1,0:T(8,128)(2,1)}, u32[]{:S(2)}, u32[]{:S(2)}) %collective-permute-start.75) | collective-permute-done | bytes 262176 | tf_op jit(solution)/shard_map/ppermute | solution.py:625
  722.3 6.9 fusion.37.ga_ref
  729.1 8.6 %scaled_grads.1 = (bf16[256,2048]{1,0:T(8,128)(2,1)}, f32[256,2048]{1,0:T(8,128)}, bf16[8,80,128]{2,1,0:T(8,128)(2,1)}) custom-call(bf16[256,2048]{1,0:T(8,128)(2,1)} %fusion.37.ga_ref, f32[256,2048]{1,0:T(8,128)} %copy-done.10, f32[256,2048]{1,0:T(8,128)} %copy-done.11, bf16[256,4096]{1,0:T(8,128)(2,1)} %features.1.qf_ref, f32[256,1]{1,0:T(8,128)} %copy-done.16, ...), custom_call_target="tpu_custom_call" | custom-call | tf_op jit(solution)/shard_map/scaled_grads/pallas_call | solution.py:406
  752.3 27.5 %attend_back.1 = (bf16[256,2048]{1,0:T(8,128)(2,1)S(1)}, f32[320,1024]{1,0:T(8,128)S(1)}, f32[320,1024]{1,0:T(8,128)S(1)}, f32[32,64,128]{2,1,0:T(8,128)S(1)}, f32[8,8,128]{2,1,0:T(8,128)S(1)}) custom-call(bf16[256,2048]{1,0:T(8,128)(2,1)S(1)} %copy-done.36, bf16[256,4096]{1,0:T(8,128)(2,1)S(1)} %copy-done.9, bf16[256,1024]{1,0:T(8,128)(2,1)S(1)} %copy-done.19, ...), custom_call_target="tpu_custom_call" | custom-call | flops 30000001024 | bytes 8388608 | tf_op jit(solution)/shard_map/attend_back/pallas_call | solution.py:495
  788.4 6.5 keys_back.1
  800.0 10.3 %fusion.44 = (bf16[2048]{0:T(1024)(128)(2,1)S(1)}, f32[256]{0:T(256)}, f32[256,2048]{1,0:T(8,128)}) fusion(bf16[1,256,2048]{2,1,0:T(8,128)(2,1)S(1)} %copy-done.47, f32[256]{0:T(256)S(1)} %copy-done.87, f32[2048]{0:T(1024)S(1)} %copy-done.74, f32[256,2048]{1,0:T(8,128)S(1)} %fusion.85, bf16[256,3072]{1,0:T(8,128)(2,1)S(1)} %constant_dynamic-update-slice_fusion.29, ...), kind=kOutput, calls=%fused_computation.59 | convolution fusion | flops 3225417472 | bytes 19412992 | tf_op jit(solution)/shard_map/dot_general | solution.py:38
  (586 shorter events, 410.2 us)
Async XLA Ops:
  16.7 53.4 %collective-permute-start.6 = (bf16[128,3072]{1,0:T(8,128)(2,1)}, bf16[128,3072]{1,0:T(8,128)(2,1)}, u32[]{:S(2)}, u32[]{:S(2)}) collective-permute-start(bf16[128,3072]{1,0:T(8,128)(2,1)} %get-tuple-element.111), channel_id=1, source_target_pairs={{0,4},{1,5},{2,6},{3,7},{4,0},{5,1},{6,2},{7,3},{8,12},{9,13},{10,... | collective-permute-start | bytes 2359304 | tf_op jit(solution)/shard_map/ppermute | solution.py:625
  19.2 51.4 %collective-permute-start.10 = (bf16[128,3072]{1,0:T(8,128)(2,1)}, bf16[128,3072]{1,0:T(8,128)(2,1)}, u32[]{:S(2)}, u32[]{:S(2)}) collective-permute-start(bf16[128,3072]{1,0:T(8,128)(2,1)} %get-tuple-element.111), channel_id=1, source_target_pairs={{0,6},{1,7},{2,0},{3,1},{4,2},{5,3},{6,4},{7,5},{8,14},{9,15},{10,... | collective-permute-start | bytes 2359304 | tf_op jit(solution)/shard_map/ppermute | solution.py:625
  139.2 44.9 %collective-permute-start.16 = (bf16[8,80,128]{2,1,0:T(8,128)(2,1)}, bf16[8,80,128]{2,1,0:T(8,128)(2,1)}, u32[]{:S(2)}, u32[]{:S(2)}) collective-permute-start(bf16[8,80,128]{2,1,0:T(8,128)(2,1)} %get-tuple-element.82), channel_id=1, source_target_pairs={{0,16},{1,17},{2,18},{3,19},{4,20},{5,21},{6,22},{7,23},{8,24},{9,... | collective-permute-start | bytes 491528 | tf_op jit(solution)/shard_map/ppermute | solution.py:625
  143.1 45.6 %collective-permute-start.14 = (bf16[64,2048]{1,0:T(8,128)(2,1)}, bf16[64,2048]{1,0:T(8,128)(2,1)S(1)}, u32[]{:S(2)}, u32[]{:S(2)}) collective-permute-start(bf16[64,2048]{1,0:T(8,128)(2,1)} %get-tuple-element.80), channel_id=1, source_target_pairs={{0,8},{1,9},{2,10},{3,11},{4,12},{5,13},{6,14},{7,15},{8,16},{9,17... | collective-permute-start | bytes 786440 | tf_op jit(solution)/shard_map/ppermute | solution.py:625
  144.5 43.0 %collective-permute-start.15 = (bf16[8,80,128]{2,1,0:T(8,128)(2,1)S(1)}, bf16[8,80,128]{2,1,0:T(8,128)(2,1)}, u32[]{:S(2)}, u32[]{:S(2)}) collective-permute-start(bf16[8,80,128]{2,1,0:T(8,128)(2,1)S(1)} %get-tuple-element.81), channel_id=1, source_target_pairs={{0,8},{1,9},{2,10},{3,11},{4,12},{5,13},{6,14},{7,15},{8,16},{9,17... | collective-permute-start | bytes 491528 | tf_op jit(solution)/shard_map/ppermute | solution.py:625
  152.8 133.4 %collective-permute-start.18 = (bf16[128,2048]{1,0:T(8,128)(2,1)}, bf16[128,2048]{1,0:T(8,128)(2,1)}, u32[]{:S(2)}, u32[]{:S(2)}) collective-permute-start(bf16[128,2048]{1,0:T(8,128)(2,1)} %get-tuple-element.109), channel_id=1, source_target_pairs={{0,1},{1,0},{2,3},{3,2},{4,5},{5,4},{6,7},{7,6},{8,9},{9,8},{10,11... | collective-permute-start | bytes 1572872 | tf_op jit(solution)/shard_map/ppermute | solution.py:625
  169.9 120.1 %collective-permute-start.20 = (bf16[128,2048]{1,0:T(8,128)(2,1)}, bf16[128,2048]{1,0:T(8,128)(2,1)S(1)}, u32[]{:S(2)}, u32[]{:S(2)}) collective-permute-start(bf16[128,2048]{1,0:T(8,128)(2,1)} %get-tuple-element.109), channel_id=1, source_target_pairs={{0,2},{1,3},{2,4},{3,5},{4,6},{5,7},{6,0},{7,1},{8,10},{9,11},{10,... | collective-permute-start | bytes 1572872 | tf_op jit(solution)/shard_map/ppermute | solution.py:625
  184.0 111.8 %collective-permute-start.24 = (bf16[128,2048]{1,0:T(8,128)(2,1)}, bf16[128,2048]{1,0:T(8,128)(2,1)S(1)}, u32[]{:S(2)}, u32[]{:S(2)}) collective-permute-start(bf16[128,2048]{1,0:T(8,128)(2,1)} %get-tuple-element.109), channel_id=1, source_target_pairs={{0,4},{1,5},{2,6},{3,7},{4,0},{5,1},{6,2},{7,3},{8,12},{9,13},{10,... | collective-permute-start | bytes 1572872 | tf_op jit(solution)/shard_map/ppermute | solution.py:625
  187.5 61.5 %collective-permute-start.51 = (bf16[64,2048]{1,0:T(8,128)(2,1)}, bf16[64,2048]{1,0:T(8,128)(2,1)S(1)}, u32[]{:S(2)}, u32[]{:S(2)}) collective-permute-start(bf16[64,2048]{1,0:T(8,128)(2,1)} %get-tuple-element.133), channel_id=1, source_target_pairs={{0,4},{1,5},{2,6},{3,7},{4,0},{5,1},{6,2},{7,3},{8,12},{9,13},{10,... | collective-permute-start | bytes 786440 | tf_op jit(solution)/shard_map/ppermute | solution.py:625
  188.7 65.8 %collective-permute-start.52 = (bf16[64,2048]{1,0:T(8,128)(2,1)}, bf16[64,2048]{1,0:T(8,128)(2,1)S(1)}, u32[]{:S(2)}, u32[]{:S(2)}) collective-permute-start(bf16[64,2048]{1,0:T(8,128)(2,1)} %get-tuple-element.132), channel_id=1, source_target_pairs={{0,4},{1,5},{2,6},{3,7},{4,0},{5,1},{6,2},{7,3},{8,12},{9,13},{10,... | collective-permute-start | bytes 786440 | tf_op jit(solution)/shard_map/ppermute | solution.py:625
  280.5 40.7 %collective-permute-start.49 = (bf16[256,2048]{1,0:T(8,128)(2,1)S(1)}, bf16[256,2048]{1,0:T(8,128)(2,1)S(1)}, u32[]{:S(2)}, u32[]{:S(2)}) collective-permute-start(bf16[256,2048]{1,0:T(8,128)(2,1)S(1)} %bitcast.178), channel_id=1, source_target_pairs={{0,1},{1,0},{2,3},{3,2},{4,5},{5,4},{6,7},{7,6},{8,9},{9,8},{10,11... | collective-permute-start | bytes 3145736 | tf_op jit(solution)/shard_map/ppermute | solution.py:625
  295.8 142.0 %collective-permute-start.33 = (bf16[2,2048,256]{2,1,0:T(8,128)(2,1)S(1)}, bf16[2,2048,256]{2,1,0:T(8,128)(2,1)S(1)}, u32[]{:S(2)}, u32[]{:S(2)}) collective-permute-start(bf16[2,2048,256]{2,1,0:T(8,128)(2,1)S(1)} %copy-done.55), channel_id=1, source_target_pairs={{0,2},{1,3},{2,0},{3,1},{4,6},{5,7},{6,4},{7,5},{8,10},{9,11},{10,... | collective-permute-start | bytes 6291464 | tf_op jit(solution)/shard_map/ppermute | solution.py:625
  331.1 55.5 %collective-permute-start.37 = (bf16[256,2048]{1,0:T(8,128)(2,1)S(1)}, bf16[256,2048]{1,0:T(8,128)(2,1)S(1)}, u32[]{:S(2)}, u32[]{:S(2)}) collective-permute-start(bf16[256,2048]{1,0:T(8,128)(2,1)S(1)} %copy-done.59), channel_id=1, source_target_pairs={{0,2},{1,3},{2,0},{3,1},{4,6},{5,7},{6,4},{7,5},{8,10},{9,11},{10,... | collective-permute-start | bytes 3145736 | tf_op jit(solution)/shard_map/ppermute | solution.py:625
  387.7 57.2 %collective-permute-start.38 = (bf16[256,2048]{1,0:T(8,128)(2,1)S(1)}, bf16[256,2048]{1,0:T(8,128)(2,1)S(1)}, u32[]{:S(2)}, u32[]{:S(2)}) collective-permute-start(bf16[256,2048]{1,0:T(8,128)(2,1)S(1)} %collective-permute-done.37), channel_id=1, source_target_pairs={{0,16},{1,17},{2,18},{3,19},{4,20},{5,21},{6,22},{7,23},{8,24},{9,... | collective-permute-start | bytes 3145736 | tf_op jit(solution)/shard_map/ppermute | solution.py:625
  387.7 64.9 %collective-permute-start.39 = (bf16[256,2048]{1,0:T(8,128)(2,1)S(1)}, bf16[256,2048]{1,0:T(8,128)(2,1)S(1)}, u32[]{:S(2)}, u32[]{:S(2)}) collective-permute-start(bf16[256,2048]{1,0:T(8,128)(2,1)S(1)} %collective-permute-done.37), channel_id=1, source_target_pairs={{0,8},{1,9},{2,10},{3,11},{4,12},{5,13},{6,14},{7,15},{8,0},{9,1},... | collective-permute-start | bytes 3145736 | tf_op jit(solution)/shard_map/ppermute | solution.py:625
  437.8 48.1 %collective-permute-start.34 = (bf16[2,2048,256]{2,1,0:T(8,128)(2,1)S(1)}, bf16[2,2048,256]{2,1,0:T(8,128)(2,1)S(1)}, u32[]{:S(2)}, u32[]{:S(2)}) collective-permute-start(bf16[2,2048,256]{2,1,0:T(8,128)(2,1)S(1)} %collective-permute-done.33), channel_id=1, source_target_pairs={{0,16},{1,17},{2,18},{3,19},{4,20},{5,21},{6,22},{7,23},{8,24},{9,... | collective-permute-start | bytes 6291464 | tf_op jit(solution)/shard_map/ppermute | solution.py:625
  439.8 59.6 %collective-permute-start.35 = (bf16[2,2048,256]{2,1,0:T(8,128)(2,1)S(1)}, bf16[2,2048,256]{2,1,0:T(8,128)(2,1)S(1)}, u32[]{:S(2)}, u32[]{:S(2)}) collective-permute-start(bf16[2,2048,256]{2,1,0:T(8,128)(2,1)S(1)} %collective-permute-done.33), channel_id=1, source_target_pairs={{0,8},{1,9},{2,10},{3,11},{4,12},{5,13},{6,14},{7,15},{8,0},{9,1},... | collective-permute-start | bytes 6291464 | tf_op jit(solution)/shard_map/ppermute | solution.py:625
  444.9 41.5 %collective-permute-start.40 = (bf16[256,2048]{1,0:T(8,128)(2,1)S(1)}, bf16[256,2048]{1,0:T(8,128)(2,1)S(1)}, u32[]{:S(2)}, u32[]{:S(2)}) collective-permute-start(bf16[256,2048]{1,0:T(8,128)(2,1)S(1)} %collective-permute-done.38), channel_id=1, source_target_pairs={{0,8},{1,9},{2,10},{3,11},{4,12},{5,13},{6,14},{7,15},{8,0},{9,1},... | collective-permute-start | bytes 3145736 | tf_op jit(solution)/shard_map/ppermute | solution.py:625
  522.9 45.1 %collective-permute-start.59 = (bf16[64,2048]{1,0:T(8,128)(2,1)}, bf16[64,2048]{1,0:T(8,128)(2,1)S(1)}, u32[]{:S(2)}, u32[]{:S(2)}) collective-permute-start(bf16[64,2048]{1,0:T(8,128)(2,1)} %get-tuple-element.126), channel_id=1, source_target_pairs={{0,1},{1,0},{2,3},{3,2},{4,5},{5,4},{6,7},{7,6},{8,9},{9,8},{10,11... | collective-permute-start | bytes 786440 | tf_op jit(solution)/shard_map/ppermute | solution.py:625
  523.6 44.3 %collective-permute-start.65 = (bf16[64,2048]{1,0:T(8,128)(2,1)}, bf16[64,2048]{1,0:T(8,128)(2,1)S(1)}, u32[]{:S(2)}, u32[]{:S(2)}) collective-permute-start(bf16[64,2048]{1,0:T(8,128)(2,1)} %get-tuple-element.127), channel_id=1, source_target_pairs={{0,1},{1,0},{2,3},{3,2},{4,5},{5,4},{6,7},{7,6},{8,9},{9,8},{10,11... | collective-permute-start | bytes 786440 | tf_op jit(solution)/shard_map/ppermute | solution.py:625
  524.9 43.1 %collective-permute-start.63 = (bf16[64,2048]{1,0:T(8,128)(2,1)}, bf16[64,2048]{1,0:T(8,128)(2,1)S(1)}, u32[]{:S(2)}, u32[]{:S(2)}) collective-permute-start(bf16[64,2048]{1,0:T(8,128)(2,1)} %get-tuple-element.128), channel_id=1, source_target_pairs={{0,1},{1,0},{2,3},{3,2},{4,5},{5,4},{6,7},{7,6},{8,9},{9,8},{10,11... | collective-permute-start | bytes 786440 | tf_op jit(solution)/shard_map/ppermute | solution.py:625
  525.7 42.3 %collective-permute-start.61 = (bf16[64,2048]{1,0:T(8,128)(2,1)}, bf16[64,2048]{1,0:T(8,128)(2,1)S(1)}, u32[]{:S(2)}, u32[]{:S(2)}) collective-permute-start(bf16[64,2048]{1,0:T(8,128)(2,1)} %get-tuple-element.129), channel_id=1, source_target_pairs={{0,1},{1,0},{2,3},{3,2},{4,5},{5,4},{6,7},{7,6},{8,9},{9,8},{10,11... | collective-permute-start | bytes 786440 | tf_op jit(solution)/shard_map/ppermute | solution.py:625
  553.6 62.0 %collective-permute-start.50 = (bf16[256,2048]{1,0:T(8,128)(2,1)S(1)}, bf16[256,2048]{1,0:T(8,128)(2,1)S(1)}, u32[]{:S(2)}, u32[]{:S(2)}) collective-permute-start(bf16[256,2048]{1,0:T(8,128)(2,1)S(1)} %slice.507), channel_id=1, source_target_pairs={{0,1},{1,0},{2,3},{3,2},{4,5},{5,4},{6,7},{7,6},{8,9},{9,8},{10,11... | collective-permute-start | bytes 3145736 | tf_op jit(solution)/shard_map/ppermute | solution.py:625
  571.4 44.2 %collective-permute-start.60 = (bf16[64,2048]{1,0:T(8,128)(2,1)S(1)}, bf16[64,2048]{1,0:T(8,128)(2,1)S(1)}, u32[]{:S(2)}, u32[]{:S(2)}) collective-permute-start(bf16[64,2048]{1,0:T(8,128)(2,1)S(1)} %get-tuple-element.116), channel_id=1, source_target_pairs={{0,4},{1,5},{2,6},{3,7},{4,0},{5,1},{6,2},{7,3},{8,12},{9,13},{10,... | collective-permute-start | bytes 786440 | tf_op jit(solution)/shard_map/ppermute | solution.py:625
  619.3 96.2 %collective-permute-start.67 = (bf16[256,2048]{1,0:T(8,128)(2,1)}, bf16[256,2048]{1,0:T(8,128)(2,1)}, u32[]{:S(2)}, u32[]{:S(2)}) collective-permute-start(bf16[256,2048]{1,0:T(8,128)(2,1)} %slice.506), channel_id=1, source_target_pairs={{0,1},{1,0},{2,3},{3,2},{4,5},{5,4},{6,7},{7,6},{8,9},{9,8},{10,11... | collective-permute-start | bytes 3145736 | tf_op jit(solution)/shard_map/ppermute | solution.py:625
  622.3 40.1 %collective-permute-start.72 = (bf16[64,2048]{1,0:T(8,128)(2,1)S(1)}, bf16[64,2048]{1,0:T(8,128)(2,1)S(1)}, u32[]{:S(2)}, u32[]{:S(2)}) collective-permute-start(bf16[64,2048]{1,0:T(8,128)(2,1)S(1)} %get-tuple-element.124), channel_id=1, source_target_pairs={{0,1},{1,0},{2,3},{3,2},{4,5},{5,4},{6,7},{7,6},{8,9},{9,8},{10,11... | collective-permute-start | bytes 786440 | tf_op jit(solution)/shard_map/ppermute | solution.py:625
  623.5 43.5 %collective-permute-start.70 = (bf16[64,2048]{1,0:T(8,128)(2,1)S(1)}, bf16[64,2048]{1,0:T(8,128)(2,1)S(1)}, u32[]{:S(2)}, u32[]{:S(2)}) collective-permute-start(bf16[64,2048]{1,0:T(8,128)(2,1)S(1)} %get-tuple-element.125), channel_id=1, source_target_pairs={{0,1},{1,0},{2,3},{3,2},{4,5},{5,4},{6,7},{7,6},{8,9},{9,8},{10,11... | collective-permute-start | bytes 786440 | tf_op jit(solution)/shard_map/ppermute | solution.py:625
  671.1 38.9 %collective-permute-start.71 = (bf16[64,2048]{1,0:T(8,128)(2,1)}, bf16[64,2048]{1,0:T(8,128)(2,1)}, u32[]{:S(2)}, u32[]{:S(2)}) collective-permute-start(bf16[64,2048]{1,0:T(8,128)(2,1)} %get-tuple-element.115), channel_id=1, source_target_pairs={{0,4},{1,5},{2,6},{3,7},{4,0},{5,1},{6,2},{7,3},{8,12},{9,13},{10,... | collective-permute-start | bytes 786440 | tf_op jit(solution)/shard_map/ppermute | solution.py:625
  671.2 44.4 %collective-permute-start.69 = (bf16[64,2048]{1,0:T(8,128)(2,1)}, bf16[64,2048]{1,0:T(8,128)(2,1)}, u32[]{:S(2)}, u32[]{:S(2)}) collective-permute-start(bf16[64,2048]{1,0:T(8,128)(2,1)} %get-tuple-element.112), channel_id=1, source_target_pairs={{0,4},{1,5},{2,6},{3,7},{4,0},{5,1},{6,2},{7,3},{8,12},{9,13},{10,... | collective-permute-start | bytes 786440 | tf_op jit(solution)/shard_map/ppermute | solution.py:625
  737.8 48.0 %collective-permute-start.78 = (bf16[8,80,128]{2,1,0:T(8,128)(2,1)}, bf16[8,80,128]{2,1,0:T(8,128)(2,1)}, u32[]{:S(2)}, u32[]{:S(2)}) collective-permute-start(bf16[8,80,128]{2,1,0:T(8,128)(2,1)} %get-tuple-element.97), channel_id=1, source_target_pairs={{24,0},{25,1},{26,2},{27,3},{28,4},{29,5},{30,6},{31,7}} | collective-permute-start | bytes 491528 | tf_op jit(solution)/shard_map/ppermute | solution.py:625
  739.4 46.4 %collective-permute-start.77 = (bf16[8,80,128]{2,1,0:T(8,128)(2,1)}, bf16[8,80,128]{2,1,0:T(8,128)(2,1)}, u32[]{:S(2)}, u32[]{:S(2)}) collective-permute-start(bf16[8,80,128]{2,1,0:T(8,128)(2,1)} %get-tuple-element.97), channel_id=1, source_target_pairs={{16,0},{17,1},{18,2},{19,3},{20,4},{21,5},{22,6},{23,7},{24,8},{25... | collective-permute-start | bytes 491528 | tf_op jit(solution)/shard_map/ppermute | solution.py:625
  740.7 45.1 %collective-permute-start.79 = (bf16[8,80,128]{2,1,0:T(8,128)(2,1)}, bf16[8,80,128]{2,1,0:T(8,128)(2,1)}, u32[]{:S(2)}, u32[]{:S(2)}) collective-permute-start(bf16[8,80,128]{2,1,0:T(8,128)(2,1)} %get-tuple-element.97), channel_id=1, source_target_pairs={{8,0},{9,1},{10,2},{11,3},{12,4},{13,5},{14,6},{15,7},{16,8},{17,9... | collective-permute-start | bytes 491528 | tf_op jit(solution)/shard_map/ppermute | solution.py:625
  (168 other events, 5273.7 us)

commit v2 on v1

--- a/solution.py
+++ b/solution.py
@@ -19,12 +19,18 @@
 FEAT = 2 * HEAD
 LOW = 128
 STATE = 80
+HALVES = 2
+VMEM_LIMIT = 58 << 20
+HALF = D // HALVES
+PER_HALF = KV_HEADS // HALVES
 SCALE = HEAD ** (-0.5)
 
 EPSILON = 1e-05
 THETA = 500000.0
 
 Z_SIZE = 4
+NEAR_BIT = 2
+FAR_BIT = 1
 CORES = 2
 F32 = jnp.float32
 BF16 = jnp.bfloat16
@@ -133,121 +139,158 @@
     return r[:size, :FEAT] + r[size:, FEAT:]
 
 
-def project_kernel(
-    x_ref, low_ref, w_ref, p_ref, cos_ref, sin_ref, maps_ref, survive_ref,
-    q_ref, kv_ref, kf_ref, rim_ref, near_ref, full_ref, keys_ref,
-):
-    n = pl.program_id(0)
+def whole(a):
+    return pl.BlockSpec(a.shape, lambda *_: (0,) * len(a.shape))
+
+
+ANYWHERE = pl.BlockSpec(memory_space=pl.ANY)
+SCALARS = pl.BlockSpec(memory_space=pltpu.SMEM)
+
+
+class Gathered:
+    def __init__(self, blocks, places, size):
+        self.blocks, self.places, self.size = blocks, places, size
+
+    def shapes(self):
+        return tuple(b.shape[0] // self.size for b in self.blocks)
+
+
+def start_rows(places, refs, counts, size, target, sem, column=0):
+    n = 0
+    columns = slice(column, column + target.shape[1])
+    for ref, count in zip(refs, counts):
+        for i in range(count):
+            to = pl.ds(pl.multiple_of(places[n] * size, size), size)
+            part = ref.at[i * size : (i + 1) * size, columns]
+            pltpu.make_async_copy(part, target.at[to], sem).start()
+            n += 1
+
+
+def wait_rows(target, sem):
+    pltpu.make_async_copy(target, target, sem).wait()
+
+
+def project_kv_kernel(*refs, counts, size):
+    n = len(counts)
+    places_ref, blocks = refs[0], refs[1 : 1 + n]
+    x_ref, low_ref, p_ref, cos_ref, sin_ref, maps_ref, survive_ref = refs[1 + n : 8 + n]
+    kv_ref, kf_ref, pack_ref, full_ref, w_ref, sem = refs[8 + n :]
     length = x_ref.shape[0]
-    q_steps = D // WIDE
-    k_steps = KVD // WIDE
-    raw = dot_nn(x_ref[...], w_ref[...]) + dot_nn(low_ref[...], p_ref[...])
-
-    @pl.when(n < q_steps)
-    def _():
-        q_ref[...] = turn(raw, cos_ref[...], sin_ref[...]).astype(BF16)
-
-    for i in range(k_steps):
-
-        @pl.when(n == q_steps + i)
-        def _():
-            keys = turn(raw, cos_ref[...], sin_ref[...]).astype(BF16)
-            keys_ref[i] = keys
-            for p in range(WIDE // FEAT):
-                at = (i * GROUPS + 2 * p) * FEAT
-                feats = pair_features(keys[:, p * FEAT : (p + 1) * FEAT], maps_ref[2 * i + p])
-                kf_ref[:, at : at + 2 * FEAT] = feats.astype(BF16)
-
-        @pl.when(n == q_steps + k_steps + i)
-        def _():
-            survive = survive_ref[...]
-            lo = low_half((length, FEAT))
-            for h in range(GROUPS):
-                p = h // 2
-                k2 = keys_ref[i][:, p * FEAT : (p + 1) * FEAT].astype(F32)
-                v2 = raw[:, p * FEAT : (p + 1) * FEAT].astype(BF16).astype(F32)
-                if h % 2:
-                    k2 = pltpu.roll(k2, HEAD, 1)
-                    v_low = pltpu.roll(v2, HEAD, 1)
-                else:
-                    v_low = v2
-                    v2 = pltpu.roll(v2, HEAD, 1)
-                g = i * GROUPS + h
-                at = g * FEAT
-                kv_ref[:, at : at + FEAT] = jnp.where(lo, k2, v2).astype(BF16)
-                ones = jnp.where(lane((length, FEAT)) < HEAD + 8, 1.0, 0.0)
-                v_one = jnp.where(lo, v_low, ones).astype(BF16)
-                feats = (kf_ref[:, at : at + FEAT].astype(F32) * survive).astype(BF16)
-                cut = length - WINDOW
-                head = dot_tn(v_one[:cut], feats[:cut])
-                tail = dot_tn(v_one[cut:], feats[cut:])
-                near_ref[g] = head[:STATE].astype(BF16)
-                full_ref[g] = (head + tail)[:STATE].astype(BF16)
-
-    @pl.when(n == pl.num_programs(0) - 1)
-    def _():
-        cut = length - WINDOW
-        rim_ref[:, : KV_HEADS * FEAT] = kv_ref[cut:, :]
-        rim_ref[:, KV_HEADS * FEAT :] = kf_ref[cut:, :]
-
-
-def project(x, low, w, p, cosine, sine, maps, survive):
+    start_rows(places_ref, blocks, counts, size, w_ref, sem, D)
+    wait_rows(w_ref, sem)
+    survive = survive_ref[...]
+    lo = low_half((length, FEAT))
+    cut = length - WINDOW
+    steps = KVD // WIDE
+    part = lambda j: slice(j * WIDE, (j + 1) * WIDE)
+    for i in range(steps):
+        raw_k, raw_v = (
+            dot_nn(x_ref[...], w_ref[:, part(j)]) + dot_nn(low_ref[...], p_ref[:, part(j)])
+            for j in (i, steps + i)
+        )
+        keys = turn(raw_k, cos_ref[...], sin_ref[...]).astype(BF16)
+        values = raw_v.astype(BF16).astype(F32)
+        for p in range(WIDE // FEAT):
+            at = (i * GROUPS + 2 * p) * FEAT
+            k2 = keys[:, p * FEAT : (p + 1) * FEAT]
+            v2 = values[:, p * FEAT : (p + 1) * FEAT]
+            feats = pair_features(k2, maps_ref[2 * i + p])
+            kf_ref[:, at : at + 2 * FEAT] = feats.astype(BF16)
+            k2 = k2.astype(F32)
+            k_other, v_other = pltpu.roll(k2, HEAD, 1), pltpu.roll(v2, HEAD, 1)
+            ones = jnp.where(lane((length, FEAT)) < HEAD + 8, 1.0, 0.0)
+            for h, kv, v in (
+                (0, jnp.where(lo, k2, v_other), v2),
+                (1, jnp.where(lo, k_other, v2), v_other),
+            ):
+                at_h = at + h * FEAT
+                kv_ref[:, at_h : at_h + FEAT] = kv.astype(BF16)
+                v_one = jnp.where(lo, v, ones).astype(BF16)
+                kept = (feats[:, h * FEAT : (h + 1) * FEAT].astype(BF16).astype(F32) * survive)
+                kept = kept.astype(BF16)
+                head = dot_tn(v_one[:cut], kept[:cut])
+                tail = dot_tn(v_one[cut:], kept[cut:])
+                at_h = slice(at_h, at_h + FEAT)
+                pack_ref[2 * WINDOW :, at_h] = head[:STATE].astype(BF16)
+                full_ref[:, at_h] = (head + tail)[:STATE].astype(BF16)
+    pack_ref[:WINDOW, :] = kv_ref[cut:, :]
+    pack_ref[WINDOW : 2 * WINDOW, :] = kf_ref[cut:, :]
+
+
+def project_kv(w, x, low, p, cosine, sine, maps, survive):
     length = x.shape[0]
-    steps = QKV // WIDE
-    whole = lambda a: pl.BlockSpec(a.shape, lambda n: (0,) * a.ndim)
-    q_last = D // WIDE - 1
     shapes = (
-        jax.ShapeDtypeStruct((length, D), BF16),
         jax.ShapeDtypeStruct((length, KV_HEADS * FEAT), BF16),
         jax.ShapeDtypeStruct((length, KV_HEADS * FEAT), BF16),
-        jax.ShapeDtypeStruct((WINDOW, 2 * KV_HEADS * FEAT), BF16),
-        jax.ShapeDtypeStruct((KV_HEADS, STATE, FEAT), BF16),
-        jax.ShapeDtypeStruct((KV_HEADS, STATE, FEAT), BF16),
-    )
+        jax.ShapeDtypeStruct((2 * WINDOW + STATE, KV_HEADS * FEAT), BF16),
+        jax.ShapeDtypeStruct((STATE, KV_HEADS * FEAT), BF16),
+    )
+    rest = (x, low, p, cosine, sine, maps, survive)
     return pl.pallas_call(
-        project_kernel,
-        grid=(steps,),
-        in_specs=[
-            whole(x), whole(low),
-            pl.BlockSpec((D, WIDE), lambda n: (0, n)),
-            pl.BlockSpec((LOW, WIDE), lambda n: (0, n)),
-            whole(cosine), whole(sine), whole(maps), whole(survive),
-        ],
-        out_specs=[pl.BlockSpec((length, WIDE), lambda n: (0, jnp.minimum(n, q_last)))]
-        + [whole(s) for s in shapes[1:]],
+        functools.partial(project_kv_kernel, counts=w.shapes(), size=w.size),
+        grid=(1,),
+        in_specs=[SCALARS] + [ANYWHERE] * len(w.blocks) + [whole(a) for a in rest],
+        out_specs=[whole(v) for v in shapes],
         out_shape=shapes,
-        scratch_shapes=[pltpu.VMEM((KVD // WIDE, length, WIDE), BF16)],
-        compiler_params=pltpu.CompilerParams(vmem_limit_bytes=40 << 20),
+        scratch_shapes=[pltpu.VMEM((D, 2 * KVD), BF16), pltpu.SemaphoreType.DMA],
+        compiler_params=pltpu.CompilerParams(vmem_limit_bytes=VMEM_LIMIT),
         cost_estimate=pl.CostEstimate(
-            flops=2 * length * D * QKV, bytes_accessed=2 * D * QKV, transcendentals=0
+            flops=4 * length * D * KVD, bytes_accessed=4 * D * KVD, transcendentals=0
         ),
-        name="project",
-    )(x, low, w, p, cosine, sine, maps, survive)
-
-
-def features_kernel(q_ref, maps_ref, out_ref):
+        name="project_kv",
+    )(w.places, *w.blocks, *rest)
+
+
+def project_q_kernel(*refs, counts, size, column):
+    n = len(counts)
+    places_ref, blocks = refs[0], refs[1 : 1 + n]
+    x_ref, low_ref, p_ref, cos_ref, sin_ref, maps_ref, q_ref, qf_ref, w_ref, sem = refs[1 + n :]
+    step = pl.program_id(0)
+
+    @pl.when(step == 0)
+    def _():
+        start_rows(places_ref, blocks, counts, size, w_ref, sem, column)
+        wait_rows(w_ref, sem)
+
+    at = pl.ds(pl.multiple_of(step * WIDE, WIDE), WIDE)
+    raw = dot_nn(x_ref[...], w_ref[:, at]) + dot_nn(low_ref[...], p_ref[...])
+    q = turn(raw, cos_ref[...], sin_ref[...]).astype(BF16)
+    q_ref[...] = q
     for p in range(WIDE // FEAT):
-        feats = pair_features(q_ref[:, p * FEAT : (p + 1) * FEAT], maps_ref[p])
-        out_ref[:, 2 * p * FEAT : 2 * (p + 1) * FEAT] = feats.astype(BF16)
-
-
-def features(q, maps):
-    length = q.shape[0]
+        feats = pair_features(q[:, p * FEAT : (p + 1) * FEAT], maps_ref[p])
+        qf_ref[:, 2 * p * FEAT : 2 * (p + 1) * FEAT] = feats.astype(BF16)
+
+
+def project_q(half, w, x, low, p, cosine, sine, maps):
+    length = x.shape[0]
+    first = half * PER_HALF
     pairs = WIDE // FEAT
     return pl.pallas_call(
-        features_kernel,
-        grid=(D // WIDE,),
-        in_specs=[
+        functools.partial(
+            project_q_kernel, counts=w.shapes(), size=w.size, column=half * HALF
+        ),
+        grid=(HALF // WIDE,),
+        in_specs=[SCALARS] + [ANYWHERE] * len(w.blocks) + [
+            whole(x), whole(low),
+            pl.BlockSpec((LOW, WIDE), lambda g: (0, first + g)),
+            whole(cosine), whole(sine),
+            pl.BlockSpec((pairs, FEAT, 2 * FEAT), lambda g: (first + g, 0, 0)),
+        ],
+        out_specs=[
             pl.BlockSpec((length, WIDE), lambda g: (0, g)),
-            pl.BlockSpec((pairs, FEAT, 2 * FEAT), lambda g: (g, 0, 0)),
+            pl.BlockSpec((length, 2 * WIDE), lambda g: (0, g)),
         ],
-        out_specs=pl.BlockSpec((length, 2 * WIDE), lambda g: (0, g)),
-        out_shape=jax.ShapeDtypeStruct((length, 2 * D), BF16),
+        out_shape=[
+            jax.ShapeDtypeStruct((length, HALF), BF16),
+            jax.ShapeDtypeStruct((length, 2 * HALF), BF16),
+        ],
+        scratch_shapes=[pltpu.VMEM((D, HALF), BF16), pltpu.SemaphoreType.DMA],
+        compiler_params=pltpu.CompilerParams(vmem_limit_bytes=VMEM_LIMIT),
         cost_estimate=pl.CostEstimate(
-            flops=8_000_000_000, bytes_accessed=6 * length * D, transcendentals=2 * length * D
+            flops=2 * length * D * HALF, bytes_accessed=2 * D * HALF, transcendentals=0
         ),
-        name="features",
-    )(q, maps)
+        name="project_q",
+    )(w.places, *w.blocks, x, low, p, cosine, sine, maps)
 
 
 def key_tiles(kv_ref, kf_ref, rim_kv_ref, rim_kf_ref, mask):
@@ -294,7 +337,7 @@
 
 
 def carried(carry_ref):
-    state = carry_ref[0]
+    state = carry_ref[...]
     ones = jnp.zeros((HEAD, FEAT), BF16) + state[HEAD : HEAD + 1, :]
     return diagonal_pair(state[:HEAD, :]), diagonal_pair(ones)
 
@@ -330,44 +373,47 @@
     out_ref[...] = att.astype(BF16)
 
 
-def group_specs(length):
+def group_specs(length, half):
+    first = half * PER_HALF
     column = lambda rows, width: pl.BlockSpec((rows, width), lambda g: (0, g))
-    whole = lambda rows, width: pl.BlockSpec((rows, width), lambda g: (0, 0))
+    shared = lambda rows, width, at: pl.BlockSpec((rows, width), lambda g: (0, at + g))
+    fixed = lambda rows, width: pl.BlockSpec((rows, width), lambda g: (0, 0))
     return dict(
         q=column(length, WIDE),
         qf=column(length, 2 * WIDE),
-        k=column(length, FEAT),
-        rim_kv=pl.BlockSpec((WINDOW, FEAT), lambda g: (0, g)),
-        rim_kf=pl.BlockSpec((WINDOW, FEAT), lambda g: (0, KV_HEADS + g)),
-        state=pl.BlockSpec((1, STATE, FEAT), lambda g: (g, 0, 0)),
-        qdoc=whole(length, 1),
-        kdoc=whole(8, WIDE),
-        gamma=column(1, WIDE),
-        wide=whole(length, WIDE),
-        maps=pl.BlockSpec((GROUPS // 2, FEAT, 2 * FEAT), lambda g: (g, 0, 0)),
-    )
-
-
-def attend(q, qf, kv, kf, rim, carry, masks):
+        k=shared(length, FEAT, first),
+        rim_kv=shared(WINDOW, FEAT, first),
+        rim_kf=pl.BlockSpec((WINDOW, FEAT), lambda g: (1, first + g)),
+        state=shared(STATE, FEAT, first),
+        back=column(STATE, FEAT),
+        qdoc=fixed(length, 1),
+        kdoc=fixed(8, WIDE),
+        gamma=shared(1, WIDE, first),
+        wide=fixed(length, WIDE),
+        maps=pl.BlockSpec((GROUPS // 2, FEAT, 2 * FEAT), lambda g: (first + g, 0, 0)),
+    )
+
+
+def attend(half, q, qf, kv, kf, rim, carry, masks):
     length = q.shape[0]
-    s = group_specs(length)
+    s = group_specs(length, half)
     return pl.pallas_call(
         attend_kernel,
-        grid=(KV_HEADS,),
+        grid=(PER_HALF,),
         in_specs=[
             s["q"], s["qf"], s["k"], s["k"], s["rim_kv"], s["rim_kf"], s["state"],
             s["qdoc"], s["kdoc"], s["qdoc"], s["gamma"],
         ],
         out_specs=[s["q"]] * 3,
         out_shape=[
-            jax.ShapeDtypeStruct((length, D), BF16),
-            jax.ShapeDtypeStruct((length, D), F32),
-            jax.ShapeDtypeStruct((length, D), F32),
+            jax.ShapeDtypeStruct((length, HALF), BF16),
+            jax.ShapeDtypeStruct((length, HALF), F32),
+            jax.ShapeDtypeStruct((length, HALF), F32),
         ],
         scratch_shapes=[pltpu.VMEM((length, WIDE), F32)] * 2,
-        compiler_params=pltpu.CompilerParams(vmem_limit_bytes=32 << 20),
+        compiler_params=pltpu.CompilerParams(vmem_limit_bytes=VMEM_LIMIT),
         cost_estimate=pl.CostEstimate(
-            flops=10_000_000_000, bytes_accessed=16 * length * D, transcendentals=0
+            flops=5_000_000_000, bytes_accessed=8 * length * D, transcendentals=0
         ),
         name="attend",
     )(q, qf, kv, kf, rim, rim, carry, masks["qdoc"], masks["kdoc"], masks["fresh"], masks["gamma"])
@@ -396,23 +442,24 @@
         at = slice(p * FEAT, (p + 1) * FEAT)
         kv += fold_pair(dot_tn(fresh_g[:, at], feats), HEAD)
         sums += fold_pair(dot_tn(fresh_gd[:, at], feats), HEAD)
-    back_ref[0, :HEAD, :] = kv.astype(BF16)
-    back_ref[0, HEAD:, :] = sums[: STATE - HEAD].astype(BF16)
-
-
-def scaled_grads(ga, att, inv, qf, masks):
+    back_ref[:HEAD, :] = kv.astype(BF16)
+    back_ref[HEAD:, :] = sums[: STATE - HEAD].astype(BF16)
+
+
+def scaled_grads(half, ga, att, inv, qf, masks):
     length = ga.shape[0]
-    s = group_specs(length)
+    s = group_specs(length, half)
     return pl.pallas_call(
         scaled_grads_kernel,
-        grid=(KV_HEADS,),
+        grid=(PER_HALF,),
         in_specs=[s["q"], s["q"], s["q"], s["qf"], s["qdoc"], s["gamma"]],
-        out_specs=[s["q"], s["q"], s["state"]],
+        out_specs=[s["q"], s["q"], s["back"]],
         out_shape=[
-            jax.ShapeDtypeStruct((length, D), BF16),
-            jax.ShapeDtypeStruct((length, D), F32),
-            jax.ShapeDtypeStruct((KV_HEADS, STATE, FEAT), BF16),
+            jax.ShapeDtypeStruct((length, HALF), BF16),
+            jax.ShapeDtypeStruct((length, HALF), F32),
+            jax.ShapeDtypeStruct((STATE, PER_HALF * FEAT), BF16),
         ],
+        compiler_params=pltpu.CompilerParams(vmem_limit_bytes=VMEM_LIMIT),
         name="scaled_grads",
     )(ga, att, inv, qf, masks["fresh"], masks["gamma"])
 
@@ -420,7 +467,7 @@
 def attend_back_kernel(
     q_ref, qf_ref, kv_ref, kf_ref, rim_kv_ref, rim_kf_ref, carry_ref, g_ref, gd_ref,
     qdoc_ref, kdoc_ref, fresh_ref, gamma_ref, maps_ref, cos_ref, sin_ref,
-    raw_ref, dkv_ref, dkf_ref, dmap_ref, logit_ref, dq_ref, dqf_ref,
+    raw_ref, dkv_ref, dkf_ref, rim_ref, dmap_ref, logit_ref, dq_ref, dqf_ref,
 ):
     length = q_ref.shape[0]
     mask = same_head(WINDOW)
@@ -456,8 +503,12 @@
         dq_ref[a:c, :] += dot_nn(ds, tile[0])
         dk = fold_heads(dot_tn(ds, q_ref[a:c, :]), mask) * SCALE
         dv = fold_heads(dot_tn(w, g), mask)
-        at = slice(t * WINDOW, (t + 1) * WINDOW)
-        dkv_ref[at, :] = jnp.where(lo, dk, dv)
+        at = slice((t - 1) * WINDOW, t * WINDOW)
+        dkv = jnp.where(lo, dk, dv)
+        if t:
+            dkv_ref[at, :] = dkv
+        else:
+            rim_ref[:WINDOW, :] = dkv.astype(BF16)
         if b < length:
             far = x[b - a :] * gamma
             parts = [jnp.where(same(b, c) & upper, far[: c - b], 0.0)]
@@ -468,7 +519,10 @@
             for p in pairs:
                 dqf_ref[b:, full(p)] += dot_nn(dl[:, half(p)], tile[2])
                 dkf += fold_pair(dot_tn(dl[:, half(p)], qf_ref[b:, full(p)]), HEAD)
-            dkf_ref[at, :] = dkf
+            if t:
+                dkf_ref[at, :] = dkf
+            else:
+                rim_ref[WINDOW:, :] = dkf.astype(BF16)
         else:
             dkf_ref[at, :] = jnp.zeros((WINDOW, FEAT), F32)
     for p in pairs:
@@ -487,34 +541,34 @@
     raw_ref[...] = turn(dq_ref[...], cos_ref[...], -sin_ref[...]).astype(BF16)
 
 
-def attend_back(q, qf, kv, kf, rim, carry, g, gd, masks, maps):
+def attend_back(half, q, qf, kv, kf, rim, carry, g, gd, masks, maps):
     length = q.shape[0]
-    extended = length + WINDOW
-    s = group_specs(length)
-    column = pl.BlockSpec((extended, FEAT), lambda g: (0, g))
+    s = group_specs(length, half)
+    column = lambda rows: pl.BlockSpec((rows, FEAT), lambda g: (0, g))
     return pl.pallas_call(
         attend_back_kernel,
-        grid=(KV_HEADS,),
+        grid=(PER_HALF,),
         in_specs=[
             s["q"], s["qf"], s["k"], s["k"], s["rim_kv"], s["rim_kf"], s["state"], s["q"], s["q"],
             s["qdoc"], s["kdoc"], s["qdoc"], s["gamma"], s["maps"], s["wide"], s["wide"],
         ],
         out_specs=[
-            s["q"], column, column,
+            s["q"], column(length), column(length), column(2 * WINDOW),
             pl.BlockSpec((GROUPS, HEAD, FEAT), lambda g: (g, 0, 0)),
             pl.BlockSpec((1, 8, FEAT), lambda g: (g, 0, 0)),
         ],
         out_shape=[
-            jax.ShapeDtypeStruct((length, D), BF16),
-            jax.ShapeDtypeStruct((extended, KV_HEADS * FEAT), F32),
-            jax.ShapeDtypeStruct((extended, KV_HEADS * FEAT), F32),
-            jax.ShapeDtypeStruct((HEADS, HEAD, FEAT), F32),
-            jax.ShapeDtypeStruct((KV_HEADS, 8, FEAT), F32),
+            jax.ShapeDtypeStruct((length, HALF), BF16),
+            jax.ShapeDtypeStruct((length, PER_HALF * FEAT), F32),
+            jax.ShapeDtypeStruct((length, PER_HALF * FEAT), F32),
+            jax.ShapeDtypeStruct((2 * WINDOW, PER_HALF * FEAT), BF16),
+            jax.ShapeDtypeStruct((HEADS // HALVES, HEAD, FEAT), F32),
+            jax.ShapeDtypeStruct((PER_HALF, 8, FEAT), F32),
         ],
         scratch_shapes=[pltpu.VMEM((length, WIDE), F32), pltpu.VMEM((length, 2 * WIDE), F32)],
-        compiler_params=pltpu.CompilerParams(vmem_limit_bytes=32 << 20),
+        compiler_params=pltpu.CompilerParams(vmem_limit_bytes=VMEM_LIMIT),
         cost_estimate=pl.CostEstimate(
-            flops=30_000_000_000, bytes_accessed=16 * length * D, transcendentals=0
+            flops=15_000_000_000, bytes_accessed=8 * length * D, transcendentals=0
         ),
         name="attend_back",
     )(
@@ -542,19 +596,19 @@
         v_one = jnp.where(lo, v_low, ones).astype(BF16)[:, :STATE]
         dkf, dv = [], []
         for back, part in ((near_ref, slice(0, cut)), (far_ref, slice(cut, length))):
-            state = back[h]
+            state = back[:, at]
             twice = jnp.concatenate([state[:HEAD], state[:HEAD]], axis=0)
             dkf.append(dot_nn(v_one[part], state))
             dv.append(dot_nt(kf[part], twice))
         rim = jnp.zeros((cut, FEAT), F32)
         dkf = (
             jnp.concatenate(dkf, axis=0) * survive
-            + dkf_ref[WINDOW:, at]
+            + dkf_ref[:, at]
             + jnp.concatenate([rim, rim_kf_ref[:, at].astype(F32)], axis=0)
         )
         dv = jnp.concatenate(dv, axis=0) * survive
         total = (
-            dkv_ref[WINDOW:, at]
+            dkv_ref[:, at]
             + jnp.concatenate([rim, rim_kv_ref[:, at].astype(F32)], axis=0)
             + jnp.where(lo, 0.0, dv)
         )
@@ -571,33 +625,314 @@
     rv_ref[...] = jnp.where(lo, pltpu.roll(dkv[0], HEAD, 1), dkv[1]).astype(BF16)
 
 
-def keys_back(kv, kf, dkv, dkf, rim, near, far, masks, maps):
+def keys_back(half, kv, kf, dkv, dkf, rim, near, far, masks, maps):
     length = kv.shape[0]
-    extended = length + WINDOW
-    pairs = KV_HEADS // 2
+    pairs = PER_HALF // 2
+    first = half * pairs
     column = lambda rows: pl.BlockSpec((rows, 2 * FEAT), lambda g: (0, g))
-    state = pl.BlockSpec((2, STATE, FEAT), lambda g: (g, 0, 0))
+    shared = pl.BlockSpec((length, 2 * FEAT), lambda g: (0, first + g))
+    state = pl.BlockSpec((STATE, 2 * FEAT), lambda g: (0, first + g))
     narrow = pl.BlockSpec((length, FEAT), lambda g: (0, 0))
     out = pl.BlockSpec((length, FEAT), lambda g: (0, g))
     return pl.pallas_call(
         keys_back_kernel,
         grid=(pairs,),
         in_specs=[
-            column(length), column(length), column(extended), column(extended),
-            column(WINDOW), pl.BlockSpec((WINDOW, 2 * FEAT), lambda g: (0, pairs + g)),
+            shared, shared, column(length), column(length),
+            column(WINDOW), pl.BlockSpec((WINDOW, 2 * FEAT), lambda g: (1, g)),
             state, state, pl.BlockSpec((length, 1), lambda g: (0, 0)),
-            pl.BlockSpec((1, FEAT, 2 * FEAT), lambda g: (g, 0, 0)), narrow, narrow,
+            pl.BlockSpec((1, FEAT, 2 * FEAT), lambda g: (first + g, 0, 0)), narrow, narrow,
         ],
         out_specs=[out, out, pl.BlockSpec((2, HEAD, FEAT), lambda g: (g, 0, 0))],
         out_shape=[
-            jax.ShapeDtypeStruct((length, KVD), BF16),
-            jax.ShapeDtypeStruct((length, KVD), BF16),
-            jax.ShapeDtypeStruct((KV_HEADS, HEAD, FEAT), F32),
+            jax.ShapeDtypeStruct((length, KVD // HALVES), BF16),
+            jax.ShapeDtypeStruct((length, KVD // HALVES), BF16),
+            jax.ShapeDtypeStruct((PER_HALF, HEAD, FEAT), F32),
         ],
+        compiler_params=pltpu.CompilerParams(vmem_limit_bytes=VMEM_LIMIT),
         name="keys_back",
     )(
         kv, kf, dkv, dkf, rim, rim, near, far, masks["survive"], maps, masks["cos"], masks["sin"]
     )
+
+
+def out_project_kernel(*refs, counts, size):
+    n = len(counts)
+    places, blocks, refs = refs[0], refs[1 : 1 + n], refs[1 + n :]
+    m0, m1, hidden, proj_in, proj_out, gain = refs[:6]
+    residual, second, low, inverse, w, sem = refs[6:]
+    start_rows(places, blocks, counts, size, w, sem)
+    reduced = dot_nn(m0[...], proj_in[:HALF, :]) + dot_nn(m1[...], proj_in[HALF:, :])
+    reduced = reduced.astype(BF16)
+    low[...] = reduced
+    wait_rows(w, sem)
+    squares = 0.0
+    for j in range(D // WIDE):
+        at = slice(j * WIDE, (j + 1) * WIDE)
+        sums = (
+            hidden[:, at].astype(F32)
+            + dot_nn(m0[...], w[:HALF, at])
+            + dot_nn(m1[...], w[HALF:, at])
+            + dot_nn(reduced, proj_out[:, at])
+        )
+        residual[:, at] = sums
+        squares = squares + jnp.sum(sums * sums, axis=1, keepdims=True)
+    inv = lax.rsqrt(squares * (1.0 / D) + EPSILON)
+    inverse[...] = jnp.zeros(inverse.shape, F32) + inv
+    second[...] = (residual[...] * inv * gain[...]).astype(BF16)
+
+
+def out_project(w, merged, hidden, proj_in, proj_out, gain):
+    length = hidden.shape[0]
+    shapes = (
+        jax.ShapeDtypeStruct((length, D), F32),
+        jax.ShapeDtypeStruct((length, D), BF16),
+        jax.ShapeDtypeStruct((length, LOW), BF16),
+        jax.ShapeDtypeStruct((length, LOW), F32),
+    )
+    rest = (*merged, hidden, proj_in, proj_out, gain)
+    return pl.pallas_call(
+        functools.partial(out_project_kernel, counts=w.shapes(), size=w.size),
+        grid=(1,),
+        in_specs=[SCALARS] + [ANYWHERE] * len(w.blocks) + [whole(a) for a in rest],
+        out_specs=[whole(v) for v in shapes],
+        out_shape=shapes,
+        scratch_shapes=[pltpu.VMEM((D, D), BF16), pltpu.SemaphoreType.DMA],
+        compiler_params=pltpu.CompilerParams(vmem_limit_bytes=VMEM_LIMIT),
+        cost_estimate=pl.CostEstimate(
+            flops=2 * length * D * D, bytes_accessed=2 * D * D, transcendentals=0
+        ),
+        name="out_project",
+    )(w.places, *w.blocks, *rest)
+
+
+def branch_back_kernel(*refs, counts, size, extra):
+    n = len(counts)
+    places, blocks, refs = refs[0], refs[1 : 1 + n], refs[1 + n :]
+    sums, refs = refs[:extra], refs[extra:]
+    cot, residual, inverse, gain, proj_in, proj_out, m0, m1, low = refs[:9]
+    grad_residual, g0, g1, grad_gain, grad_in, grad_out, w, sem = refs[9:]
+    start_rows(places, blocks, counts, size, w, sem)
+    total = sums[0][...].astype(F32)
+    for v in sums[1:]:
+        total = total + v[...].astype(F32)
+    inv = inverse[:, :1]
+    normed = residual[...] * inv
+    product = total * normed
+    grad_gain[...] = jnp.sum(product, axis=0, keepdims=True)
+    scaled = total * gain[...]
+    mean = jnp.sum(scaled * normed, axis=1, keepdims=True) * (1.0 / D)
+    grad = cot[...].astype(F32) + inv * (scaled - normed * mean)
+    grad_residual[...] = grad
+    branch = grad.astype(BF16)
+    grad_low = dot_nt(branch, proj_out[...]).astype(BF16)
+    grad_out[...] = dot_tn(low[...], branch)
+    for i, m in enumerate((m0, m1)):
+        grad_in[:, i * HALF : (i + 1) * HALF] = dot_tn(grad_low, m[...])
+    wait_rows(w, sem)
+    for j in range(D // WIDE):
+        at = slice(j * WIDE, (j + 1) * WIDE)
+        i, col = j // (HALF // WIDE), (j % (HALF // WIDE)) * WIDE
+        back = dot_nt(grad_low, proj_in[at, :]) + dot_nt(branch, w[at, :])
+        (g0, g1)[i][:, col : col + WIDE] = back.astype(BF16)
+
+
+def branch_back(w, sums, cot, residual, inverse, gain, proj_in, proj_out, merged, low):
+    length = cot.shape[0]
+    shapes = (
+        jax.ShapeDtypeStruct((length, D), F32),
+        jax.ShapeDtypeStruct((length, HALF), BF16),
+        jax.ShapeDtypeStruct((length, HALF), BF16),
+        jax.ShapeDtypeStruct((1, D), F32),
+        jax.ShapeDtypeStruct((LOW, D), F32),
+        jax.ShapeDtypeStruct((LOW, D), F32),
+    )
+    rest = (*sums, cot, residual, inverse, gain, proj_in, proj_out, *merged, low)
+    return pl.pallas_call(
+        functools.partial(
+            branch_back_kernel, counts=w.shapes(), size=w.size, extra=len(sums)
+        ),
+        grid=(1,),
+        in_specs=[SCALARS] + [ANYWHERE] * len(w.blocks) + [whole(a) for a in rest],
+        out_specs=[whole(v) for v in shapes],
+        out_shape=shapes,
+        scratch_shapes=[pltpu.VMEM((D, D), BF16), pltpu.SemaphoreType.DMA],
+        compiler_params=pltpu.CompilerParams(vmem_limit_bytes=VMEM_LIMIT),
+        cost_estimate=pl.CostEstimate(
+            flops=2 * length * D * D, bytes_accessed=2 * D * D, transcendentals=0
+        ),
+        name="branch_back",
+    )(w.places, *w.blocks, *rest)
+
+
+def inputs_back_kernel(*refs, counts, size):
+    n = len(counts)
+    places, blocks, refs = refs[0], refs[1 : 1 + n], refs[1 + n :]
+    raws, refs = refs[:6], refs[6:]
+    p_in, p_out, low, x, hidden, gain, grad_residual = refs[:7]
+    grad_tokens, grad_gain, grad_in, grad_out, w, raw, back, sem = refs[7:]
+    start_rows(places, blocks, counts, size, w, sem)
+    at = 0
+    for r in raws:
+        raw[:, at : at + r.shape[1]] = r[...]
+        at += r.shape[1]
+    grad_low = dot_nt(raw[...], p_out[...]).astype(BF16)
+    grad_out[...] = dot_tn(low[...], raw[...])
+    grad_in[...] = dot_tn(grad_low, x[...])
+    wait_rows(w, sem)
+    values = hidden[...].astype(F32)
+    inv = lax.rsqrt(jnp.sum(values * values, axis=1, keepdims=True) * (1.0 / D) + EPSILON)
+    mean = 0.0
+    for j in range(D // WIDE):
+        at = slice(j * WIDE, (j + 1) * WIDE)
+        part = dot_nt(grad_low, p_in[at, :]) + dot_nt(raw[...], w[at, :])
+        normed = hidden[:, at].astype(F32) * inv
+        product = part * normed
+        grad_gain[:, at] = jnp.sum(product, axis=0, keepdims=True)
+        mean = mean + jnp.sum(product * gain[:, at], axis=1, keepdims=True)
+        back[:, at] = part
+    mean = mean * (1.0 / D)
+    grad_tokens[...] = grad_residual[...] + inv * (
+        back[...] * gain[...] - values * inv * mean
+    )
+
+
+def inputs_back(w, raws, p_in, p_out, low, x, hidden, gain, grad_residual):
+    length = x.shape[0]
+    shapes = (
+        jax.ShapeDtypeStruct((length, D), F32),
+        jax.ShapeDtypeStruct((1, D), F32),
+        jax.ShapeDtypeStruct((LOW, D), F32),
+        jax.ShapeDtypeStruct((LOW, QKV), F32),
+    )
+    rest = (*raws, p_in, p_out, low, x, hidden, gain, grad_residual)
+    return pl.pallas_call(
+        functools.partial(inputs_back_kernel, counts=w.shapes(), size=w.size),
+        grid=(1,),
+        in_specs=[SCALARS] + [ANYWHERE] * len(w.blocks) + [whole(a) for a in rest],
+        out_specs=[whole(v) for v in shapes],
+        out_shape=shapes,
+        scratch_shapes=[
+            pltpu.VMEM((D, QKV), BF16),
+            pltpu.VMEM((length, QKV), BF16),
+            pltpu.VMEM((length, D), F32),
+            pltpu.SemaphoreType.DMA,
+        ],
+        compiler_params=pltpu.CompilerParams(vmem_limit_bytes=VMEM_LIMIT),
+        cost_estimate=pl.CostEstimate(
+            flops=2 * length * D * QKV, bytes_accessed=2 * D * QKV, transcendentals=0
+        ),
+        name="inputs_back",
+    )(w.places, *w.blocks, *rest)
+
+
+def mlp_kernel(places_ref, *refs, rows, parts, tile):
+    n = len(rows[0]) + len(rows[1])
+    tokens, refs = refs[:n], refs[n:]
+    own_gu, own_dn = refs[:2]
+    pair_gu, pair_dn, refs = refs[2 : 2 + parts], refs[2 + parts : 2 + 2 * parts], refs[2 + 2 * parts :]
+    out_ref, back_ref, h, c, gu, dn, out, back, row_sem, gu_sem, dn_sem = refs
+    step, steps = pl.program_id(0), pl.num_programs(0)
+    own_tiles = own_gu.shape[2] // tile
+    width = D // parts
+
+    def fetch(i, slot):
+        @pl.when(i < own_tiles)
+        def _():
+            at = pl.ds(pl.multiple_of(i * tile, tile), tile)
+            pltpu.make_async_copy(own_gu.at[:, :, at], gu.at[slot], gu_sem.at[slot]).start()
+            pltpu.make_async_copy(own_dn.at[at, :], dn.at[slot], dn_sem.at[slot]).start()
+
+        @pl.when(i >= own_tiles)
+        def _():
+            at = pl.ds(pl.multiple_of((i - own_tiles) * tile, tile), tile)
+            for k in range(parts):
+                there = pl.ds(pl.multiple_of(places_ref[k] * width, width), width)
+                pltpu.make_async_copy(
+                    pair_gu[k].at[:, :, at], gu.at[slot, :, there, :], gu_sem.at[slot]
+                ).start()
+                pltpu.make_async_copy(
+                    pair_dn[k].at[at, :], dn.at[slot, :, there], dn_sem.at[slot]
+                ).start()
+
+    @pl.when(step == 0)
+    def _():
+        fetch(step, 0)
+        copies = []
+        for target, sizes in zip((h, c), rows):
+            at = 0
+            for size in sizes:
+                i = len(copies)
+                there = target.at[at : at + size]
+                copies.append(pltpu.make_async_copy(tokens[i], there, row_sem.at[i]))
+                at += size
+        for copy in copies:
+            copy.start()
+        out[...] = jnp.zeros_like(out)
+        back[...] = jnp.zeros_like(back)
+        for copy in copies:
+            copy.wait()
+
+    slot = step % 2
+
+    @pl.when(step + 1 < steps)
+    def _():
+        fetch(step + 1, 1 - slot)
+
+    pltpu.make_async_copy(own_gu.at[:, :, pl.ds(0, tile)], gu.at[slot], gu_sem.at[slot]).wait()
+    pltpu.make_async_copy(own_dn.at[pl.ds(0, tile), :], dn.at[slot], dn_sem.at[slot]).wait()
+    w_gate, w_up, w_down = gu.at[slot, 0], gu.at[slot, 1], dn.at[slot]
+    gate = dot_nn(h[...], w_gate[...])
+    up = dot_nn(h[...], w_up[...])
+    grad = dot_nt(c[...], w_down[...])
+    sig = jax.nn.sigmoid(gate)
+    silu = gate * sig
+    act = (silu * up).astype(BF16)
+    grad_gate = (grad * up * sig * (1.0 + gate * (1.0 - sig))).astype(BF16)
+    grad_up = (grad * silu).astype(BF16)
+    out[...] += dot_nn(act, w_down[...])
+    back[...] += dot_nt(grad_gate, w_gate[...]) + dot_nt(grad_up, w_up[...])
+
+    @pl.when(step == steps - 1)
+    def _():
+        out_ref[...] = out[...].astype(BF16)
+        back_ref[...] = back[...].astype(BF16)
+
+
+def mlp(second, cot, own_gu, own_dn, pair, places):
+    rows = tuple(v.shape[0] for v in second), tuple(v.shape[0] for v in cot)
+    total = sum(rows[0])
+    hidden = own_gu.shape[2]
+    tile = min(256, hidden)
+    parts = len(pair)
+    anywhere = pl.BlockSpec(memory_space=pl.ANY)
+    whole = pl.BlockSpec((total, D), lambda i, p: (0, 0))
+    return pl.pallas_call(
+        functools.partial(mlp_kernel, rows=rows, parts=parts, tile=tile),
+        grid_spec=pltpu.PrefetchScalarGridSpec(
+            num_scalar_prefetch=1,
+            grid=(2 * hidden // tile,),
+            in_specs=[anywhere] * (len(second) + len(cot) + 2 + 2 * parts),
+            out_specs=[whole, whole],
+            scratch_shapes=[
+                pltpu.VMEM((total, D), BF16),
+                pltpu.VMEM((total, D), BF16),
+                pltpu.VMEM((2, 2, D, tile), BF16),
+                pltpu.VMEM((2, tile, D), BF16),
+                pltpu.VMEM((total, D), F32),
+                pltpu.VMEM((total, D), F32),
+                pltpu.SemaphoreType.DMA((len(second) + len(cot),)),
+                pltpu.SemaphoreType.DMA((2,)),
+                pltpu.SemaphoreType.DMA((2,)),
+            ],
+        ),
+        out_shape=[jax.ShapeDtypeStruct((total, D), BF16)] * 2,
+        compiler_params=pltpu.CompilerParams(vmem_limit_bytes=VMEM_LIMIT),
+        cost_estimate=pl.CostEstimate(
+            flops=12 * total * D * hidden * 2, bytes_accessed=12 * D * hidden, transcendentals=0
+        ),
+        name="mlp",
+    )(places, *second, *cot, own_gu, own_dn, *[p[0] for p in pair], *[p[1] for p in pair])
 
 
 class Grid:
@@ -658,77 +993,111 @@
     return lax.optimization_barrier((values, *events))[0]
 
 
-def gather_rows(grid, shard):
-    half = shard.shape[0] // CORES
-    own = lax.dynamic_slice_in_dim(shard, grid.c * half, half, 0)
-    pieces = []
-    for kz in range(grid.zs):
-        from_z = own if kz == 0 else grid.along_z(own, kz)
-        for kx in range(grid.xs):
-            piece = from_z if kx == 0 else grid.along_x(from_z, kx)
-            row = ((grid.z - kz) % grid.zs) * grid.xs + (grid.x - kx) % grid.xs
-            pieces.append((piece, (row * CORES + grid.c) * half))
-            if kz + kx:
-                other = grid.flip_core(piece)
-            else:
-                other = lax.dynamic_slice_in_dim(shard, (1 - grid.c) * half, half, 0)
-            pieces.append((other, (row * CORES + 1 - grid.c) * half))
-    return pieces
-
-
-def assemble(grid, pieces):
-    piece = pieces[0][0]
-    full = jnp.zeros((piece.shape[0] * len(pieces), piece.shape[1]), piece.dtype)
-    for piece, row in pieces:
-        full = lax.dynamic_update_slice(full, piece, (row, 0))
-    return full
-
-
-def gather_pair(grid, gate_up, down):
-    part = gate_up.shape[2] // grid.seq
-    gu = lax.dynamic_slice_in_dim(gate_up, grid.s * part, part, 2)
-    dn = lax.dynamic_slice_in_dim(down, grid.s * part, part, 0)
-    got = [grid.flip_z((gu, dn), 1)]
-    for ky in range(1, grid.ys):
-        got.append(grid.along_y(got[0], ky))
-    got = got + [grid.flip_core(v) for v in got]
-    return (
-        jnp.concatenate([v[0] for v in got], axis=2),
-        jnp.concatenate([v[1] for v in got], axis=0),
-    )
-
-
-def spread(grid, block):
-    near = [block] + [grid.along_x(block, k) for k in range(1, grid.xs)]
-    parts = 4
+class Gather:
+    def __init__(self, grid, shard):
+        self.grid = grid
+        self.size = shard.shape[0] // grid.seq
+        self.own = lax.dynamic_slice_in_dim(shard, grid.s * self.size, self.size, 0)
+
+    def over_z(self):
+        grid = self.grid
+        pieces = [self.own] + [grid.along_z(self.own, k) for k in range(1, grid.zs)]
+        half = grid.zs // 2
+        self.halves = [jnp.concatenate(pieces[:half]), jnp.concatenate(pieces[half:])]
+
+    def first(self):
+        grid = self.grid
+        a, b = self.halves
+        self.moved = [
+            [grid.along_x(a, k) for k in range(1, grid.xs)],
+            [grid.along_y(b, k) for k in range(1, grid.ys)],
+        ]
+
+    def second(self):
+        grid = self.grid
+        a, b = (jnp.concatenate([h, *m]) for h, m in zip(self.halves, self.moved))
+        self.blocks = [a, b]
+        self.last = [grid.along_y(a, k) for k in range(1, grid.ys)]
+        self.last += [grid.along_x(b, k) for k in range(1, grid.xs)]
+
+    def cores(self):
+        self.over = [self.grid.flip_core(b) for b in self.blocks]
+
+    def result(self):
+        grid = self.grid
+        blocks = self.blocks + self.last
+        blocks = blocks + self.over + [grid.flip_core(b) for b in self.last]
+        places = []
+        kzs = range(grid.zs // 2), range(grid.zs // 2, grid.zs)
+        a = [(kx, 0, kz) for kx in range(grid.xs) for kz in kzs[0]]
+        b = [(0, ky, kz) for ky in range(grid.ys) for kz in kzs[1]]
+        moves = a + b
+        for k in range(1, grid.ys):
+            moves = moves + [(kx, k, kz) for kx, _, kz in a]
+        for k in range(1, grid.xs):
+            moves = moves + [(k, ky, kz) for _, ky, kz in b]
+        for core in range(CORES):
+            c = (grid.c + core) % CORES
+            for kx, ky, kz in moves:
+                z, x, y = (grid.z - kz) % grid.zs, (grid.x - kx) % grid.xs, (grid.y - ky) % grid.ys
+                places.append((z * grid.xs + x) * grid.seq + y * CORES + c)
+        return Gathered(blocks, jnp.stack(places).astype(jnp.int32), self.size)
+
+
+class Pair:
+    def __init__(self, grid, gate_up, down):
+        self.grid = grid
+        part = D // grid.seq
+        self.gu = lax.dynamic_slice_in_dim(gate_up, grid.s * part, part, 1)
+        self.dn = lax.dynamic_slice_in_dim(down, grid.s * part, part, 1)
+
+    def gate_up_z(self):
+        self.gu = [self.grid.flip_z(self.gu, FAR_BIT)]
+
+    def down_z(self):
+        self.dn = [self.grid.flip_z(self.dn, FAR_BIT)]
+
+    def gate_up_y(self):
+        self.gu += [self.grid.along_y(self.gu[0], k) for k in range(1, self.grid.ys)]
+
+    def down_y(self):
+        self.dn += [self.grid.along_y(self.dn[0], k) for k in range(1, self.grid.ys)]
+
+    def result(self):
+        grid = self.grid
+        gus = self.gu + [grid.flip_core(v) for v in self.gu]
+        dns = self.dn + [grid.flip_core(v) for v in self.dn]
+        places = [grid.s] + [(grid.y - k) % grid.ys * CORES + grid.c for k in range(1, grid.ys)]
+        places = places + [p + 1 - 2 * grid.c for p in places]
+        return list(zip(gus, dns)), jnp.stack(places).astype(jnp.int32)
+
+
+def spread_near(grid, block):
+    return [block] + [grid.along_x(block, k) for k in range(1, grid.xs)]
+
+
+def spread_far(grid, block, parts):
     size = block.shape[0] // parts
-    far = [[] for _ in range(grid.xs)]
-    for p in range(parts):
-        piece = grid.flip_z(block[p * size : (p + 1) * size], 2)
-        far[0].append(piece)
-        for k in range(1, grid.xs):
-            far[k].append(grid.along_x(piece, k))
-    return jnp.concatenate(near, axis=0), jnp.concatenate([v for f in far for v in f], axis=0)
-
-
-def collect(grid, near, far, length):
-    parts = 4
+    pieces = [grid.flip_z(block[p * size : (p + 1) * size], NEAR_BIT) for p in range(parts)]
+    return pieces, lambda pieces: list(pieces) + [
+        grid.along_x(piece, k) for k in range(1, grid.xs) for piece in pieces
+    ]
+
+
+def collect(grid, near, far, length, parts):
     size = length // parts
-    total = near[:length]
-    for k in range(1, grid.xs):
-        total = total + grid.along_x(
-            near[k * length : (k + 1) * length].astype(BF16), -k
-        ).astype(F32)
-    back = []
+    terms = [near[:length]]
+    send = []
     for p in range(parts):
         lo = p * size
-        piece = far[lo : lo + size]
+        total = far[lo : lo + size]
         for k in range(1, grid.xs):
-            piece = piece + grid.along_x(
-                far[k * length + lo : k * length + lo + size].astype(BF16), -k
-            ).astype(F32)
-        back.append(grid.flip_z(piece.astype(BF16), 2).astype(F32))
-    return total + jnp.concatenate(back, axis=0)
+            other = grid.along_x(far[k * length + lo : k * length + lo + size], -k)
+            total = (total.astype(F32) + other.astype(F32)).astype(BF16)
+        send.append(total)
+    for k in range(1, grid.xs):
+        terms.append(grid.along_x(near[k * length : (k + 1) * length], -k))
+    return terms, send
 
 
 def total_over_all(grid, values):
@@ -780,7 +1149,16 @@
 
 
 def documents(grid, starts, length):
-    resets = lax.all_gather(starts.astype(BF16), "seq", tiled=True).astype(jnp.int32)
+    own = starts.astype(BF16)
+    other = grid.flip_core(own)
+    chip = jnp.where(grid.c == 0, jnp.concatenate([own, other]), jnp.concatenate([other, own]))
+    resets = jnp.zeros((grid.ys, chip.shape[0]), BF16)
+    resets = lax.dynamic_update_slice(resets, chip[None], (grid.y, 0))
+    for k in range(1, grid.ys):
+        got = grid.along_y(chip, k)
+        resets = lax.dynamic_update_slice(resets, got[None], ((grid.y - k) % grid.ys, 0))
+    heard = resets
+    resets = resets.reshape(-1).astype(jnp.int32)
     places = jnp.arange(resets.shape[0], dtype=jnp.int32)
     docs = jnp.cumsum(jnp.where(places == 0, 1, resets))
     padded = jnp.concatenate([jnp.full((WINDOW,), -1, jnp.int32), docs])
@@ -803,7 +1181,7 @@
     pick = lambda v, k: lax.dynamic_index_in_dim(v, jnp.clip(grid.s + k, 0, grid.seq - 1), 0, False)
     former = [pick(earlier, -k) * (grid.s - k >= 0) for k in range(1, grid.seq)]
     latter = [pick(later, k) * (grid.s + k < grid.seq) for k in range(1, grid.seq)]
-    return masks, former, latter
+    return masks, former, latter, heard
 
 
 def local(
@@ -815,22 +1193,21 @@
     grid = Grid()
     length = tokens.shape[1]
     rank = query_in.shape[1]
-    hidden = tokens[0].astype(F32)
+    hidden = tokens[0]
     grad_out = cotangent[0]
-    gain_first = norm_first.astype(F32)
-    gain_second = norm_second.astype(F32)
-
-    qkv_shard = jnp.concatenate([w_query, w_key, w_value], axis=1)
-    qkv_full = assemble(grid, gather_rows(grid, qkv_shard))
-    grad_out, w_out, w_gate_up, w_down = after((grad_out, w_out, w_gate_up, w_down), qkv_full)
-    output_full = assemble(grid, gather_rows(grid, w_out))
-    pair_gate_up, pair_down = gather_pair(grid, w_gate_up, w_down)
-    cot_near, cot_far = spread(grid, grad_out)
-
-    inverse_first = lax.rsqrt(jnp.mean(hidden * hidden, axis=-1, keepdims=True) + EPSILON)
-    normed_first = hidden * inverse_first
-    inputs = (normed_first * gain_first).astype(BF16)
-    masks, former, latter = documents(grid, doc_starts[0], length)
+    gain_first = norm_first.astype(F32)[None, :]
+    gain_second = norm_second.astype(F32)[None, :]
+
+    masks, former, latter, heard = documents(grid, doc_starts[0], length)
+    qkv = Gather(grid, jnp.concatenate([w_query, w_key, w_value], axis=1))
+    out = Gather(grid, w_out)
+    pair = Pair(grid, w_gate_up, w_down)
+    cot_near = spread_near(grid, grad_out)
+    qkv.over_z()
+
+    values = hidden.astype(F32)
+    inverse_first = lax.rsqrt(jnp.mean(values * values, axis=-1, keepdims=True) + EPSILON)
+    inputs = (values * inverse_first * gain_first).astype(BF16)
     gamma = jax.nn.sigmoid(window_logit)
     masks["gamma"] = jnp.repeat(gamma, HEAD)[None, :]
     half = HEAD // 2
@@ -843,90 +1220,111 @@
     maps_q, maps_k = pair_maps(map_query), pair_maps(map_key)
     qkv_in = adapters(query_in, key_in, value_in, 1)
     qkv_out = adapters(query_out, key_out, value_out, 0)
-
+    o_in = jnp.pad(proj_in, ((0, 0), (0, LOW - rank)))
+    o_out = jnp.pad(proj_out, ((0, LOW - rank), (0, 0)))
     low = dot_nn(inputs, qkv_in).astype(BF16)
-    queries, kv, kf, rim, near, full = project(
-        inputs, low, qkv_full, qkv_out, masks["cos"], masks["sin"], maps_k, masks["survive"]
-    )
-    rim = grid.along_seq(rim, 1)
-    carry = former[0] * grid.along_seq(near, 1).astype(F32)
+
+    cot_near, qkv.halves, heard, pair.gu = after((cot_near, qkv.halves, heard, pair.gu))
+    qkv.first()
+    pair.gate_up_z()
+    ready = (masks, former, latter, maps_q, maps_k, qkv_in, qkv_out, o_in, o_out, inputs, low)
+    qkv.moved, ready = after((qkv.moved, ready))
+    masks, former, latter, maps_q, maps_k, qkv_in, qkv_out, o_in, o_out, inputs, low = ready
+    cosine, sine = masks["cos"], masks["sin"]
+    qkv.second()
+    qkv.cores()
+    qkv.last, qkv.over, out.own, pair.gu = after((qkv.last, qkv.over, out.own, pair.gu))
+    w_qkv = qkv.result()
+    out.over_z()
+    kv, kf, pack, full = project_kv(
+        w_qkv, inputs, low, qkv_out[:, D:], cosine, sine, maps_k, masks["survive"]
+    )
+    rim = grid.along_seq(pack, 1)
+    carry = former[0] * rim[2 * WINDOW :].astype(F32)
     for k in range(2, grid.seq):
         carry = carry + former[k - 1] * grid.along_seq(full, k).astype(F32)
     carry = carry.astype(BF16)
-    qf = features(queries, maps_q)
-    merged, attended, inverse = attend(queries, qf, kv, kf, rim, carry, masks)
-
-    out_low = dot_nn(merged, proj_in).astype(BF16)
-    residual = hidden + dot_nn(merged, output_full) + dot_nn(out_low, proj_out)
-    inverse_second = lax.rsqrt(jnp.mean(residual * residual, axis=-1, keepdims=True) + EPSILON)
-    normed_second = residual * inverse_second
-    second_in = (normed_second * gain_second).astype(BF16)
-    sides = spread(grid, second_in)
-    grad_act = [
-        [
-            dot_nt(cot, down)
-            for down in (w_down, pair_down)
-        ]
-        for cot in (cot_near, cot_far)
+    first = project_q(0, w_qkv, inputs, low, qkv_out, cosine, sine, maps_q)
+    rim, carry, first, out.halves, pair.gu, pair.dn, grad_out = after(
+        (rim, carry, first, out.halves, pair.gu, pair.dn, grad_out)
+    )
+    out.first()
+    out.second()
+    out.cores()
+    pair.gate_up_y()
+    pair.down_z()
+    cot_far, relay = spread_far(grid, grad_out, 1)
+    queries, merged, attended, inverse = [], [], [], []
+    for i in range(HALVES):
+        q, qf = project_q(i, w_qkv, inputs, low, qkv_out, cosine, sine, maps_q) if i else first
+        queries.append((q, qf))
+        block = attend(i, q, qf, kv, kf, rim, carry, masks)
+        merged.append(block[0])
+        attended.append(block[1])
+        inverse.append(block[2])
+
+    merged, out.last, cot_far, pair.dn = after((merged, out.last, cot_far, pair.dn))
+    w_o = out.result()
+    pair.down_y()
+    cot_far = relay(cot_far)
+    pair, pair_places = pair.result()
+    residual, second_in, out_low, inverse_second = out_project(
+        w_o, merged, hidden, o_in, o_out, gain_second
+    )
+    near = spread_near(grid, second_in)
+    far, relay = spread_far(grid, second_in, 2)
+    far = relay(after(far, near))
+    near_out, near_grad = mlp(near, cot_near, w_gate_up, w_down, pair, pair_places)
+    far, near_out, near_grad = after((far, near_out, near_grad))
+    far_out, far_grad = mlp(far, cot_far, w_gate_up, w_down, pair, pair_places)
+    terms, send = collect(grid, near_grad, far_grad, length, 2)
+    near_out, far_out = after((near_out, far_out), send)
+    terms.append(jnp.concatenate([grid.flip_z(v, NEAR_BIT) for v in send], axis=0))
+
+    grad_residual, *grad_merged, grad_gain_two, grad_proj_in, grad_proj_out = branch_back(
+        w_o, terms, grad_out, residual, inverse_second, gain_second, o_in, o_out, merged, out_low
+    )
+    scaled = [
+        scaled_grads(i, grad_merged[i], attended[i], inverse[i], queries[i][1], masks)
+        for i in range(HALVES)
     ]
-    mlp_parts, back_parts = [], []
-    for side, rows in enumerate(sides):
-        mlp_part = back_part = 0.0
-        for which, (both, down) in enumerate(((w_gate_up, w_down), (pair_gate_up, pair_down))):
-            gate = dot_nn(rows, both[0])
-            up = dot_nn(rows, both[1])
-            sigmoid_gate = jax.nn.sigmoid(gate)
-            silu = gate * sigmoid_gate
-            activation = (silu * up).astype(BF16)
-            mlp_part = mlp_part + dot_nn(activation, down)
-            grads = grad_act[side][which]
-            grad_gate = grads * up * sigmoid_gate * (1.0 + gate * (1.0 - sigmoid_gate))
-            grad_up = (grads * silu).astype(BF16)
-            for grad, full in ((grad_gate.astype(BF16), both[0]), (grad_up, both[1])):
-                back_part = back_part + dot_nt(grad, full)
-        mlp_parts.append(mlp_part)
-        back_parts.append(back_part)
-    grad_second = collect(grid, back_parts[0], back_parts[1], length)
-    mlp_parts = after(mlp_parts, grad_second)
-    mlp_out = collect(grid, mlp_parts[0], mlp_parts[1], length)
-    block_out = (residual + mlp_out).astype(BF16)
-
-    def norm_back(grad_normed, normed, inverse_rms, gain):
-        scaled = grad_normed * gain
-        back = inverse_rms * (scaled - normed * jnp.mean(scaled * normed, axis=-1, keepdims=True))
-        return back, jnp.sum(grad_normed * normed, axis=0)
-
-    grad_norm_part, grad_gain_two = norm_back(
-        grad_second, normed_second, inverse_second, gain_second
-    )
-    grad_residual = grad_out.astype(F32) + grad_norm_part
-    grad_branch = grad_residual.astype(BF16)
-    grad_out_low = dot_nt(grad_branch, proj_out).astype(BF16)
-    grad_merged = (dot_nt(grad_branch, output_full) + dot_nt(grad_out_low, proj_in)).astype(BF16)
-    grad_proj_out = dot_tn(out_low, grad_branch)
-    grad_proj_in = dot_tn(grad_out_low, merged)
-
-    grads, grad_den, back = scaled_grads(grad_merged, attended, inverse, qf, masks)
+    back = jnp.concatenate([v[2] for v in scaled], axis=1)
     far_back = jnp.zeros(back.shape, F32)
     for k in range(2, grid.seq):
         far_back = far_back + latter[k - 1] * grid.along_seq(back, -k).astype(F32)
     near_back = far_back + latter[0] * grid.along_seq(back, -1).astype(F32)
-    raw_query, dkv, dkf, dmap_query, dlogit = attend_back(
-        queries, qf, kv, kf, rim, carry, grads, grad_den, masks, maps_q
-    )
-    rim_back = jnp.concatenate([dkv[:WINDOW], dkf[:WINDOW]], axis=1).astype(BF16)
-    rim_back = grid.along_seq(rim_back, -1)
-    raw_key, raw_value, dmap_key = keys_back(
-        kv, kf, dkv, dkf, rim_back, near_back.astype(BF16), far_back.astype(BF16), masks, maps_k
-    )
-    raw = jnp.concatenate([raw_query, raw_key, raw_value], axis=1)
-    grad_low = dot_nt(raw, qkv_out).astype(BF16)
-    grad_inputs = dot_nt(raw, qkv_full) + dot_nt(grad_low, qkv_in)
-    grad_qkv_out = dot_tn(low, raw)
-    grad_qkv_in = dot_tn(grad_low, inputs)
-    grad_first_part, grad_gain_one = norm_back(grad_inputs, normed_first, inverse_first, gain_first)
-    grad_tokens = grad_residual + grad_first_part
+    near_back, far_back = near_back.astype(BF16), far_back.astype(BF16)
+    out_terms, send = collect(grid, near_out, far_out, length, 1)
+    scaled, out_terms, send = after((scaled, out_terms, send))
+    out_terms += [grid.flip_z(v, NEAR_BIT) for v in send]
+    backs = [
+        attend_back(i, *queries[i], kv, kf, rim, carry, *scaled[i][:2], masks, maps_q)
+        for i in range(HALVES)
+    ]
+    raw_query = [v[0] for v in backs]
+    rim_back = [grid.along_seq(v[3], -1) for v in backs]
+    rim_back, out_terms = after((rim_back, out_terms))
+    block_out = residual
+    for term in out_terms:
+        block_out = block_out + term.astype(F32)
+    block_out = block_out.astype(BF16)
+    raw_key, raw_value, dmap_key = [], [], []
+    for i, (_, dkv, dkf, *_) in enumerate(backs):
+        k, v, m = keys_back(
+            i, kv, kf, dkv, dkf, rim_back[i], near_back, far_back, masks, maps_k
+        )
+        raw_key.append(k)
+        raw_value.append(v)
+        dmap_key.append(m)
+    dmap_query = jnp.concatenate([v[4] for v in backs], axis=0)
+    dmap_key = jnp.concatenate(dmap_key, axis=0)
+    dlogit = jnp.concatenate([v[5] for v in backs], axis=0)
+    grad_tokens, grad_gain_one, grad_qkv_in, grad_qkv_out = inputs_back(
+        w_qkv, [*raw_query, *raw_key, *raw_value], qkv_in, qkv_out, low, inputs,
+        hidden, gain_first, grad_residual,
+    )
     grad_logit = dlogit[:, :GROUPS, 0].reshape(HEADS) * (1.0 - gamma)
+    grad_proj_in, grad_proj_out = grad_proj_in[:rank], grad_proj_out[:rank]
 
     blocks = lambda v: v.reshape(8, grid.seq, -1).swapaxes(0, 1)
     plain = lambda v: v.reshape(grid.seq, 8, -1)

time: 860 us -> 606 us (0.70)
  matrix products: 156 us -> 1.06 us
  waiting for transfers between devices: 365 us -> 240 us
  Pallas kernels: 79.8 us -> 199 us
  local copies, waits for them, and re-layouts: 105 us -> 52.3 us
  starting transfers between devices: 105 us -> 68.9 us
    ppermute x85 -> x61, waiting for transfers between devices: 365 us -> 240 us  [send(): lax.ppermute(v, ('seq', 'rows'), route)]
    pallas_call x6 -> x16, Pallas kernels: 79.8 us -> 199 us  [the longest x2 70.5 us: mlp(): pl.pallas_call(functools.partial(mlp_kernel, rows=rows, parts=parts, tile...]
    dot_general x22 -> x0, matrix products: 94.3 us -> none  [the longest x18 91.4 us: dot_nt(): lax.dot_general(a, b, (((1,), (1,)), ((), ())), preferred_element_type=F32)]
    dot_general x16 -> x1, matrix products: 61.5 us -> 1.06 us  [dot_nn(): return jnp.dot(a, b, preferred_element_type=F32)]
    dynamic_update_slice x32 -> x2, local copies, waits for them, and re-layouts: 37.4 us -> 0.08 us  [the longest x1 0.04 us: documents(): resets = lax.dynamic_update_slice(resets, chip[None], (grid.y, 0))]
    ppermute x85 -> x61, starting transfers between devices: 105 us -> 68.9 us  [send(): lax.ppermute(v, ('seq', 'rows'), route)]
    unnamed x255 -> x130, local copies, waits for them, and re-layouts: 30.3 us -> 10.9 us
    broadcast_in_dim x5 -> x2, local copies, waits for them, and re-layouts: 10.9 us -> 0.01 us  [the longest x1 0.01 us: documents(): got[None]]
  transfers between devices with their start and end apart: 85 -> 61, of which waited for: 38 -> 28; matrix products, arithmetic and copies ran while one was open for 23% -> 10% of each run, Pallas kernels for 6% -> 24%
where the time goes in v2:
time: 606 us; the launch traced here: 597 us
  waiting for transfers between devices  240 us (40%)
  Pallas kernels  199 us (33%)
  starting transfers between devices  68.9 us (11%)
  local copies, waits for them, and re-layouts  52.3 us (9%)
  other arithmetic  29.9 us (5%)
    ppermute x61, waiting for transfers between devices, send(): lax.ppermute(v, ('seq', 'rows'), route)  240 us
    pallas_call x2, Pallas kernels, mlp(): pl.pallas_call(functools.partial(mlp_kernel, rows=rows, parts=parts, tile...  70.5 us
    ppermute x61, starting transfers between devices, send(): lax.ppermute(v, ('seq', 'rows'), route)  68.9 us
    pallas_call x2, Pallas kernels, attend_back(): pl.pallas_call(attend_back_kernel, grid=(PER_HALF,), in_specs=[s['q'], s[...  31.4 us
    pallas_call x2, Pallas kernels, project_q(): pl.pallas_call(functools.partial(project_q_kernel, counts=w.shapes(), siz...  19.7 us
    pallas_call x2, Pallas kernels, attend(): pl.pallas_call(attend_kernel, grid=(PER_HALF,), in_specs=[s['q'], s['qf']...  16.1 us
    pallas_call x1, Pallas kernels, inputs_back(): pl.pallas_call(functools.partial(inputs_back_kernel, counts=w.shapes(), s...  14.2 us
  transfers between devices with their start and end apart: 61, of which 28 were waited for; matrix products, arithmetic and copies ran while one was open for 10% of the time, Pallas kernels for 24%

profile of v2, /device:TPU:0, one launch (start us, length us, event | category | flops | bytes accessed | tf_op | source)
XLA Modules:
  0.0 597.0 jit_solution(3125889329167717828)
XLA Ops:
  2.6 4.0 collective-permute-start.2
  51.4 4.3 collective-permute-start.12
  57.0 4.1 collective-permute-done.6
  67.4 33.9 %collective-permute-done.12.refs_6_.refs_8_ = bf16[2,512,1024]{2,1,0:T(8,128)(2,1)} collective-permute-done((bf16[2,512,1024]{2,1,0:T(8,128)(2,1)}, bf16[2,512,1024]{2,1,0:T(8,128)(2,1)}, u32[]{:S(2)}, u32[]{:S(2)}) %collective-permute-start.12) | collective-permute-done | bytes 2097184 | tf_op jit(solution)/shard_map/ppermute | solution.py:960
  118.0 9.0 %project_kv.1 = (bf16[256,1024]{1,0:T(8,128)(2,1)}, bf16[256,1024]{1,0:T(8,128)(2,1)}, bf16[208,1024]{1,0:T(8,128)(2,1)}, bf16[80,1024]{1,0:T(8,128)(2,1)}) custom-call(s32[32]{0:T(128)} %stack.179.refs_0_, bf16[256,3072]{1,0:T(8,128)(2,1)} %copy-done.3, bf16[256,3072]{1,0:T(8,128)(2,1)} %copy-done.4, bf16[256,3072]{1,0:T(8,128)(2,1)} %collective-permute-done.8.refs_3_, ...), custom_call_target="tpu_custom_call" | custom-call | flops 1073741824 | bytes 4194304 | tf_op jit(solution)/shard_map/project_kv/pallas_call | solution.py:229
  135.2 9.8 %project_q.2 = (bf16[256,1024]{1,0:T(8,128)(2,1)}, bf16[256,2048]{1,0:T(8,128)(2,1)}) custom-call(s32[32]{0:T(128)} %stack.179.refs_0_, bf16[256,3072]{1,0:T(8,128)(2,1)} %copy-done.3, bf16[256,3072]{1,0:T(8,128)(2,1)} %copy-done.4, bf16[256,3072]{1,0:T(8,128)(2,1)} %collective-permute-done.8.refs_3_, bf16[256,3072]{1,0:T(8,128)(2,1)} %collective-permute-done.9.refs_4_, ...), custom_call_target="tpu_custom_call" | custom-call | flops 1073741824 | bytes 4194304 | tf_op jit(solution)/shard_map/project_q/pallas_call | solution.py:268
  149.8 8.9 %collective-permute-done.22 = bf16[128,2048]{1,0:T(8,128)(2,1)S(1)} collective-permute-done((bf16[128,2048]{1,0:T(8,128)(2,1)S(1)}, bf16[128,2048]{1,0:T(8,128)(2,1)S(1)}, u32[]{:S(2)}, u32[]{:S(2)}) %collective-permute-start.22) | collective-permute-done | bytes 524320 | tf_op jit(solution)/shard_map/ppermute | solution.py:960
  164.0 9.8 %project_q.3 = (bf16[256,1024]{1,0:T(8,128)(2,1)}, bf16[256,2048]{1,0:T(8,128)(2,1)}) custom-call(s32[32]{0:T(128)} %stack.179.refs_0_, bf16[256,3072]{1,0:T(8,128)(2,1)} %copy-done.3, bf16[256,3072]{1,0:T(8,128)(2,1)} %copy-done.4, bf16[256,3072]{1,0:T(8,128)(2,1)} %collective-permute-done.8.refs_3_, bf16[256,3072]{1,0:T(8,128)(2,1)} %collective-permute-done.9.refs_4_, ...), custom_call_target="tpu_custom_call" | custom-call | flops 1073741824 | bytes 4194304 | tf_op jit(solution)/shard_map/project_q/pallas_call | solution.py:268
  173.9 8.0 %attend.2 = (bf16[256,1024]{1,0:T(8,128)(2,1)}, f32[256,1024]{1,0:T(8,128)}, f32[256,1024]{1,0:T(8,128)}) custom-call(bf16[256,1024]{1,0:T(8,128)(2,1)} %get-tuple-element.206.q_ref, bf16[256,2048]{1,0:T(8,128)(2,1)} %get-tuple-element.207.qf_ref, bf16[256,1024]{1,0:T(8,128)(2,1)} %get-tuple-element.208.kv_ref, bf16[256,1024]{1,0:T(8,128)(2,1)} %get-tuple-element.209.kf_ref, ...), custom_call_target="tpu_custom_call" | custom-call | flops 5000000000 | bytes 4194304 | tf_op jit(solution)/shard_map/attend/pallas_call | solution.py:400
  181.9 8.1 %attend.3 = (bf16[256,1024]{1,0:T(8,128)(2,1)}, f32[256,1024]{1,0:T(8,128)}, f32[256,1024]{1,0:T(8,128)}) custom-call(bf16[256,1024]{1,0:T(8,128)(2,1)} %get-tuple-element.217.q_ref, bf16[256,2048]{1,0:T(8,128)(2,1)} %get-tuple-element.218.qf_ref, bf16[256,1024]{1,0:T(8,128)(2,1)} %get-tuple-element.208.kv_ref, bf16[256,1024]{1,0:T(8,128)(2,1)} %get-tuple-element.209.kf_ref, ...), custom_call_target="tpu_custom_call" | custom-call | flops 5000000000 | bytes 4194304 | tf_op jit(solution)/shard_map/attend/pallas_call | solution.py:400
  200.0 31.5 %collective-permute-done.36.refs_7_.refs_9_ = bf16[2,512,1024]{2,1,0:T(8,128)(2,1)} collective-permute-done((bf16[2,512,1024]{2,1,0:T(8,128)(2,1)}, bf16[2,512,1024]{2,1,0:T(8,128)(2,1)}, u32[]{:S(2)}, u32[]{:S(2)}) %collective-permute-start.36) | collective-permute-done | bytes 2097184 | tf_op jit(solution)/shard_map/ppermute | solution.py:960
  233.5 9.6 %out_project.1 = (f32[256,2048]{1,0:T(8,128)}, bf16[256,2048]{1,0:T(8,128)(2,1)}, bf16[256,128]{1,0:T(8,128)(2,1)}, f32[256,128]{1,0:T(8,128)}) custom-call(s32[32]{0:T(128)} %stack.179.refs_0_, bf16[256,2048]{1,0:T(8,128)(2,1)} %copy-done.9, bf16[256,2048]{1,0:T(8,128)(2,1)} %copy-done.10, bf16[256,2048]{1,0:T(8,128)(2,1)} %collective-permute-done.23.refs_3_, ...), custom_call_target="tpu_custom_call" | custom-call | flops 2147483648 | bytes 8388608 | tf_op jit(solution)/shard_map/out_project/pallas_call | solution.py:694
  252.0 29.0 %collective-permute-done.32.refs_1_ = bf16[128,2048]{1,0:T(8,128)(2,1)S(1)} collective-permute-done((bf16[128,2048]{1,0:T(8,128)(2,1)S(1)}, bf16[128,2048]{1,0:T(8,128)(2,1)S(1)}, u32[]{:S(2)}, u32[]{:S(2)}) %collective-permute-start.32) | collective-permute-done | bytes 524320 | tf_op jit(solution)/shard_map/ppermute | solution.py:960
  281.0 11.2 %collective-permute-done.31.refs_0_ = bf16[128,2048]{1,0:T(8,128)(2,1)S(1)} collective-permute-done((bf16[128,2048]{1,0:T(8,128)(2,1)S(1)}, bf16[128,2048]{1,0:T(8,128)(2,1)S(1)}, u32[]{:S(2)}, u32[]{:S(2)}) %collective-permute-start.31) | collective-permute-done | bytes 524320 | tf_op jit(solution)/shard_map/ppermute | solution.py:960
  298.1 35.2 %mlp.2 = (bf16[512,2048]{1,0:T(8,128)(2,1)}, bf16[512,2048]{1,0:T(8,128)(2,1)}) custom-call(s32[4]{0:T(128)} %pad_add_fusion.places_ref, bf16[256,2048]{1,0:T(8,128)(2,1)} %get-tuple-element.229.refs_0_, bf16[256,2048]{1,0:T(8,128)(2,1)} %collective-permute-done.33.refs_1_, bf16[256,2048]{1,0:T(8,128)(2,1)} %bitcast.32.refs_2_.refs_12_, ...), custom_call_target="tpu_custom_call" | custom-call | flops 25769803776 | bytes 25165824 | tf_op jit(solution)/shard_map/mlp/pallas_call | solution.py:910
  333.3 8.5 %collective-permute-done.35.refs_3_ = bf16[128,2048]{1,0:T(8,128)(2,1)S(1)} collective-permute-done((bf16[128,2048]{1,0:T(8,128)(2,1)}, bf16[128,2048]{1,0:T(8,128)(2,1)S(1)}, u32[]{:S(2)}, u32[]{:S(2)}) %collective-permute-start.35) | collective-permute-done | bytes 524320 | tf_op jit(solution)/shard_map/ppermute | solution.py:960
  343.6 35.3 %mlp.3 = (bf16[512,2048]{1,0:T(8,128)(2,1)}, bf16[512,2048]{1,0:T(8,128)(2,1)}) custom-call(s32[4]{0:T(128)} %pad_add_fusion.places_ref, bf16[128,2048]{1,0:T(8,128)(2,1)} %copy-done.56, bf16[128,2048]{1,0:T(8,128)(2,1)} %copy-done.55, bf16[128,2048]{1,0:T(8,128)(2,1)} %copy-done.57, bf16[128,2048]{1,0:T(8,128)(2,1)} %copy-done.58, ...), custom_call_target="tpu_custom_call" | custom-call | flops 25769803776 | bytes 25165824 | tf_op jit(solution)/shard_map/mlp/pallas_call | solution.py:910
  384.7 10.5 %collective-permute-done.44 = bf16[128,2048]{1,0:T(8,128)(2,1)S(1)} collective-permute-done((bf16[128,2048]{1,0:T(8,128)(2,1)S(1)}, bf16[128,2048]{1,0:T(8,128)(2,1)S(1)}, u32[]{:S(2)}, u32[]{:S(2)}) %collective-permute-start.44) | collective-permute-done | bytes 524320 | tf_op jit(solution)/shard_map/ppermute | solution.py:960
  395.2 11.2 %collective-permute-done.46 = bf16[128,2048]{1,0:T(8,128)(2,1)S(1)} collective-permute-done((bf16[128,2048]{1,0:T(8,128)(2,1)S(1)}, bf16[128,2048]{1,0:T(8,128)(2,1)S(1)}, u32[]{:S(2)}, u32[]{:S(2)}) %collective-permute-start.46) | collective-permute-done | bytes 524320 | tf_op jit(solution)/shard_map/ppermute | solution.py:960
  414.4 27.1 %collective-permute-done.45 = bf16[128,2048]{1,0:T(8,128)(2,1)S(1)} collective-permute-done((bf16[128,2048]{1,0:T(8,128)(2,1)S(1)}, bf16[128,2048]{1,0:T(8,128)(2,1)S(1)}, u32[]{:S(2)}, u32[]{:S(2)}) %collective-permute-start.45) | collective-permute-done | bytes 524320 | tf_op jit(solution)/shard_map/ppermute | solution.py:960
  441.5 11.1 %collective-permute-done.47 = bf16[128,2048]{1,0:T(8,128)(2,1)S(1)} collective-permute-done((bf16[128,2048]{1,0:T(8,128)(2,1)S(1)}, bf16[128,2048]{1,0:T(8,128)(2,1)S(1)}, u32[]{:S(2)}, u32[]{:S(2)}) %collective-permute-start.47) | collective-permute-done | bytes 524320 | tf_op jit(solution)/shard_map/ppermute | solution.py:960
  454.7 10.2 %branch_back.1 = (f32[256,2048]{1,0:T(8,128)}, bf16[256,1024]{1,0:T(8,128)(2,1)}, bf16[256,1024]{1,0:T(8,128)(2,1)}, f32[1,2048]{1,0:T(1,128)}, f32[128,2048]{1,0:T(8,128)}, /*index=5*/f32[128,2048]{1,0:T(8,128)}) custom-call(s32[32]{0:T(128)} %stack.179.refs_0_, bf16[256,2048]{1,0:T(8,128)(2,1)} %copy-done.9, bf16[256,2048]{1,0:T(8,128)(2,1)} %copy-done.10, ...), custom_call_target="tpu_custom_call" | custom-call | flops 2147483648 | bytes 8388608 | tf_op jit(solution)/shard_map/branch_back/pallas_call | solution.py:751
  464.9 5.0 scaled_grads.3
  469.9 5.0 scaled_grads.2
  492.1 15.7 %attend_back.2 = (bf16[256,1024]{1,0:T(8,128)(2,1)}, f32[256,512]{1,0:T(8,128)}, f32[256,512]{1,0:T(8,128)}, bf16[128,512]{1,0:T(8,128)(2,1)}, f32[16,64,128]{2,1,0:T(8,128)}, /*index=5*/f32[4,8,128]{2,1,0:T(8,128)}) custom-call(bf16[256,1024]{1,0:T(8,128)(2,1)} %get-tuple-element.206.q_ref, bf16[256,2048]{1,0:T(8,128)(2,1)} %get-tuple-element.207.qf_ref, ...), custom_call_target="tpu_custom_call" | custom-call | flops 15000000512 | bytes 4194304 | tf_op jit(solution)/shard_map/attend_back/pallas_call | solution.py:548
  507.9 15.7 %attend_back.3 = (bf16[256,1024]{1,0:T(8,128)(2,1)}, f32[256,512]{1,0:T(8,128)}, f32[256,512]{1,0:T(8,128)}, bf16[128,512]{1,0:T(8,128)(2,1)}, f32[16,64,128]{2,1,0:T(8,128)}, /*index=5*/f32[4,8,128]{2,1,0:T(8,128)}) custom-call(bf16[256,1024]{1,0:T(8,128)(2,1)} %get-tuple-element.217.q_ref, bf16[256,2048]{1,0:T(8,128)(2,1)} %get-tuple-element.218.qf_ref, ...), custom_call_target="tpu_custom_call" | custom-call | flops 15000000512 | bytes 4194304 | tf_op jit(solution)/shard_map/attend_back/pallas_call | solution.py:548
  529.8 9.8 %collective-permute-done.52 = bf16[256,2048]{1,0:T(8,128)(2,1)S(1)} collective-permute-done((bf16[256,2048]{1,0:T(8,128)(2,1)}, bf16[256,2048]{1,0:T(8,128)(2,1)S(1)}, u32[]{:S(2)}, u32[]{:S(2)}) %collective-permute-start.52) | collective-permute-done | bytes 1048608 | tf_op jit(solution)/shard_map/ppermute | solution.py:960
  539.7 4.5 keys_back.3
  544.2 4.1 keys_back.2
  548.3 14.2 %inputs_back.1 = (f32[256,2048]{1,0:T(8,128)}, f32[1,2048]{1,0:T(1,128)}, f32[128,2048]{1,0:T(8,128)}, f32[128,3072]{1,0:T(8,128)}) custom-call(s32[32]{0:T(128)} %stack.179.refs_0_, bf16[256,3072]{1,0:T(8,128)(2,1)} %copy-done.3, bf16[256,3072]{1,0:T(8,128)(2,1)} %copy-done.4, bf16[256,3072]{1,0:T(8,128)(2,1)} %collective-permute-done.8.refs_3_, ...), custom_call_target="tpu_custom_call" | custom-call | flops 3221225472 | bytes 12582912 | tf_op jit(solution)/shard_map/inputs_back/pallas_call | solution.py:809
  568.7 5.7 collective-permute-done.57
  579.7 5.0 collective-permute-done.59
  (371 shorter events, 176.0 us)
Async XLA Ops:
  2.6 37.3 %collective-permute-start.2 = (bf16[64,3072]{1,0:T(8,128)(2,1)}, bf16[64,3072]{1,0:T(8,128)(2,1)}, u32[]{:S(2)}, u32[]{:S(2)}) collective-permute-start(bf16[64,3072]{1,0:T(8,128)(2,1)} %fusion.11), channel_id=1, source_target_pairs={{0,4},{1,5},{2,6},{3,7},{4,0},{5,1},{6,2},{7,3},{8,12},{9,13},{10,... | collective-permute-start | bytes 1179656 | tf_op jit(solution)/shard_map/ppermute | solution.py:960
  6.7 32.1 %collective-permute-start.1 = (bf16[64,3072]{1,0:T(8,128)(2,1)}, bf16[64,3072]{1,0:T(8,128)(2,1)}, u32[]{:S(2)}, u32[]{:S(2)}) collective-permute-start(bf16[64,3072]{1,0:T(8,128)(2,1)} %fusion.11), channel_id=1, source_target_pairs={{0,2},{1,3},{2,4},{3,5},{4,6},{5,7},{6,0},{7,1},{8,10},{9,11},{10,... | collective-permute-start | bytes 1179656 | tf_op jit(solution)/shard_map/ppermute | solution.py:960
  8.2 31.7 %collective-permute-start.3 = (bf16[64,3072]{1,0:T(8,128)(2,1)}, bf16[64,3072]{1,0:T(8,128)(2,1)}, u32[]{:S(2)}, u32[]{:S(2)}) collective-permute-start(bf16[64,3072]{1,0:T(8,128)(2,1)} %fusion.11), channel_id=1, source_target_pairs={{0,6},{1,7},{2,0},{3,1},{4,2},{5,3},{6,4},{7,5},{8,14},{9,15},{10,... | collective-permute-start | bytes 1179656 | tf_op jit(solution)/shard_map/ppermute | solution.py:960
  11.7 30.3 %collective-permute-start = (bf16[256,2048]{1,0:T(8,128)(2,1)}, bf16[256,2048]{1,0:T(8,128)(2,1)}, u32[]{:S(2)}, u32[]{:S(2)}) collective-permute-start(bf16[256,2048]{1,0:T(8,128)(2,1)} %bitcast.32.refs_2_.refs_12_), channel_id=1, source_target_pairs={{0,1},{1,0},{2,3},{3,2},{4,5},{5,4},{6,7},{7,6},{8,9},{9,8},{10,11... | collective-permute-start | bytes 3145736 | tf_op jit(solution)/shard_map/ppermute | solution.py:960
  51.4 49.9 %collective-permute-start.12 = (bf16[2,512,1024]{2,1,0:T(8,128)(2,1)}, bf16[2,512,1024]{2,1,0:T(8,128)(2,1)}, u32[]{:S(2)}, u32[]{:S(2)}) collective-permute-start(bf16[2,512,1024]{2,1,0:T(8,128)(2,1)} %constant_dynamic-slice_fusion.2), channel_id=1, source_target_pairs={{0,2},{1,3},{2,0},{3,1},{4,6},{5,7},{6,4},{7,5},{8,10},{9,11},{10,... | collective-permute-start | bytes 6291464 | tf_op jit(solution)/shard_map/ppermute | solution.py:960
  62.8 38.5 %collective-permute-start.11 = (bf16[256,3072]{1,0:T(8,128)(2,1)S(1)}, bf16[256,3072]{1,0:T(8,128)(2,1)S(1)}, u32[]{:S(2)}, u32[]{:S(2)}) collective-permute-start(bf16[256,3072]{1,0:T(8,128)(2,1)S(1)} %constant_dynamic-update-slice_fusion.2.refs_2_), channel_id=1, source_target_pairs={{0,8},{1,9},{2,10},{3,11},{4,12},{5,13},{6,14},{7,15},{8,0},{9,1},... | collective-permute-start | bytes 4718600 | tf_op jit(solution)/shard_map/ppermute | solution.py:960
  62.9 38.4 %collective-permute-start.9 = (bf16[256,3072]{1,0:T(8,128)(2,1)S(1)}, bf16[256,3072]{1,0:T(8,128)(2,1)}, u32[]{:S(2)}, u32[]{:S(2)}) collective-permute-start(bf16[256,3072]{1,0:T(8,128)(2,1)S(1)} %constant_dynamic-update-slice_fusion.2.refs_2_), channel_id=1, source_target_pairs={{0,1},{1,0},{2,3},{3,2},{4,5},{5,4},{6,7},{7,6},{8,9},{9,8},{10,11... | collective-permute-start | bytes 4718600 | tf_op jit(solution)/shard_map/ppermute | solution.py:960
  65.6 35.7 %collective-permute-start.10 = (bf16[256,3072]{1,0:T(8,128)(2,1)S(1)}, bf16[256,3072]{1,0:T(8,128)(2,1)S(1)}, u32[]{:S(2)}, u32[]{:S(2)}) collective-permute-start(bf16[256,3072]{1,0:T(8,128)(2,1)S(1)} %constant_dynamic-update-slice_fusion.refs_1_), channel_id=1, source_target_pairs={{0,8},{1,9},{2,10},{3,11},{4,12},{5,13},{6,14},{7,15},{8,0},{9,1},... | collective-permute-start | bytes 4718600 | tf_op jit(solution)/shard_map/ppermute | solution.py:960
  65.9 36.7 %collective-permute-start.8 = (bf16[256,3072]{1,0:T(8,128)(2,1)S(1)}, bf16[256,3072]{1,0:T(8,128)(2,1)}, u32[]{:S(2)}, u32[]{:S(2)}) collective-permute-start(bf16[256,3072]{1,0:T(8,128)(2,1)S(1)} %constant_dynamic-update-slice_fusion.refs_1_), channel_id=1, source_target_pairs={{0,16},{1,17},{2,18},{3,19},{4,20},{5,21},{6,22},{7,23},{8,24},{9,... | collective-permute-start | bytes 4718600 | tf_op jit(solution)/shard_map/ppermute | solution.py:960
  103.1 25.2 %collective-permute-start.18 = (bf16[64,2048]{1,0:T(8,128)(2,1)S(1)}, bf16[64,2048]{1,0:T(8,128)(2,1)S(1)}, u32[]{:S(2)}, u32[]{:S(2)}) collective-permute-start(bf16[64,2048]{1,0:T(8,128)(2,1)S(1)} %constant_dynamic-slice_fusion.1), channel_id=1, source_target_pairs={{0,2},{1,3},{2,4},{3,5},{4,6},{5,7},{6,0},{7,1},{8,10},{9,11},{10,... | collective-permute-start | bytes 786440 | tf_op jit(solution)/shard_map/ppermute | solution.py:960
  149.0 44.9 %collective-permute-start.26 = (bf16[1024,512]{1,0:T(8,128)(2,1)}, bf16[1024,512]{1,0:T(8,128)(2,1)}, u32[]{:S(2)}, u32[]{:S(2)}) collective-permute-start(bf16[1024,512]{1,0:T(8,128)(2,1)} %constant_dynamic-slice_fusion), channel_id=1, source_target_pairs={{0,2},{1,3},{2,0},{3,1},{4,6},{5,7},{6,4},{7,5},{8,10},{9,11},{10,... | collective-permute-start | bytes 3145736 | tf_op jit(solution)/shard_map/ppermute | solution.py:960
  149.1 47.2 %collective-permute-start.25 = (bf16[256,2048]{1,0:T(8,128)(2,1)}, bf16[256,2048]{1,0:T(8,128)(2,1)}, u32[]{:S(2)}, u32[]{:S(2)}) collective-permute-start(bf16[256,2048]{1,0:T(8,128)(2,1)} %bitcast.32.refs_2_.refs_12_), channel_id=1, source_target_pairs={{0,4},{1,5},{2,6},{3,7},{4,0},{5,1},{6,2},{7,3},{8,12},{9,13},{10,... | collective-permute-start | bytes 3145736 | tf_op jit(solution)/shard_map/ppermute | solution.py:960
  158.7 37.6 %collective-permute-start.24 = (bf16[256,2048]{1,0:T(8,128)(2,1)S(1)}, bf16[256,2048]{1,0:T(8,128)(2,1)S(1)}, u32[]{:S(2)}, u32[]{:S(2)}) collective-permute-start(bf16[256,2048]{1,0:T(8,128)(2,1)S(1)} %constant_dynamic-update-slice_fusion.6.refs_2_), channel_id=1, source_target_pairs={{0,1},{1,0},{2,3},{3,2},{4,5},{5,4},{6,7},{7,6},{8,9},{9,8},{10,11... | collective-permute-start | bytes 3145736 | tf_op jit(solution)/shard_map/ppermute | solution.py:960
  160.4 36.0 %collective-permute-start.23 = (bf16[256,2048]{1,0:T(8,128)(2,1)S(1)}, bf16[256,2048]{1,0:T(8,128)(2,1)}, u32[]{:S(2)}, u32[]{:S(2)}) collective-permute-start(bf16[256,2048]{1,0:T(8,128)(2,1)S(1)} %constant_dynamic-update-slice_fusion.4.refs_1_), channel_id=1, source_target_pairs={{0,16},{1,17},{2,18},{3,19},{4,20},{5,21},{6,22},{7,23},{8,24},{9,... | collective-permute-start | bytes 3145736 | tf_op jit(solution)/shard_map/ppermute | solution.py:960
  162.0 69.6 %collective-permute-start.36 = (bf16[2,512,1024]{2,1,0:T(8,128)(2,1)}, bf16[2,512,1024]{2,1,0:T(8,128)(2,1)}, u32[]{:S(2)}, u32[]{:S(2)}) collective-permute-start(bf16[2,512,1024]{2,1,0:T(8,128)(2,1)} %collective-permute-done.12.refs_6_.refs_8_), channel_id=1, source_target_pairs={{0,16},{1,17},{2,18},{3,19},{4,20},{5,21},{6,22},{7,23},{8,24},{9,... | collective-permute-start | bytes 6291464 | tf_op jit(solution)/shard_map/ppermute | solution.py:960
  196.3 35.2 %collective-permute-start.29 = (bf16[256,2048]{1,0:T(8,128)(2,1)}, bf16[256,2048]{1,0:T(8,128)(2,1)S(1)}, u32[]{:S(2)}, u32[]{:S(2)}) collective-permute-start(bf16[256,2048]{1,0:T(8,128)(2,1)} %collective-permute-done.23.refs_3_), channel_id=1, source_target_pairs={{0,8},{1,9},{2,10},{3,11},{4,12},{5,13},{6,14},{7,15},{8,0},{9,1},... | collective-permute-start | bytes 3145736 | tf_op jit(solution)/shard_map/ppermute | solution.py:960
  196.9 34.7 %collective-permute-start.30 = (bf16[256,2048]{1,0:T(8,128)(2,1)S(1)}, bf16[256,2048]{1,0:T(8,128)(2,1)S(1)}, u32[]{:S(2)}, u32[]{:S(2)}) collective-permute-start(bf16[256,2048]{1,0:T(8,128)(2,1)S(1)} %collective-permute-done.24.refs_4_), channel_id=1, source_target_pairs={{0,8},{1,9},{2,10},{3,11},{4,12},{5,13},{6,14},{7,15},{8,0},{9,1},... | collective-permute-start | bytes 3145736 | tf_op jit(solution)/shard_map/ppermute | solution.py:960
  197.6 97.1 %collective-permute-start.37 = (bf16[2,512,1024]{2,1,0:T(8,128)(2,1)}, bf16[2,512,1024]{2,1,0:T(8,128)(2,1)}, u32[]{:S(2)}, u32[]{:S(2)}) collective-permute-start(bf16[2,512,1024]{2,1,0:T(8,128)(2,1)} %collective-permute-done.12.refs_6_.refs_8_), channel_id=1, source_target_pairs={{0,8},{1,9},{2,10},{3,11},{4,12},{5,13},{6,14},{7,15},{8,0},{9,1},... | collective-permute-start | bytes 6291464 | tf_op jit(solution)/shard_map/ppermute | solution.py:960
  199.5 51.3 %collective-permute-start.39 = (bf16[1024,512]{1,0:T(8,128)(2,1)}, bf16[1024,512]{1,0:T(8,128)(2,1)}, u32[]{:S(2)}, u32[]{:S(2)}) collective-permute-start(bf16[1024,512]{1,0:T(8,128)(2,1)} %collective-permute-done.26.refs_10_.refs_12_), channel_id=1, source_target_pairs={{0,16},{1,17},{2,18},{3,19},{4,20},{5,21},{6,22},{7,23},{8,24},{9,... | collective-permute-start | bytes 3145736 | tf_op jit(solution)/shard_map/ppermute | solution.py:960
  231.6 65.2 %collective-permute-start.38 = (bf16[2,512,1024]{2,1,0:T(8,128)(2,1)}, bf16[2,512,1024]{2,1,0:T(8,128)(2,1)S(1)}, u32[]{:S(2)}, u32[]{:S(2)}) collective-permute-start(bf16[2,512,1024]{2,1,0:T(8,128)(2,1)} %collective-permute-done.36.refs_7_.refs_9_), channel_id=1, source_target_pairs={{0,8},{1,9},{2,10},{3,11},{4,12},{5,13},{6,14},{7,15},{8,0},{9,1},... | collective-permute-start | bytes 6291464 | tf_op jit(solution)/shard_map/ppermute | solution.py:960
  244.5 36.4 %collective-permute-start.32 = (bf16[128,2048]{1,0:T(8,128)(2,1)S(1)}, bf16[128,2048]{1,0:T(8,128)(2,1)S(1)}, u32[]{:S(2)}, u32[]{:S(2)}) collective-permute-start(bf16[128,2048]{1,0:T(8,128)(2,1)S(1)} %get-tuple-element.313), channel_id=1, source_target_pairs={{0,4},{1,5},{2,6},{3,7},{4,0},{5,1},{6,2},{7,3},{8,12},{9,13},{10,... | collective-permute-start | bytes 1572872 | tf_op jit(solution)/shard_map/ppermute | solution.py:960
  244.6 47.6 %collective-permute-start.31 = (bf16[128,2048]{1,0:T(8,128)(2,1)S(1)}, bf16[128,2048]{1,0:T(8,128)(2,1)S(1)}, u32[]{:S(2)}, u32[]{:S(2)}) collective-permute-start(bf16[128,2048]{1,0:T(8,128)(2,1)S(1)} %get-tuple-element.314), channel_id=1, source_target_pairs={{0,4},{1,5},{2,6},{3,7},{4,0},{5,1},{6,2},{7,3},{8,12},{9,13},{10,... | collective-permute-start | bytes 1572872 | tf_op jit(solution)/shard_map/ppermute | solution.py:960
  250.8 42.8 %collective-permute-start.33 = (bf16[256,2048]{1,0:T(8,128)(2,1)S(1)}, bf16[256,2048]{1,0:T(8,128)(2,1)}, u32[]{:S(2)}, u32[]{:S(2)}) collective-permute-start(bf16[256,2048]{1,0:T(8,128)(2,1)S(1)} %copy-done.25), channel_id=1, source_target_pairs={{0,1},{1,0},{2,3},{3,2},{4,5},{5,4},{6,7},{7,6},{8,9},{9,8},{10,11... | collective-permute-start | bytes 3145736 | tf_op jit(solution)/shard_map/ppermute | solution.py:960
  293.6 48.2 %collective-permute-start.43 = (bf16[256,2048]{1,0:T(8,128)(2,1)}, bf16[256,2048]{1,0:T(8,128)(2,1)S(1)}, u32[]{:S(2)}, u32[]{:S(2)}) collective-permute-start(bf16[256,2048]{1,0:T(8,128)(2,1)} %collective-permute-done.25.refs_4_), channel_id=1, source_target_pairs={{0,1},{1,0},{2,3},{3,2},{4,5},{5,4},{6,7},{7,6},{8,9},{9,8},{10,11... | collective-permute-start | bytes 3145736 | tf_op jit(solution)/shard_map/ppermute | solution.py:960
  294.7 38.5 %collective-permute-start.34 = (bf16[128,2048]{1,0:T(8,128)(2,1)}, bf16[128,2048]{1,0:T(8,128)(2,1)S(1)}, u32[]{:S(2)}, u32[]{:S(2)}) collective-permute-start(bf16[128,2048]{1,0:T(8,128)(2,1)} %copy-done.56), channel_id=1, source_target_pairs={{0,1},{1,0},{2,3},{3,2},{4,5},{5,4},{6,7},{7,6},{8,9},{9,8},{10,11... | collective-permute-start | bytes 1572872 | tf_op jit(solution)/shard_map/ppermute | solution.py:960
  295.6 46.1 %collective-permute-start.35 = (bf16[128,2048]{1,0:T(8,128)(2,1)}, bf16[128,2048]{1,0:T(8,128)(2,1)S(1)}, u32[]{:S(2)}, u32[]{:S(2)}) collective-permute-start(bf16[128,2048]{1,0:T(8,128)(2,1)} %copy-done.55), channel_id=1, source_target_pairs={{0,1},{1,0},{2,3},{3,2},{4,5},{5,4},{6,7},{7,6},{8,9},{9,8},{10,11... | collective-permute-start | bytes 1572872 | tf_op jit(solution)/shard_map/ppermute | solution.py:960
  383.5 70.1 %collective-permute-start.42 = (bf16[256,2048]{1,0:T(8,128)(2,1)S(1)}, bf16[256,2048]{1,0:T(8,128)(2,1)S(1)}, u32[]{:S(2)}, u32[]{:S(2)}) collective-permute-start(bf16[256,2048]{1,0:T(8,128)(2,1)S(1)} %get-tuple-element.311), channel_id=1, source_target_pairs={{0,1},{1,0},{2,3},{3,2},{4,5},{5,4},{6,7},{7,6},{8,9},{9,8},{10,11... | collective-permute-start | bytes 3145736 | tf_op jit(solution)/shard_map/ppermute | solution.py:960
  406.8 34.7 %collective-permute-start.45 = (bf16[128,2048]{1,0:T(8,128)(2,1)S(1)}, bf16[128,2048]{1,0:T(8,128)(2,1)S(1)}, u32[]{:S(2)}, u32[]{:S(2)}) collective-permute-start(bf16[128,2048]{1,0:T(8,128)(2,1)S(1)} %get-tuple-element.307), channel_id=1, source_target_pairs={{0,4},{1,5},{2,6},{3,7},{4,0},{5,1},{6,2},{7,3},{8,12},{9,13},{10,... | collective-permute-start | bytes 1572872 | tf_op jit(solution)/shard_map/ppermute | solution.py:960
  406.9 45.7 %collective-permute-start.47 = (bf16[128,2048]{1,0:T(8,128)(2,1)S(1)}, bf16[128,2048]{1,0:T(8,128)(2,1)S(1)}, u32[]{:S(2)}, u32[]{:S(2)}) collective-permute-start(bf16[128,2048]{1,0:T(8,128)(2,1)S(1)} %get-tuple-element.308), channel_id=1, source_target_pairs={{0,4},{1,5},{2,6},{3,7},{4,0},{5,1},{6,2},{7,3},{8,12},{9,13},{10,... | collective-permute-start | bytes 1572872 | tf_op jit(solution)/shard_map/ppermute | solution.py:960
  410.8 79.9 %collective-permute-start.49 = (bf16[256,2048]{1,0:T(8,128)(2,1)}, bf16[256,2048]{1,0:T(8,128)(2,1)S(1)}, u32[]{:S(2)}, u32[]{:S(2)}) collective-permute-start(bf16[256,2048]{1,0:T(8,128)(2,1)} %slice.249), channel_id=1, source_target_pairs={{0,1},{1,0},{2,3},{3,2},{4,5},{5,4},{6,7},{7,6},{8,9},{9,8},{10,11... | collective-permute-start | bytes 3145736 | tf_op jit(solution)/shard_map/ppermute | solution.py:960
  413.5 78.6 %collective-permute-start.48 = (bf16[256,2048]{1,0:T(8,128)(2,1)}, bf16[256,2048]{1,0:T(8,128)(2,1)}, u32[]{:S(2)}, u32[]{:S(2)}) collective-permute-start(bf16[256,2048]{1,0:T(8,128)(2,1)} %get-tuple-element.305), channel_id=1, source_target_pairs={{0,1},{1,0},{2,3},{3,2},{4,5},{5,4},{6,7},{7,6},{8,9},{9,8},{10,11... | collective-permute-start | bytes 3145736 | tf_op jit(solution)/shard_map/ppermute | solution.py:960
  492.1 47.5 %collective-permute-start.52 = (bf16[256,2048]{1,0:T(8,128)(2,1)}, bf16[256,2048]{1,0:T(8,128)(2,1)S(1)}, u32[]{:S(2)}, u32[]{:S(2)}) collective-permute-start(bf16[256,2048]{1,0:T(8,128)(2,1)} %add_convert_fusion.1), channel_id=1, source_target_pairs={{0,4},{1,5},{2,6},{3,7},{4,0},{5,1},{6,2},{7,3},{8,12},{9,13},{10,... | collective-permute-start | bytes 3145736 | tf_op jit(solution)/shard_map/ppermute | solution.py:960
  (91 other events, 1154.8 us)

commit v3 on v2

--- a/solution.py
+++ b/solution.py
@@ -826,33 +826,44 @@
     )(w.places, *w.blocks, *rest)
 
 
-def mlp_kernel(places_ref, *refs, rows, parts, tile):
+def mlp_kernel(place_ref, *refs, rows, paired, tile, own, carried_in):
     n = len(rows[0]) + len(rows[1])
     tokens, refs = refs[:n], refs[n:]
     own_gu, own_dn = refs[:2]
-    pair_gu, pair_dn, refs = refs[2 : 2 + parts], refs[2 + parts : 2 + 2 * parts], refs[2 + 2 * parts :]
+    pair, refs = (refs[2], refs[3:]) if paired else (None, refs[2:])
+    sums, refs = (refs[:2], refs[2:]) if carried_in else (None, refs)
     out_ref, back_ref, h, c, gu, dn, out, back, row_sem, gu_sem, dn_sem = refs
     step, steps = pl.program_id(0), pl.num_programs(0)
-    own_tiles = own_gu.shape[2] // tile
-    width = D // parts
-
-    def fetch(i, slot):
-        @pl.when(i < own_tiles)
+    own_tiles = own_gu.shape[2] // tile if own else 0
+
+    def fetch(n, slot):
+        @pl.when(n < own_tiles)
         def _():
-            at = pl.ds(pl.multiple_of(i * tile, tile), tile)
+            at = pl.ds(pl.multiple_of(n * tile, tile), tile)
             pltpu.make_async_copy(own_gu.at[:, :, at], gu.at[slot], gu_sem.at[slot]).start()
             pltpu.make_async_copy(own_dn.at[at, :], dn.at[slot], dn_sem.at[slot]).start()
 
-        @pl.when(i >= own_tiles)
+        if not paired:
+            return
+
+        @pl.when(n >= own_tiles)
         def _():
-            at = pl.ds(pl.multiple_of((i - own_tiles) * tile, tile), tile)
-            for k in range(parts):
-                there = pl.ds(pl.multiple_of(places_ref[k] * width, width), width)
+            first = (n - own_tiles) * tile
+            at = pl.ds(pl.multiple_of(first, tile), tile)
+            width = pair.shape[1] // 3
+            row = pl.ds(pl.multiple_of(2 * width + first % width, tile), tile)
+            column = pl.ds(pl.multiple_of(first // width * width, width), width)
+            for k in range(D // width):
+                part = pair.at[2 * k + place_ref[0]]
+                there = slice(k * width, (k + 1) * width)
+                for i in range(2):
+                    pltpu.make_async_copy(
+                        part.at[i * width : (i + 1) * width, at],
+                        gu.at[slot, i, there, :],
+                        gu_sem.at[slot],
+                    ).start()
                 pltpu.make_async_copy(
-                    pair_gu[k].at[:, :, at], gu.at[slot, :, there, :], gu_sem.at[slot]
-                ).start()
-                pltpu.make_async_copy(
-                    pair_dn[k].at[at, :], dn.at[slot, :, there], dn_sem.at[slot]
+                    part.at[row, column], dn.at[slot, :, there], dn_sem.at[slot]
                 ).start()
 
     @pl.when(step == 0)
@@ -868,8 +879,13 @@
                 at += size
         for copy in copies:
             copy.start()
-        out[...] = jnp.zeros_like(out)
-        back[...] = jnp.zeros_like(back)
+        if carried_in:
+            for i, target in enumerate((out, back)):
+                copies.append(pltpu.make_async_copy(sums[i], target, row_sem.at[len(copies)]))
+                copies[-1].start()
+        else:
+            out[...] = jnp.zeros_like(out)
+            back[...] = jnp.zeros_like(back)
         for copy in copies:
             copy.wait()
 
@@ -895,25 +911,35 @@
 
     @pl.when(step == steps - 1)
     def _():
-        out_ref[...] = out[...].astype(BF16)
-        back_ref[...] = back[...].astype(BF16)
-
-
-def mlp(second, cot, own_gu, own_dn, pair, places):
+        out_ref[...] = out[...].astype(out_ref.dtype)
+        back_ref[...] = back[...].astype(back_ref.dtype)
+
+
+def mlp(second, cot, own_gu, own_dn, pair=None, place=None, own=True, sums=()):
     rows = tuple(v.shape[0] for v in second), tuple(v.shape[0] for v in cot)
     total = sum(rows[0])
     hidden = own_gu.shape[2]
     tile = min(256, hidden)
-    parts = len(pair)
-    anywhere = pl.BlockSpec(memory_space=pl.ANY)
-    whole = pl.BlockSpec((total, D), lambda i, p: (0, 0))
+    shards = own + (pair is not None)
+    kind = F32 if pair is None else BF16
+    if pair is None:
+        place = jnp.zeros((1,), jnp.int32)
+    block = pl.BlockSpec((total, D), lambda i, p: (0, 0))
+    arrays = (*second, *cot, own_gu, own_dn, *(() if pair is None else (pair,)), *sums)
     return pl.pallas_call(
-        functools.partial(mlp_kernel, rows=rows, parts=parts, tile=tile),
+        functools.partial(
+            mlp_kernel,
+            rows=rows,
+            paired=pair is not None,
+            tile=tile,
+            own=own,
+            carried_in=bool(sums),
+        ),
         grid_spec=pltpu.PrefetchScalarGridSpec(
             num_scalar_prefetch=1,
-            grid=(2 * hidden // tile,),
-            in_specs=[anywhere] * (len(second) + len(cot) + 2 + 2 * parts),
-            out_specs=[whole, whole],
+            grid=(shards * hidden // tile,),
+            in_specs=[ANYWHERE] * len(arrays),
+            out_specs=[block, block],
             scratch_shapes=[
                 pltpu.VMEM((total, D), BF16),
                 pltpu.VMEM((total, D), BF16),
@@ -921,18 +947,20 @@
                 pltpu.VMEM((2, tile, D), BF16),
                 pltpu.VMEM((total, D), F32),
                 pltpu.VMEM((total, D), F32),
-                pltpu.SemaphoreType.DMA((len(second) + len(cot),)),
+                pltpu.SemaphoreType.DMA((len(second) + len(cot) + len(sums),)),
                 pltpu.SemaphoreType.DMA((2,)),
                 pltpu.SemaphoreType.DMA((2,)),
             ],
         ),
-        out_shape=[jax.ShapeDtypeStruct((total, D), BF16)] * 2,
+        out_shape=[jax.ShapeDtypeStruct((total, D), kind)] * 2,
         compiler_params=pltpu.CompilerParams(vmem_limit_bytes=VMEM_LIMIT),
         cost_estimate=pl.CostEstimate(
-            flops=12 * total * D * hidden * 2, bytes_accessed=12 * D * hidden, transcendentals=0
+            flops=12 * total * D * hidden * shards,
+            bytes_accessed=6 * D * hidden * shards,
+            transcendentals=0,
         ),
         name="mlp",
-    )(places, *second, *cot, own_gu, own_dn, *[p[0] for p in pair], *[p[1] for p in pair])
+    )(place, *arrays)
 
 
 class Grid:
@@ -974,10 +1002,13 @@
     def flip_core(self, value):
         return self.send(value, lambda y, c, z, x: (y, 1 - c, z, x))
 
-    def flip_row(self, value, bit):
+    def flip_x(self, value, bit):
+        return self.send(value, lambda y, c, z, x: (y, c, z, x ^ bit))
+
+    def flip_seq(self, value, bit):
         def move(y, c, z, x):
-            r = (z * self.xs + x) ^ bit
-            return (y, c, r // self.xs, r % self.xs)
+            s = (y * CORES + c) ^ bit
+            return (s // CORES, s % CORES, z, x)
 
         return self.send(value, move)
 
@@ -1044,32 +1075,24 @@
         return Gathered(blocks, jnp.stack(places).astype(jnp.int32), self.size)
 
 
-class Pair:
-    def __init__(self, grid, gate_up, down):
-        self.grid = grid
-        part = D // grid.seq
-        self.gu = lax.dynamic_slice_in_dim(gate_up, grid.s * part, part, 1)
-        self.dn = lax.dynamic_slice_in_dim(down, grid.s * part, part, 1)
-
-    def gate_up_z(self):
-        self.gu = [self.grid.flip_z(self.gu, FAR_BIT)]
-
-    def down_z(self):
-        self.dn = [self.grid.flip_z(self.dn, FAR_BIT)]
-
-    def gate_up_y(self):
-        self.gu += [self.grid.along_y(self.gu[0], k) for k in range(1, self.grid.ys)]
-
-    def down_y(self):
-        self.dn += [self.grid.along_y(self.dn[0], k) for k in range(1, self.grid.ys)]
-
-    def result(self):
-        grid = self.grid
-        gus = self.gu + [grid.flip_core(v) for v in self.gu]
-        dns = self.dn + [grid.flip_core(v) for v in self.dn]
-        places = [grid.s] + [(grid.y - k) % grid.ys * CORES + grid.c for k in range(1, grid.ys)]
-        places = places + [p + 1 - 2 * grid.c for p in places]
-        return list(zip(gus, dns)), jnp.stack(places).astype(jnp.int32)
+def pair_part(grid, gate_up, down):
+    part = D // grid.seq
+    hidden = down.shape[0]
+    size = (1, part, hidden)
+    gu = [lax.dynamic_slice(gate_up, (i, grid.s * part, 0), size)[0] for i in range(2)]
+    dn = lax.dynamic_slice_in_dim(down, grid.s * part, part, 1)
+    dn = jnp.concatenate([dn[i : i + part] for i in range(0, hidden, part)], axis=1)
+    return jnp.concatenate([*gu, dn], axis=0)
+
+
+def gather_pair(grid, part):
+    groups = []
+    for z in range(0, grid.zs, 2):
+        for x in range(grid.xs):
+            rows = [(z + i) * grid.xs + x for i in range(2)]
+            groups.append([s * grid.rows + r for s in range(grid.seq) for r in rows])
+    parts = lax.all_gather(part, ("seq", "rows"), axis_index_groups=groups)
+    return parts, (1 - grid.z % 2).reshape(1).astype(jnp.int32)
 
 
 def spread_near(grid, block):
@@ -1078,45 +1101,47 @@
 
 def spread_far(grid, block, parts):
     size = block.shape[0] // parts
-    pieces = [grid.flip_z(block[p * size : (p + 1) * size], NEAR_BIT) for p in range(parts)]
-    return pieces, lambda pieces: list(pieces) + [
-        grid.along_x(piece, k) for k in range(1, grid.xs) for piece in pieces
-    ]
-
-
-def collect(grid, near, far, length, parts):
+    return [grid.flip_z(block[p * size : (p + 1) * size], NEAR_BIT) for p in range(parts)]
+
+
+def relay(grid, pieces):
+    moved = [grid.along_x(piece, k) for k in range(1, grid.xs) for piece in pieces]
+    return list(pieces) + moved
+
+
+def collect_near(grid, near, length):
+    blocks = [near[k * length : (k + 1) * length] for k in range(grid.xs)]
+    return [blocks[0]] + [grid.along_x(blocks[k], -k) for k in range(1, grid.xs)]
+
+
+def collect_far(grid, far, length, parts):
     size = length // parts
-    terms = [near[:length]]
-    send = []
+    send, total = [], None
     for p in range(parts):
         lo = p * size
+        far = after(far, total)
         total = far[lo : lo + size]
         for k in range(1, grid.xs):
             other = grid.along_x(far[k * length + lo : k * length + lo + size], -k)
             total = (total.astype(F32) + other.astype(F32)).astype(BF16)
         send.append(total)
-    for k in range(1, grid.xs):
-        terms.append(grid.along_x(near[k * length : (k + 1) * length], -k))
-    return terms, send
+    return send
 
 
 def total_over_all(grid, values):
     widths = [v.shape[2] for v in values]
     packed = jnp.concatenate([v.astype(BF16) for v in values], axis=2)
     packed = jnp.pad(packed, ((0, 0), (0, 0), (0, -packed.shape[2] % FEAT)))
-    packed = packed.reshape(grid.ys, CORES, 8, -1)
-    own = lax.dynamic_index_in_dim(packed, grid.c, 1, False)
-    other = lax.dynamic_index_in_dim(packed, 1 - grid.c, 1, False)
-    both = (own.astype(F32) + grid.flip_core(other).astype(F32)).astype(BF16)
-    total = lax.dynamic_index_in_dim(both, grid.y, 0, False).astype(F32)
-    for k in range(1, grid.ys):
-        part = lax.dynamic_index_in_dim(both, (grid.y + k) % grid.ys, 0, False)
-        total = total + grid.along_y(part, k).astype(F32)
-    bit = 1
-    while bit < grid.rows:
+    chunk = lambda i: lax.dynamic_index_in_dim(packed, i, 0, False)
+    total = chunk(grid.s).astype(F32)
+    for k in range(1, grid.seq):
+        total = total + grid.flip_seq(chunk(grid.s ^ k), k).astype(F32)
+    for flip, count in ((grid.flip_z, grid.zs), (grid.flip_x, grid.xs)):
         mine = total.astype(BF16)
-        total = mine.astype(F32) + grid.flip_row(mine, bit).astype(F32)
-        bit *= 2
+        terms = [mine.astype(F32)] + [flip(mine, k).astype(F32) for k in range(1, count)]
+        while len(terms) > 1:
+            terms = [a + b for a, b in zip(terms[::2], terms[1::2])]
+        total = terms[0]
     out, at = [], 0
     for w in widths:
         out.append(total[:, at : at + w])
@@ -1201,7 +1226,6 @@
     masks, former, latter, heard = documents(grid, doc_starts[0], length)
     qkv = Gather(grid, jnp.concatenate([w_query, w_key, w_value], axis=1))
     out = Gather(grid, w_out)
-    pair = Pair(grid, w_gate_up, w_down)
     cot_near = spread_near(grid, grad_out)
     qkv.over_z()
 
@@ -1224,60 +1248,78 @@
     o_out = jnp.pad(proj_out, ((0, LOW - rank), (0, 0)))
     low = dot_nn(inputs, qkv_in).astype(BF16)
 
-    cot_near, qkv.halves, heard, pair.gu = after((cot_near, qkv.halves, heard, pair.gu))
+    cot_near, qkv.halves, heard, out.own = after((cot_near, qkv.halves, heard, out.own))
     qkv.first()
-    pair.gate_up_z()
+    out.over_z()
     ready = (masks, former, latter, maps_q, maps_k, qkv_in, qkv_out, o_in, o_out, inputs, low)
-    qkv.moved, ready = after((qkv.moved, ready))
+    mine = w_gate_up, w_down
+    qkv.moved, out.halves, ready, mine, grad_out = after(
+        (qkv.moved, out.halves, ready, mine, grad_out)
+    )
+    pair = pair_part(grid, *mine)
     masks, former, latter, maps_q, maps_k, qkv_in, qkv_out, o_in, o_out, inputs, low = ready
     cosine, sine = masks["cos"], masks["sin"]
     qkv.second()
     qkv.cores()
-    qkv.last, qkv.over, out.own, pair.gu = after((qkv.last, qkv.over, out.own, pair.gu))
+    half = length // 2
+    cot_far = spread_far(grid, grad_out[:half], 1)
+    late = grad_out[half:]
+    qkv.last, qkv.over, out.halves, cot_far, late, pair = after(
+        (qkv.last, qkv.over, out.halves, cot_far, late, pair)
+    )
+    pair = gather_pair(grid, pair)
     w_qkv = qkv.result()
-    out.over_z()
+    out.first()
     kv, kf, pack, full = project_kv(
         w_qkv, inputs, low, qkv_out[:, D:], cosine, sine, maps_k, masks["survive"]
     )
+    kv, kf, pack, full, out.moved = after((kv, kf, pack, full, out.moved))
     rim = grid.along_seq(pack, 1)
+    fulls = [grid.along_seq(full, k) for k in range(2, grid.seq)]
+    out.second()
+    queries = [
+        project_q(i, w_qkv, inputs, low, qkv_out, cosine, sine, maps_q) for i in range(HALVES)
+    ]
+    rim, fulls, queries, out.blocks, out.last, late = after(
+        (rim, fulls, queries, out.blocks, out.last, late)
+    )
+    out.cores()
+    w_o = out.result()
+    cot_far += spread_far(grid, late, 1)
     carry = former[0] * rim[2 * WINDOW :].astype(F32)
-    for k in range(2, grid.seq):
-        carry = carry + former[k - 1] * grid.along_seq(full, k).astype(F32)
+    for w, full in zip(former[1:], fulls):
+        carry = carry + w * full.astype(F32)
     carry = carry.astype(BF16)
-    first = project_q(0, w_qkv, inputs, low, qkv_out, cosine, sine, maps_q)
-    rim, carry, first, out.halves, pair.gu, pair.dn, grad_out = after(
-        (rim, carry, first, out.halves, pair.gu, pair.dn, grad_out)
-    )
-    out.first()
-    out.second()
-    out.cores()
-    pair.gate_up_y()
-    pair.down_z()
-    cot_far, relay = spread_far(grid, grad_out, 1)
-    queries, merged, attended, inverse = [], [], [], []
+    merged, attended, inverse = [], [], []
     for i in range(HALVES):
-        q, qf = project_q(i, w_qkv, inputs, low, qkv_out, cosine, sine, maps_q) if i else first
-        queries.append((q, qf))
-        block = attend(i, q, qf, kv, kf, rim, carry, masks)
+        block = attend(i, *queries[i], kv, kf, rim, carry, masks)
         merged.append(block[0])
         attended.append(block[1])
         inverse.append(block[2])
-
-    merged, out.last, cot_far, pair.dn = after((merged, out.last, cot_far, pair.dn))
-    w_o = out.result()
-    pair.down_y()
-    cot_far = relay(cot_far)
-    pair, pair_places = pair.result()
+    merged, w_o.blocks, cot_far = after((merged, w_o.blocks, cot_far))
+    moved = relay(grid, cot_far[:1])[1:]
     residual, second_in, out_low, inverse_second = out_project(
         w_o, merged, hidden, o_in, o_out, gain_second
     )
+    second_in, moved = after((second_in, moved))
     near = spread_near(grid, second_in)
-    far, relay = spread_far(grid, second_in, 2)
-    far = relay(after(far, near))
-    near_out, near_grad = mlp(near, cot_near, w_gate_up, w_down, pair, pair_places)
+    far = spread_far(grid, second_in[:half], 1)
+    near, far, late, cot_far = after((near, far, second_in[half:], cot_far))
+    others = relay(grid, cot_far[1:])[1:]
+    cot_far = cot_far + [v for pieces in zip(moved, others) for v in pieces]
+    far += spread_far(grid, late, 1)
+    moved = relay(grid, far[:1])[1:]
+    sums = mlp(near, cot_near, w_gate_up, w_down)
+    sums, far, moved = after((sums, far, moved))
+    others = relay(grid, far[1:])[1:]
+    far = far + [v for pieces in zip(moved, others) for v in pieces]
+    shard = w_gate_up, w_down, *pair
+    near_out, near_grad = mlp(near, cot_near, *shard, own=False, sums=sums)
     far, near_out, near_grad = after((far, near_out, near_grad))
-    far_out, far_grad = mlp(far, cot_far, w_gate_up, w_down, pair, pair_places)
-    terms, send = collect(grid, near_grad, far_grad, length, 2)
+    far_out, far_grad = mlp(far, cot_far, *shard)
+    terms = collect_near(grid, near_grad, length)
+    far_grad, terms = after((far_grad, terms))
+    send = collect_far(grid, far_grad, length, 2)
     near_out, far_out = after((near_out, far_out), send)
     terms.append(jnp.concatenate([grid.flip_z(v, NEAR_BIT) for v in send], axis=0))
 
@@ -1294,20 +1336,17 @@
         far_back = far_back + latter[k - 1] * grid.along_seq(back, -k).astype(F32)
     near_back = far_back + latter[0] * grid.along_seq(back, -1).astype(F32)
     near_back, far_back = near_back.astype(BF16), far_back.astype(BF16)
-    out_terms, send = collect(grid, near_out, far_out, length, 1)
+    out_terms = collect_near(grid, near_out, length)
+    send = collect_far(grid, far_out, length, 1)
     scaled, out_terms, send = after((scaled, out_terms, send))
     out_terms += [grid.flip_z(v, NEAR_BIT) for v in send]
-    backs = [
-        attend_back(i, *queries[i], kv, kf, rim, carry, *scaled[i][:2], masks, maps_q)
-        for i in range(HALVES)
-    ]
+    backs = []
+    for i in range(HALVES):
+        backs.append(
+            attend_back(i, *queries[i], kv, kf, rim, carry, *scaled[i][:2], masks, maps_q)
+        )
     raw_query = [v[0] for v in backs]
     rim_back = [grid.along_seq(v[3], -1) for v in backs]
-    rim_back, out_terms = after((rim_back, out_terms))
-    block_out = residual
-    for term in out_terms:
-        block_out = block_out + term.astype(F32)
-    block_out = block_out.astype(BF16)
     raw_key, raw_value, dmap_key = [], [], []
     for i, (_, dkv, dkf, *_) in enumerate(backs):
         k, v, m = keys_back(
@@ -1316,6 +1355,11 @@
         raw_key.append(k)
         raw_value.append(v)
         dmap_key.append(m)
+    raw_key, out_terms = after((raw_key, out_terms))
+    block_out = residual
+    for term in out_terms:
+        block_out = block_out + term.astype(F32)
+    block_out = block_out.astype(BF16)
     dmap_query = jnp.concatenate([v[4] for v in backs], axis=0)
     dmap_key = jnp.concatenate(dmap_key, axis=0)
     dlogit = jnp.concatenate([v[5] for v in backs], axis=0)

time: 606 us -> 565 us (0.932)
  waiting for transfers between devices: 240 us -> 164 us
  other arithmetic: 29.9 us -> 44.1 us
  between operations: 5.87 us -> 19.4 us
  Pallas kernels: 199 us -> 207 us
    ppermute x61 -> x57, waiting for transfers between devices: 240 us -> 163 us  [send(): lax.ppermute(v, ('seq', 'rows'), route)]
    concatenate x0 -> x1, other arithmetic: none -> 9.23 us  [pair_part(): return jnp.concatenate([*gu, dn], axis=0)]
    pallas_call x2 -> x3, Pallas kernels: 70.5 us -> 77.9 us  [mlp(): pl.pallas_call(functools.partial(mlp_kernel, rows=rows, paired=pair is no...]
    ppermute x61 -> x57, starting transfers between devices: 68.9 us -> 71.1 us  [send(): lax.ppermute(v, ('seq', 'rows'), route)]
  transfers between devices with their start and end apart: 61 -> 58, of which waited for: 28 -> 25; matrix products, arithmetic and copies ran while one was open for 10% -> 14% of each run, Pallas kernels for 24% -> 34%
where the time goes in v3:
time: 565 us; the launch traced here: 559 us
  Pallas kernels  207 us (37%)
  waiting for transfers between devices  164 us (29%)
  starting transfers between devices  71.2 us (13%)
  local copies, waits for them, and re-layouts  52.6 us (9%)
  other arithmetic  44.1 us (8%)
  between operations  19.4 us (3%)
    ppermute x57, waiting for transfers between devices, send(): lax.ppermute(v, ('seq', 'rows'), route)  163 us
    pallas_call x3, Pallas kernels, mlp(): pl.pallas_call(functools.partial(mlp_kernel, rows=rows, paired=pair is no...  77.9 us
    ppermute x57, starting transfers between devices, send(): lax.ppermute(v, ('seq', 'rows'), route)  71.1 us
    pallas_call x2, Pallas kernels, attend_back(): pl.pallas_call(attend_back_kernel, grid=(PER_HALF,), in_specs=[s['q'], s[...  31.2 us
    pallas_call x2, Pallas kernels, project_q(): pl.pallas_call(functools.partial(project_q_kernel, counts=w.shapes(), siz...  20 us
    pallas_call x2, Pallas kernels, attend(): pl.pallas_call(attend_kernel, grid=(PER_HALF,), in_specs=[s['q'], s['qf']...  16.1 us
    pallas_call x1, Pallas kernels, inputs_back(): pl.pallas_call(functools.partial(inputs_back_kernel, counts=w.shapes(), s...  14.5 us
  transfers between devices with their start and end apart: 58, of which 25 were waited for; matrix products, arithmetic and copies ran while one was open for 14% of the time, Pallas kernels for 34%

profile of v3, /device:TPU:0, one launch (start us, length us, event | category | flops | bytes accessed | tf_op | source)
XLA Modules:
  0.0 559.0 jit_solution(2555042465846138373)
XLA Ops:
  8.4 4.1 collective-permute-start.2
  57.4 13.8 %collective-permute-done.8 = bf16[64,2048]{1,0:T(8,128)(2,1)S(1)} collective-permute-done((bf16[64,2048]{1,0:T(8,128)(2,1)}, bf16[64,2048]{1,0:T(8,128)(2,1)S(1)}, u32[]{:S(2)}, u32[]{:S(2)}) %collective-permute-start.8) | collective-permute-done | bytes 262176 | tf_op jit(solution)/shard_map/ppermute | solution.py:988
  88.7 9.2 %maximum_maximum_fusion = bf16[1536,1024]{1,0:T(8,128)(2,1)} fusion(bf16[512,512]{1,0:T(8,128)(2,1)S(1)} %get-tuple-element.388, bf16[512,512]{1,0:T(8,128)(2,1)S(1)} %get-tuple-element.387, bf16[512,1024]{1,0:T(8,128)(2,1)S(1)} %get-tuple-element.386, bf16[512,1024]{1,0:T(8,128)(2,1)S(1)} %get-tuple-element.385), kind=kLoop, calls=%fused_computation | loop fusion | flops 12582912 | bytes 6291456 | tf_op jit(solution)/shard_map/concatenate | solution.py:1085
  98.0 11.7 %collective-permute-done.15.refs_4_ = bf16[128,2048]{1,0:T(8,128)(2,1)} collective-permute-done((bf16[128,2048]{1,0:T(8,128)(2,1)}, bf16[128,2048]{1,0:T(8,128)(2,1)}, u32[]{:S(2)}, u32[]{:S(2)}) %collective-permute-start.15) | collective-permute-done | bytes 524320 | tf_op jit(solution)/shard_map/ppermute | solution.py:988
  130.4 9.1 %project_kv.1 = (bf16[256,1024]{1,0:T(8,128)(2,1)}, bf16[256,1024]{1,0:T(8,128)(2,1)}, bf16[208,1024]{1,0:T(8,128)(2,1)}, bf16[80,1024]{1,0:T(8,128)(2,1)}) custom-call(s32[32]{0:T(128)} %stack.164.refs_0_, bf16[256,3072]{1,0:T(8,128)(2,1)} %copy-done.3, bf16[256,3072]{1,0:T(8,128)(2,1)} %copy-done.4, bf16[256,3072]{1,0:T(8,128)(2,1)} %collective-permute-done.11.refs_3_, ...), custom_call_target="tpu_custom_call" | custom-call | flops 1073741824 | bytes 4194304 | tf_op jit(solution)/shard_map/project_kv/pallas_call | solution.py:229
  154.8 10.0 %project_q.3 = (bf16[256,1024]{1,0:T(8,128)(2,1)}, bf16[256,2048]{1,0:T(8,128)(2,1)}) custom-call(s32[32]{0:T(128)} %stack.164.refs_0_, bf16[256,3072]{1,0:T(8,128)(2,1)} %copy-done.3, bf16[256,3072]{1,0:T(8,128)(2,1)} %copy-done.4, bf16[256,3072]{1,0:T(8,128)(2,1)} %collective-permute-done.11.refs_3_, bf16[256,3072]{1,0:T(8,128)(2,1)} %collective-permute-done.12.refs_4_, ...), custom_call_target="tpu_custom_call" | custom-call | flops 1073741824 | bytes 4194304 | tf_op jit(solution)/shard_map/project_q/pallas_call | solution.py:268
  164.9 10.0 %project_q.2 = (bf16[256,1024]{1,0:T(8,128)(2,1)}, bf16[256,2048]{1,0:T(8,128)(2,1)}) custom-call(s32[32]{0:T(128)} %stack.164.refs_0_, bf16[256,3072]{1,0:T(8,128)(2,1)} %copy-done.3, bf16[256,3072]{1,0:T(8,128)(2,1)} %copy-done.4, bf16[256,3072]{1,0:T(8,128)(2,1)} %collective-permute-done.11.refs_3_, bf16[256,3072]{1,0:T(8,128)(2,1)} %collective-permute-done.12.refs_4_, ...), custom_call_target="tpu_custom_call" | custom-call | flops 1073741824 | bytes 4194304 | tf_op jit(solution)/shard_map/project_q/pallas_call | solution.py:268
  174.9 12.8 %collective-permute-done.21 = bf16[80,1024]{1,0:T(8,128)(2,1)S(1)} collective-permute-done((bf16[80,1024]{1,0:T(8,128)(2,1)S(1)}, bf16[80,1024]{1,0:T(8,128)(2,1)S(1)}, u32[]{:S(2)}, u32[]{:S(2)}) %collective-permute-start.21) | collective-permute-done | bytes 163872 | tf_op jit(solution)/shard_map/ppermute | solution.py:988
  187.7 5.3 collective-permute-done.22
  202.2 8.1 %attend.3 = (bf16[256,1024]{1,0:T(8,128)(2,1)}, f32[256,1024]{1,0:T(8,128)}, f32[256,1024]{1,0:T(8,128)}) custom-call(bf16[256,1024]{1,0:T(8,128)(2,1)} %get-tuple-element.270.q_ref, bf16[256,2048]{1,0:T(8,128)(2,1)} %get-tuple-element.271.qf_ref, bf16[256,1024]{1,0:T(8,128)(2,1)} %get-tuple-element.257.kv_ref, bf16[256,1024]{1,0:T(8,128)(2,1)} %get-tuple-element.258.kf_ref, ...), custom_call_target="tpu_custom_call" | custom-call | flops 5000000000 | bytes 4194304 | tf_op jit(solution)/shard_map/attend/pallas_call | solution.py:400
  210.4 8.0 %attend.2 = (bf16[256,1024]{1,0:T(8,128)(2,1)}, f32[256,1024]{1,0:T(8,128)}, f32[256,1024]{1,0:T(8,128)}) custom-call(bf16[256,1024]{1,0:T(8,128)(2,1)} %get-tuple-element.255.q_ref, bf16[256,2048]{1,0:T(8,128)(2,1)} %get-tuple-element.256.qf_ref, bf16[256,1024]{1,0:T(8,128)(2,1)} %get-tuple-element.257.kv_ref, bf16[256,1024]{1,0:T(8,128)(2,1)} %get-tuple-element.258.kf_ref, ...), custom_call_target="tpu_custom_call" | custom-call | flops 5000000000 | bytes 4194304 | tf_op jit(solution)/shard_map/attend/pallas_call | solution.py:400
  218.4 6.2 %collective-permute-done.29.refs_5_ = bf16[128,2048]{1,0:T(8,128)(2,1)} collective-permute-done((bf16[128,2048]{1,0:T(8,128)(2,1)S(1)}, bf16[128,2048]{1,0:T(8,128)(2,1)}, u32[]{:S(2)}, u32[]{:S(2)}) %collective-permute-start.29) | collective-permute-done | bytes 524320 | tf_op jit(solution)/shard_map/ppermute | solution.py:988
  226.8 9.7 %out_project.1 = (f32[256,2048]{1,0:T(8,128)}, bf16[256,2048]{1,0:T(8,128)(2,1)}, bf16[256,128]{1,0:T(8,128)(2,1)}, f32[256,128]{1,0:T(8,128)}) custom-call(s32[32]{0:T(128)} %stack.164.refs_0_, bf16[256,2048]{1,0:T(8,128)(2,1)} %constant_dynamic-update-slice_fusion.4.refs_1_, bf16[256,2048]{1,0:T(8,128)(2,1)} %constant_dynamic-update-slice_fusion.6.refs_2_, ...), custom_call_target="tpu_custom_call" | custom-call | flops 2147483648 | bytes 8388608 | tf_op jit(solution)/shard_map/out_project/pallas_call | solution.py:694
  241.5 23.7 %collective-permute-done.32.refs_0_ = bf16[128,2048]{1,0:T(8,128)(2,1)S(1)} collective-permute-done((bf16[128,2048]{1,0:T(8,128)(2,1)S(1)}, bf16[128,2048]{1,0:T(8,128)(2,1)S(1)}, u32[]{:S(2)}, u32[]{:S(2)}) %collective-permute-start.32) | collective-permute-done | bytes 524320 | tf_op jit(solution)/shard_map/ppermute | solution.py:988
  267.4 21.5 %mlp.3 = (f32[512,2048]{1,0:T(8,128)}, f32[512,2048]{1,0:T(8,128)}) custom-call(s32[1]{0:T(128)} %constant.643.clone.1.place_ref, bf16[256,2048]{1,0:T(8,128)(2,1)} %get-tuple-element.296.refs_0_, bf16[256,2048]{1,0:T(8,128)(2,1)} %copy-done.20, bf16[256,2048]{1,0:T(8,128)(2,1)} %bitcast.138, bf16[256,2048]{1,0:T(8,128)(2,1)} %collective-permute-done.refs_3_, ...), custom_call_target="tpu_custom_call" | custom-call | flops 12884901888 | bytes 12582912 | tf_op jit(solution)/shard_map/mlp/pallas_call | solution.py:929
  290.2 22.3 %mlp.4 = (bf16[512,2048]{1,0:T(8,128)(2,1)}, bf16[512,2048]{1,0:T(8,128)(2,1)}) custom-call(s32[1]{0:T(128)} %bitcast.57.place_ref, bf16[256,2048]{1,0:T(8,128)(2,1)} %get-tuple-element.296.refs_0_, bf16[256,2048]{1,0:T(8,128)(2,1)} %copy-done.20, bf16[256,2048]{1,0:T(8,128)(2,1)} %bitcast.139, bf16[256,2048]{1,0:T(8,128)(2,1)} %collective-permute-done.refs_3_, ...), custom_call_target="tpu_custom_call" | custom-call | flops 12884901888 | bytes 12582912 | tf_op jit(solution)/shard_map/mlp/pallas_call | solution.py:929
  317.1 34.2 %mlp.5 = (bf16[512,2048]{1,0:T(8,128)(2,1)}, bf16[512,2048]{1,0:T(8,128)(2,1)}) custom-call(s32[1]{0:T(128)} %bitcast.57.place_ref, bf16[128,2048]{1,0:T(8,128)(2,1)} %copy-done.49, bf16[128,2048]{1,0:T(8,128)(2,1)} %copy-done.50, bf16[128,2048]{1,0:T(8,128)(2,1)} %copy-done.51, bf16[128,2048]{1,0:T(8,128)(2,1)} %copy-done.52, ...), custom_call_target="tpu_custom_call" | custom-call | flops 25769803776 | bytes 25165824 | tf_op jit(solution)/shard_map/mlp/pallas_call | solution.py:929
  353.4 12.2 %collective-permute-done.38 = bf16[128,2048]{1,0:T(8,128)(2,1)S(1)} collective-permute-done((bf16[128,2048]{1,0:T(8,128)(2,1)S(1)}, bf16[128,2048]{1,0:T(8,128)(2,1)S(1)}, u32[]{:S(2)}, u32[]{:S(2)}) %collective-permute-start.38) | collective-permute-done | bytes 524320 | tf_op jit(solution)/shard_map/ppermute | solution.py:988
  368.6 10.1 %collective-permute-done.40 = bf16[128,2048]{1,0:T(8,128)(2,1)S(1)} collective-permute-done((bf16[128,2048]{1,0:T(8,128)(2,1)S(1)}, bf16[128,2048]{1,0:T(8,128)(2,1)S(1)}, u32[]{:S(2)}, u32[]{:S(2)}) %collective-permute-start.40) | collective-permute-done | bytes 524320 | tf_op jit(solution)/shard_map/ppermute | solution.py:988
  383.5 17.2 %collective-permute-done.39 = bf16[128,2048]{1,0:T(8,128)(2,1)S(1)} collective-permute-done((bf16[128,2048]{1,0:T(8,128)(2,1)S(1)}, bf16[128,2048]{1,0:T(8,128)(2,1)S(1)}, u32[]{:S(2)}, u32[]{:S(2)}) %collective-permute-start.39) | collective-permute-done | bytes 524320 | tf_op jit(solution)/shard_map/ppermute | solution.py:988
  400.7 11.1 %collective-permute-done.41 = bf16[128,2048]{1,0:T(8,128)(2,1)S(1)} collective-permute-done((bf16[128,2048]{1,0:T(8,128)(2,1)S(1)}, bf16[128,2048]{1,0:T(8,128)(2,1)S(1)}, u32[]{:S(2)}, u32[]{:S(2)}) %collective-permute-start.41) | collective-permute-done | bytes 524320 | tf_op jit(solution)/shard_map/ppermute | solution.py:988
  412.9 10.3 %branch_back.1 = (f32[256,2048]{1,0:T(8,128)}, bf16[256,1024]{1,0:T(8,128)(2,1)}, bf16[256,1024]{1,0:T(8,128)(2,1)}, f32[1,2048]{1,0:T(1,128)}, f32[128,2048]{1,0:T(8,128)}, /*index=5*/f32[128,2048]{1,0:T(8,128)}) custom-call(s32[32]{0:T(128)} %stack.164.refs_0_, bf16[256,2048]{1,0:T(8,128)(2,1)} %constant_dynamic-update-slice_fusion.4.refs_1_, ...), custom_call_target="tpu_custom_call" | custom-call | flops 2147483648 | bytes 8388608 | tf_op jit(solution)/shard_map/branch_back/pallas_call | solution.py:751
  423.1 4.9 scaled_grads.3
  428.1 5.0 scaled_grads.2
  449.1 15.6 %attend_back.3 = (bf16[256,1024]{1,0:T(8,128)(2,1)}, f32[256,512]{1,0:T(8,128)}, f32[256,512]{1,0:T(8,128)}, bf16[128,512]{1,0:T(8,128)(2,1)}, f32[16,64,128]{2,1,0:T(8,128)}, /*index=5*/f32[4,8,128]{2,1,0:T(8,128)}) custom-call(bf16[256,1024]{1,0:T(8,128)(2,1)} %get-tuple-element.270.q_ref, bf16[256,2048]{1,0:T(8,128)(2,1)} %get-tuple-element.271.qf_ref, ...), custom_call_target="tpu_custom_call" | custom-call | flops 15000000512 | bytes 4194304 | tf_op jit(solution)/shard_map/attend_back/pallas_call | solution.py:548
  464.8 15.6 %attend_back.2 = (bf16[256,1024]{1,0:T(8,128)(2,1)}, f32[256,512]{1,0:T(8,128)}, f32[256,512]{1,0:T(8,128)}, bf16[128,512]{1,0:T(8,128)(2,1)}, f32[16,64,128]{2,1,0:T(8,128)}, /*index=5*/f32[4,8,128]{2,1,0:T(8,128)}) custom-call(bf16[256,1024]{1,0:T(8,128)(2,1)} %get-tuple-element.255.q_ref, bf16[256,2048]{1,0:T(8,128)(2,1)} %get-tuple-element.256.qf_ref, ...), custom_call_target="tpu_custom_call" | custom-call | flops 15000000512 | bytes 4194304 | tf_op jit(solution)/shard_map/attend_back/pallas_call | solution.py:548
  486.3 4.4 keys_back.3
  492.3 4.1 keys_back.2
  497.6 14.5 %inputs_back.1 = (f32[256,2048]{1,0:T(8,128)}, f32[1,2048]{1,0:T(1,128)}, f32[128,2048]{1,0:T(8,128)}, f32[128,3072]{1,0:T(8,128)}) custom-call(s32[32]{0:T(128)} %stack.164.refs_0_, bf16[256,3072]{1,0:T(8,128)(2,1)} %copy-done.3, bf16[256,3072]{1,0:T(8,128)(2,1)} %copy-done.4, bf16[256,3072]{1,0:T(8,128)(2,1)} %collective-permute-done.11.refs_3_, ...), custom_call_target="tpu_custom_call" | custom-call | flops 3221225472 | bytes 12582912 | tf_op jit(solution)/shard_map/inputs_back/pallas_call | solution.py:809
  518.8 5.1 collective-permute-done.51
  531.0 4.0 collective-permute-done.53
  535.0 6.9 %collective-permute-done.54 = bf16[8,8704]{1,0:T(8,128)(2,1)S(1)} collective-permute-done((bf16[8,8704]{1,0:T(8,128)(2,1)S(1)}, bf16[8,8704]{1,0:T(8,128)(2,1)S(1)}, u32[]{:S(2)}, u32[]{:S(2)}) %collective-permute-start.54) | collective-permute-done | bytes 139296 | tf_op jit(solution)/shard_map/ppermute | solution.py:988
  (358 shorter events, 179.0 us)
Async XLA Ops:
  7.3 283.0 %all-gather.3.cloned.1.call-start = ((), (), s32[]{:S(2)}) async-start(), calls=%async_computation | async-start | bytes 28311552 | tf_op jit(solution)/shard_map/all_gather | solution.py:1094
  8.4 39.0 %collective-permute-start.2 = (bf16[64,3072]{1,0:T(8,128)(2,1)S(1)}, bf16[64,3072]{1,0:T(8,128)(2,1)}, u32[]{:S(2)}, u32[]{:S(2)}) collective-permute-start(bf16[64,3072]{1,0:T(8,128)(2,1)S(1)} %fusion.10), channel_id=1, source_target_pairs={{0,4},{1,5},{2,6},{3,7},{4,0},{5,1},{6,2},{7,3},{8,12},{9,13},{10,... | collective-permute-start | bytes 1179656 | tf_op jit(solution)/shard_map/ppermute | solution.py:988
  12.6 34.9 %collective-permute-start.3 = (bf16[64,3072]{1,0:T(8,128)(2,1)S(1)}, bf16[64,3072]{1,0:T(8,128)(2,1)}, u32[]{:S(2)}, u32[]{:S(2)}) collective-permute-start(bf16[64,3072]{1,0:T(8,128)(2,1)S(1)} %fusion.10), channel_id=1, source_target_pairs={{0,6},{1,7},{2,0},{3,1},{4,2},{5,3},{6,4},{7,5},{8,14},{9,15},{10,... | collective-permute-start | bytes 1179656 | tf_op jit(solution)/shard_map/ppermute | solution.py:988
  13.9 32.4 %collective-permute-start.1 = (bf16[64,3072]{1,0:T(8,128)(2,1)S(1)}, bf16[64,3072]{1,0:T(8,128)(2,1)}, u32[]{:S(2)}, u32[]{:S(2)}) collective-permute-start(bf16[64,3072]{1,0:T(8,128)(2,1)S(1)} %fusion.10), channel_id=1, source_target_pairs={{0,2},{1,3},{2,4},{3,5},{4,6},{5,7},{6,0},{7,1},{8,10},{9,11},{10,... | collective-permute-start | bytes 1179656 | tf_op jit(solution)/shard_map/ppermute | solution.py:988
  15.8 32.8 %collective-permute-start = (bf16[256,2048]{1,0:T(8,128)(2,1)}, bf16[256,2048]{1,0:T(8,128)(2,1)}, u32[]{:S(2)}, u32[]{:S(2)}) collective-permute-start(bf16[256,2048]{1,0:T(8,128)(2,1)} %bitcast.136), channel_id=1, source_target_pairs={{0,1},{1,0},{2,3},{3,2},{4,5},{5,4},{6,7},{7,6},{8,9},{9,8},{10,11... | collective-permute-start | bytes 3145736 | tf_op jit(solution)/shard_map/ppermute | solution.py:988
  48.6 24.4 %collective-permute-start.10 = (bf16[64,2048]{1,0:T(8,128)(2,1)}, bf16[64,2048]{1,0:T(8,128)(2,1)S(1)}, u32[]{:S(2)}, u32[]{:S(2)}) collective-permute-start(bf16[64,2048]{1,0:T(8,128)(2,1)} %constant_dynamic-slice_fusion), channel_id=1, source_target_pairs={{0,6},{1,7},{2,0},{3,1},{4,2},{5,3},{6,4},{7,5},{8,14},{9,15},{10,... | collective-permute-start | bytes 786440 | tf_op jit(solution)/shard_map/ppermute | solution.py:988
  51.8 23.8 %collective-permute-start.9 = (bf16[64,2048]{1,0:T(8,128)(2,1)}, bf16[64,2048]{1,0:T(8,128)(2,1)S(1)}, u32[]{:S(2)}, u32[]{:S(2)}) collective-permute-start(bf16[64,2048]{1,0:T(8,128)(2,1)} %constant_dynamic-slice_fusion), channel_id=1, source_target_pairs={{0,4},{1,5},{2,6},{3,7},{4,0},{5,1},{6,2},{7,3},{8,12},{9,13},{10,... | collective-permute-start | bytes 786440 | tf_op jit(solution)/shard_map/ppermute | solution.py:988
  77.3 36.0 %collective-permute-start.12 = (bf16[256,3072]{1,0:T(8,128)(2,1)S(1)}, bf16[256,3072]{1,0:T(8,128)(2,1)}, u32[]{:S(2)}, u32[]{:S(2)}) collective-permute-start(bf16[256,3072]{1,0:T(8,128)(2,1)S(1)} %constant_dynamic-update-slice_fusion.2.refs_2_), channel_id=1, source_target_pairs={{0,1},{1,0},{2,3},{3,2},{4,5},{5,4},{6,7},{7,6},{8,9},{9,8},{10,11... | collective-permute-start | bytes 4718600 | tf_op jit(solution)/shard_map/ppermute | solution.py:988
  78.8 34.4 %collective-permute-start.14 = (bf16[256,3072]{1,0:T(8,128)(2,1)S(1)}, bf16[256,3072]{1,0:T(8,128)(2,1)}, u32[]{:S(2)}, u32[]{:S(2)}) collective-permute-start(bf16[256,3072]{1,0:T(8,128)(2,1)S(1)} %constant_dynamic-update-slice_fusion.2.refs_2_), channel_id=1, source_target_pairs={{0,8},{1,9},{2,10},{3,11},{4,12},{5,13},{6,14},{7,15},{8,0},{9,1},... | collective-permute-start | bytes 4718600 | tf_op jit(solution)/shard_map/ppermute | solution.py:988
  78.9 37.0 %collective-permute-start.11 = (bf16[256,3072]{1,0:T(8,128)(2,1)S(1)}, bf16[256,3072]{1,0:T(8,128)(2,1)}, u32[]{:S(2)}, u32[]{:S(2)}) collective-permute-start(bf16[256,3072]{1,0:T(8,128)(2,1)S(1)} %constant_dynamic-update-slice_fusion.refs_1_), channel_id=1, source_target_pairs={{0,16},{1,17},{2,18},{3,19},{4,20},{5,21},{6,22},{7,23},{8,24},{9,... | collective-permute-start | bytes 4718600 | tf_op jit(solution)/shard_map/ppermute | solution.py:988
  80.5 35.4 %collective-permute-start.13 = (bf16[256,3072]{1,0:T(8,128)(2,1)S(1)}, bf16[256,3072]{1,0:T(8,128)(2,1)}, u32[]{:S(2)}, u32[]{:S(2)}) collective-permute-start(bf16[256,3072]{1,0:T(8,128)(2,1)S(1)} %constant_dynamic-update-slice_fusion.refs_1_), channel_id=1, source_target_pairs={{0,8},{1,9},{2,10},{3,11},{4,12},{5,13},{6,14},{7,15},{8,0},{9,1},... | collective-permute-start | bytes 4718600 | tf_op jit(solution)/shard_map/ppermute | solution.py:988
  83.0 26.7 %collective-permute-start.15 = (bf16[128,2048]{1,0:T(8,128)(2,1)}, bf16[128,2048]{1,0:T(8,128)(2,1)}, u32[]{:S(2)}, u32[]{:S(2)}) collective-permute-start(bf16[128,2048]{1,0:T(8,128)(2,1)} %get-tuple-element.396), channel_id=1, source_target_pairs={{0,4},{1,5},{2,6},{3,7},{4,0},{5,1},{6,2},{7,3},{8,12},{9,13},{10,... | collective-permute-start | bytes 1572872 | tf_op jit(solution)/shard_map/ppermute | solution.py:988
  143.5 49.4 %collective-permute-start.24 = (bf16[256,2048]{1,0:T(8,128)(2,1)}, bf16[256,2048]{1,0:T(8,128)(2,1)S(1)}, u32[]{:S(2)}, u32[]{:S(2)}) collective-permute-start(bf16[256,2048]{1,0:T(8,128)(2,1)} %constant_dynamic-update-slice_fusion.6.refs_2_), channel_id=1, source_target_pairs={{0,1},{1,0},{2,3},{3,2},{4,5},{5,4},{6,7},{7,6},{8,9},{9,8},{10,11... | collective-permute-start | bytes 3145736 | tf_op jit(solution)/shard_map/ppermute | solution.py:988
  145.9 47.1 %collective-permute-start.23 = (bf16[256,2048]{1,0:T(8,128)(2,1)}, bf16[256,2048]{1,0:T(8,128)(2,1)S(1)}, u32[]{:S(2)}, u32[]{:S(2)}) collective-permute-start(bf16[256,2048]{1,0:T(8,128)(2,1)} %constant_dynamic-update-slice_fusion.4.refs_1_), channel_id=1, source_target_pairs={{0,16},{1,17},{2,18},{3,19},{4,20},{5,21},{6,22},{7,23},{8,24},{9,... | collective-permute-start | bytes 3145736 | tf_op jit(solution)/shard_map/ppermute | solution.py:988
  147.5 45.5 %collective-permute-start.20 = (bf16[208,1024]{1,0:T(8,128)(2,1)S(1)}, bf16[208,1024]{1,0:T(8,128)(2,1)S(1)}, u32[]{:S(2)}, u32[]{:S(2)}) collective-permute-start(bf16[208,1024]{1,0:T(8,128)(2,1)S(1)} %copy-done.53), channel_id=1, source_target_pairs={{0,8},{1,9},{2,10},{3,11},{4,12},{5,13},{6,14},{7,15},{8,16},{9,17... | collective-permute-start | bytes 1277960 | tf_op jit(solution)/shard_map/ppermute | solution.py:988
  150.4 37.3 %collective-permute-start.21 = (bf16[80,1024]{1,0:T(8,128)(2,1)S(1)}, bf16[80,1024]{1,0:T(8,128)(2,1)S(1)}, u32[]{:S(2)}, u32[]{:S(2)}) collective-permute-start(bf16[80,1024]{1,0:T(8,128)(2,1)S(1)} %copy-done.54), channel_id=1, source_target_pairs={{0,16},{1,17},{2,18},{3,19},{4,20},{5,21},{6,22},{7,23},{8,24},{9,... | collective-permute-start | bytes 491528 | tf_op jit(solution)/shard_map/ppermute | solution.py:988
  153.3 39.6 %collective-permute-start.22 = (bf16[80,1024]{1,0:T(8,128)(2,1)S(1)}, bf16[80,1024]{1,0:T(8,128)(2,1)S(1)}, u32[]{:S(2)}, u32[]{:S(2)}) collective-permute-start(bf16[80,1024]{1,0:T(8,128)(2,1)S(1)} %copy-done.54), channel_id=1, source_target_pairs={{0,24},{1,25},{2,26},{3,27},{4,28},{5,29},{6,30},{7,31}} | collective-permute-start | bytes 491528 | tf_op jit(solution)/shard_map/ppermute | solution.py:988
  193.7 30.9 %collective-permute-start.25 = (bf16[256,2048]{1,0:T(8,128)(2,1)}, bf16[256,2048]{1,0:T(8,128)(2,1)S(1)}, u32[]{:S(2)}, u32[]{:S(2)}) collective-permute-start(bf16[256,2048]{1,0:T(8,128)(2,1)} %constant_dynamic-update-slice_fusion.4.refs_1_), channel_id=1, source_target_pairs={{0,8},{1,9},{2,10},{3,11},{4,12},{5,13},{6,14},{7,15},{8,0},{9,1},... | collective-permute-start | bytes 3145736 | tf_op jit(solution)/shard_map/ppermute | solution.py:988
  197.3 27.3 %collective-permute-start.26 = (bf16[256,2048]{1,0:T(8,128)(2,1)}, bf16[256,2048]{1,0:T(8,128)(2,1)S(1)}, u32[]{:S(2)}, u32[]{:S(2)}) collective-permute-start(bf16[256,2048]{1,0:T(8,128)(2,1)} %constant_dynamic-update-slice_fusion.6.refs_2_), channel_id=1, source_target_pairs={{0,8},{1,9},{2,10},{3,11},{4,12},{5,13},{6,14},{7,15},{8,0},{9,1},... | collective-permute-start | bytes 3145736 | tf_op jit(solution)/shard_map/ppermute | solution.py:988
  197.3 27.4 %collective-permute-start.27 = (bf16[256,2048]{1,0:T(8,128)(2,1)S(1)}, bf16[256,2048]{1,0:T(8,128)(2,1)S(1)}, u32[]{:S(2)}, u32[]{:S(2)}) collective-permute-start(bf16[256,2048]{1,0:T(8,128)(2,1)S(1)} %collective-permute-done.23.refs_3_), channel_id=1, source_target_pairs={{0,8},{1,9},{2,10},{3,11},{4,12},{5,13},{6,14},{7,15},{8,0},{9,1},... | collective-permute-start | bytes 3145736 | tf_op jit(solution)/shard_map/ppermute | solution.py:988
  197.8 26.9 %collective-permute-start.28 = (bf16[256,2048]{1,0:T(8,128)(2,1)S(1)}, bf16[256,2048]{1,0:T(8,128)(2,1)}, u32[]{:S(2)}, u32[]{:S(2)}) collective-permute-start(bf16[256,2048]{1,0:T(8,128)(2,1)S(1)} %collective-permute-done.24.refs_4_), channel_id=1, source_target_pairs={{0,8},{1,9},{2,10},{3,11},{4,12},{5,13},{6,14},{7,15},{8,0},{9,1},... | collective-permute-start | bytes 3145736 | tf_op jit(solution)/shard_map/ppermute | solution.py:988
  197.8 26.8 %collective-permute-start.29 = (bf16[128,2048]{1,0:T(8,128)(2,1)S(1)}, bf16[128,2048]{1,0:T(8,128)(2,1)}, u32[]{:S(2)}, u32[]{:S(2)}) collective-permute-start(bf16[128,2048]{1,0:T(8,128)(2,1)S(1)} %copy-done.27), channel_id=1, source_target_pairs={{0,4},{1,5},{2,6},{3,7},{4,0},{5,1},{6,2},{7,3},{8,12},{9,13},{10,... | collective-permute-start | bytes 1572872 | tf_op jit(solution)/shard_map/ppermute | solution.py:988
  238.7 26.5 %collective-permute-start.31 = (bf16[256,2048]{1,0:T(8,128)(2,1)}, bf16[256,2048]{1,0:T(8,128)(2,1)S(1)}, u32[]{:S(2)}, u32[]{:S(2)}) collective-permute-start(bf16[256,2048]{1,0:T(8,128)(2,1)} %get-tuple-element.296.refs_0_), channel_id=1, source_target_pairs={{0,1},{1,0},{2,3},{3,2},{4,5},{5,4},{6,7},{7,6},{8,9},{9,8},{10,11... | collective-permute-start | bytes 3145736 | tf_op jit(solution)/shard_map/ppermute | solution.py:988
  265.2 24.4 %collective-permute-start.33 = (bf16[128,2048]{1,0:T(8,128)(2,1)S(1)}, bf16[128,2048]{1,0:T(8,128)(2,1)S(1)}, u32[]{:S(2)}, u32[]{:S(2)}) collective-permute-start(bf16[128,2048]{1,0:T(8,128)(2,1)S(1)} %get-tuple-element.303), channel_id=1, source_target_pairs={{0,4},{1,5},{2,6},{3,7},{4,0},{5,1},{6,2},{7,3},{8,12},{9,13},{10,... | collective-permute-start | bytes 1572872 | tf_op jit(solution)/shard_map/ppermute | solution.py:988
  265.3 24.4 %collective-permute-start.34 = (bf16[128,2048]{1,0:T(8,128)(2,1)S(1)}, bf16[128,2048]{1,0:T(8,128)(2,1)S(1)}, u32[]{:S(2)}, u32[]{:S(2)}) collective-permute-start(bf16[128,2048]{1,0:T(8,128)(2,1)S(1)} %collective-permute-done.32.refs_0_), channel_id=1, source_target_pairs={{0,1},{1,0},{2,3},{3,2},{4,5},{5,4},{6,7},{7,6},{8,9},{9,8},{10,11... | collective-permute-start | bytes 1572872 | tf_op jit(solution)/shard_map/ppermute | solution.py:988
  265.9 51.2 %collective-permute-start.36 = (bf16[128,2048]{1,0:T(8,128)(2,1)}, bf16[128,2048]{1,0:T(8,128)(2,1)}, u32[]{:S(2)}, u32[]{:S(2)}) collective-permute-start(bf16[128,2048]{1,0:T(8,128)(2,1)} %collective-permute-done.29.refs_5_), channel_id=1, source_target_pairs={{0,1},{1,0},{2,3},{3,2},{4,5},{5,4},{6,7},{7,6},{8,9},{9,8},{10,11... | collective-permute-start | bytes 1572872 | tf_op jit(solution)/shard_map/ppermute | solution.py:988
  315.5 35.7 %collective-permute-start.37 = (bf16[256,2048]{1,0:T(8,128)(2,1)S(1)}, bf16[256,2048]{1,0:T(8,128)(2,1)S(1)}, u32[]{:S(2)}, u32[]{:S(2)}) collective-permute-start(bf16[256,2048]{1,0:T(8,128)(2,1)S(1)} %get-tuple-element.391), channel_id=1, source_target_pairs={{0,1},{1,0},{2,3},{3,2},{4,5},{5,4},{6,7},{7,6},{8,9},{9,8},{10,11... | collective-permute-start | bytes 3145736 | tf_op jit(solution)/shard_map/ppermute | solution.py:988
  367.4 33.2 %collective-permute-start.39 = (bf16[128,2048]{1,0:T(8,128)(2,1)S(1)}, bf16[128,2048]{1,0:T(8,128)(2,1)S(1)}, u32[]{:S(2)}, u32[]{:S(2)}) collective-permute-start(bf16[128,2048]{1,0:T(8,128)(2,1)S(1)} %add_convert_fusion.3), channel_id=1, source_target_pairs={{0,4},{1,5},{2,6},{3,7},{4,0},{5,1},{6,2},{7,3},{8,12},{9,13},{10,... | collective-permute-start | bytes 1572872 | tf_op jit(solution)/shard_map/ppermute | solution.py:988
  378.8 33.0 %collective-permute-start.41 = (bf16[128,2048]{1,0:T(8,128)(2,1)S(1)}, bf16[128,2048]{1,0:T(8,128)(2,1)S(1)}, u32[]{:S(2)}, u32[]{:S(2)}) collective-permute-start(bf16[128,2048]{1,0:T(8,128)(2,1)S(1)} %add_convert_fusion.2), channel_id=1, source_target_pairs={{0,4},{1,5},{2,6},{3,7},{4,0},{5,1},{6,2},{7,3},{8,12},{9,13},{10,... | collective-permute-start | bytes 1572872 | tf_op jit(solution)/shard_map/ppermute | solution.py:988
  380.0 67.8 %collective-permute-start.43 = (bf16[256,2048]{1,0:T(8,128)(2,1)}, bf16[256,2048]{1,0:T(8,128)(2,1)S(1)}, u32[]{:S(2)}, u32[]{:S(2)}) collective-permute-start(bf16[256,2048]{1,0:T(8,128)(2,1)} %slice.298), channel_id=1, source_target_pairs={{0,1},{1,0},{2,3},{3,2},{4,5},{5,4},{6,7},{7,6},{8,9},{9,8},{10,11... | collective-permute-start | bytes 3145736 | tf_op jit(solution)/shard_map/ppermute | solution.py:988
  382.1 67.1 %collective-permute-start.42 = (bf16[256,2048]{1,0:T(8,128)(2,1)}, bf16[256,2048]{1,0:T(8,128)(2,1)}, u32[]{:S(2)}, u32[]{:S(2)}) collective-permute-start(bf16[256,2048]{1,0:T(8,128)(2,1)} %get-tuple-element.389), channel_id=1, source_target_pairs={{0,1},{1,0},{2,3},{3,2},{4,5},{5,4},{6,7},{7,6},{8,9},{9,8},{10,11... | collective-permute-start | bytes 3145736 | tf_op jit(solution)/shard_map/ppermute | solution.py:988
  449.1 48.4 %collective-permute-start.49 = (bf16[256,2048]{1,0:T(8,128)(2,1)}, bf16[256,2048]{1,0:T(8,128)(2,1)S(1)}, u32[]{:S(2)}, u32[]{:S(2)}) collective-permute-start(bf16[256,2048]{1,0:T(8,128)(2,1)} %add_convert_fusion.1), channel_id=1, source_target_pairs={{0,4},{1,5},{2,6},{3,7},{4,0},{5,1},{6,2},{7,3},{8,12},{9,13},{10,... | collective-permute-start | bytes 3145736 | tf_op jit(solution)/shard_map/ppermute | solution.py:988
  (84 other events, 961.9 us)
Sparse Core Ops, SparseCore 0:
  116.0 169.5 all-gather.2

commit v4 on v3

--- a/solution.py
+++ b/solution.py
@@ -1025,10 +1025,12 @@
 
 
 class Gather:
-    def __init__(self, grid, shard):
+    def __init__(self, grid, *shards):
         self.grid = grid
-        self.size = shard.shape[0] // grid.seq
-        self.own = lax.dynamic_slice_in_dim(shard, grid.s * self.size, self.size, 0)
+        self.size = shards[0].shape[0] // grid.seq
+        at = grid.s * self.size
+        own = [lax.dynamic_slice_in_dim(v, at, self.size, 0) for v in shards]
+        self.own = jnp.concatenate(own, axis=1) if len(own) > 1 else own[0]
 
     def over_z(self):
         grid = self.grid
@@ -1224,7 +1226,7 @@
     gain_second = norm_second.astype(F32)[None, :]
 
     masks, former, latter, heard = documents(grid, doc_starts[0], length)
-    qkv = Gather(grid, jnp.concatenate([w_query, w_key, w_value], axis=1))
+    qkv = Gather(grid, w_query, w_key, w_value)
     out = Gather(grid, w_out)
     cot_near = spread_near(grid, grad_out)
     qkv.over_z()
@@ -1273,19 +1275,14 @@
     kv, kf, pack, full = project_kv(
         w_qkv, inputs, low, qkv_out[:, D:], cosine, sine, maps_k, masks["survive"]
     )
-    kv, kf, pack, full, out.moved = after((kv, kf, pack, full, out.moved))
+    kv, kf, pack, full, out.moved, late = after((kv, kf, pack, full, out.moved, late))
+    cot_far += spread_far(grid, late, 1)
     rim = grid.along_seq(pack, 1)
     fulls = [grid.along_seq(full, k) for k in range(2, grid.seq)]
+    queries = [project_q(0, w_qkv, inputs, low, qkv_out, cosine, sine, maps_q)]
+    rim, fulls, out.moved, queries = after((rim, fulls, out.moved, queries))
     out.second()
-    queries = [
-        project_q(i, w_qkv, inputs, low, qkv_out, cosine, sine, maps_q) for i in range(HALVES)
-    ]
-    rim, fulls, queries, out.blocks, out.last, late = after(
-        (rim, fulls, queries, out.blocks, out.last, late)
-    )
-    out.cores()
-    w_o = out.result()
-    cot_far += spread_far(grid, late, 1)
+    queries.append(project_q(1, w_qkv, inputs, low, qkv_out, cosine, sine, maps_q))
     carry = former[0] * rim[2 * WINDOW :].astype(F32)
     for w, full in zip(former[1:], fulls):
         carry = carry + w * full.astype(F32)
@@ -1296,7 +1293,13 @@
         merged.append(block[0])
         attended.append(block[1])
         inverse.append(block[2])
-    merged, w_o.blocks, cot_far = after((merged, w_o.blocks, cot_far))
+        if i == 0:
+            out.blocks, out.last, merged, queries, cot_far = after(
+                (out.blocks, out.last, merged, queries, cot_far)
+            )
+            out.cores()
+            w_o = out.result()
+    merged, w_o.blocks, cot_far[0] = after((merged, w_o.blocks, cot_far[0]))
     moved = relay(grid, cot_far[:1])[1:]
     residual, second_in, out_low, inverse_second = out_project(
         w_o, merged, hidden, o_in, o_out, gain_second
@@ -1331,20 +1334,22 @@
         for i in range(HALVES)
     ]
     back = jnp.concatenate([v[2] for v in scaled], axis=1)
-    far_back = jnp.zeros(back.shape, F32)
-    for k in range(2, grid.seq):
-        far_back = far_back + latter[k - 1] * grid.along_seq(back, -k).astype(F32)
-    near_back = far_back + latter[0] * grid.along_seq(back, -1).astype(F32)
-    near_back, far_back = near_back.astype(BF16), far_back.astype(BF16)
     out_terms = collect_near(grid, near_out, length)
     send = collect_far(grid, far_out, length, 1)
-    scaled, out_terms, send = after((scaled, out_terms, send))
+    back, scaled, out_terms, send = after((back, scaled, out_terms, send))
     out_terms += [grid.flip_z(v, NEAR_BIT) for v in send]
+    returned = [grid.along_seq(back, -k) for k in range(1, grid.seq)]
     backs = []
     for i in range(HALVES):
         backs.append(
             attend_back(i, *queries[i], kv, kf, rim, carry, *scaled[i][:2], masks, maps_q)
         )
+        scaled, returned, backs = after((scaled, returned, backs))
+    far_back = jnp.zeros(back.shape, F32)
+    for w, v in zip(latter[1:], returned[1:]):
+        far_back = far_back + w * v.astype(F32)
+    near_back = far_back + latter[0] * returned[0].astype(F32)
+    near_back, far_back = near_back.astype(BF16), far_back.astype(BF16)
     raw_query = [v[0] for v in backs]
     rim_back = [grid.along_seq(v[3], -1) for v in backs]
     raw_key, raw_value, dmap_key = [], [], []

time: 565 us -> 558 us (0.988)
  waiting for transfers between devices: 164 us -> 146 us
  starting transfers between devices: 71.2 us -> 78.6 us
    ppermute x57, waiting for transfers between devices: 163 us -> 142 us  [send(): lax.ppermute(v, ('seq', 'rows'), route)]
    ppermute x57, starting transfers between devices: 71.1 us -> 78.5 us  [send(): lax.ppermute(v, ('seq', 'rows'), route)]
  transfers between devices with their start and end apart: 58 -> 58, of which waited for: 25 -> 21; matrix products, arithmetic and copies ran while one was open for 14% -> 14% of each run, Pallas kernels for 34% -> 35%
where the time goes in v4:
time: 558 us; the launch traced here: 552 us
  Pallas kernels  208 us (37%)
  waiting for transfers between devices  146 us (26%)
  starting transfers between devices  78.6 us (14%)
  local copies, waits for them, and re-layouts  51.8 us (9%)
  other arithmetic  47 us (8%)
  between operations  19.5 us (3%)
    ppermute x57, waiting for transfers between devices, send(): lax.ppermute(v, ('seq', 'rows'), route)  142 us
    ppermute x57, starting transfers between devices, send(): lax.ppermute(v, ('seq', 'rows'), route)  78.5 us
    pallas_call x3, Pallas kernels, mlp(): pl.pallas_call(functools.partial(mlp_kernel, rows=rows, paired=pair is no...  78 us
    pallas_call x2, Pallas kernels, attend_back(): pl.pallas_call(attend_back_kernel, grid=(PER_HALF,), in_specs=[s['q'], s[...  31.4 us
    pallas_call x2, Pallas kernels, project_q(): pl.pallas_call(functools.partial(project_q_kernel, counts=w.shapes(), siz...  20 us
    pallas_call x2, Pallas kernels, attend(): pl.pallas_call(attend_kernel, grid=(PER_HALF,), in_specs=[s['q'], s['qf']...  16.1 us
    pallas_call x1, Pallas kernels, inputs_back(): pl.pallas_call(functools.partial(inputs_back_kernel, counts=w.shapes(), s...  14.5 us
  transfers between devices with their start and end apart: 58, of which 21 were waited for; matrix products, arithmetic and copies ran while one was open for 14% of the time, Pallas kernels for 35%

profile of v4, /device:TPU:0, one launch (start us, length us, event | category | flops | bytes accessed | tf_op | source)
XLA Modules:
  0.0 551.6 jit_solution(14416026060996321020)
XLA Ops:
  10.1 4.0 collective-permute-start.2
  59.2 13.6 %collective-permute-done.8 = bf16[64,2048]{1,0:T(8,128)(2,1)S(1)} collective-permute-done((bf16[64,2048]{1,0:T(8,128)(2,1)S(1)}, bf16[64,2048]{1,0:T(8,128)(2,1)S(1)}, u32[]{:S(2)}, u32[]{:S(2)}) %collective-permute-start.8) | collective-permute-done | bytes 262176 | tf_op jit(solution)/shard_map/ppermute | solution.py:988
  90.2 9.2 %maximum_maximum_fusion = bf16[1536,1024]{1,0:T(8,128)(2,1)} fusion(bf16[512,512]{1,0:T(8,128)(2,1)S(1)} %get-tuple-element.454, bf16[512,512]{1,0:T(8,128)(2,1)S(1)} %get-tuple-element.453, bf16[512,1024]{1,0:T(8,128)(2,1)S(1)} %get-tuple-element.452, bf16[512,1024]{1,0:T(8,128)(2,1)S(1)} %get-tuple-element.451), kind=kLoop, calls=%fused_computation | loop fusion | flops 12582912 | bytes 6291456 | tf_op jit(solution)/shard_map/concatenate | solution.py:1087
  99.4 11.8 %collective-permute-done.15.refs_4_ = bf16[128,2048]{1,0:T(8,128)(2,1)} collective-permute-done((bf16[128,2048]{1,0:T(8,128)(2,1)}, bf16[128,2048]{1,0:T(8,128)(2,1)}, u32[]{:S(2)}, u32[]{:S(2)}) %collective-permute-start.15) | collective-permute-done | bytes 524320 | tf_op jit(solution)/shard_map/ppermute | solution.py:988
  128.2 9.1 %project_kv.1 = (bf16[256,1024]{1,0:T(8,128)(2,1)}, bf16[256,1024]{1,0:T(8,128)(2,1)}, bf16[208,1024]{1,0:T(8,128)(2,1)}, bf16[80,1024]{1,0:T(8,128)(2,1)}) custom-call(s32[32]{0:T(128)} %stack.164.refs_0_, bf16[256,3072]{1,0:T(8,128)(2,1)} %copy-done.3, bf16[256,3072]{1,0:T(8,128)(2,1)} %copy-done.4, bf16[256,3072]{1,0:T(8,128)(2,1)} %collective-permute-done.11.refs_3_, ...), custom_call_target="tpu_custom_call" | custom-call | flops 1073741824 | bytes 4194304 | tf_op jit(solution)/shard_map/project_kv/pallas_call | solution.py:229
  143.7 10.0 %project_q.2 = (bf16[256,1024]{1,0:T(8,128)(2,1)}, bf16[256,2048]{1,0:T(8,128)(2,1)}) custom-call(s32[32]{0:T(128)} %stack.164.refs_0_, bf16[256,3072]{1,0:T(8,128)(2,1)} %copy-done.3, bf16[256,3072]{1,0:T(8,128)(2,1)} %copy-done.4, bf16[256,3072]{1,0:T(8,128)(2,1)} %collective-permute-done.11.refs_3_, bf16[256,3072]{1,0:T(8,128)(2,1)} %collective-permute-done.12.refs_4_, ...), custom_call_target="tpu_custom_call" | custom-call | flops 1073741824 | bytes 4194304 | tf_op jit(solution)/shard_map/project_q/pallas_call | solution.py:268
  164.7 10.0 %project_q.3 = (bf16[256,1024]{1,0:T(8,128)(2,1)}, bf16[256,2048]{1,0:T(8,128)(2,1)}) custom-call(s32[32]{0:T(128)} %stack.164.refs_0_, bf16[256,3072]{1,0:T(8,128)(2,1)} %copy-done.3, bf16[256,3072]{1,0:T(8,128)(2,1)} %copy-done.4, bf16[256,3072]{1,0:T(8,128)(2,1)} %collective-permute-done.11.refs_3_, bf16[256,3072]{1,0:T(8,128)(2,1)} %collective-permute-done.12.refs_4_, ...), custom_call_target="tpu_custom_call" | custom-call | flops 1073741824 | bytes 4194304 | tf_op jit(solution)/shard_map/project_q/pallas_call | solution.py:268
  176.4 8.0 %attend.2 = (bf16[256,1024]{1,0:T(8,128)(2,1)}, f32[256,1024]{1,0:T(8,128)}, f32[256,1024]{1,0:T(8,128)}) custom-call(bf16[256,1024]{1,0:T(8,128)(2,1)} %get-tuple-element.386.q_ref, bf16[256,2048]{1,0:T(8,128)(2,1)} %get-tuple-element.367.qf_ref, bf16[256,1024]{1,0:T(8,128)(2,1)} %get-tuple-element.290.kv_ref, bf16[256,1024]{1,0:T(8,128)(2,1)} %get-tuple-element.291.kf_ref, ...), custom_call_target="tpu_custom_call" | custom-call | flops 5000000000 | bytes 4194304 | tf_op jit(solution)/shard_map/attend/pallas_call | solution.py:400
  187.5 6.5 %collective-permute-done.23.refs_3_ = bf16[256,2048]{1,0:T(8,128)(2,1)} collective-permute-done((bf16[256,2048]{1,0:T(8,128)(2,1)S(1)}, bf16[256,2048]{1,0:T(8,128)(2,1)}, u32[]{:S(2)}, u32[]{:S(2)}) %collective-permute-start.23) | collective-permute-done | bytes 1048608 | tf_op jit(solution)/shard_map/ppermute | solution.py:988
  197.7 8.1 %attend.3 = (bf16[256,1024]{1,0:T(8,128)(2,1)}, f32[256,1024]{1,0:T(8,128)}, f32[256,1024]{1,0:T(8,128)}) custom-call(bf16[256,1024]{1,0:T(8,128)(2,1)} %get-tuple-element.308.q_ref, bf16[256,2048]{1,0:T(8,128)(2,1)} %get-tuple-element.309.qf_ref, bf16[256,1024]{1,0:T(8,128)(2,1)} %get-tuple-element.290.kv_ref, bf16[256,1024]{1,0:T(8,128)(2,1)} %get-tuple-element.291.kf_ref, ...), custom_call_target="tpu_custom_call" | custom-call | flops 5000000000 | bytes 4194304 | tf_op jit(solution)/shard_map/attend/pallas_call | solution.py:400
  207.5 9.8 %out_project.1 = (f32[256,2048]{1,0:T(8,128)}, bf16[256,2048]{1,0:T(8,128)(2,1)}, bf16[256,128]{1,0:T(8,128)(2,1)}, f32[256,128]{1,0:T(8,128)}) custom-call(s32[32]{0:T(128)} %stack.164.refs_0_, bf16[256,2048]{1,0:T(8,128)(2,1)} %copy-done.10, bf16[256,2048]{1,0:T(8,128)(2,1)} %copy-done.9, bf16[256,2048]{1,0:T(8,128)(2,1)} %collective-permute-done.23.refs_3_, ...), custom_call_target="tpu_custom_call" | custom-call | flops 2147483648 | bytes 8388608 | tf_op jit(solution)/shard_map/out_project/pallas_call | solution.py:694
  226.5 22.8 %collective-permute-done.32.refs_0_ = bf16[128,2048]{1,0:T(8,128)(2,1)S(1)} collective-permute-done((bf16[128,2048]{1,0:T(8,128)(2,1)S(1)}, bf16[128,2048]{1,0:T(8,128)(2,1)S(1)}, u32[]{:S(2)}, u32[]{:S(2)}) %collective-permute-start.32) | collective-permute-done | bytes 524320 | tf_op jit(solution)/shard_map/ppermute | solution.py:988
  251.6 21.5 %mlp.3 = (f32[512,2048]{1,0:T(8,128)}, f32[512,2048]{1,0:T(8,128)}) custom-call(s32[1]{0:T(128)} %constant.643.clone.1.place_ref, bf16[256,2048]{1,0:T(8,128)(2,1)} %get-tuple-element.333.refs_0_, bf16[256,2048]{1,0:T(8,128)(2,1)} %copy-done.21, bf16[256,2048]{1,0:T(8,128)(2,1)} %bitcast.138, bf16[256,2048]{1,0:T(8,128)(2,1)} %collective-permute-done.refs_3_, ...), custom_call_target="tpu_custom_call" | custom-call | flops 12884901888 | bytes 12582912 | tf_op jit(solution)/shard_map/mlp/pallas_call | solution.py:929
  274.7 3.9 all-gather.3.cloned.1.call-done
  278.6 22.3 %mlp.4 = (bf16[512,2048]{1,0:T(8,128)(2,1)}, bf16[512,2048]{1,0:T(8,128)(2,1)}) custom-call(s32[1]{0:T(128)} %bitcast.57.place_ref, bf16[256,2048]{1,0:T(8,128)(2,1)} %get-tuple-element.333.refs_0_, bf16[256,2048]{1,0:T(8,128)(2,1)} %copy-done.21, bf16[256,2048]{1,0:T(8,128)(2,1)} %bitcast.139, bf16[256,2048]{1,0:T(8,128)(2,1)} %collective-permute-done.refs_3_, ...), custom_call_target="tpu_custom_call" | custom-call | flops 12884901888 | bytes 12582912 | tf_op jit(solution)/shard_map/mlp/pallas_call | solution.py:929
  305.4 34.2 %mlp.5 = (bf16[512,2048]{1,0:T(8,128)(2,1)}, bf16[512,2048]{1,0:T(8,128)(2,1)}) custom-call(s32[1]{0:T(128)} %bitcast.57.place_ref, bf16[128,2048]{1,0:T(8,128)(2,1)} %copy-done.52, bf16[128,2048]{1,0:T(8,128)(2,1)} %copy-done.53, bf16[128,2048]{1,0:T(8,128)(2,1)} %copy-done.54, bf16[128,2048]{1,0:T(8,128)(2,1)} %copy-done.55, ...), custom_call_target="tpu_custom_call" | custom-call | flops 25769803776 | bytes 25165824 | tf_op jit(solution)/shard_map/mlp/pallas_call | solution.py:929
  341.7 12.0 %collective-permute-done.38 = bf16[128,2048]{1,0:T(8,128)(2,1)S(1)} collective-permute-done((bf16[128,2048]{1,0:T(8,128)(2,1)S(1)}, bf16[128,2048]{1,0:T(8,128)(2,1)S(1)}, u32[]{:S(2)}, u32[]{:S(2)}) %collective-permute-start.38) | collective-permute-done | bytes 524320 | tf_op jit(solution)/shard_map/ppermute | solution.py:988
  359.8 11.7 %collective-permute-done.40 = bf16[128,2048]{1,0:T(8,128)(2,1)} collective-permute-done((bf16[128,2048]{1,0:T(8,128)(2,1)}, bf16[128,2048]{1,0:T(8,128)(2,1)}, u32[]{:S(2)}, u32[]{:S(2)}) %collective-permute-start.40) | collective-permute-done | bytes 524320 | tf_op jit(solution)/shard_map/ppermute | solution.py:988
  378.7 16.8 %collective-permute-done.39 = bf16[128,2048]{1,0:T(8,128)(2,1)S(1)} collective-permute-done((bf16[128,2048]{1,0:T(8,128)(2,1)}, bf16[128,2048]{1,0:T(8,128)(2,1)S(1)}, u32[]{:S(2)}, u32[]{:S(2)}) %collective-permute-start.39) | collective-permute-done | bytes 524320 | tf_op jit(solution)/shard_map/ppermute | solution.py:988
  395.5 11.2 %collective-permute-done.41 = bf16[128,2048]{1,0:T(8,128)(2,1)S(1)} collective-permute-done((bf16[128,2048]{1,0:T(8,128)(2,1)S(1)}, bf16[128,2048]{1,0:T(8,128)(2,1)S(1)}, u32[]{:S(2)}, u32[]{:S(2)}) %collective-permute-start.41) | collective-permute-done | bytes 524320 | tf_op jit(solution)/shard_map/ppermute | solution.py:988
  407.9 10.3 %branch_back.1 = (f32[256,2048]{1,0:T(8,128)}, bf16[256,1024]{1,0:T(8,128)(2,1)}, bf16[256,1024]{1,0:T(8,128)(2,1)}, f32[1,2048]{1,0:T(1,128)}, f32[128,2048]{1,0:T(8,128)}, /*index=5*/f32[128,2048]{1,0:T(8,128)}) custom-call(s32[32]{0:T(128)} %stack.164.refs_0_, bf16[256,2048]{1,0:T(8,128)(2,1)} %copy-done.10, bf16[256,2048]{1,0:T(8,128)(2,1)} %copy-done.9, ...), custom_call_target="tpu_custom_call" | custom-call | flops 2147483648 | bytes 8388608 | tf_op jit(solution)/shard_map/branch_back/pallas_call | solution.py:751
  420.7 4.9 scaled_grads.3
  425.6 5.0 scaled_grads.2
  437.1 15.6 %attend_back.2 = (bf16[256,1024]{1,0:T(8,128)(2,1)}, f32[256,512]{1,0:T(8,128)}, f32[256,512]{1,0:T(8,128)}, bf16[128,512]{1,0:T(8,128)(2,1)}, f32[16,64,128]{2,1,0:T(8,128)}, /*index=5*/f32[4,8,128]{2,1,0:T(8,128)}) custom-call(bf16[256,1024]{1,0:T(8,128)(2,1)} %get-tuple-element.386.q_ref, bf16[256,2048]{1,0:T(8,128)(2,1)} %get-tuple-element.367.qf_ref, ...), custom_call_target="tpu_custom_call" | custom-call | flops 15000000512 | bytes 4194304 | tf_op jit(solution)/shard_map/attend_back/pallas_call | solution.py:548
  452.8 15.8 %attend_back.3 = (bf16[256,1024]{1,0:T(8,128)(2,1)}, f32[256,512]{1,0:T(8,128)}, f32[256,512]{1,0:T(8,128)}, bf16[128,512]{1,0:T(8,128)(2,1)}, f32[16,64,128]{2,1,0:T(8,128)}, /*index=5*/f32[4,8,128]{2,1,0:T(8,128)}) custom-call(bf16[256,1024]{1,0:T(8,128)(2,1)} %get-tuple-element.308.q_ref, bf16[256,2048]{1,0:T(8,128)(2,1)} %get-tuple-element.309.qf_ref, ...), custom_call_target="tpu_custom_call" | custom-call | flops 15000000512 | bytes 4194304 | tf_op jit(solution)/shard_map/attend_back/pallas_call | solution.py:548
  476.5 4.4 keys_back.3
  482.5 4.1 keys_back.2
  487.7 14.5 %inputs_back.1 = (f32[256,2048]{1,0:T(8,128)}, f32[1,2048]{1,0:T(1,128)}, f32[128,2048]{1,0:T(8,128)}, f32[128,3072]{1,0:T(8,128)}) custom-call(s32[32]{0:T(128)} %stack.164.refs_0_, bf16[256,3072]{1,0:T(8,128)(2,1)} %copy-done.3, bf16[256,3072]{1,0:T(8,128)(2,1)} %copy-done.4, bf16[256,3072]{1,0:T(8,128)(2,1)} %collective-permute-done.11.refs_3_, ...), custom_call_target="tpu_custom_call" | custom-call | flops 3221225472 | bytes 12582912 | tf_op jit(solution)/shard_map/inputs_back/pallas_call | solution.py:809
  504.4 5.5 collective-permute-start.50
  512.7 4.5 collective-permute-done.51
  524.6 4.5 collective-permute-done.53
  529.1 5.4 collective-permute-done.55
  (359 shorter events, 181.0 us)
Async XLA Ops:
  7.3 271.4 %all-gather.3.cloned.1.call-start = ((), (), s32[]{:S(2)}) async-start(), calls=%async_computation | async-start | bytes 28311552 | tf_op jit(solution)/shard_map/all_gather | solution.py:1096
  10.1 39.9 %collective-permute-start.2 = (bf16[64,3072]{1,0:T(8,128)(2,1)}, bf16[64,3072]{1,0:T(8,128)(2,1)}, u32[]{:S(2)}, u32[]{:S(2)}) collective-permute-start(bf16[64,3072]{1,0:T(8,128)(2,1)} %pad_maximum_fusion.7), channel_id=1, source_target_pairs={{0,4},{1,5},{2,6},{3,7},{4,0},{5,1},{6,2},{7,3},{8,12},{9,13},{10,... | collective-permute-start | bytes 1179656 | tf_op jit(solution)/shard_map/ppermute | solution.py:988
  14.1 35.8 %collective-permute-start.3 = (bf16[64,3072]{1,0:T(8,128)(2,1)}, bf16[64,3072]{1,0:T(8,128)(2,1)}, u32[]{:S(2)}, u32[]{:S(2)}) collective-permute-start(bf16[64,3072]{1,0:T(8,128)(2,1)} %pad_maximum_fusion.7), channel_id=1, source_target_pairs={{0,6},{1,7},{2,0},{3,1},{4,2},{5,3},{6,4},{7,5},{8,14},{9,15},{10,... | collective-permute-start | bytes 1179656 | tf_op jit(solution)/shard_map/ppermute | solution.py:988
  15.5 33.4 %collective-permute-start.1 = (bf16[64,3072]{1,0:T(8,128)(2,1)}, bf16[64,3072]{1,0:T(8,128)(2,1)}, u32[]{:S(2)}, u32[]{:S(2)}) collective-permute-start(bf16[64,3072]{1,0:T(8,128)(2,1)} %pad_maximum_fusion.7), channel_id=1, source_target_pairs={{0,2},{1,3},{2,4},{3,5},{4,6},{5,7},{6,0},{7,1},{8,10},{9,11},{10,... | collective-permute-start | bytes 1179656 | tf_op jit(solution)/shard_map/ppermute | solution.py:988
  17.4 33.8 %collective-permute-start = (bf16[256,2048]{1,0:T(8,128)(2,1)}, bf16[256,2048]{1,0:T(8,128)(2,1)}, u32[]{:S(2)}, u32[]{:S(2)}) collective-permute-start(bf16[256,2048]{1,0:T(8,128)(2,1)} %bitcast.136), channel_id=1, source_target_pairs={{0,1},{1,0},{2,3},{3,2},{4,5},{5,4},{6,7},{7,6},{8,9},{9,8},{10,11... | collective-permute-start | bytes 3145736 | tf_op jit(solution)/shard_map/ppermute | solution.py:988
  51.2 22.5 %collective-permute-start.10 = (bf16[64,2048]{1,0:T(8,128)(2,1)S(1)}, bf16[64,2048]{1,0:T(8,128)(2,1)S(1)}, u32[]{:S(2)}, u32[]{:S(2)}) collective-permute-start(bf16[64,2048]{1,0:T(8,128)(2,1)S(1)} %copy-done.23), channel_id=1, source_target_pairs={{0,6},{1,7},{2,0},{3,1},{4,2},{5,3},{6,4},{7,5},{8,14},{9,15},{10,... | collective-permute-start | bytes 786440 | tf_op jit(solution)/shard_map/ppermute | solution.py:988
  54.4 22.8 %collective-permute-start.9 = (bf16[64,2048]{1,0:T(8,128)(2,1)S(1)}, bf16[64,2048]{1,0:T(8,128)(2,1)S(1)}, u32[]{:S(2)}, u32[]{:S(2)}) collective-permute-start(bf16[64,2048]{1,0:T(8,128)(2,1)S(1)} %copy-done.23), channel_id=1, source_target_pairs={{0,4},{1,5},{2,6},{3,7},{4,0},{5,1},{6,2},{7,3},{8,12},{9,13},{10,... | collective-permute-start | bytes 786440 | tf_op jit(solution)/shard_map/ppermute | solution.py:988
  56.0 22.0 %collective-permute-start.7 = (bf16[128,3072]{1,0:T(8,128)(2,1)S(1)}, bf16[128,3072]{1,0:T(8,128)(2,1)S(1)}, u32[]{:S(2)}, u32[]{:S(2)}) collective-permute-start(bf16[128,3072]{1,0:T(8,128)(2,1)S(1)} %pad_maximum_fusion.2), channel_id=1, source_target_pairs={{0,16},{1,17},{2,18},{3,19},{4,20},{5,21},{6,22},{7,23},{8,24},{9,... | collective-permute-start | bytes 2359304 | tf_op jit(solution)/shard_map/ppermute | solution.py:988
  57.6 20.4 %collective-permute-start.6 = (bf16[128,3072]{1,0:T(8,128)(2,1)S(1)}, bf16[128,3072]{1,0:T(8,128)(2,1)S(1)}, u32[]{:S(2)}, u32[]{:S(2)}) collective-permute-start(bf16[128,3072]{1,0:T(8,128)(2,1)S(1)} %pad_maximum_fusion.1), channel_id=1, source_target_pairs={{0,1},{1,0},{2,3},{3,2},{4,5},{5,4},{6,7},{7,6},{8,9},{9,8},{10,11... | collective-permute-start | bytes 2359304 | tf_op jit(solution)/shard_map/ppermute | solution.py:988
  78.9 35.7 %collective-permute-start.12 = (bf16[256,3072]{1,0:T(8,128)(2,1)S(1)}, bf16[256,3072]{1,0:T(8,128)(2,1)}, u32[]{:S(2)}, u32[]{:S(2)}) collective-permute-start(bf16[256,3072]{1,0:T(8,128)(2,1)S(1)} %constant_dynamic-update-slice_fusion.2.refs_2_), channel_id=1, source_target_pairs={{0,1},{1,0},{2,3},{3,2},{4,5},{5,4},{6,7},{7,6},{8,9},{9,8},{10,11... | collective-permute-start | bytes 4718600 | tf_op jit(solution)/shard_map/ppermute | solution.py:988
  80.4 34.2 %collective-permute-start.14 = (bf16[256,3072]{1,0:T(8,128)(2,1)S(1)}, bf16[256,3072]{1,0:T(8,128)(2,1)}, u32[]{:S(2)}, u32[]{:S(2)}) collective-permute-start(bf16[256,3072]{1,0:T(8,128)(2,1)S(1)} %constant_dynamic-update-slice_fusion.2.refs_2_), channel_id=1, source_target_pairs={{0,8},{1,9},{2,10},{3,11},{4,12},{5,13},{6,14},{7,15},{8,0},{9,1},... | collective-permute-start | bytes 4718600 | tf_op jit(solution)/shard_map/ppermute | solution.py:988
  80.5 37.0 %collective-permute-start.11 = (bf16[256,3072]{1,0:T(8,128)(2,1)S(1)}, bf16[256,3072]{1,0:T(8,128)(2,1)}, u32[]{:S(2)}, u32[]{:S(2)}) collective-permute-start(bf16[256,3072]{1,0:T(8,128)(2,1)S(1)} %constant_dynamic-update-slice_fusion.refs_1_), channel_id=1, source_target_pairs={{0,16},{1,17},{2,18},{3,19},{4,20},{5,21},{6,22},{7,23},{8,24},{9,... | collective-permute-start | bytes 4718600 | tf_op jit(solution)/shard_map/ppermute | solution.py:988
  82.1 35.4 %collective-permute-start.13 = (bf16[256,3072]{1,0:T(8,128)(2,1)S(1)}, bf16[256,3072]{1,0:T(8,128)(2,1)}, u32[]{:S(2)}, u32[]{:S(2)}) collective-permute-start(bf16[256,3072]{1,0:T(8,128)(2,1)S(1)} %constant_dynamic-update-slice_fusion.refs_1_), channel_id=1, source_target_pairs={{0,8},{1,9},{2,10},{3,11},{4,12},{5,13},{6,14},{7,15},{8,0},{9,1},... | collective-permute-start | bytes 4718600 | tf_op jit(solution)/shard_map/ppermute | solution.py:988
  84.6 26.6 %collective-permute-start.15 = (bf16[128,2048]{1,0:T(8,128)(2,1)}, bf16[128,2048]{1,0:T(8,128)(2,1)}, u32[]{:S(2)}, u32[]{:S(2)}) collective-permute-start(bf16[128,2048]{1,0:T(8,128)(2,1)} %get-tuple-element.462), channel_id=1, source_target_pairs={{0,4},{1,5},{2,6},{3,7},{4,0},{5,1},{6,2},{7,3},{8,12},{9,13},{10,... | collective-permute-start | bytes 1572872 | tf_op jit(solution)/shard_map/ppermute | solution.py:988
  118.1 19.2 %collective-permute-start.18 = (bf16[128,2048]{1,0:T(8,128)(2,1)}, bf16[128,2048]{1,0:T(8,128)(2,1)}, u32[]{:S(2)}, u32[]{:S(2)}) collective-permute-start(bf16[128,2048]{1,0:T(8,128)(2,1)} %pad_maximum_fusion.4), channel_id=1, source_target_pairs={{0,1},{1,0},{2,3},{3,2},{4,5},{5,4},{6,7},{7,6},{8,9},{9,8},{10,11... | collective-permute-start | bytes 1572872 | tf_op jit(solution)/shard_map/ppermute | solution.py:988
  118.6 18.7 %collective-permute-start.19 = (bf16[128,2048]{1,0:T(8,128)(2,1)}, bf16[128,2048]{1,0:T(8,128)(2,1)}, u32[]{:S(2)}, u32[]{:S(2)}) collective-permute-start(bf16[128,2048]{1,0:T(8,128)(2,1)} %pad_maximum_fusion.5), channel_id=1, source_target_pairs={{0,16},{1,17},{2,18},{3,19},{4,20},{5,21},{6,22},{7,23},{8,24},{9,... | collective-permute-start | bytes 1572872 | tf_op jit(solution)/shard_map/ppermute | solution.py:988
  155.9 31.6 %collective-permute-start.24 = (bf16[256,2048]{1,0:T(8,128)(2,1)S(1)}, bf16[256,2048]{1,0:T(8,128)(2,1)S(1)}, u32[]{:S(2)}, u32[]{:S(2)}) collective-permute-start(bf16[256,2048]{1,0:T(8,128)(2,1)S(1)} %constant_dynamic-update-slice_fusion.6.refs_2_), channel_id=1, source_target_pairs={{0,1},{1,0},{2,3},{3,2},{4,5},{5,4},{6,7},{7,6},{8,9},{9,8},{10,11... | collective-permute-start | bytes 3145736 | tf_op jit(solution)/shard_map/ppermute | solution.py:988
  158.4 35.6 %collective-permute-start.23 = (bf16[256,2048]{1,0:T(8,128)(2,1)S(1)}, bf16[256,2048]{1,0:T(8,128)(2,1)}, u32[]{:S(2)}, u32[]{:S(2)}) collective-permute-start(bf16[256,2048]{1,0:T(8,128)(2,1)S(1)} %constant_dynamic-update-slice_fusion.4.refs_1_), channel_id=1, source_target_pairs={{0,16},{1,17},{2,18},{3,19},{4,20},{5,21},{6,22},{7,23},{8,24},{9,... | collective-permute-start | bytes 3145736 | tf_op jit(solution)/shard_map/ppermute | solution.py:988
  161.8 25.7 %collective-permute-start.25 = (bf16[128,2048]{1,0:T(8,128)(2,1)}, bf16[128,2048]{1,0:T(8,128)(2,1)}, u32[]{:S(2)}, u32[]{:S(2)}) collective-permute-start(bf16[128,2048]{1,0:T(8,128)(2,1)} %get-tuple-element.306), channel_id=1, source_target_pairs={{0,4},{1,5},{2,6},{3,7},{4,0},{5,1},{6,2},{7,3},{8,12},{9,13},{10,... | collective-permute-start | bytes 1572872 | tf_op jit(solution)/shard_map/ppermute | solution.py:988
  220.4 29.0 %collective-permute-start.31 = (bf16[256,2048]{1,0:T(8,128)(2,1)}, bf16[256,2048]{1,0:T(8,128)(2,1)S(1)}, u32[]{:S(2)}, u32[]{:S(2)}) collective-permute-start(bf16[256,2048]{1,0:T(8,128)(2,1)} %get-tuple-element.333.refs_0_), channel_id=1, source_target_pairs={{0,1},{1,0},{2,3},{3,2},{4,5},{5,4},{6,7},{7,6},{8,9},{9,8},{10,11... | collective-permute-start | bytes 3145736 | tf_op jit(solution)/shard_map/ppermute | solution.py:988
  222.7 26.7 %collective-permute-start.32 = (bf16[128,2048]{1,0:T(8,128)(2,1)S(1)}, bf16[128,2048]{1,0:T(8,128)(2,1)S(1)}, u32[]{:S(2)}, u32[]{:S(2)}) collective-permute-start(bf16[128,2048]{1,0:T(8,128)(2,1)S(1)} %get-tuple-element.460), channel_id=1, source_target_pairs={{0,4},{1,5},{2,6},{3,7},{4,0},{5,1},{6,2},{7,3},{8,12},{9,13},{10,... | collective-permute-start | bytes 1572872 | tf_op jit(solution)/shard_map/ppermute | solution.py:988
  249.4 23.7 %collective-permute-start.33 = (bf16[128,2048]{1,0:T(8,128)(2,1)S(1)}, bf16[128,2048]{1,0:T(8,128)(2,1)S(1)}, u32[]{:S(2)}, u32[]{:S(2)}) collective-permute-start(bf16[128,2048]{1,0:T(8,128)(2,1)S(1)} %get-tuple-element.340), channel_id=1, source_target_pairs={{0,4},{1,5},{2,6},{3,7},{4,0},{5,1},{6,2},{7,3},{8,12},{9,13},{10,... | collective-permute-start | bytes 1572872 | tf_op jit(solution)/shard_map/ppermute | solution.py:988
  249.5 23.7 %collective-permute-start.34 = (bf16[128,2048]{1,0:T(8,128)(2,1)S(1)}, bf16[128,2048]{1,0:T(8,128)(2,1)S(1)}, u32[]{:S(2)}, u32[]{:S(2)}) collective-permute-start(bf16[128,2048]{1,0:T(8,128)(2,1)S(1)} %collective-permute-done.32.refs_0_), channel_id=1, source_target_pairs={{0,1},{1,0},{2,3},{3,2},{4,5},{5,4},{6,7},{7,6},{8,9},{9,8},{10,11... | collective-permute-start | bytes 1572872 | tf_op jit(solution)/shard_map/ppermute | solution.py:988
  250.2 55.1 %collective-permute-start.36 = (bf16[128,2048]{1,0:T(8,128)(2,1)}, bf16[128,2048]{1,0:T(8,128)(2,1)}, u32[]{:S(2)}, u32[]{:S(2)}) collective-permute-start(bf16[128,2048]{1,0:T(8,128)(2,1)} %collective-permute-done.25.refs_5_), channel_id=1, source_target_pairs={{0,1},{1,0},{2,3},{3,2},{4,5},{5,4},{6,7},{7,6},{8,9},{9,8},{10,11... | collective-permute-start | bytes 1572872 | tf_op jit(solution)/shard_map/ppermute | solution.py:988
  274.0 26.9 %collective-permute-start.35 = (bf16[128,2048]{1,0:T(8,128)(2,1)S(1)}, bf16[128,2048]{1,0:T(8,128)(2,1)S(1)}, u32[]{:S(2)}, u32[]{:S(2)}) collective-permute-start(bf16[128,2048]{1,0:T(8,128)(2,1)S(1)} %collective-permute-done.33.refs_1_), channel_id=1, source_target_pairs={{0,1},{1,0},{2,3},{3,2},{4,5},{5,4},{6,7},{7,6},{8,9},{9,8},{10,11... | collective-permute-start | bytes 1572872 | tf_op jit(solution)/shard_map/ppermute | solution.py:988
  303.9 35.7 %collective-permute-start.37 = (bf16[256,2048]{1,0:T(8,128)(2,1)S(1)}, bf16[256,2048]{1,0:T(8,128)(2,1)S(1)}, u32[]{:S(2)}, u32[]{:S(2)}) collective-permute-start(bf16[256,2048]{1,0:T(8,128)(2,1)S(1)} %get-tuple-element.457), channel_id=1, source_target_pairs={{0,1},{1,0},{2,3},{3,2},{4,5},{5,4},{6,7},{7,6},{8,9},{9,8},{10,11... | collective-permute-start | bytes 3145736 | tf_op jit(solution)/shard_map/ppermute | solution.py:988
  358.1 37.4 %collective-permute-start.39 = (bf16[128,2048]{1,0:T(8,128)(2,1)}, bf16[128,2048]{1,0:T(8,128)(2,1)S(1)}, u32[]{:S(2)}, u32[]{:S(2)}) collective-permute-start(bf16[128,2048]{1,0:T(8,128)(2,1)} %add_convert_fusion.3), channel_id=1, source_target_pairs={{0,4},{1,5},{2,6},{3,7},{4,0},{5,1},{6,2},{7,3},{8,12},{9,13},{10,... | collective-permute-start | bytes 1572872 | tf_op jit(solution)/shard_map/ppermute | solution.py:988
  372.9 33.8 %collective-permute-start.41 = (bf16[128,2048]{1,0:T(8,128)(2,1)S(1)}, bf16[128,2048]{1,0:T(8,128)(2,1)S(1)}, u32[]{:S(2)}, u32[]{:S(2)}) collective-permute-start(bf16[128,2048]{1,0:T(8,128)(2,1)S(1)} %add_convert_fusion.2), channel_id=1, source_target_pairs={{0,4},{1,5},{2,6},{3,7},{4,0},{5,1},{6,2},{7,3},{8,12},{9,13},{10,... | collective-permute-start | bytes 1572872 | tf_op jit(solution)/shard_map/ppermute | solution.py:988
  375.2 56.3 %collective-permute-start.43 = (bf16[256,2048]{1,0:T(8,128)(2,1)S(1)}, bf16[256,2048]{1,0:T(8,128)(2,1)}, u32[]{:S(2)}, u32[]{:S(2)}) collective-permute-start(bf16[256,2048]{1,0:T(8,128)(2,1)S(1)} %slice.298), channel_id=1, source_target_pairs={{0,1},{1,0},{2,3},{3,2},{4,5},{5,4},{6,7},{7,6},{8,9},{9,8},{10,11... | collective-permute-start | bytes 3145736 | tf_op jit(solution)/shard_map/ppermute | solution.py:988
  376.7 56.4 %collective-permute-start.42 = (bf16[256,2048]{1,0:T(8,128)(2,1)}, bf16[256,2048]{1,0:T(8,128)(2,1)}, u32[]{:S(2)}, u32[]{:S(2)}) collective-permute-start(bf16[256,2048]{1,0:T(8,128)(2,1)} %get-tuple-element.455), channel_id=1, source_target_pairs={{0,1},{1,0},{2,3},{3,2},{4,5},{5,4},{6,7},{7,6},{8,9},{9,8},{10,11... | collective-permute-start | bytes 3145736 | tf_op jit(solution)/shard_map/ppermute | solution.py:988
  433.1 19.6 %collective-permute-start.44 = (bf16[80,1024]{1,0:T(8,128)(2,1)S(1)}, bf16[80,1024]{1,0:T(8,128)(2,1)S(1)}, u32[]{:S(2)}, u32[]{:S(2)}) collective-permute-start(bf16[80,1024]{1,0:T(8,128)(2,1)S(1)} %pad_maximum_fusion.8), channel_id=1, source_target_pairs={{8,0},{9,1},{10,2},{11,3},{12,4},{13,5},{14,6},{15,7},{16,8},{17,9... | collective-permute-start | bytes 491528 | tf_op jit(solution)/shard_map/ppermute | solution.py:988
  437.0 50.7 %collective-permute-start.49 = (bf16[256,2048]{1,0:T(8,128)(2,1)S(1)}, bf16[256,2048]{1,0:T(8,128)(2,1)S(1)}, u32[]{:S(2)}, u32[]{:S(2)}) collective-permute-start(bf16[256,2048]{1,0:T(8,128)(2,1)S(1)} %add_convert_fusion.1), channel_id=1, source_target_pairs={{0,4},{1,5},{2,6},{3,7},{4,0},{5,1},{6,2},{7,3},{8,12},{9,13},{10,... | collective-permute-start | bytes 3145736 | tf_op jit(solution)/shard_map/ppermute | solution.py:988
  (84 other events, 975.6 us)
Sparse Core Ops, SparseCore 0:
  117.6 160.9 all-gather.2

commit v5 on v4

--- a/solution.py
+++ b/solution.py
@@ -244,7 +244,8 @@
 def project_q_kernel(*refs, counts, size, column):
     n = len(counts)
     places_ref, blocks = refs[0], refs[1 : 1 + n]
-    x_ref, low_ref, p_ref, cos_ref, sin_ref, maps_ref, q_ref, qf_ref, w_ref, sem = refs[1 + n :]
+    x_ref, low_ref, p_ref, cos_ref, sin_ref, maps_ref = refs[1 + n : 7 + n]
+    q_ref, qf_ref, w_ref, sem = refs[-4:]
     step = pl.program_id(0)
 
     @pl.when(step == 0)
@@ -261,10 +262,11 @@
         qf_ref[:, 2 * p * FEAT : 2 * (p + 1) * FEAT] = feats.astype(BF16)
 
 
-def project_q(half, w, x, low, p, cosine, sine, maps):
+def project_q(half, w, x, low, p, cosine, sine, maps, former=()):
     length = x.shape[0]
     first = half * PER_HALF
     pairs = WIDE // FEAT
+    arrays = (w.places, *w.blocks, x, low, p, cosine, sine, maps, *former)
     return pl.pallas_call(
         functools.partial(
             project_q_kernel, counts=w.shapes(), size=w.size, column=half * HALF
@@ -275,22 +277,23 @@
             pl.BlockSpec((LOW, WIDE), lambda g: (0, first + g)),
             whole(cosine), whole(sine),
             pl.BlockSpec((pairs, FEAT, 2 * FEAT), lambda g: (first + g, 0, 0)),
-        ],
+        ] + [ANYWHERE] * len(former),
         out_specs=[
-            pl.BlockSpec((length, WIDE), lambda g: (0, g)),
-            pl.BlockSpec((length, 2 * WIDE), lambda g: (0, g)),
+            pl.BlockSpec((length, WIDE), lambda g: (0, first + g)),
+            pl.BlockSpec((length, 2 * WIDE), lambda g: (0, first + g)),
         ],
         out_shape=[
-            jax.ShapeDtypeStruct((length, HALF), BF16),
-            jax.ShapeDtypeStruct((length, 2 * HALF), BF16),
+            jax.ShapeDtypeStruct((length, D), BF16),
+            jax.ShapeDtypeStruct((length, 2 * D), BF16),
         ],
+        input_output_aliases={len(arrays) - len(former) + i: i for i in range(len(former))},
         scratch_shapes=[pltpu.VMEM((D, HALF), BF16), pltpu.SemaphoreType.DMA],
         compiler_params=pltpu.CompilerParams(vmem_limit_bytes=VMEM_LIMIT),
         cost_estimate=pl.CostEstimate(
             flops=2 * length * D * HALF, bytes_accessed=2 * D * HALF, transcendentals=0
         ),
         name="project_q",
-    )(w.places, *w.blocks, x, low, p, cosine, sine, maps)
+    )(*arrays)
 
 
 def key_tiles(kv_ref, kf_ref, rim_kv_ref, rim_kf_ref, mask):
@@ -344,9 +347,9 @@
 
 def attend_kernel(
     q_ref, qf_ref, kv_ref, kf_ref, rim_kv_ref, rim_kf_ref, carry_ref,
-    qdoc_ref, kdoc_ref, fresh_ref, gamma_ref,
-    out_ref, att_ref, inv_ref, num_ref, den_ref,
+    qdoc_ref, kdoc_ref, fresh_ref, gamma_ref, *refs,
 ):
+    out_ref, att_ref, inv_ref, num_ref, den_ref = refs[-5:]
     length = q_ref.shape[0]
     mask = same_head(WINDOW)
     ones = mask.astype(BF16)
@@ -373,50 +376,52 @@
     out_ref[...] = att.astype(BF16)
 
 
-def group_specs(length, half):
-    first = half * PER_HALF
-    column = lambda rows, width: pl.BlockSpec((rows, width), lambda g: (0, g))
-    shared = lambda rows, width, at: pl.BlockSpec((rows, width), lambda g: (0, at + g))
+def group_specs(length, first=0):
+    column = lambda rows, width: pl.BlockSpec((rows, width), lambda g: (0, first + g))
     fixed = lambda rows, width: pl.BlockSpec((rows, width), lambda g: (0, 0))
     return dict(
         q=column(length, WIDE),
         qf=column(length, 2 * WIDE),
-        k=shared(length, FEAT, first),
-        rim_kv=shared(WINDOW, FEAT, first),
+        k=column(length, FEAT),
+        rim_kv=column(WINDOW, FEAT),
         rim_kf=pl.BlockSpec((WINDOW, FEAT), lambda g: (1, first + g)),
-        state=shared(STATE, FEAT, first),
-        back=column(STATE, FEAT),
+        state=column(STATE, FEAT),
         qdoc=fixed(length, 1),
         kdoc=fixed(8, WIDE),
-        gamma=shared(1, WIDE, first),
+        gamma=column(1, WIDE),
         wide=fixed(length, WIDE),
         maps=pl.BlockSpec((GROUPS // 2, FEAT, 2 * FEAT), lambda g: (first + g, 0, 0)),
     )
 
 
-def attend(half, q, qf, kv, kf, rim, carry, masks):
+def attend(half, q, qf, kv, kf, rim, carry, masks, former=()):
     length = q.shape[0]
-    s = group_specs(length, half)
+    s = group_specs(length, half * PER_HALF)
+    arrays = (
+        q, qf, kv, kf, rim, rim, carry,
+        masks["qdoc"], masks["kdoc"], masks["fresh"], masks["gamma"], *former,
+    )
     return pl.pallas_call(
         attend_kernel,
         grid=(PER_HALF,),
         in_specs=[
             s["q"], s["qf"], s["k"], s["k"], s["rim_kv"], s["rim_kf"], s["state"],
             s["qdoc"], s["kdoc"], s["qdoc"], s["gamma"],
-        ],
+        ] + [ANYWHERE] * len(former),
         out_specs=[s["q"]] * 3,
         out_shape=[
-            jax.ShapeDtypeStruct((length, HALF), BF16),
-            jax.ShapeDtypeStruct((length, HALF), F32),
-            jax.ShapeDtypeStruct((length, HALF), F32),
+            jax.ShapeDtypeStruct((length, D), BF16),
+            jax.ShapeDtypeStruct((length, D), F32),
+            jax.ShapeDtypeStruct((length, D), F32),
         ],
+        input_output_aliases={len(arrays) - len(former) + i: i for i in range(len(former))},
         scratch_shapes=[pltpu.VMEM((length, WIDE), F32)] * 2,
         compiler_params=pltpu.CompilerParams(vmem_limit_bytes=VMEM_LIMIT),
         cost_estimate=pl.CostEstimate(
             flops=5_000_000_000, bytes_accessed=8 * length * D, transcendentals=0
         ),
         name="attend",
-    )(q, qf, kv, kf, rim, rim, carry, masks["qdoc"], masks["kdoc"], masks["fresh"], masks["gamma"])
+    )(*arrays)
 
 
 def scaled_grads_kernel(
@@ -446,18 +451,18 @@
     back_ref[HEAD:, :] = sums[: STATE - HEAD].astype(BF16)
 
 
-def scaled_grads(half, ga, att, inv, qf, masks):
+def scaled_grads(ga, att, inv, qf, masks):
     length = ga.shape[0]
-    s = group_specs(length, half)
+    s = group_specs(length)
     return pl.pallas_call(
         scaled_grads_kernel,
-        grid=(PER_HALF,),
+        grid=(KV_HEADS,),
         in_specs=[s["q"], s["q"], s["q"], s["qf"], s["qdoc"], s["gamma"]],
-        out_specs=[s["q"], s["q"], s["back"]],
+        out_specs=[s["q"], s["q"], s["state"]],
         out_shape=[
-            jax.ShapeDtypeStruct((length, HALF), BF16),
-            jax.ShapeDtypeStruct((length, HALF), F32),
-            jax.ShapeDtypeStruct((STATE, PER_HALF * FEAT), BF16),
+            jax.ShapeDtypeStruct((length, D), BF16),
+            jax.ShapeDtypeStruct((length, D), F32),
+            jax.ShapeDtypeStruct((STATE, KV_HEADS * FEAT), BF16),
         ],
         compiler_params=pltpu.CompilerParams(vmem_limit_bytes=VMEM_LIMIT),
         name="scaled_grads",
@@ -541,13 +546,13 @@
     raw_ref[...] = turn(dq_ref[...], cos_ref[...], -sin_ref[...]).astype(BF16)
 
 
-def attend_back(half, q, qf, kv, kf, rim, carry, g, gd, masks, maps):
+def attend_back(q, qf, kv, kf, rim, carry, g, gd, masks, maps):
     length = q.shape[0]
-    s = group_specs(length, half)
+    s = group_specs(length)
     column = lambda rows: pl.BlockSpec((rows, FEAT), lambda g: (0, g))
     return pl.pallas_call(
         attend_back_kernel,
-        grid=(PER_HALF,),
+        grid=(KV_HEADS,),
         in_specs=[
             s["q"], s["qf"], s["k"], s["k"], s["rim_kv"], s["rim_kf"], s["state"], s["q"], s["q"],
             s["qdoc"], s["kdoc"], s["qdoc"], s["gamma"], s["maps"], s["wide"], s["wide"],
@@ -558,12 +563,12 @@
             pl.BlockSpec((1, 8, FEAT), lambda g: (g, 0, 0)),
         ],
         out_shape=[
-            jax.ShapeDtypeStruct((length, HALF), BF16),
-            jax.ShapeDtypeStruct((length, PER_HALF * FEAT), F32),
-            jax.ShapeDtypeStruct((length, PER_HALF * FEAT), F32),
-            jax.ShapeDtypeStruct((2 * WINDOW, PER_HALF * FEAT), BF16),
-            jax.ShapeDtypeStruct((HEADS // HALVES, HEAD, FEAT), F32),
-            jax.ShapeDtypeStruct((PER_HALF, 8, FEAT), F32),
+            jax.ShapeDtypeStruct((length, D), BF16),
+            jax.ShapeDtypeStruct((length, KV_HEADS * FEAT), F32),
+            jax.ShapeDtypeStruct((length, KV_HEADS * FEAT), F32),
+            jax.ShapeDtypeStruct((2 * WINDOW, KV_HEADS * FEAT), BF16),
+            jax.ShapeDtypeStruct((HEADS, HEAD, FEAT), F32),
+            jax.ShapeDtypeStruct((KV_HEADS, 8, FEAT), F32),
         ],
         scratch_shapes=[pltpu.VMEM((length, WIDE), F32), pltpu.VMEM((length, 2 * WIDE), F32)],
         compiler_params=pltpu.CompilerParams(vmem_limit_bytes=VMEM_LIMIT),
@@ -625,29 +630,27 @@
     rv_ref[...] = jnp.where(lo, pltpu.roll(dkv[0], HEAD, 1), dkv[1]).astype(BF16)
 
 
-def keys_back(half, kv, kf, dkv, dkf, rim, near, far, masks, maps):
+def keys_back(kv, kf, dkv, dkf, rim, near, far, masks, maps):
     length = kv.shape[0]
-    pairs = PER_HALF // 2
-    first = half * pairs
+    pairs = KV_HEADS // 2
     column = lambda rows: pl.BlockSpec((rows, 2 * FEAT), lambda g: (0, g))
-    shared = pl.BlockSpec((length, 2 * FEAT), lambda g: (0, first + g))
-    state = pl.BlockSpec((STATE, 2 * FEAT), lambda g: (0, first + g))
+    state = pl.BlockSpec((STATE, 2 * FEAT), lambda g: (0, g))
     narrow = pl.BlockSpec((length, FEAT), lambda g: (0, 0))
     out = pl.BlockSpec((length, FEAT), lambda g: (0, g))
     return pl.pallas_call(
         keys_back_kernel,
         grid=(pairs,),
         in_specs=[
-            shared, shared, column(length), column(length),
+            column(length), column(length), column(length), column(length),
             column(WINDOW), pl.BlockSpec((WINDOW, 2 * FEAT), lambda g: (1, g)),
             state, state, pl.BlockSpec((length, 1), lambda g: (0, 0)),
-            pl.BlockSpec((1, FEAT, 2 * FEAT), lambda g: (first + g, 0, 0)), narrow, narrow,
+            pl.BlockSpec((1, FEAT, 2 * FEAT), lambda g: (g, 0, 0)), narrow, narrow,
         ],
         out_specs=[out, out, pl.BlockSpec((2, HEAD, FEAT), lambda g: (g, 0, 0))],
         out_shape=[
-            jax.ShapeDtypeStruct((length, KVD // HALVES), BF16),
-            jax.ShapeDtypeStruct((length, KVD // HALVES), BF16),
-            jax.ShapeDtypeStruct((PER_HALF, HEAD, FEAT), F32),
+            jax.ShapeDtypeStruct((length, KVD), BF16),
+            jax.ShapeDtypeStruct((length, KVD), BF16),
+            jax.ShapeDtypeStruct((KV_HEADS, HEAD, FEAT), F32),
         ],
         compiler_params=pltpu.CompilerParams(vmem_limit_bytes=VMEM_LIMIT),
         name="keys_back",
@@ -659,11 +662,10 @@
 def out_project_kernel(*refs, counts, size):
     n = len(counts)
     places, blocks, refs = refs[0], refs[1 : 1 + n], refs[1 + n :]
-    m0, m1, hidden, proj_in, proj_out, gain = refs[:6]
-    residual, second, low, inverse, w, sem = refs[6:]
+    m, hidden, proj_in, proj_out, gain = refs[:5]
+    residual, second, low, inverse, w, sem = refs[5:]
     start_rows(places, blocks, counts, size, w, sem)
-    reduced = dot_nn(m0[...], proj_in[:HALF, :]) + dot_nn(m1[...], proj_in[HALF:, :])
-    reduced = reduced.astype(BF16)
+    reduced = dot_nn(m[...], proj_in[...]).astype(BF16)
     low[...] = reduced
     wait_rows(w, sem)
     squares = 0.0
@@ -671,8 +673,7 @@
         at = slice(j * WIDE, (j + 1) * WIDE)
         sums = (
             hidden[:, at].astype(F32)
-            + dot_nn(m0[...], w[:HALF, at])
-            + dot_nn(m1[...], w[HALF:, at])
+            + dot_nn(m[...], w[:, at])
             + dot_nn(reduced, proj_out[:, at])
         )
         residual[:, at] = sums
@@ -690,7 +691,7 @@
         jax.ShapeDtypeStruct((length, LOW), BF16),
         jax.ShapeDtypeStruct((length, LOW), F32),
     )
-    rest = (*merged, hidden, proj_in, proj_out, gain)
+    rest = (merged, hidden, proj_in, proj_out, gain)
     return pl.pallas_call(
         functools.partial(out_project_kernel, counts=w.shapes(), size=w.size),
         grid=(1,),
@@ -710,8 +711,8 @@
     n = len(counts)
     places, blocks, refs = refs[0], refs[1 : 1 + n], refs[1 + n :]
     sums, refs = refs[:extra], refs[extra:]
-    cot, residual, inverse, gain, proj_in, proj_out, m0, m1, low = refs[:9]
-    grad_residual, g0, g1, grad_gain, grad_in, grad_out, w, sem = refs[9:]
+    cot, residual, inverse, gain, proj_in, proj_out, m, low = refs[:8]
+    grad_residual, back_ref, grad_gain, grad_in, grad_out, w, sem = refs[8:]
     start_rows(places, blocks, counts, size, w, sem)
     total = sums[0][...].astype(F32)
     for v in sums[1:]:
@@ -727,27 +728,24 @@
     branch = grad.astype(BF16)
     grad_low = dot_nt(branch, proj_out[...]).astype(BF16)
     grad_out[...] = dot_tn(low[...], branch)
-    for i, m in enumerate((m0, m1)):
-        grad_in[:, i * HALF : (i + 1) * HALF] = dot_tn(grad_low, m[...])
+    grad_in[...] = dot_tn(grad_low, m[...])
     wait_rows(w, sem)
     for j in range(D // WIDE):
         at = slice(j * WIDE, (j + 1) * WIDE)
-        i, col = j // (HALF // WIDE), (j % (HALF // WIDE)) * WIDE
         back = dot_nt(grad_low, proj_in[at, :]) + dot_nt(branch, w[at, :])
-        (g0, g1)[i][:, col : col + WIDE] = back.astype(BF16)
+        back_ref[:, at] = back.astype(BF16)
 
 
 def branch_back(w, sums, cot, residual, inverse, gain, proj_in, proj_out, merged, low):
     length = cot.shape[0]
     shapes = (
         jax.ShapeDtypeStruct((length, D), F32),
-        jax.ShapeDtypeStruct((length, HALF), BF16),
-        jax.ShapeDtypeStruct((length, HALF), BF16),
+        jax.ShapeDtypeStruct((length, D), BF16),
         jax.ShapeDtypeStruct((1, D), F32),
         jax.ShapeDtypeStruct((LOW, D), F32),
         jax.ShapeDtypeStruct((LOW, D), F32),
     )
-    rest = (*sums, cot, residual, inverse, gain, proj_in, proj_out, *merged, low)
+    rest = (*sums, cot, residual, inverse, gain, proj_in, proj_out, merged, low)
     return pl.pallas_call(
         functools.partial(
             branch_back_kernel, counts=w.shapes(), size=w.size, extra=len(sums)
@@ -768,7 +766,7 @@
 def inputs_back_kernel(*refs, counts, size):
     n = len(counts)
     places, blocks, refs = refs[0], refs[1 : 1 + n], refs[1 + n :]
-    raws, refs = refs[:6], refs[6:]
+    raws, refs = refs[:3], refs[3:]
     p_in, p_out, low, x, hidden, gain, grad_residual = refs[:7]
     grad_tokens, grad_gain, grad_in, grad_out, w, raw, back, sem = refs[7:]
     start_rows(places, blocks, counts, size, w, sem)
@@ -1279,26 +1277,21 @@
     cot_far += spread_far(grid, late, 1)
     rim = grid.along_seq(pack, 1)
     fulls = [grid.along_seq(full, k) for k in range(2, grid.seq)]
-    queries = [project_q(0, w_qkv, inputs, low, qkv_out, cosine, sine, maps_q)]
+    queries = project_q(0, w_qkv, inputs, low, qkv_out, cosine, sine, maps_q)
     rim, fulls, out.moved, queries = after((rim, fulls, out.moved, queries))
     out.second()
-    queries.append(project_q(1, w_qkv, inputs, low, qkv_out, cosine, sine, maps_q))
+    queries = project_q(1, w_qkv, inputs, low, qkv_out, cosine, sine, maps_q, queries)
     carry = former[0] * rim[2 * WINDOW :].astype(F32)
     for w, full in zip(former[1:], fulls):
         carry = carry + w * full.astype(F32)
     carry = carry.astype(BF16)
-    merged, attended, inverse = [], [], []
-    for i in range(HALVES):
-        block = attend(i, *queries[i], kv, kf, rim, carry, masks)
-        merged.append(block[0])
-        attended.append(block[1])
-        inverse.append(block[2])
-        if i == 0:
-            out.blocks, out.last, merged, queries, cot_far = after(
-                (out.blocks, out.last, merged, queries, cot_far)
-            )
-            out.cores()
-            w_o = out.result()
+    block = attend(0, *queries, kv, kf, rim, carry, masks)
+    out.blocks, out.last, block, queries, cot_far = after(
+        (out.blocks, out.last, block, queries, cot_far)
+    )
+    out.cores()
+    w_o = out.result()
+    merged, attended, inverse = attend(1, *queries, kv, kf, rim, carry, masks, block)
     merged, w_o.blocks, cot_far[0] = after((merged, w_o.blocks, cot_far[0]))
     moved = relay(grid, cot_far[:1])[1:]
     residual, second_in, out_low, inverse_second = out_project(
@@ -1326,50 +1319,35 @@
     near_out, far_out = after((near_out, far_out), send)
     terms.append(jnp.concatenate([grid.flip_z(v, NEAR_BIT) for v in send], axis=0))
 
-    grad_residual, *grad_merged, grad_gain_two, grad_proj_in, grad_proj_out = branch_back(
+    grad_residual, grad_merged, grad_gain_two, grad_proj_in, grad_proj_out = branch_back(
         w_o, terms, grad_out, residual, inverse_second, gain_second, o_in, o_out, merged, out_low
     )
-    scaled = [
-        scaled_grads(i, grad_merged[i], attended[i], inverse[i], queries[i][1], masks)
-        for i in range(HALVES)
-    ]
-    back = jnp.concatenate([v[2] for v in scaled], axis=1)
+    *scaled, back = scaled_grads(grad_merged, attended, inverse, queries[1], masks)
     out_terms = collect_near(grid, near_out, length)
     send = collect_far(grid, far_out, length, 1)
     back, scaled, out_terms, send = after((back, scaled, out_terms, send))
     out_terms += [grid.flip_z(v, NEAR_BIT) for v in send]
     returned = [grid.along_seq(back, -k) for k in range(1, grid.seq)]
-    backs = []
-    for i in range(HALVES):
-        backs.append(
-            attend_back(i, *queries[i], kv, kf, rim, carry, *scaled[i][:2], masks, maps_q)
-        )
-        scaled, returned, backs = after((scaled, returned, backs))
+    raw_query, dkv, dkf, rim_back, dmap_query, dlogit = attend_back(
+        *queries, kv, kf, rim, carry, *scaled, masks, maps_q
+    )
+    rim_back = grid.along_seq(rim_back, -1)
+    returned, dkv = after((returned, dkv))
     far_back = jnp.zeros(back.shape, F32)
     for w, v in zip(latter[1:], returned[1:]):
         far_back = far_back + w * v.astype(F32)
     near_back = far_back + latter[0] * returned[0].astype(F32)
     near_back, far_back = near_back.astype(BF16), far_back.astype(BF16)
-    raw_query = [v[0] for v in backs]
-    rim_back = [grid.along_seq(v[3], -1) for v in backs]
-    raw_key, raw_value, dmap_key = [], [], []
-    for i, (_, dkv, dkf, *_) in enumerate(backs):
-        k, v, m = keys_back(
-            i, kv, kf, dkv, dkf, rim_back[i], near_back, far_back, masks, maps_k
-        )
-        raw_key.append(k)
-        raw_value.append(v)
-        dmap_key.append(m)
+    raw_key, raw_value, dmap_key = keys_back(
+        kv, kf, dkv, dkf, rim_back, near_back, far_back, masks, maps_k
+    )
     raw_key, out_terms = after((raw_key, out_terms))
     block_out = residual
     for term in out_terms:
         block_out = block_out + term.astype(F32)
     block_out = block_out.astype(BF16)
-    dmap_query = jnp.concatenate([v[4] for v in backs], axis=0)
-    dmap_key = jnp.concatenate(dmap_key, axis=0)
-    dlogit = jnp.concatenate([v[5] for v in backs], axis=0)
     grad_tokens, grad_gain_one, grad_qkv_in, grad_qkv_out = inputs_back(
-        w_qkv, [*raw_query, *raw_key, *raw_value], qkv_in, qkv_out, low, inputs,
+        w_qkv, [raw_query, raw_key, raw_value], qkv_in, qkv_out, low, inputs,
         hidden, gain_first, grad_residual,
     )
     grad_logit = dlogit[:, :GROUPS, 0].reshape(HEADS) * (1.0 - gamma)

time: 558 us -> 549 us (0.984)
  Pallas kernels: 208 us -> 201 us
  waiting for transfers between devices: 146 us -> 153 us
  other arithmetic: 47 us -> 41.1 us
    ppermute x57 -> x56, waiting for transfers between devices: 142 us -> 149 us  [send(): lax.ppermute(v, ('seq', 'rows'), route)]
    pallas_call x6 -> x3, Pallas kernels: 49.8 us -> 44 us  [the longest x1 28.8 us: attend_back(): pl.pallas_call(attend_back_kernel, grid=(KV_HEADS,), in_specs=[s['q'], s[...]
    ppermute x57 -> x56, starting transfers between devices: 78.5 us -> 73.8 us  [send(): lax.ppermute(v, ('seq', 'rows'), route)]
  transfers between devices with their start and end apart: 58 -> 57, of which waited for: 21 -> 22; matrix products, arithmetic and copies ran while one was open for 14% -> 14% of each run, Pallas kernels for 35% -> 34%
where the time goes in v5:
time: 549 us; the launch traced here: 544 us
  Pallas kernels  201 us (37%)
  waiting for transfers between devices  153 us (28%)
  starting transfers between devices  73.8 us (13%)
  local copies, waits for them, and re-layouts  54.3 us (10%)
  other arithmetic  41.1 us (7%)
  between operations  19.4 us (4%)
    ppermute x56, waiting for transfers between devices, send(): lax.ppermute(v, ('seq', 'rows'), route)  149 us
    pallas_call x3, Pallas kernels, mlp(): pl.pallas_call(functools.partial(mlp_kernel, rows=rows, paired=pair is no...  77.9 us
    ppermute x56, starting transfers between devices, send(): lax.ppermute(v, ('seq', 'rows'), route)  73.8 us
    pallas_call x1, Pallas kernels, attend_back(): pl.pallas_call(attend_back_kernel, grid=(KV_HEADS,), in_specs=[s['q'], s[...  28.8 us
    pallas_call x2, Pallas kernels, project_q(): pl.pallas_call(functools.partial(project_q_kernel, counts=w.shapes(), siz...  19.7 us
    pallas_call x2, Pallas kernels, attend(): pl.pallas_call(attend_kernel, grid=(PER_HALF,), in_specs=[s['q'], s['qf']...  16 us
    pallas_call x1, Pallas kernels, inputs_back(): pl.pallas_call(functools.partial(inputs_back_kernel, counts=w.shapes(), s...  14.1 us
  transfers between devices with their start and end apart: 57, of which 22 were waited for; matrix products, arithmetic and copies ran while one was open for 14% of the time, Pallas kernels for 34%

profile of v5, /device:TPU:0, one launch (start us, length us, event | category | flops | bytes accessed | tf_op | source)
XLA Modules:
  0.0 543.7 jit_solution(12292844526305237555)
XLA Ops:
  10.1 4.0 collective-permute-start.2
  59.4 13.5 %collective-permute-done.8 = bf16[64,2048]{1,0:T(8,128)(2,1)S(1)} collective-permute-done((bf16[64,2048]{1,0:T(8,128)(2,1)S(1)}, bf16[64,2048]{1,0:T(8,128)(2,1)S(1)}, u32[]{:S(2)}, u32[]{:S(2)}) %collective-permute-start.8) | collective-permute-done | bytes 262176 | tf_op jit(solution)/shard_map/ppermute | solution.py:986
  73.7 3.5 collective-permute-done.9
  90.1 9.3 %maximum_maximum_fusion = bf16[1536,1024]{1,0:T(8,128)(2,1)} fusion(bf16[512,512]{1,0:T(8,128)(2,1)S(1)} %get-tuple-element.376, bf16[512,512]{1,0:T(8,128)(2,1)S(1)} %get-tuple-element.375, bf16[512,1024]{1,0:T(8,128)(2,1)S(1)} %get-tuple-element.374, bf16[512,1024]{1,0:T(8,128)(2,1)S(1)} %get-tuple-element.373), kind=kLoop, calls=%fused_computation | loop fusion | flops 12582912 | bytes 6291456 | tf_op jit(solution)/shard_map/concatenate | solution.py:1085
  99.4 11.8 %collective-permute-done.15.refs_4_ = bf16[128,2048]{1,0:T(8,128)(2,1)} collective-permute-done((bf16[128,2048]{1,0:T(8,128)(2,1)}, bf16[128,2048]{1,0:T(8,128)(2,1)}, u32[]{:S(2)}, u32[]{:S(2)}) %collective-permute-start.15) | collective-permute-done | bytes 524320 | tf_op jit(solution)/shard_map/ppermute | solution.py:986
  111.2 3.4 collective-permute-done.12.refs_4_
  128.2 9.1 %project_kv.1 = (bf16[256,1024]{1,0:T(8,128)(2,1)}, bf16[256,1024]{1,0:T(8,128)(2,1)}, bf16[208,1024]{1,0:T(8,128)(2,1)}, bf16[80,1024]{1,0:T(8,128)(2,1)}) custom-call(s32[32]{0:T(128)} %stack.164.refs_0_, bf16[256,3072]{1,0:T(8,128)(2,1)} %copy-done.3, bf16[256,3072]{1,0:T(8,128)(2,1)} %copy-done.4, bf16[256,3072]{1,0:T(8,128)(2,1)} %collective-permute-done.11.refs_3_, ...), custom_call_target="tpu_custom_call" | custom-call | flops 1073741824 | bytes 4194304 | tf_op jit(solution)/shard_map/project_kv/pallas_call | solution.py:229
  144.1 9.9 %project_q.2 = (bf16[256,2048]{1,0:T(8,128)(2,1)}, bf16[256,4096]{1,0:T(8,128)(2,1)}) custom-call(s32[32]{0:T(128)} %stack.164.refs_0_, bf16[256,3072]{1,0:T(8,128)(2,1)} %copy-done.3, bf16[256,3072]{1,0:T(8,128)(2,1)} %copy-done.4, bf16[256,3072]{1,0:T(8,128)(2,1)} %collective-permute-done.11.refs_3_, bf16[256,3072]{1,0:T(8,128)(2,1)} %collective-permute-done.12.refs_4_, ...), custom_call_target="tpu_custom_call" | custom-call | flops 1073741824 | bytes 4194304 | tf_op jit(solution)/shard_map/project_q/pallas_call | solution.py:270
  166.3 9.8 %project_q.3 = (bf16[256,2048]{1,0:T(8,128)(2,1)}, bf16[256,4096]{1,0:T(8,128)(2,1)}) custom-call(s32[32]{0:T(128)} %stack.164.refs_0_, bf16[256,3072]{1,0:T(8,128)(2,1)} %copy-done.3, bf16[256,3072]{1,0:T(8,128)(2,1)} %copy-done.4, bf16[256,3072]{1,0:T(8,128)(2,1)} %collective-permute-done.11.refs_3_, ...), custom_call_target="tpu_custom_call", output_to_operand_aliasing={{0}: (15, {}), {1}: (16, {})} | custom-call | flops 1073741824 | bytes 4194304 | tf_op jit(solution)/shard_map/project_q/pallas_call | solution.py:270
  176.1 8.0 %attend.2 = (bf16[256,2048]{1,0:T(8,128)(2,1)}, f32[256,2048]{1,0:T(8,128)}, f32[256,2048]{1,0:T(8,128)}) custom-call(bf16[256,2048]{1,0:T(8,128)(2,1)} %get-tuple-element.270.q_ref, bf16[256,4096]{1,0:T(8,128)(2,1)} %get-tuple-element.271.qf_ref, bf16[256,1024]{1,0:T(8,128)(2,1)} %get-tuple-element.253.kv_ref, bf16[256,1024]{1,0:T(8,128)(2,1)} %get-tuple-element.254.kf_ref, ...), custom_call_target="tpu_custom_call" | custom-call | flops 5000000000 | bytes 4194304 | tf_op jit(solution)/shard_map/attend/pallas_call | solution.py:404
  187.5 6.5 %collective-permute-done.23.refs_3_ = bf16[256,2048]{1,0:T(8,128)(2,1)} collective-permute-done((bf16[256,2048]{1,0:T(8,128)(2,1)S(1)}, bf16[256,2048]{1,0:T(8,128)(2,1)}, u32[]{:S(2)}, u32[]{:S(2)}) %collective-permute-start.23) | collective-permute-done | bytes 1048608 | tf_op jit(solution)/shard_map/ppermute | solution.py:986
  197.7 8.0 %attend.3 = (bf16[256,2048]{1,0:T(8,128)(2,1)}, f32[256,2048]{1,0:T(8,128)}, f32[256,2048]{1,0:T(8,128)}) custom-call(bf16[256,2048]{1,0:T(8,128)(2,1)} %get-tuple-element.270.q_ref, bf16[256,4096]{1,0:T(8,128)(2,1)} %get-tuple-element.271.qf_ref, ...), custom_call_target="tpu_custom_call", output_to_operand_aliasing={{0}: (11, {}), {1}: (12, {}), {2}: (13, {})} | custom-call | flops 5000000000 | bytes 4194304 | tf_op jit(solution)/shard_map/attend/pallas_call | solution.py:404
  207.4 9.9 %out_project.1 = (f32[256,2048]{1,0:T(8,128)}, bf16[256,2048]{1,0:T(8,128)(2,1)}, bf16[256,128]{1,0:T(8,128)(2,1)}, f32[256,128]{1,0:T(8,128)}) custom-call(s32[32]{0:T(128)} %stack.164.refs_0_, bf16[256,2048]{1,0:T(8,128)(2,1)} %copy-done.10, bf16[256,2048]{1,0:T(8,128)(2,1)} %copy-done.9, bf16[256,2048]{1,0:T(8,128)(2,1)} %collective-permute-done.23.refs_3_, ...), custom_call_target="tpu_custom_call" | custom-call | flops 2147483648 | bytes 8388608 | tf_op jit(solution)/shard_map/out_project/pallas_call | solution.py:695
  222.6 3.8 collective-permute-start.32
  226.4 22.9 %collective-permute-done.32.refs_0_ = bf16[128,2048]{1,0:T(8,128)(2,1)S(1)} collective-permute-done((bf16[128,2048]{1,0:T(8,128)(2,1)S(1)}, bf16[128,2048]{1,0:T(8,128)(2,1)S(1)}, u32[]{:S(2)}, u32[]{:S(2)}) %collective-permute-start.32) | collective-permute-done | bytes 524320 | tf_op jit(solution)/shard_map/ppermute | solution.py:986
  251.5 21.3 %mlp.3 = (f32[512,2048]{1,0:T(8,128)}, f32[512,2048]{1,0:T(8,128)}) custom-call(s32[1]{0:T(128)} %constant.643.clone.1.place_ref, bf16[256,2048]{1,0:T(8,128)(2,1)} %get-tuple-element.297.refs_0_, bf16[256,2048]{1,0:T(8,128)(2,1)} %copy-done.21, bf16[256,2048]{1,0:T(8,128)(2,1)} %bitcast.138, bf16[256,2048]{1,0:T(8,128)(2,1)} %collective-permute-done.refs_3_, ...), custom_call_target="tpu_custom_call" | custom-call | flops 12884901888 | bytes 12582912 | tf_op jit(solution)/shard_map/mlp/pallas_call | solution.py:927
  274.3 4.3 all-gather.3.cloned.1.call-done
  278.6 22.3 %mlp.4 = (bf16[512,2048]{1,0:T(8,128)(2,1)}, bf16[512,2048]{1,0:T(8,128)(2,1)}) custom-call(s32[1]{0:T(128)} %bitcast.57.place_ref, bf16[256,2048]{1,0:T(8,128)(2,1)} %get-tuple-element.297.refs_0_, bf16[256,2048]{1,0:T(8,128)(2,1)} %copy-done.21, bf16[256,2048]{1,0:T(8,128)(2,1)} %bitcast.139, bf16[256,2048]{1,0:T(8,128)(2,1)} %collective-permute-done.refs_3_, ...), custom_call_target="tpu_custom_call" | custom-call | flops 12884901888 | bytes 12582912 | tf_op jit(solution)/shard_map/mlp/pallas_call | solution.py:927
  305.4 34.3 %mlp.5 = (bf16[512,2048]{1,0:T(8,128)(2,1)}, bf16[512,2048]{1,0:T(8,128)(2,1)}) custom-call(s32[1]{0:T(128)} %bitcast.57.place_ref, bf16[128,2048]{1,0:T(8,128)(2,1)} %copy-done.44, bf16[128,2048]{1,0:T(8,128)(2,1)} %copy-done.45, bf16[128,2048]{1,0:T(8,128)(2,1)} %copy-done.46, bf16[128,2048]{1,0:T(8,128)(2,1)} %copy-done.47, ...), custom_call_target="tpu_custom_call" | custom-call | flops 25769803776 | bytes 25165824 | tf_op jit(solution)/shard_map/mlp/pallas_call | solution.py:927
  341.8 11.9 %collective-permute-done.38 = bf16[128,2048]{1,0:T(8,128)(2,1)S(1)} collective-permute-done((bf16[128,2048]{1,0:T(8,128)(2,1)S(1)}, bf16[128,2048]{1,0:T(8,128)(2,1)S(1)}, u32[]{:S(2)}, u32[]{:S(2)}) %collective-permute-start.38) | collective-permute-done | bytes 524320 | tf_op jit(solution)/shard_map/ppermute | solution.py:986
  359.9 11.6 %collective-permute-done.40 = bf16[128,2048]{1,0:T(8,128)(2,1)} collective-permute-done((bf16[128,2048]{1,0:T(8,128)(2,1)}, bf16[128,2048]{1,0:T(8,128)(2,1)}, u32[]{:S(2)}, u32[]{:S(2)}) %collective-permute-start.40) | collective-permute-done | bytes 524320 | tf_op jit(solution)/shard_map/ppermute | solution.py:986
  378.8 16.5 %collective-permute-done.39 = bf16[128,2048]{1,0:T(8,128)(2,1)S(1)} collective-permute-done((bf16[128,2048]{1,0:T(8,128)(2,1)}, bf16[128,2048]{1,0:T(8,128)(2,1)S(1)}, u32[]{:S(2)}, u32[]{:S(2)}) %collective-permute-start.39) | collective-permute-done | bytes 524320 | tf_op jit(solution)/shard_map/ppermute | solution.py:986
  395.3 11.2 %collective-permute-done.41 = bf16[128,2048]{1,0:T(8,128)(2,1)S(1)} collective-permute-done((bf16[128,2048]{1,0:T(8,128)(2,1)S(1)}, bf16[128,2048]{1,0:T(8,128)(2,1)S(1)}, u32[]{:S(2)}, u32[]{:S(2)}) %collective-permute-start.41) | collective-permute-done | bytes 524320 | tf_op jit(solution)/shard_map/ppermute | solution.py:986
  407.6 10.4 %branch_back.1 = (f32[256,2048]{1,0:T(8,128)}, bf16[256,2048]{1,0:T(8,128)(2,1)}, f32[1,2048]{1,0:T(1,128)}, f32[128,2048]{1,0:T(8,128)}, f32[128,2048]{1,0:T(8,128)}) custom-call(s32[32]{0:T(128)} %stack.164.refs_0_, bf16[256,2048]{1,0:T(8,128)(2,1)} %copy-done.10, bf16[256,2048]{1,0:T(8,128)(2,1)} %copy-done.9, ...), custom_call_target="tpu_custom_call" | custom-call | flops 2147483648 | bytes 8388608 | tf_op jit(solution)/shard_map/branch_back/pallas_call | solution.py:749
  420.5 8.6 %scaled_grads.1 = (bf16[256,2048]{1,0:T(8,128)(2,1)}, f32[256,2048]{1,0:T(8,128)}, bf16[80,1024]{1,0:T(8,128)(2,1)}) custom-call(bf16[256,2048]{1,0:T(8,128)(2,1)} %get-tuple-element.328.ga_ref, f32[256,2048]{1,0:T(8,128)} %get-tuple-element.329.att_ref, f32[256,2048]{1,0:T(8,128)} %get-tuple-element.330.inv_ref, ...), custom_call_target="tpu_custom_call" | custom-call | tf_op jit(solution)/shard_map/scaled_grads/pallas_call | solution.py:457
  434.8 28.8 %attend_back.1 = (bf16[256,2048]{1,0:T(8,128)(2,1)}, f32[256,1024]{1,0:T(8,128)}, f32[256,1024]{1,0:T(8,128)}, bf16[128,1024]{1,0:T(8,128)(2,1)}, f32[32,64,128]{2,1,0:T(8,128)}, /*index=5*/f32[8,8,128]{2,1,0:T(8,128)}) custom-call(bf16[256,2048]{1,0:T(8,128)(2,1)} %get-tuple-element.270.q_ref, bf16[256,4096]{1,0:T(8,128)(2,1)} %get-tuple-element.271.qf_ref, ...), custom_call_target="tpu_custom_call" | custom-call | flops 15000000512 | bytes 4194304 | tf_op jit(solution)/shard_map/attend_back/pallas_call | solution.py:553
  469.3 6.6 %keys_back.1 = (bf16[256,512]{1,0:T(8,128)(2,1)}, bf16[256,512]{1,0:T(8,128)(2,1)}, f32[8,64,128]{2,1,0:T(8,128)}) custom-call(bf16[256,1024]{1,0:T(8,128)(2,1)} %get-tuple-element.253.kv_ref, bf16[256,1024]{1,0:T(8,128)(2,1)} %get-tuple-element.254.kf_ref, f32[256,1024]{1,0:T(8,128)} %get-tuple-element.342.dkv_ref, f32[256,1024]{1,0:T(8,128)} %get-tuple-element.343.dkf_ref, ...), custom_call_target="tpu_custom_call" | custom-call | tf_op jit(solution)/shard_map/keys_back/pallas_call | solution.py:640
  477.0 6.8 %collective-permute-done.48 = bf16[256,2048]{1,0:T(8,128)(2,1)} collective-permute-done((bf16[256,2048]{1,0:T(8,128)(2,1)S(1)}, bf16[256,2048]{1,0:T(8,128)(2,1)}, u32[]{:S(2)}, u32[]{:S(2)}) %collective-permute-start.48) | collective-permute-done | bytes 1048608 | tf_op jit(solution)/shard_map/ppermute | solution.py:986
  483.8 14.1 %inputs_back.1 = (f32[256,2048]{1,0:T(8,128)}, f32[1,2048]{1,0:T(1,128)}, f32[128,2048]{1,0:T(8,128)}, f32[128,3072]{1,0:T(8,128)}) custom-call(s32[32]{0:T(128)} %stack.164.refs_0_, bf16[256,3072]{1,0:T(8,128)(2,1)} %copy-done.3, bf16[256,3072]{1,0:T(8,128)(2,1)} %copy-done.4, bf16[256,3072]{1,0:T(8,128)(2,1)} %collective-permute-done.11.refs_3_, ...), custom_call_target="tpu_custom_call" | custom-call | flops 3221225472 | bytes 12582912 | tf_op jit(solution)/shard_map/inputs_back/pallas_call | solution.py:807
  504.7 4.5 collective-permute-done.50
  517.1 3.8 collective-permute-done.52
  520.8 5.7 %collective-permute-done.53 = bf16[8,8704]{1,0:T(8,128)(2,1)S(1)} collective-permute-done((bf16[8,8704]{1,0:T(8,128)(2,1)S(1)}, bf16[8,8704]{1,0:T(8,128)(2,1)S(1)}, u32[]{:S(2)}, u32[]{:S(2)}) %collective-permute-start.53) | collective-permute-done | bytes 139296 | tf_op jit(solution)/shard_map/ppermute | solution.py:986
  (335 shorter events, 168.2 us)
Async XLA Ops:
  7.3 271.3 %all-gather.3.cloned.1.call-start = ((), (), s32[]{:S(2)}) async-start(), calls=%async_computation | async-start | bytes 28311552 | tf_op jit(solution)/shard_map/all_gather | solution.py:1094
  10.1 39.8 %collective-permute-start.2 = (bf16[64,3072]{1,0:T(8,128)(2,1)}, bf16[64,3072]{1,0:T(8,128)(2,1)}, u32[]{:S(2)}, u32[]{:S(2)}) collective-permute-start(bf16[64,3072]{1,0:T(8,128)(2,1)} %pad_maximum_fusion.6), channel_id=1, source_target_pairs={{0,4},{1,5},{2,6},{3,7},{4,0},{5,1},{6,2},{7,3},{8,12},{9,13},{10,... | collective-permute-start | bytes 1179656 | tf_op jit(solution)/shard_map/ppermute | solution.py:986
  14.1 35.8 %collective-permute-start.3 = (bf16[64,3072]{1,0:T(8,128)(2,1)}, bf16[64,3072]{1,0:T(8,128)(2,1)}, u32[]{:S(2)}, u32[]{:S(2)}) collective-permute-start(bf16[64,3072]{1,0:T(8,128)(2,1)} %pad_maximum_fusion.6), channel_id=1, source_target_pairs={{0,6},{1,7},{2,0},{3,1},{4,2},{5,3},{6,4},{7,5},{8,14},{9,15},{10,... | collective-permute-start | bytes 1179656 | tf_op jit(solution)/shard_map/ppermute | solution.py:986
  15.5 33.4 %collective-permute-start.1 = (bf16[64,3072]{1,0:T(8,128)(2,1)}, bf16[64,3072]{1,0:T(8,128)(2,1)}, u32[]{:S(2)}, u32[]{:S(2)}) collective-permute-start(bf16[64,3072]{1,0:T(8,128)(2,1)} %pad_maximum_fusion.6), channel_id=1, source_target_pairs={{0,2},{1,3},{2,4},{3,5},{4,6},{5,7},{6,0},{7,1},{8,10},{9,11},{10,... | collective-permute-start | bytes 1179656 | tf_op jit(solution)/shard_map/ppermute | solution.py:986
  17.4 33.7 %collective-permute-start = (bf16[256,2048]{1,0:T(8,128)(2,1)}, bf16[256,2048]{1,0:T(8,128)(2,1)}, u32[]{:S(2)}, u32[]{:S(2)}) collective-permute-start(bf16[256,2048]{1,0:T(8,128)(2,1)} %bitcast.136), channel_id=1, source_target_pairs={{0,1},{1,0},{2,3},{3,2},{4,5},{5,4},{6,7},{7,6},{8,9},{9,8},{10,11... | collective-permute-start | bytes 3145736 | tf_op jit(solution)/shard_map/ppermute | solution.py:986
  51.1 22.6 %collective-permute-start.10 = (bf16[64,2048]{1,0:T(8,128)(2,1)S(1)}, bf16[64,2048]{1,0:T(8,128)(2,1)S(1)}, u32[]{:S(2)}, u32[]{:S(2)}) collective-permute-start(bf16[64,2048]{1,0:T(8,128)(2,1)S(1)} %copy-done.24), channel_id=1, source_target_pairs={{0,6},{1,7},{2,0},{3,1},{4,2},{5,3},{6,4},{7,5},{8,14},{9,15},{10,... | collective-permute-start | bytes 786440 | tf_op jit(solution)/shard_map/ppermute | solution.py:986
  54.3 22.9 %collective-permute-start.9 = (bf16[64,2048]{1,0:T(8,128)(2,1)S(1)}, bf16[64,2048]{1,0:T(8,128)(2,1)S(1)}, u32[]{:S(2)}, u32[]{:S(2)}) collective-permute-start(bf16[64,2048]{1,0:T(8,128)(2,1)S(1)} %copy-done.24), channel_id=1, source_target_pairs={{0,4},{1,5},{2,6},{3,7},{4,0},{5,1},{6,2},{7,3},{8,12},{9,13},{10,... | collective-permute-start | bytes 786440 | tf_op jit(solution)/shard_map/ppermute | solution.py:986
  56.2 21.9 %collective-permute-start.7 = (bf16[128,3072]{1,0:T(8,128)(2,1)S(1)}, bf16[128,3072]{1,0:T(8,128)(2,1)S(1)}, u32[]{:S(2)}, u32[]{:S(2)}) collective-permute-start(bf16[128,3072]{1,0:T(8,128)(2,1)S(1)} %pad_maximum_fusion.2), channel_id=1, source_target_pairs={{0,16},{1,17},{2,18},{3,19},{4,20},{5,21},{6,22},{7,23},{8,24},{9,... | collective-permute-start | bytes 2359304 | tf_op jit(solution)/shard_map/ppermute | solution.py:986
  57.7 20.3 %collective-permute-start.6 = (bf16[128,3072]{1,0:T(8,128)(2,1)S(1)}, bf16[128,3072]{1,0:T(8,128)(2,1)S(1)}, u32[]{:S(2)}, u32[]{:S(2)}) collective-permute-start(bf16[128,3072]{1,0:T(8,128)(2,1)S(1)} %pad_maximum_fusion.1), channel_id=1, source_target_pairs={{0,1},{1,0},{2,3},{3,2},{4,5},{5,4},{6,7},{7,6},{8,9},{9,8},{10,11... | collective-permute-start | bytes 2359304 | tf_op jit(solution)/shard_map/ppermute | solution.py:986
  78.9 35.7 %collective-permute-start.12 = (bf16[256,3072]{1,0:T(8,128)(2,1)S(1)}, bf16[256,3072]{1,0:T(8,128)(2,1)}, u32[]{:S(2)}, u32[]{:S(2)}) collective-permute-start(bf16[256,3072]{1,0:T(8,128)(2,1)S(1)} %constant_dynamic-update-slice_fusion.2.refs_2_), channel_id=1, source_target_pairs={{0,1},{1,0},{2,3},{3,2},{4,5},{5,4},{6,7},{7,6},{8,9},{9,8},{10,11... | collective-permute-start | bytes 4718600 | tf_op jit(solution)/shard_map/ppermute | solution.py:986
  80.4 34.2 %collective-permute-start.14 = (bf16[256,3072]{1,0:T(8,128)(2,1)S(1)}, bf16[256,3072]{1,0:T(8,128)(2,1)}, u32[]{:S(2)}, u32[]{:S(2)}) collective-permute-start(bf16[256,3072]{1,0:T(8,128)(2,1)S(1)} %constant_dynamic-update-slice_fusion.2.refs_2_), channel_id=1, source_target_pairs={{0,8},{1,9},{2,10},{3,11},{4,12},{5,13},{6,14},{7,15},{8,0},{9,1},... | collective-permute-start | bytes 4718600 | tf_op jit(solution)/shard_map/ppermute | solution.py:986
  80.5 37.0 %collective-permute-start.11 = (bf16[256,3072]{1,0:T(8,128)(2,1)S(1)}, bf16[256,3072]{1,0:T(8,128)(2,1)}, u32[]{:S(2)}, u32[]{:S(2)}) collective-permute-start(bf16[256,3072]{1,0:T(8,128)(2,1)S(1)} %constant_dynamic-update-slice_fusion.refs_1_), channel_id=1, source_target_pairs={{0,16},{1,17},{2,18},{3,19},{4,20},{5,21},{6,22},{7,23},{8,24},{9,... | collective-permute-start | bytes 4718600 | tf_op jit(solution)/shard_map/ppermute | solution.py:986
  82.1 35.4 %collective-permute-start.13 = (bf16[256,3072]{1,0:T(8,128)(2,1)S(1)}, bf16[256,3072]{1,0:T(8,128)(2,1)}, u32[]{:S(2)}, u32[]{:S(2)}) collective-permute-start(bf16[256,3072]{1,0:T(8,128)(2,1)S(1)} %constant_dynamic-update-slice_fusion.refs_1_), channel_id=1, source_target_pairs={{0,8},{1,9},{2,10},{3,11},{4,12},{5,13},{6,14},{7,15},{8,0},{9,1},... | collective-permute-start | bytes 4718600 | tf_op jit(solution)/shard_map/ppermute | solution.py:986
  84.6 26.6 %collective-permute-start.15 = (bf16[128,2048]{1,0:T(8,128)(2,1)}, bf16[128,2048]{1,0:T(8,128)(2,1)}, u32[]{:S(2)}, u32[]{:S(2)}) collective-permute-start(bf16[128,2048]{1,0:T(8,128)(2,1)} %get-tuple-element.384), channel_id=1, source_target_pairs={{0,4},{1,5},{2,6},{3,7},{4,0},{5,1},{6,2},{7,3},{8,12},{9,13},{10,... | collective-permute-start | bytes 1572872 | tf_op jit(solution)/shard_map/ppermute | solution.py:986
  155.9 31.6 %collective-permute-start.24 = (bf16[256,2048]{1,0:T(8,128)(2,1)S(1)}, bf16[256,2048]{1,0:T(8,128)(2,1)S(1)}, u32[]{:S(2)}, u32[]{:S(2)}) collective-permute-start(bf16[256,2048]{1,0:T(8,128)(2,1)S(1)} %constant_dynamic-update-slice_fusion.6.refs_2_), channel_id=1, source_target_pairs={{0,1},{1,0},{2,3},{3,2},{4,5},{5,4},{6,7},{7,6},{8,9},{9,8},{10,11... | collective-permute-start | bytes 3145736 | tf_op jit(solution)/shard_map/ppermute | solution.py:986
  158.4 35.6 %collective-permute-start.23 = (bf16[256,2048]{1,0:T(8,128)(2,1)S(1)}, bf16[256,2048]{1,0:T(8,128)(2,1)}, u32[]{:S(2)}, u32[]{:S(2)}) collective-permute-start(bf16[256,2048]{1,0:T(8,128)(2,1)S(1)} %constant_dynamic-update-slice_fusion.4.refs_1_), channel_id=1, source_target_pairs={{0,16},{1,17},{2,18},{3,19},{4,20},{5,21},{6,22},{7,23},{8,24},{9,... | collective-permute-start | bytes 3145736 | tf_op jit(solution)/shard_map/ppermute | solution.py:986
  161.8 25.7 %collective-permute-start.25 = (bf16[128,2048]{1,0:T(8,128)(2,1)}, bf16[128,2048]{1,0:T(8,128)(2,1)}, u32[]{:S(2)}, u32[]{:S(2)}) collective-permute-start(bf16[128,2048]{1,0:T(8,128)(2,1)} %get-tuple-element.269), channel_id=1, source_target_pairs={{0,4},{1,5},{2,6},{3,7},{4,0},{5,1},{6,2},{7,3},{8,12},{9,13},{10,... | collective-permute-start | bytes 1572872 | tf_op jit(solution)/shard_map/ppermute | solution.py:986
  220.4 28.9 %collective-permute-start.31 = (bf16[256,2048]{1,0:T(8,128)(2,1)}, bf16[256,2048]{1,0:T(8,128)(2,1)S(1)}, u32[]{:S(2)}, u32[]{:S(2)}) collective-permute-start(bf16[256,2048]{1,0:T(8,128)(2,1)} %get-tuple-element.297.refs_0_), channel_id=1, source_target_pairs={{0,1},{1,0},{2,3},{3,2},{4,5},{5,4},{6,7},{7,6},{8,9},{9,8},{10,11... | collective-permute-start | bytes 3145736 | tf_op jit(solution)/shard_map/ppermute | solution.py:986
  222.6 26.7 %collective-permute-start.32 = (bf16[128,2048]{1,0:T(8,128)(2,1)S(1)}, bf16[128,2048]{1,0:T(8,128)(2,1)S(1)}, u32[]{:S(2)}, u32[]{:S(2)}) collective-permute-start(bf16[128,2048]{1,0:T(8,128)(2,1)S(1)} %get-tuple-element.382), channel_id=1, source_target_pairs={{0,4},{1,5},{2,6},{3,7},{4,0},{5,1},{6,2},{7,3},{8,12},{9,13},{10,... | collective-permute-start | bytes 1572872 | tf_op jit(solution)/shard_map/ppermute | solution.py:986
  249.3 23.5 %collective-permute-start.33 = (bf16[128,2048]{1,0:T(8,128)(2,1)S(1)}, bf16[128,2048]{1,0:T(8,128)(2,1)S(1)}, u32[]{:S(2)}, u32[]{:S(2)}) collective-permute-start(bf16[128,2048]{1,0:T(8,128)(2,1)S(1)} %get-tuple-element.304), channel_id=1, source_target_pairs={{0,4},{1,5},{2,6},{3,7},{4,0},{5,1},{6,2},{7,3},{8,12},{9,13},{10,... | collective-permute-start | bytes 1572872 | tf_op jit(solution)/shard_map/ppermute | solution.py:986
  249.4 23.5 %collective-permute-start.34 = (bf16[128,2048]{1,0:T(8,128)(2,1)S(1)}, bf16[128,2048]{1,0:T(8,128)(2,1)S(1)}, u32[]{:S(2)}, u32[]{:S(2)}) collective-permute-start(bf16[128,2048]{1,0:T(8,128)(2,1)S(1)} %collective-permute-done.32.refs_0_), channel_id=1, source_target_pairs={{0,1},{1,0},{2,3},{3,2},{4,5},{5,4},{6,7},{7,6},{8,9},{9,8},{10,11... | collective-permute-start | bytes 1572872 | tf_op jit(solution)/shard_map/ppermute | solution.py:986
  250.1 55.3 %collective-permute-start.36 = (bf16[128,2048]{1,0:T(8,128)(2,1)}, bf16[128,2048]{1,0:T(8,128)(2,1)}, u32[]{:S(2)}, u32[]{:S(2)}) collective-permute-start(bf16[128,2048]{1,0:T(8,128)(2,1)} %collective-permute-done.25.refs_5_), channel_id=1, source_target_pairs={{0,1},{1,0},{2,3},{3,2},{4,5},{5,4},{6,7},{7,6},{8,9},{9,8},{10,11... | collective-permute-start | bytes 1572872 | tf_op jit(solution)/shard_map/ppermute | solution.py:986
  273.7 27.2 %collective-permute-start.35 = (bf16[128,2048]{1,0:T(8,128)(2,1)S(1)}, bf16[128,2048]{1,0:T(8,128)(2,1)S(1)}, u32[]{:S(2)}, u32[]{:S(2)}) collective-permute-start(bf16[128,2048]{1,0:T(8,128)(2,1)S(1)} %collective-permute-done.33.refs_1_), channel_id=1, source_target_pairs={{0,1},{1,0},{2,3},{3,2},{4,5},{5,4},{6,7},{7,6},{8,9},{9,8},{10,11... | collective-permute-start | bytes 1572872 | tf_op jit(solution)/shard_map/ppermute | solution.py:986
  303.9 35.8 %collective-permute-start.37 = (bf16[256,2048]{1,0:T(8,128)(2,1)S(1)}, bf16[256,2048]{1,0:T(8,128)(2,1)S(1)}, u32[]{:S(2)}, u32[]{:S(2)}) collective-permute-start(bf16[256,2048]{1,0:T(8,128)(2,1)S(1)} %get-tuple-element.379), channel_id=1, source_target_pairs={{0,1},{1,0},{2,3},{3,2},{4,5},{5,4},{6,7},{7,6},{8,9},{9,8},{10,11... | collective-permute-start | bytes 3145736 | tf_op jit(solution)/shard_map/ppermute | solution.py:986
  358.2 37.2 %collective-permute-start.39 = (bf16[128,2048]{1,0:T(8,128)(2,1)}, bf16[128,2048]{1,0:T(8,128)(2,1)S(1)}, u32[]{:S(2)}, u32[]{:S(2)}) collective-permute-start(bf16[128,2048]{1,0:T(8,128)(2,1)} %add_convert_fusion.3), channel_id=1, source_target_pairs={{0,4},{1,5},{2,6},{3,7},{4,0},{5,1},{6,2},{7,3},{8,12},{9,13},{10,... | collective-permute-start | bytes 1572872 | tf_op jit(solution)/shard_map/ppermute | solution.py:986
  372.9 33.7 %collective-permute-start.41 = (bf16[128,2048]{1,0:T(8,128)(2,1)S(1)}, bf16[128,2048]{1,0:T(8,128)(2,1)S(1)}, u32[]{:S(2)}, u32[]{:S(2)}) collective-permute-start(bf16[128,2048]{1,0:T(8,128)(2,1)S(1)} %add_convert_fusion.2), channel_id=1, source_target_pairs={{0,4},{1,5},{2,6},{3,7},{4,0},{5,1},{6,2},{7,3},{8,12},{9,13},{10,... | collective-permute-start | bytes 1572872 | tf_op jit(solution)/shard_map/ppermute | solution.py:986
  375.2 53.9 %collective-permute-start.43 = (bf16[256,2048]{1,0:T(8,128)(2,1)S(1)}, bf16[256,2048]{1,0:T(8,128)(2,1)}, u32[]{:S(2)}, u32[]{:S(2)}) collective-permute-start(bf16[256,2048]{1,0:T(8,128)(2,1)S(1)} %slice.298), channel_id=1, source_target_pairs={{0,1},{1,0},{2,3},{3,2},{4,5},{5,4},{6,7},{7,6},{8,9},{9,8},{10,11... | collective-permute-start | bytes 3145736 | tf_op jit(solution)/shard_map/ppermute | solution.py:986
  376.8 54.0 %collective-permute-start.42 = (bf16[256,2048]{1,0:T(8,128)(2,1)}, bf16[256,2048]{1,0:T(8,128)(2,1)}, u32[]{:S(2)}, u32[]{:S(2)}) collective-permute-start(bf16[256,2048]{1,0:T(8,128)(2,1)} %get-tuple-element.377), channel_id=1, source_target_pairs={{0,1},{1,0},{2,3},{3,2},{4,5},{5,4},{6,7},{7,6},{8,9},{9,8},{10,11... | collective-permute-start | bytes 3145736 | tf_op jit(solution)/shard_map/ppermute | solution.py:986
  430.8 37.0 %collective-permute-start.44 = (bf16[80,1024]{1,0:T(8,128)(2,1)S(1)}, bf16[80,1024]{1,0:T(8,128)(2,1)S(1)}, u32[]{:S(2)}, u32[]{:S(2)}) collective-permute-start(bf16[80,1024]{1,0:T(8,128)(2,1)S(1)} %copy-done.48), channel_id=1, source_target_pairs={{8,0},{9,1},{10,2},{11,3},{12,4},{13,5},{14,6},{15,7},{16,8},{17,9... | collective-permute-start | bytes 491528 | tf_op jit(solution)/shard_map/ppermute | solution.py:986
  432.1 35.7 %collective-permute-start.45 = (bf16[80,1024]{1,0:T(8,128)(2,1)S(1)}, bf16[80,1024]{1,0:T(8,128)(2,1)S(1)}, u32[]{:S(2)}, u32[]{:S(2)}) collective-permute-start(bf16[80,1024]{1,0:T(8,128)(2,1)S(1)} %copy-done.48), channel_id=1, source_target_pairs={{16,0},{17,1},{18,2},{19,3},{20,4},{21,5},{22,6},{23,7},{24,8},{25... | collective-permute-start | bytes 491528 | tf_op jit(solution)/shard_map/ppermute | solution.py:986
  433.4 34.4 %collective-permute-start.46 = (bf16[80,1024]{1,0:T(8,128)(2,1)S(1)}, bf16[80,1024]{1,0:T(8,128)(2,1)S(1)}, u32[]{:S(2)}, u32[]{:S(2)}) collective-permute-start(bf16[80,1024]{1,0:T(8,128)(2,1)S(1)} %copy-done.48), channel_id=1, source_target_pairs={{24,0},{25,1},{26,2},{27,3},{28,4},{29,5},{30,6},{31,7}} | collective-permute-start | bytes 491528 | tf_op jit(solution)/shard_map/ppermute | solution.py:986
  434.7 49.1 %collective-permute-start.48 = (bf16[256,2048]{1,0:T(8,128)(2,1)S(1)}, bf16[256,2048]{1,0:T(8,128)(2,1)}, u32[]{:S(2)}, u32[]{:S(2)}) collective-permute-start(bf16[256,2048]{1,0:T(8,128)(2,1)S(1)} %add_convert_fusion.1), channel_id=1, source_target_pairs={{0,4},{1,5},{2,6},{3,7},{4,0},{5,1},{6,2},{7,3},{8,12},{9,13},{10,... | collective-permute-start | bytes 3145736 | tf_op jit(solution)/shard_map/ppermute | solution.py:986
  (76 other events, 879.9 us)
Sparse Core Ops, SparseCore 0:
  117.6 160.8 all-gather.2

commit v6 on v5

--- a/solution.py
+++ b/solution.py
@@ -830,7 +830,8 @@
     own_gu, own_dn = refs[:2]
     pair, refs = (refs[2], refs[3:]) if paired else (None, refs[2:])
     sums, refs = (refs[:2], refs[2:]) if carried_in else (None, refs)
-    out_ref, back_ref, h, c, gu, dn, out, back, row_sem, gu_sem, dn_sem = refs
+    results, (h, c, gu, dn, out, back, row_sem, gu_sem, dn_sem) = refs[:-9], refs[-9:]
+    n_out = h.shape[0] // results[0].shape[0]
     step, steps = pl.program_id(0), pl.num_programs(0)
     own_tiles = own_gu.shape[2] // tile if own else 0
 
@@ -909,11 +910,13 @@
 
     @pl.when(step == steps - 1)
     def _():
-        out_ref[...] = out[...].astype(out_ref.dtype)
-        back_ref[...] = back[...].astype(back_ref.dtype)
-
-
-def mlp(second, cot, own_gu, own_dn, pair=None, place=None, own=True, sums=()):
+        for total, blocks in ((out, results[:n_out]), (back, results[n_out:])):
+            size = blocks[0].shape[0]
+            for i, ref in enumerate(blocks):
+                ref[...] = total[i * size : (i + 1) * size].astype(ref.dtype)
+
+
+def mlp(second, cot, own_gu, own_dn, pair=None, place=None, own=True, sums=(), split=None):
     rows = tuple(v.shape[0] for v in second), tuple(v.shape[0] for v in cot)
     total = sum(rows[0])
     hidden = own_gu.shape[2]
@@ -922,7 +925,7 @@
     kind = F32 if pair is None else BF16
     if pair is None:
         place = jnp.zeros((1,), jnp.int32)
-    block = pl.BlockSpec((total, D), lambda i, p: (0, 0))
+    blocks = [n for n in split or (total, total) for _ in range(total // n)]
     arrays = (*second, *cot, own_gu, own_dn, *(() if pair is None else (pair,)), *sums)
     return pl.pallas_call(
         functools.partial(
@@ -937,7 +940,7 @@
             num_scalar_prefetch=1,
             grid=(shards * hidden // tile,),
             in_specs=[ANYWHERE] * len(arrays),
-            out_specs=[block, block],
+            out_specs=[pl.BlockSpec((n, D), lambda i, p: (0, 0)) for n in blocks],
             scratch_shapes=[
                 pltpu.VMEM((total, D), BF16),
                 pltpu.VMEM((total, D), BF16),
@@ -950,7 +953,7 @@
                 pltpu.SemaphoreType.DMA((2,)),
             ],
         ),
-        out_shape=[jax.ShapeDtypeStruct((total, D), kind)] * 2,
+        out_shape=[jax.ShapeDtypeStruct((n, D), kind) for n in blocks],
         compiler_params=pltpu.CompilerParams(vmem_limit_bytes=VMEM_LIMIT),
         cost_estimate=pl.CostEstimate(
             flops=12 * total * D * hidden * shards,
@@ -1110,19 +1113,16 @@
 
 
 def collect_near(grid, near, length):
-    blocks = [near[k * length : (k + 1) * length] for k in range(grid.xs)]
-    return [blocks[0]] + [grid.along_x(blocks[k], -k) for k in range(1, grid.xs)]
+    return [near[0]] + [grid.along_x(near[k], -k) for k in range(1, grid.xs)]
 
 
 def collect_far(grid, far, length, parts):
-    size = length // parts
     send, total = [], None
     for p in range(parts):
-        lo = p * size
         far = after(far, total)
-        total = far[lo : lo + size]
+        total = far[p]
         for k in range(1, grid.xs):
-            other = grid.along_x(far[k * length + lo : k * length + lo + size], -k)
+            other = grid.along_x(far[k * parts + p], -k)
             total = (total.astype(F32) + other.astype(F32)).astype(BF16)
         send.append(total)
     return send
@@ -1310,9 +1310,11 @@
     others = relay(grid, far[1:])[1:]
     far = far + [v for pieces in zip(moved, others) for v in pieces]
     shard = w_gate_up, w_down, *pair
-    near_out, near_grad = mlp(near, cot_near, *shard, own=False, sums=sums)
+    results = mlp(near, cot_near, *shard, own=False, sums=sums, split=(length, length))
+    near_out, near_grad = results[: grid.xs], results[grid.xs :]
     far, near_out, near_grad = after((far, near_out, near_grad))
-    far_out, far_grad = mlp(far, cot_far, *shard)
+    results = mlp(far, cot_far, *shard, split=(length, half))
+    far_out, far_grad = results[: grid.xs], results[grid.xs :]
     terms = collect_near(grid, near_grad, length)
     far_grad, terms = after((far_grad, terms))
     send = collect_far(grid, far_grad, length, 2)

time: 549 us -> 543 us (0.989)
  local copies, waits for them, and re-layouts: 54.3 us -> 46.8 us
    slice x5 -> x0, local copies, waits for them, and re-layouts: 7.89 us -> none  [the longest x2 4.43 us: collect_near(): blocks = [near[k * length:(k + 1) * length] for k in range(grid.xs)]]
  transfers between devices with their start and end apart: 57 -> 57, of which waited for: 22 -> 23; matrix products, arithmetic and copies ran while one was open for 14% -> 13% of each run, Pallas kernels for 34% -> 35%
where the time goes in v6:
time: 543 us; the launch traced here: 538 us
  Pallas kernels  202 us (37%)
  waiting for transfers between devices  155 us (29%)
  starting transfers between devices  72.3 us (13%)
  local copies, waits for them, and re-layouts  46.8 us (9%)
  other arithmetic  41.1 us (8%)
  between operations  19.3 us (4%)
    ppermute x56, waiting for transfers between devices, send(): lax.ppermute(v, ('seq', 'rows'), route)  151 us
    pallas_call x3, Pallas kernels, mlp(): pl.pallas_call(functools.partial(mlp_kernel, rows=rows, paired=pair is no...  78 us
    ppermute x56, starting transfers between devices, send(): lax.ppermute(v, ('seq', 'rows'), route)  72.3 us
    pallas_call x1, Pallas kernels, attend_back(): pl.pallas_call(attend_back_kernel, grid=(KV_HEADS,), in_specs=[s['q'], s[...  28.8 us
    pallas_call x2, Pallas kernels, project_q(): pl.pallas_call(functools.partial(project_q_kernel, counts=w.shapes(), siz...  19.7 us
    pallas_call x2, Pallas kernels, attend(): pl.pallas_call(attend_kernel, grid=(PER_HALF,), in_specs=[s['q'], s['qf']...  16 us
    pallas_call x1, Pallas kernels, inputs_back(): pl.pallas_call(functools.partial(inputs_back_kernel, counts=w.shapes(), s...  14.5 us
  transfers between devices with their start and end apart: 57, of which 23 were waited for; matrix products, arithmetic and copies ran while one was open for 13% of the time, Pallas kernels for 35%

profile of v6, /device:TPU:0, one launch (start us, length us, event | category | flops | bytes accessed | tf_op | source)
XLA Modules:
  0.0 537.7 jit_solution(16274682809203799397)
XLA Ops:
  10.1 4.0 collective-permute-start.2
  59.4 13.5 %collective-permute-done.8 = bf16[64,2048]{1,0:T(8,128)(2,1)S(1)} collective-permute-done((bf16[64,2048]{1,0:T(8,128)(2,1)S(1)}, bf16[64,2048]{1,0:T(8,128)(2,1)S(1)}, u32[]{:S(2)}, u32[]{:S(2)}) %collective-permute-start.8) | collective-permute-done | bytes 262176 | tf_op jit(solution)/shard_map/ppermute | solution.py:989
  73.7 3.5 collective-permute-done.9
  90.2 9.2 %maximum_maximum_fusion = bf16[1536,1024]{1,0:T(8,128)(2,1)} fusion(bf16[512,512]{1,0:T(8,128)(2,1)S(1)} %get-tuple-element.416, bf16[512,512]{1,0:T(8,128)(2,1)S(1)} %get-tuple-element.415, bf16[512,1024]{1,0:T(8,128)(2,1)S(1)} %get-tuple-element.414, bf16[512,1024]{1,0:T(8,128)(2,1)S(1)} %get-tuple-element.413), kind=kLoop, calls=%fused_computation | loop fusion | flops 12582912 | bytes 6291456 | tf_op jit(solution)/shard_map/concatenate | solution.py:1088
  99.5 11.8 %collective-permute-done.15.refs_4_ = bf16[128,2048]{1,0:T(8,128)(2,1)} collective-permute-done((bf16[128,2048]{1,0:T(8,128)(2,1)}, bf16[128,2048]{1,0:T(8,128)(2,1)}, u32[]{:S(2)}, u32[]{:S(2)}) %collective-permute-start.15) | collective-permute-done | bytes 524320 | tf_op jit(solution)/shard_map/ppermute | solution.py:989
  111.2 3.3 collective-permute-done.12.refs_4_
  128.4 9.2 %project_kv.1 = (bf16[256,1024]{1,0:T(8,128)(2,1)}, bf16[256,1024]{1,0:T(8,128)(2,1)}, bf16[208,1024]{1,0:T(8,128)(2,1)}, bf16[80,1024]{1,0:T(8,128)(2,1)}) custom-call(s32[32]{0:T(128)} %stack.164.refs_0_, bf16[256,3072]{1,0:T(8,128)(2,1)} %copy-done.3, bf16[256,3072]{1,0:T(8,128)(2,1)} %copy-done.4, bf16[256,3072]{1,0:T(8,128)(2,1)} %collective-permute-done.11.refs_3_, ...), custom_call_target="tpu_custom_call" | custom-call | flops 1073741824 | bytes 4194304 | tf_op jit(solution)/shard_map/project_kv/pallas_call | solution.py:229
  144.0 9.9 %project_q.2 = (bf16[256,2048]{1,0:T(8,128)(2,1)}, bf16[256,4096]{1,0:T(8,128)(2,1)}) custom-call(s32[32]{0:T(128)} %stack.164.refs_0_, bf16[256,3072]{1,0:T(8,128)(2,1)} %copy-done.3, bf16[256,3072]{1,0:T(8,128)(2,1)} %copy-done.4, bf16[256,3072]{1,0:T(8,128)(2,1)} %collective-permute-done.11.refs_3_, bf16[256,3072]{1,0:T(8,128)(2,1)} %collective-permute-done.12.refs_4_, ...), custom_call_target="tpu_custom_call" | custom-call | flops 1073741824 | bytes 4194304 | tf_op jit(solution)/shard_map/project_q/pallas_call | solution.py:270
  166.4 9.8 %project_q.3 = (bf16[256,2048]{1,0:T(8,128)(2,1)}, bf16[256,4096]{1,0:T(8,128)(2,1)}) custom-call(s32[32]{0:T(128)} %stack.164.refs_0_, bf16[256,3072]{1,0:T(8,128)(2,1)} %copy-done.3, bf16[256,3072]{1,0:T(8,128)(2,1)} %copy-done.4, bf16[256,3072]{1,0:T(8,128)(2,1)} %collective-permute-done.11.refs_3_, ...), custom_call_target="tpu_custom_call", output_to_operand_aliasing={{0}: (15, {}), {1}: (16, {})} | custom-call | flops 1073741824 | bytes 4194304 | tf_op jit(solution)/shard_map/project_q/pallas_call | solution.py:270
  176.2 8.0 %attend.2 = (bf16[256,2048]{1,0:T(8,128)(2,1)}, f32[256,2048]{1,0:T(8,128)}, f32[256,2048]{1,0:T(8,128)}) custom-call(bf16[256,2048]{1,0:T(8,128)(2,1)} %get-tuple-element.290.q_ref, bf16[256,4096]{1,0:T(8,128)(2,1)} %get-tuple-element.291.qf_ref, bf16[256,1024]{1,0:T(8,128)(2,1)} %get-tuple-element.273.kv_ref, bf16[256,1024]{1,0:T(8,128)(2,1)} %get-tuple-element.274.kf_ref, ...), custom_call_target="tpu_custom_call" | custom-call | flops 5000000000 | bytes 4194304 | tf_op jit(solution)/shard_map/attend/pallas_call | solution.py:404
  187.6 6.6 %collective-permute-done.23.refs_3_ = bf16[256,2048]{1,0:T(8,128)(2,1)} collective-permute-done((bf16[256,2048]{1,0:T(8,128)(2,1)S(1)}, bf16[256,2048]{1,0:T(8,128)(2,1)}, u32[]{:S(2)}, u32[]{:S(2)}) %collective-permute-start.23) | collective-permute-done | bytes 1048608 | tf_op jit(solution)/shard_map/ppermute | solution.py:989
  197.9 8.0 %attend.3 = (bf16[256,2048]{1,0:T(8,128)(2,1)}, f32[256,2048]{1,0:T(8,128)}, f32[256,2048]{1,0:T(8,128)}) custom-call(bf16[256,2048]{1,0:T(8,128)(2,1)} %get-tuple-element.290.q_ref, bf16[256,4096]{1,0:T(8,128)(2,1)} %get-tuple-element.291.qf_ref, ...), custom_call_target="tpu_custom_call", output_to_operand_aliasing={{0}: (11, {}), {1}: (12, {}), {2}: (13, {})} | custom-call | flops 5000000000 | bytes 4194304 | tf_op jit(solution)/shard_map/attend/pallas_call | solution.py:404
  207.5 9.9 %out_project.1 = (f32[256,2048]{1,0:T(8,128)}, bf16[256,2048]{1,0:T(8,128)(2,1)}, bf16[256,128]{1,0:T(8,128)(2,1)}, f32[256,128]{1,0:T(8,128)}) custom-call(s32[32]{0:T(128)} %stack.164.refs_0_, bf16[256,2048]{1,0:T(8,128)(2,1)} %copy-done.10, bf16[256,2048]{1,0:T(8,128)(2,1)} %copy-done.9, bf16[256,2048]{1,0:T(8,128)(2,1)} %collective-permute-done.23.refs_3_, ...), custom_call_target="tpu_custom_call" | custom-call | flops 2147483648 | bytes 8388608 | tf_op jit(solution)/shard_map/out_project/pallas_call | solution.py:695
  222.7 3.8 collective-permute-start.32
  226.5 22.8 %collective-permute-done.32.refs_0_ = bf16[128,2048]{1,0:T(8,128)(2,1)} collective-permute-done((bf16[128,2048]{1,0:T(8,128)(2,1)S(1)}, bf16[128,2048]{1,0:T(8,128)(2,1)}, u32[]{:S(2)}, u32[]{:S(2)}) %collective-permute-start.32) | collective-permute-done | bytes 524320 | tf_op jit(solution)/shard_map/ppermute | solution.py:989
  251.4 21.3 %mlp.3 = (f32[512,2048]{1,0:T(8,128)}, f32[512,2048]{1,0:T(8,128)}) custom-call(s32[1]{0:T(128)} %constant.643.clone.1.place_ref, bf16[256,2048]{1,0:T(8,128)(2,1)} %get-tuple-element.317.refs_0_, bf16[256,2048]{1,0:T(8,128)(2,1)} %copy-done.19, bf16[256,2048]{1,0:T(8,128)(2,1)} %bitcast.138, bf16[256,2048]{1,0:T(8,128)(2,1)} %collective-permute-done.refs_3_, ...), custom_call_target="tpu_custom_call" | custom-call | flops 12884901888 | bytes 12582912 | tf_op jit(solution)/shard_map/mlp/pallas_call | solution.py:930
  274.5 4.1 all-gather.3.cloned.1.call-done
  278.6 22.3 %mlp.4 = (bf16[256,2048]{1,0:T(8,128)(2,1)}, bf16[256,2048]{1,0:T(8,128)(2,1)}, bf16[256,2048]{1,0:T(8,128)(2,1)}, bf16[256,2048]{1,0:T(8,128)(2,1)}) custom-call(s32[1]{0:T(128)} %bitcast.57.place_ref, bf16[256,2048]{1,0:T(8,128)(2,1)} %get-tuple-element.317.refs_0_, bf16[256,2048]{1,0:T(8,128)(2,1)} %copy-done.19, bf16[256,2048]{1,0:T(8,128)(2,1)} %bitcast.139, ...), custom_call_target="tpu_custom_call" | custom-call | flops 12884901888 | bytes 12582912 | tf_op jit(solution)/shard_map/mlp/pallas_call | solution.py:930
  302.5 34.3 %mlp.5 = (bf16[256,2048]{1,0:T(8,128)(2,1)}, bf16[256,2048]{1,0:T(8,128)(2,1)}, bf16[128,2048]{1,0:T(8,128)(2,1)}, bf16[128,2048]{1,0:T(8,128)(2,1)}, bf16[128,2...) custom-call(s32[1]{0:T(128)} %bitcast.57.place_ref, bf16[128,2048]{1,0:T(8,128)(2,1)} %collective-permute-done.32.refs_0_, ...), custom_call_target="tpu_custom_call" | custom-call | flops 25769803776 | bytes 25165824 | tf_op jit(solution)/shard_map/mlp/pallas_call | solution.py:930
  337.6 12.0 %collective-permute-done.38 = bf16[128,2048]{1,0:T(8,128)(2,1)S(1)} collective-permute-done((bf16[128,2048]{1,0:T(8,128)(2,1)}, bf16[128,2048]{1,0:T(8,128)(2,1)S(1)}, u32[]{:S(2)}, u32[]{:S(2)}) %collective-permute-start.38) | collective-permute-done | bytes 524320 | tf_op jit(solution)/shard_map/ppermute | solution.py:989
  353.1 11.7 %collective-permute-done.40 = bf16[128,2048]{1,0:T(8,128)(2,1)S(1)} collective-permute-done((bf16[128,2048]{1,0:T(8,128)(2,1)}, bf16[128,2048]{1,0:T(8,128)(2,1)S(1)}, u32[]{:S(2)}, u32[]{:S(2)}) %collective-permute-start.40) | collective-permute-done | bytes 524320 | tf_op jit(solution)/shard_map/ppermute | solution.py:989
  369.3 20.0 %collective-permute-done.39 = bf16[128,2048]{1,0:T(8,128)(2,1)} collective-permute-done((bf16[128,2048]{1,0:T(8,128)(2,1)S(1)}, bf16[128,2048]{1,0:T(8,128)(2,1)}, u32[]{:S(2)}, u32[]{:S(2)}) %collective-permute-start.39) | collective-permute-done | bytes 524320 | tf_op jit(solution)/shard_map/ppermute | solution.py:989
  389.3 11.2 %collective-permute-done.41 = bf16[128,2048]{1,0:T(8,128)(2,1)} collective-permute-done((bf16[128,2048]{1,0:T(8,128)(2,1)S(1)}, bf16[128,2048]{1,0:T(8,128)(2,1)}, u32[]{:S(2)}, u32[]{:S(2)}) %collective-permute-start.41) | collective-permute-done | bytes 524320 | tf_op jit(solution)/shard_map/ppermute | solution.py:989
  402.8 10.5 %branch_back.1 = (f32[256,2048]{1,0:T(8,128)}, bf16[256,2048]{1,0:T(8,128)(2,1)}, f32[1,2048]{1,0:T(1,128)}, f32[128,2048]{1,0:T(8,128)}, f32[128,2048]{1,0:T(8,128)}) custom-call(s32[32]{0:T(128)} %stack.164.refs_0_, bf16[256,2048]{1,0:T(8,128)(2,1)} %copy-done.10, bf16[256,2048]{1,0:T(8,128)(2,1)} %copy-done.9, ...), custom_call_target="tpu_custom_call" | custom-call | flops 2147483648 | bytes 8388608 | tf_op jit(solution)/shard_map/branch_back/pallas_call | solution.py:749
  415.8 8.7 %scaled_grads.1 = (bf16[256,2048]{1,0:T(8,128)(2,1)}, f32[256,2048]{1,0:T(8,128)}, bf16[80,1024]{1,0:T(8,128)(2,1)}) custom-call(bf16[256,2048]{1,0:T(8,128)(2,1)} %get-tuple-element.362.ga_ref, f32[256,2048]{1,0:T(8,128)} %get-tuple-element.363.att_ref, f32[256,2048]{1,0:T(8,128)} %get-tuple-element.364.inv_ref, ...), custom_call_target="tpu_custom_call" | custom-call | tf_op jit(solution)/shard_map/scaled_grads/pallas_call | solution.py:457
  428.9 28.8 %attend_back.1 = (bf16[256,2048]{1,0:T(8,128)(2,1)}, f32[256,1024]{1,0:T(8,128)}, f32[256,1024]{1,0:T(8,128)}, bf16[128,1024]{1,0:T(8,128)(2,1)}, f32[32,64,128]{2,1,0:T(8,128)}, /*index=5*/f32[8,8,128]{2,1,0:T(8,128)}) custom-call(bf16[256,2048]{1,0:T(8,128)(2,1)} %get-tuple-element.290.q_ref, bf16[256,4096]{1,0:T(8,128)(2,1)} %get-tuple-element.291.qf_ref, ...), custom_call_target="tpu_custom_call" | custom-call | flops 15000000512 | bytes 4194304 | tf_op jit(solution)/shard_map/attend_back/pallas_call | solution.py:553
  464.4 6.6 %keys_back.1 = (bf16[256,512]{1,0:T(8,128)(2,1)}, bf16[256,512]{1,0:T(8,128)(2,1)}, f32[8,64,128]{2,1,0:T(8,128)}) custom-call(bf16[256,1024]{1,0:T(8,128)(2,1)} %get-tuple-element.273.kv_ref, bf16[256,1024]{1,0:T(8,128)(2,1)} %get-tuple-element.274.kf_ref, f32[256,1024]{1,0:T(8,128)} %get-tuple-element.382.dkv_ref, f32[256,1024]{1,0:T(8,128)} %get-tuple-element.383.dkf_ref, ...), custom_call_target="tpu_custom_call" | custom-call | tf_op jit(solution)/shard_map/keys_back/pallas_call | solution.py:640
  472.1 5.9 %collective-permute-done.48 = bf16[256,2048]{1,0:T(8,128)(2,1)S(1)} collective-permute-done((bf16[256,2048]{1,0:T(8,128)(2,1)S(1)}, bf16[256,2048]{1,0:T(8,128)(2,1)S(1)}, u32[]{:S(2)}, u32[]{:S(2)}) %collective-permute-start.48) | collective-permute-done | bytes 1048608 | tf_op jit(solution)/shard_map/ppermute | solution.py:989
  478.1 14.5 %inputs_back.1 = (f32[256,2048]{1,0:T(8,128)}, f32[1,2048]{1,0:T(1,128)}, f32[128,2048]{1,0:T(8,128)}, f32[128,3072]{1,0:T(8,128)}) custom-call(s32[32]{0:T(128)} %stack.164.refs_0_, bf16[256,3072]{1,0:T(8,128)(2,1)} %copy-done.3, bf16[256,3072]{1,0:T(8,128)(2,1)} %copy-done.4, bf16[256,3072]{1,0:T(8,128)(2,1)} %collective-permute-done.11.refs_3_, ...), custom_call_target="tpu_custom_call" | custom-call | flops 3221225472 | bytes 12582912 | tf_op jit(solution)/shard_map/inputs_back/pallas_call | solution.py:807
  498.7 4.5 collective-permute-done.50
  511.1 3.8 collective-permute-done.52
  514.9 5.7 %collective-permute-done.53 = bf16[8,8704]{1,0:T(8,128)(2,1)S(1)} collective-permute-done((bf16[8,8704]{1,0:T(8,128)(2,1)S(1)}, bf16[8,8704]{1,0:T(8,128)(2,1)S(1)}, u32[]{:S(2)}, u32[]{:S(2)}) %collective-permute-start.53) | collective-permute-done | bytes 139296 | tf_op jit(solution)/shard_map/ppermute | solution.py:989
  (330 shorter events, 159.0 us)
Async XLA Ops:
  7.3 271.3 %all-gather.3.cloned.1.call-start = ((), (), s32[]{:S(2)}) async-start(), calls=%async_computation | async-start | bytes 28311552 | tf_op jit(solution)/shard_map/all_gather | solution.py:1097
  10.1 39.8 %collective-permute-start.2 = (bf16[64,3072]{1,0:T(8,128)(2,1)}, bf16[64,3072]{1,0:T(8,128)(2,1)}, u32[]{:S(2)}, u32[]{:S(2)}) collective-permute-start(bf16[64,3072]{1,0:T(8,128)(2,1)} %pad_maximum_fusion.6), channel_id=1, source_target_pairs={{0,4},{1,5},{2,6},{3,7},{4,0},{5,1},{6,2},{7,3},{8,12},{9,13},{10,... | collective-permute-start | bytes 1179656 | tf_op jit(solution)/shard_map/ppermute | solution.py:989
  14.1 35.8 %collective-permute-start.3 = (bf16[64,3072]{1,0:T(8,128)(2,1)}, bf16[64,3072]{1,0:T(8,128)(2,1)}, u32[]{:S(2)}, u32[]{:S(2)}) collective-permute-start(bf16[64,3072]{1,0:T(8,128)(2,1)} %pad_maximum_fusion.6), channel_id=1, source_target_pairs={{0,6},{1,7},{2,0},{3,1},{4,2},{5,3},{6,4},{7,5},{8,14},{9,15},{10,... | collective-permute-start | bytes 1179656 | tf_op jit(solution)/shard_map/ppermute | solution.py:989
  15.5 33.4 %collective-permute-start.1 = (bf16[64,3072]{1,0:T(8,128)(2,1)}, bf16[64,3072]{1,0:T(8,128)(2,1)}, u32[]{:S(2)}, u32[]{:S(2)}) collective-permute-start(bf16[64,3072]{1,0:T(8,128)(2,1)} %pad_maximum_fusion.6), channel_id=1, source_target_pairs={{0,2},{1,3},{2,4},{3,5},{4,6},{5,7},{6,0},{7,1},{8,10},{9,11},{10,... | collective-permute-start | bytes 1179656 | tf_op jit(solution)/shard_map/ppermute | solution.py:989
  17.4 33.7 %collective-permute-start = (bf16[256,2048]{1,0:T(8,128)(2,1)}, bf16[256,2048]{1,0:T(8,128)(2,1)}, u32[]{:S(2)}, u32[]{:S(2)}) collective-permute-start(bf16[256,2048]{1,0:T(8,128)(2,1)} %bitcast.136), channel_id=1, source_target_pairs={{0,1},{1,0},{2,3},{3,2},{4,5},{5,4},{6,7},{7,6},{8,9},{9,8},{10,11... | collective-permute-start | bytes 3145736 | tf_op jit(solution)/shard_map/ppermute | solution.py:989
  51.1 22.6 %collective-permute-start.10 = (bf16[64,2048]{1,0:T(8,128)(2,1)S(1)}, bf16[64,2048]{1,0:T(8,128)(2,1)S(1)}, u32[]{:S(2)}, u32[]{:S(2)}) collective-permute-start(bf16[64,2048]{1,0:T(8,128)(2,1)S(1)} %copy-done.22), channel_id=1, source_target_pairs={{0,6},{1,7},{2,0},{3,1},{4,2},{5,3},{6,4},{7,5},{8,14},{9,15},{10,... | collective-permute-start | bytes 786440 | tf_op jit(solution)/shard_map/ppermute | solution.py:989
  54.3 22.9 %collective-permute-start.9 = (bf16[64,2048]{1,0:T(8,128)(2,1)S(1)}, bf16[64,2048]{1,0:T(8,128)(2,1)S(1)}, u32[]{:S(2)}, u32[]{:S(2)}) collective-permute-start(bf16[64,2048]{1,0:T(8,128)(2,1)S(1)} %copy-done.22), channel_id=1, source_target_pairs={{0,4},{1,5},{2,6},{3,7},{4,0},{5,1},{6,2},{7,3},{8,12},{9,13},{10,... | collective-permute-start | bytes 786440 | tf_op jit(solution)/shard_map/ppermute | solution.py:989
  56.2 21.9 %collective-permute-start.7 = (bf16[128,3072]{1,0:T(8,128)(2,1)S(1)}, bf16[128,3072]{1,0:T(8,128)(2,1)S(1)}, u32[]{:S(2)}, u32[]{:S(2)}) collective-permute-start(bf16[128,3072]{1,0:T(8,128)(2,1)S(1)} %pad_maximum_fusion.2), channel_id=1, source_target_pairs={{0,16},{1,17},{2,18},{3,19},{4,20},{5,21},{6,22},{7,23},{8,24},{9,... | collective-permute-start | bytes 2359304 | tf_op jit(solution)/shard_map/ppermute | solution.py:989
  57.7 20.3 %collective-permute-start.6 = (bf16[128,3072]{1,0:T(8,128)(2,1)S(1)}, bf16[128,3072]{1,0:T(8,128)(2,1)S(1)}, u32[]{:S(2)}, u32[]{:S(2)}) collective-permute-start(bf16[128,3072]{1,0:T(8,128)(2,1)S(1)} %pad_maximum_fusion.1), channel_id=1, source_target_pairs={{0,1},{1,0},{2,3},{3,2},{4,5},{5,4},{6,7},{7,6},{8,9},{9,8},{10,11... | collective-permute-start | bytes 2359304 | tf_op jit(solution)/shard_map/ppermute | solution.py:989
  78.9 35.7 %collective-permute-start.12 = (bf16[256,3072]{1,0:T(8,128)(2,1)S(1)}, bf16[256,3072]{1,0:T(8,128)(2,1)}, u32[]{:S(2)}, u32[]{:S(2)}) collective-permute-start(bf16[256,3072]{1,0:T(8,128)(2,1)S(1)} %constant_dynamic-update-slice_fusion.2.refs_2_), channel_id=1, source_target_pairs={{0,1},{1,0},{2,3},{3,2},{4,5},{5,4},{6,7},{7,6},{8,9},{9,8},{10,11... | collective-permute-start | bytes 4718600 | tf_op jit(solution)/shard_map/ppermute | solution.py:989
  80.4 34.2 %collective-permute-start.14 = (bf16[256,3072]{1,0:T(8,128)(2,1)S(1)}, bf16[256,3072]{1,0:T(8,128)(2,1)}, u32[]{:S(2)}, u32[]{:S(2)}) collective-permute-start(bf16[256,3072]{1,0:T(8,128)(2,1)S(1)} %constant_dynamic-update-slice_fusion.2.refs_2_), channel_id=1, source_target_pairs={{0,8},{1,9},{2,10},{3,11},{4,12},{5,13},{6,14},{7,15},{8,0},{9,1},... | collective-permute-start | bytes 4718600 | tf_op jit(solution)/shard_map/ppermute | solution.py:989
  80.5 37.0 %collective-permute-start.11 = (bf16[256,3072]{1,0:T(8,128)(2,1)S(1)}, bf16[256,3072]{1,0:T(8,128)(2,1)}, u32[]{:S(2)}, u32[]{:S(2)}) collective-permute-start(bf16[256,3072]{1,0:T(8,128)(2,1)S(1)} %constant_dynamic-update-slice_fusion.refs_1_), channel_id=1, source_target_pairs={{0,16},{1,17},{2,18},{3,19},{4,20},{5,21},{6,22},{7,23},{8,24},{9,... | collective-permute-start | bytes 4718600 | tf_op jit(solution)/shard_map/ppermute | solution.py:989
  82.1 35.4 %collective-permute-start.13 = (bf16[256,3072]{1,0:T(8,128)(2,1)S(1)}, bf16[256,3072]{1,0:T(8,128)(2,1)}, u32[]{:S(2)}, u32[]{:S(2)}) collective-permute-start(bf16[256,3072]{1,0:T(8,128)(2,1)S(1)} %constant_dynamic-update-slice_fusion.refs_1_), channel_id=1, source_target_pairs={{0,8},{1,9},{2,10},{3,11},{4,12},{5,13},{6,14},{7,15},{8,0},{9,1},... | collective-permute-start | bytes 4718600 | tf_op jit(solution)/shard_map/ppermute | solution.py:989
  84.7 26.6 %collective-permute-start.15 = (bf16[128,2048]{1,0:T(8,128)(2,1)}, bf16[128,2048]{1,0:T(8,128)(2,1)}, u32[]{:S(2)}, u32[]{:S(2)}) collective-permute-start(bf16[128,2048]{1,0:T(8,128)(2,1)} %get-tuple-element.420), channel_id=1, source_target_pairs={{0,4},{1,5},{2,6},{3,7},{4,0},{5,1},{6,2},{7,3},{8,12},{9,13},{10,... | collective-permute-start | bytes 1572872 | tf_op jit(solution)/shard_map/ppermute | solution.py:989
  156.0 31.6 %collective-permute-start.24 = (bf16[256,2048]{1,0:T(8,128)(2,1)S(1)}, bf16[256,2048]{1,0:T(8,128)(2,1)S(1)}, u32[]{:S(2)}, u32[]{:S(2)}) collective-permute-start(bf16[256,2048]{1,0:T(8,128)(2,1)S(1)} %constant_dynamic-update-slice_fusion.6.refs_2_), channel_id=1, source_target_pairs={{0,1},{1,0},{2,3},{3,2},{4,5},{5,4},{6,7},{7,6},{8,9},{9,8},{10,11... | collective-permute-start | bytes 3145736 | tf_op jit(solution)/shard_map/ppermute | solution.py:989
  158.5 35.7 %collective-permute-start.23 = (bf16[256,2048]{1,0:T(8,128)(2,1)S(1)}, bf16[256,2048]{1,0:T(8,128)(2,1)}, u32[]{:S(2)}, u32[]{:S(2)}) collective-permute-start(bf16[256,2048]{1,0:T(8,128)(2,1)S(1)} %constant_dynamic-update-slice_fusion.4.refs_1_), channel_id=1, source_target_pairs={{0,16},{1,17},{2,18},{3,19},{4,20},{5,21},{6,22},{7,23},{8,24},{9,... | collective-permute-start | bytes 3145736 | tf_op jit(solution)/shard_map/ppermute | solution.py:989
  161.9 25.7 %collective-permute-start.25 = (bf16[128,2048]{1,0:T(8,128)(2,1)}, bf16[128,2048]{1,0:T(8,128)(2,1)S(1)}, u32[]{:S(2)}, u32[]{:S(2)}) collective-permute-start(bf16[128,2048]{1,0:T(8,128)(2,1)} %get-tuple-element.289), channel_id=1, source_target_pairs={{0,4},{1,5},{2,6},{3,7},{4,0},{5,1},{6,2},{7,3},{8,12},{9,13},{10,... | collective-permute-start | bytes 1572872 | tf_op jit(solution)/shard_map/ppermute | solution.py:989
  220.5 28.8 %collective-permute-start.31 = (bf16[256,2048]{1,0:T(8,128)(2,1)}, bf16[256,2048]{1,0:T(8,128)(2,1)S(1)}, u32[]{:S(2)}, u32[]{:S(2)}) collective-permute-start(bf16[256,2048]{1,0:T(8,128)(2,1)} %get-tuple-element.317.refs_0_), channel_id=1, source_target_pairs={{0,1},{1,0},{2,3},{3,2},{4,5},{5,4},{6,7},{7,6},{8,9},{9,8},{10,11... | collective-permute-start | bytes 3145736 | tf_op jit(solution)/shard_map/ppermute | solution.py:989
  222.7 26.6 %collective-permute-start.32 = (bf16[128,2048]{1,0:T(8,128)(2,1)S(1)}, bf16[128,2048]{1,0:T(8,128)(2,1)}, u32[]{:S(2)}, u32[]{:S(2)}) collective-permute-start(bf16[128,2048]{1,0:T(8,128)(2,1)S(1)} %get-tuple-element.418), channel_id=1, source_target_pairs={{0,4},{1,5},{2,6},{3,7},{4,0},{5,1},{6,2},{7,3},{8,12},{9,13},{10,... | collective-permute-start | bytes 1572872 | tf_op jit(solution)/shard_map/ppermute | solution.py:989
  249.3 23.8 %collective-permute-start.33 = (bf16[128,2048]{1,0:T(8,128)(2,1)S(1)}, bf16[128,2048]{1,0:T(8,128)(2,1)S(1)}, u32[]{:S(2)}, u32[]{:S(2)}) collective-permute-start(bf16[128,2048]{1,0:T(8,128)(2,1)S(1)} %get-tuple-element.324), channel_id=1, source_target_pairs={{0,4},{1,5},{2,6},{3,7},{4,0},{5,1},{6,2},{7,3},{8,12},{9,13},{10,... | collective-permute-start | bytes 1572872 | tf_op jit(solution)/shard_map/ppermute | solution.py:989
  249.3 23.8 %collective-permute-start.34 = (bf16[128,2048]{1,0:T(8,128)(2,1)}, bf16[128,2048]{1,0:T(8,128)(2,1)S(1)}, u32[]{:S(2)}, u32[]{:S(2)}) collective-permute-start(bf16[128,2048]{1,0:T(8,128)(2,1)} %collective-permute-done.32.refs_0_), channel_id=1, source_target_pairs={{0,1},{1,0},{2,3},{3,2},{4,5},{5,4},{6,7},{7,6},{8,9},{9,8},{10,11... | collective-permute-start | bytes 1572872 | tf_op jit(solution)/shard_map/ppermute | solution.py:989
  250.2 52.3 %collective-permute-start.36 = (bf16[128,2048]{1,0:T(8,128)(2,1)S(1)}, bf16[128,2048]{1,0:T(8,128)(2,1)}, u32[]{:S(2)}, u32[]{:S(2)}) collective-permute-start(bf16[128,2048]{1,0:T(8,128)(2,1)S(1)} %copy-done.44), channel_id=1, source_target_pairs={{0,1},{1,0},{2,3},{3,2},{4,5},{5,4},{6,7},{7,6},{8,9},{9,8},{10,11... | collective-permute-start | bytes 1572872 | tf_op jit(solution)/shard_map/ppermute | solution.py:989
  274.0 27.0 %collective-permute-start.35 = (bf16[128,2048]{1,0:T(8,128)(2,1)S(1)}, bf16[128,2048]{1,0:T(8,128)(2,1)S(1)}, u32[]{:S(2)}, u32[]{:S(2)}) collective-permute-start(bf16[128,2048]{1,0:T(8,128)(2,1)S(1)} %collective-permute-done.33.refs_1_), channel_id=1, source_target_pairs={{0,1},{1,0},{2,3},{3,2},{4,5},{5,4},{6,7},{7,6},{8,9},{9,8},{10,11... | collective-permute-start | bytes 1572872 | tf_op jit(solution)/shard_map/ppermute | solution.py:989
  301.0 35.9 %collective-permute-start.37 = (bf16[256,2048]{1,0:T(8,128)(2,1)}, bf16[256,2048]{1,0:T(8,128)(2,1)S(1)}, u32[]{:S(2)}, u32[]{:S(2)}) collective-permute-start(bf16[256,2048]{1,0:T(8,128)(2,1)} %get-tuple-element.347), channel_id=1, source_target_pairs={{0,1},{1,0},{2,3},{3,2},{4,5},{5,4},{6,7},{7,6},{8,9},{9,8},{10,11... | collective-permute-start | bytes 3145736 | tf_op jit(solution)/shard_map/ppermute | solution.py:989
  351.3 38.0 %collective-permute-start.39 = (bf16[128,2048]{1,0:T(8,128)(2,1)S(1)}, bf16[128,2048]{1,0:T(8,128)(2,1)}, u32[]{:S(2)}, u32[]{:S(2)}) collective-permute-start(bf16[128,2048]{1,0:T(8,128)(2,1)S(1)} %add_convert_fusion.3), channel_id=1, source_target_pairs={{0,4},{1,5},{2,6},{3,7},{4,0},{5,1},{6,2},{7,3},{8,12},{9,13},{10,... | collective-permute-start | bytes 1572872 | tf_op jit(solution)/shard_map/ppermute | solution.py:989
  365.9 34.6 %collective-permute-start.41 = (bf16[128,2048]{1,0:T(8,128)(2,1)S(1)}, bf16[128,2048]{1,0:T(8,128)(2,1)}, u32[]{:S(2)}, u32[]{:S(2)}) collective-permute-start(bf16[128,2048]{1,0:T(8,128)(2,1)S(1)} %add_convert_fusion.2), channel_id=1, source_target_pairs={{0,4},{1,5},{2,6},{3,7},{4,0},{5,1},{6,2},{7,3},{8,12},{9,13},{10,... | collective-permute-start | bytes 1572872 | tf_op jit(solution)/shard_map/ppermute | solution.py:989
  367.2 57.2 %collective-permute-start.43 = (bf16[256,2048]{1,0:T(8,128)(2,1)}, bf16[256,2048]{1,0:T(8,128)(2,1)S(1)}, u32[]{:S(2)}, u32[]{:S(2)}) collective-permute-start(bf16[256,2048]{1,0:T(8,128)(2,1)} %get-tuple-element.377), channel_id=1, source_target_pairs={{0,1},{1,0},{2,3},{3,2},{4,5},{5,4},{6,7},{7,6},{8,9},{9,8},{10,11... | collective-permute-start | bytes 3145736 | tf_op jit(solution)/shard_map/ppermute | solution.py:989
  367.2 57.6 %collective-permute-start.42 = (bf16[256,2048]{1,0:T(8,128)(2,1)}, bf16[256,2048]{1,0:T(8,128)(2,1)}, u32[]{:S(2)}, u32[]{:S(2)}) collective-permute-start(bf16[256,2048]{1,0:T(8,128)(2,1)} %get-tuple-element.373), channel_id=1, source_target_pairs={{0,1},{1,0},{2,3},{3,2},{4,5},{5,4},{6,7},{7,6},{8,9},{9,8},{10,11... | collective-permute-start | bytes 3145736 | tf_op jit(solution)/shard_map/ppermute | solution.py:989
  424.9 37.0 %collective-permute-start.44 = (bf16[80,1024]{1,0:T(8,128)(2,1)}, bf16[80,1024]{1,0:T(8,128)(2,1)S(1)}, u32[]{:S(2)}, u32[]{:S(2)}) collective-permute-start(bf16[80,1024]{1,0:T(8,128)(2,1)} %get-tuple-element.378), channel_id=1, source_target_pairs={{8,0},{9,1},{10,2},{11,3},{12,4},{13,5},{14,6},{15,7},{16,8},{17,9... | collective-permute-start | bytes 491528 | tf_op jit(solution)/shard_map/ppermute | solution.py:989
  426.2 35.7 %collective-permute-start.45 = (bf16[80,1024]{1,0:T(8,128)(2,1)}, bf16[80,1024]{1,0:T(8,128)(2,1)}, u32[]{:S(2)}, u32[]{:S(2)}) collective-permute-start(bf16[80,1024]{1,0:T(8,128)(2,1)} %get-tuple-element.378), channel_id=1, source_target_pairs={{16,0},{17,1},{18,2},{19,3},{20,4},{21,5},{22,6},{23,7},{24,8},{25... | collective-permute-start | bytes 491528 | tf_op jit(solution)/shard_map/ppermute | solution.py:989
  427.5 34.4 %collective-permute-start.46 = (bf16[80,1024]{1,0:T(8,128)(2,1)}, bf16[80,1024]{1,0:T(8,128)(2,1)}, u32[]{:S(2)}, u32[]{:S(2)}) collective-permute-start(bf16[80,1024]{1,0:T(8,128)(2,1)} %get-tuple-element.378), channel_id=1, source_target_pairs={{24,0},{25,1},{26,2},{27,3},{28,4},{29,5},{30,6},{31,7}} | collective-permute-start | bytes 491528 | tf_op jit(solution)/shard_map/ppermute | solution.py:989
  428.8 49.3 %collective-permute-start.48 = (bf16[256,2048]{1,0:T(8,128)(2,1)S(1)}, bf16[256,2048]{1,0:T(8,128)(2,1)S(1)}, u32[]{:S(2)}, u32[]{:S(2)}) collective-permute-start(bf16[256,2048]{1,0:T(8,128)(2,1)S(1)} %add_convert_fusion.1), channel_id=1, source_target_pairs={{0,4},{1,5},{2,6},{3,7},{4,0},{5,1},{6,2},{7,3},{8,12},{9,13},{10,... | collective-permute-start | bytes 3145736 | tf_op jit(solution)/shard_map/ppermute | solution.py:989
  (76 other events, 948.2 us)
Sparse Core Ops, SparseCore 0:
  117.6 160.9 all-gather.2
